TPU v7x, 32 devices: a whole 2x2x4 slice. The times are simulated.
32 devices in a mesh: dp: 16 (over z, x, core), rep: 2 (over y).
Axes of the slice: x: 2, y: 2, z: 4, core: 2. Of those that a mesh axis runs over, the one named last changes fastest.
Arguments:
- block_input: bfloat16 [32, 512, 512], P(('dp', 'rep')), may hold values from -6 to 6
- segment_ids: int32 [32, 512], P(('dp', 'rep')), may hold values from 0 to 3, never falling along the last dimension, each value on 1 to 256 neighbouring positions
- cotangent: bfloat16 [32, 512, 512], P(('dp', 'rep')), may hold values from -6 to 6
- master_weights: float32 [3151872], P(('dp', 'rep')), may hold values from -2 to 2
- momentum: float32 [3151872], P(('dp', 'rep')), may hold values from -4096 to 4096
- weight_average: float32 [3151872], P(('dp', 'rep')), may hold values from -2 to 2
Outputs:
- block_output: float32 [32, 512, 512], P(('dp', 'rep'))
- input_grad: float32 [32, 512, 512], P(('dp', 'rep'))
- weight_grad: float32 [3151872], P(('dp', 'rep'))
- vector_grad: float32 [4096], P(('dp', 'rep'))
- new_momentum: float32 [3151872], P(('dp', 'rep'))
- new_average: float32 [3151872], P(('dp', 'rep'))
- new_weights: float32 [3151872], P(('dp', 'rep'))
Inputs may be any that keep to these rules, and one draw needn't show every extreme that they name: `segment_ids`: segment numbers never fall along a row, and every number occurs in each row.
All inputs are finite; a program needn't handle non-finite values.
Results may differ from a plain program's by a relative error of at most 0.025.
The roundings to bfloat16 on the way count: a program that leaves them out, or rounds other values in their place, can miss the bound.
Values may be sent and summed in bfloat16 or wider, within the bound.
No kernel may reach another device: no remote copies, remote signals or barrier semaphores. Data moves between devices by JAX's collectives and lax.ppermute only.
A program may use at most 128 MiB of HBM per device.

v0:
```python
import math

import jax
import jax.numpy as jnp
from jax import lax
from jax.sharding import PartitionSpec as P

FF = 2048
HEADS = 8
REC = 2


norm_eps = 1e-05
mom_decay = 0.9
avg_keep = 0.8
rate_base = 0.006


def unpack(flat_vec, width, hidden):
    offset = 4 * width * width
    attn_weight = flat_vec[:offset].reshape(width, 4 * width)
    w_in = flat_vec[offset : offset + width * hidden].reshape(width, hidden)
    offset = offset + width * hidden
    w_out = flat_vec[offset : offset + hidden * width].reshape(hidden, width)
    offset = offset + hidden * width
    bias_in = flat_vec[offset : offset + hidden]
    offset = offset + hidden
    vectors = flat_vec[offset : offset + 8 * width].reshape(8, width)
    return (attn_weight, w_in, w_out, bias_in, vectors)


def smooth_act(values):
    return jax.nn.gelu(values, approximate=True)


def norm_forward(resid, gain, shift):
    center = resid - jnp.mean(resid, axis=-1, keepdims=True)
    variance = jnp.mean(center * center, axis=-1, keepdims=True)
    inv_std = lax.rsqrt(variance + norm_eps)
    normed = center * inv_std
    return (normed * gain + shift, normed, inv_std)


def norm_backward(upstream, normed, inv_std, gain):
    gain_grad = jnp.sum(upstream * normed, axis=0)
    shift_grad = jnp.sum(upstream, axis=0)
    scaled = upstream * gain
    resid_grad = inv_std * (
        scaled
        - jnp.mean(scaled, axis=-1, keepdims=True)
        - normed * jnp.mean(scaled * normed, axis=-1, keepdims=True)
    )
    return (resid_grad, gain_grad, shift_grad)


def block_probs(query_blk, seg_blk, keys_heads, segment_row, scale_factor, lse_blk):
    scores = (
        jnp.einsum("qhd,khd->hqk", query_blk, keys_heads, preferred_element_type=jnp.float32)
        * scale_factor
    )
    allowed = seg_blk[:, None] == segment_row[None, :]
    scores = jnp.where(allowed[None], scores, -1e30)
    if lse_blk is None:
        peak = jnp.max(scores, axis=-1, keepdims=True)
        total = jnp.sum(jnp.exp(scores - peak), axis=-1, keepdims=True)
        lse_blk = peak + jnp.log(total)
    return (jnp.exp(scores - lse_blk), lse_blk)


def attention_forward(queries, keys_b, values_b, segment_row, scale_factor):
    length, width = queries.shape
    head_dim = width // HEADS
    block = min(512, length)
    count = length // block
    query_blocks = queries.reshape(count, block, HEADS, head_dim)
    seg_blocks = segment_row.reshape(count, block)
    keys_heads = keys_b.reshape(length, HEADS, head_dim)
    values_heads = values_b.reshape(length, HEADS, head_dim)

    def one_block(pair):
        query_blk, seg_blk = pair
        probs, lse_blk = block_probs(
            query_blk, seg_blk, keys_heads, segment_row, scale_factor, None
        )
        context = jnp.einsum(
            "hqk,khd->qhd",
            probs.astype(jnp.bfloat16),
            values_heads,
            preferred_element_type=jnp.float32,
        )
        return (context, lse_blk)

    context, lse = lax.map(one_block, (query_blocks, seg_blocks))
    return (context.reshape(length, width), lse)


def attention_backward(queries, keys_b, values_b, context_grad, segment_row, lse, scale_factor):
    length, width = queries.shape
    head_dim = width // HEADS
    block = min(512, length)
    count = length // block
    query_blocks = queries.reshape(count, block, HEADS, head_dim)
    grad_blocks = context_grad.reshape(count, block, HEADS, head_dim)
    seg_blocks = segment_row.reshape(count, block)
    keys_heads = keys_b.reshape(length, HEADS, head_dim)
    values_heads = values_b.reshape(length, HEADS, head_dim)

    def one_block(carry, item):
        key_acc, value_acc = carry
        query_blk, grad_blk, seg_blk, lse_blk = item
        probs, unused = block_probs(
            query_blk, seg_blk, keys_heads, segment_row, scale_factor, lse_blk
        )
        prob_grad = jnp.einsum(
            "qhd,khd->hqk", grad_blk, values_heads, preferred_element_type=jnp.float32
        )
        score_grad = (
            probs * (prob_grad - jnp.sum(prob_grad * probs, axis=-1, keepdims=True))
        ).astype(jnp.bfloat16)
        query_grad = (
            jnp.einsum("hqk,khd->qhd", score_grad, keys_heads, preferred_element_type=jnp.float32)
            * scale_factor
        )
        key_acc = (
            key_acc
            + jnp.einsum("hqk,qhd->khd", score_grad, query_blk, preferred_element_type=jnp.float32)
            * scale_factor
        )
        value_acc = value_acc + jnp.einsum(
            "hqk,qhd->khd", probs.astype(jnp.bfloat16), grad_blk, preferred_element_type=jnp.float32
        )
        return ((key_acc, value_acc), query_grad)

    zeros_heads = jnp.zeros((length, HEADS, head_dim), jnp.float32)
    (key_grad, value_grad), query_grad = lax.scan(
        one_block, (zeros_heads, zeros_heads), (query_blocks, grad_blocks, seg_blocks, lse)
    )
    return (
        query_grad.reshape(length, width).astype(jnp.bfloat16),
        key_grad.reshape(length, width).astype(jnp.bfloat16),
        value_grad.reshape(length, width).astype(jnp.bfloat16),
    )


def layer_forward(inputs, weights, segment_row):
    attn_weight, w_in, w_out, bias_in, vectors_low = weights
    vectors = vectors_low.astype(jnp.float32)
    length, width = inputs.shape
    scale_factor = 1.0 / math.sqrt(width // HEADS)
    inputs_b = inputs.astype(jnp.bfloat16)
    projected = jnp.dot(inputs_b, attn_weight[:, : 3 * width], preferred_element_type=jnp.float32)
    queries = (projected[:, :width] + vectors[0]).astype(jnp.bfloat16)
    keys_b = projected[:, width : 2 * width].astype(jnp.bfloat16)
    values_b = (projected[:, 2 * width :] + vectors[1]).astype(jnp.bfloat16)
    context, lse = attention_forward(queries, keys_b, values_b, segment_row, scale_factor)
    context_b = context.astype(jnp.bfloat16)
    attended = (
        jnp.dot(context_b, attn_weight[:, 3 * width :], preferred_element_type=jnp.float32)
        + vectors[2]
    )
    first, first_hat, first_std = norm_forward(inputs + attended, vectors[4], vectors[5])
    first_b = first.astype(jnp.bfloat16)
    pre_act = jnp.dot(first_b, w_in, preferred_element_type=jnp.float32) + bias_in.astype(
        jnp.float32
    )
    hidden_b = smooth_act(pre_act).astype(jnp.bfloat16)
    branch = jnp.dot(hidden_b, w_out, preferred_element_type=jnp.float32) + vectors[3]
    output, out_hat, out_std = norm_forward(first + branch, vectors[6], vectors[7])
    kept_parts = (
        vectors,
        inputs_b,
        queries,
        keys_b,
        values_b,
        lse,
        context_b,
        first_hat,
        first_std,
        first_b,
        pre_act,
        hidden_b,
        out_hat,
        out_std,
        scale_factor,
    )
    return (output, kept_parts)


def layer_backward(inputs, weights, segment_row, upstream):
    attn_weight, w_in, w_out, bias_in, vectors_low = weights
    unused, kept_parts = layer_forward(inputs, weights, segment_row)
    (
        vectors,
        inputs_b,
        queries,
        keys_b,
        values_b,
        lse,
        context_b,
        first_hat,
        first_std,
        first_b,
        pre_act,
        hidden_b,
        out_hat,
        out_std,
        scale_factor,
    ) = kept_parts
    width = inputs.shape[1]
    resid_two, gain_two, shift_two = norm_backward(upstream, out_hat, out_std, vectors[6])
    branch_grad = resid_two.astype(jnp.bfloat16)
    bias_two = jnp.sum(branch_grad.astype(jnp.float32), axis=0)
    w_out_grad = jnp.einsum("tf,td->fd", hidden_b, branch_grad, preferred_element_type=jnp.float32)
    hidden_grad = jnp.einsum(
        "td,fd->tf", branch_grad, w_out, preferred_element_type=jnp.float32
    ).astype(jnp.bfloat16)
    unused_act, act_pull = jax.vjp(smooth_act, pre_act)
    (pre_grad_full,) = act_pull(hidden_grad.astype(jnp.float32))
    pre_grad = pre_grad_full.astype(jnp.bfloat16)
    bias_one = jnp.sum(pre_grad.astype(jnp.float32), axis=0)
    w_in_grad = jnp.einsum("td,tf->df", first_b, pre_grad, preferred_element_type=jnp.float32)
    first_grad = resid_two + jnp.einsum(
        "tf,df->td", pre_grad, w_in, preferred_element_type=jnp.float32
    )
    resid_one, gain_one, shift_one = norm_backward(first_grad, first_hat, first_std, vectors[4])
    attend_grad = resid_one.astype(jnp.bfloat16)
    bias_attend = jnp.sum(attend_grad.astype(jnp.float32), axis=0)
    w_o_grad = jnp.einsum("td,te->de", context_b, attend_grad, preferred_element_type=jnp.float32)
    context_grad = jnp.einsum(
        "te,de->td", attend_grad, attn_weight[:, 3 * width :], preferred_element_type=jnp.float32
    ).astype(jnp.bfloat16)
    query_grad, key_grad, value_grad = attention_backward(
        queries, keys_b, values_b, context_grad, segment_row, lse, scale_factor
    )
    bias_query = jnp.sum(query_grad.astype(jnp.float32), axis=0)
    bias_value = jnp.sum(value_grad.astype(jnp.float32), axis=0)
    joined_grad = jnp.concatenate([query_grad, key_grad, value_grad], axis=1)
    w_qkv_grad = jnp.einsum("td,te->de", inputs_b, joined_grad, preferred_element_type=jnp.float32)
    input_grad = resid_one + jnp.einsum(
        "te,de->td", joined_grad, attn_weight[:, : 3 * width], preferred_element_type=jnp.float32
    )
    attn_grad = jnp.concatenate([w_qkv_grad, w_o_grad], axis=1)
    vector_grads = jnp.stack(
        [bias_query, bias_value, bias_attend, bias_two, gain_one, shift_one, gain_two, shift_two]
    )
    flat_grad = jnp.concatenate(
        [
            attn_grad.reshape(-1),
            w_in_grad.reshape(-1),
            w_out_grad.reshape(-1),
            bias_one,
            vector_grads.reshape(-1),
        ]
    )
    return (input_grad, flat_grad)


def shards(block_input, segment_ids, cotangent, master_weights, momentum, weight_average):
    width = block_input.shape[2]
    length = block_input.shape[1]
    segment_row = segment_ids[0]
    shard_low = master_weights.astype(jnp.bfloat16)
    state = block_input[0].astype(jnp.float32)
    stored = []
    for layer_index in range(REC):
        gathered = lax.all_gather(shard_low, ("dp", "rep"), axis=0, tiled=True)
        stored.append(state)
        state, unused = layer_forward(state, unpack(gathered, width, FF), segment_row)
    block_output = state[None]
    upstream = cotangent[0].astype(jnp.float32)
    grad_total = jnp.zeros(
        (master_weights.shape[0] * lax.axis_size("dp") * lax.axis_size("rep"),), jnp.float32
    )
    for layer_index in reversed(range(REC)):
        gathered = lax.all_gather(shard_low, ("dp", "rep"), axis=0, tiled=True)
        upstream, flat_grad = layer_backward(
            stored[layer_index], unpack(gathered, width, FF), segment_row, upstream
        )
        grad_total = grad_total + flat_grad
    vector_total = grad_total[grad_total.shape[0] - 8 * width :]
    weight_grad, vector_grad = (
        lax.psum_scatter(grad_total, ("dp", "rep"), scatter_dimension=0, tiled=True),
        lax.psum_scatter(vector_total, ("dp", "rep"), scatter_dimension=0, tiled=True),
    )
    token_count = block_input.shape[0] * length * lax.axis_size("dp") * lax.axis_size("rep")
    rate = rate_base / math.sqrt(token_count)
    new_momentum = mom_decay * momentum + weight_grad
    new_weights = master_weights - rate * (weight_grad + mom_decay * new_momentum)
    new_average = avg_keep * weight_average + (1.0 - avg_keep) * new_weights
    return (
        block_output,
        upstream[None],
        weight_grad,
        vector_grad,
        new_momentum,
        new_average,
        new_weights,
    )


def solution(mesh):
    return jax.shard_map(
        shards,
        mesh=mesh,
        in_specs=(
            P(("dp", "rep"), None, None),
            P(("dp", "rep"), None),
            P(("dp", "rep"), None, None),
            P(("dp", "rep")),
            P(("dp", "rep")),
            P(("dp", "rep")),
        ),
        out_specs=(
            P(("dp", "rep"), None, None),
            P(("dp", "rep"), None, None),
            P(("dp", "rep")),
            P(("dp", "rep")),
            P(("dp", "rep")),
            P(("dp", "rep")),
            P(("dp", "rep")),
        ),
        check_vma=False,
    )
```

profile of v0, /device:TPU:0, one launch (start us, length us, event | category | flops | bytes accessed | tf_op | source)
XLA Modules:
  0.0 588.3 jit_solution(4096382887517347770)
XLA Ops:
  8.3 3.1 broadcast.212
  11.3 4.4 dynamic-update-slice
  18.1 157.7 %all-reduce.6.cloned.1.call-done = bf16[3151872]{0:T(1024)(128)(2,1)} async-done(((bf16[3151872]{0:T(1024)(128)(2,1)}), bf16[3151872]{0:T(1024)(128)(2,1)}) %all-reduce.6.cloned.1.call-update) | async-done | bytes 6303760
  175.7 5.6 fusion.85
  181.3 2.8 slice.170
  191.0 2.4 convolution_convert_fusion.7
  194.1 2.8 slice.183
  196.9 4.5 slice.186
  203.6 2.2 fusion.89
  209.5 2.5 copy.97
  212.1 2.5 copy.98
  214.6 2.0 copy.63
  216.6 1.7 add_convert_fusion
  218.4 2.7 fusion.1
  222.9 2.3 convolution_convert_fusion.6
  226.1 1.8 fusion.77
  228.0 2.2 fusion.91
  232.4 3.8 convert_reduce_fusion.1
  236.2 1.9 multiply_reduce_fusion.4
  239.0 3.0 multiply_reduce_fusion.1
  242.0 2.8 multiply_convert_fusion.1
  247.3 2.4 convert_reduce_fusion.9
  253.1 3.8 convert_reduce_fusion
  259.7 3.2 multiply_reduce_fusion
  262.8 3.1 convert_reduce_fusion.5
  266.0 3.3 convolution_bitcast_fusion.3
  269.2 2.6 multiply_convert_fusion
  275.8 4.3 convolution_bitcast_fusion.2
  280.1 4.0 convolution_bitcast_fusion.4
  284.2 3.3 convolution_bitcast_fusion.5
  287.5 2.7 fusion.52
  291.0 5.2 copy.104
  297.1 2.4 pad_maximum_fusion
  299.5 5.6 copy.79
  305.1 3.1 copy.103
  308.3 2.4 constant_dynamic-update-slice_fusion.9
  311.9 3.0 copy.105
  315.2 3.4 copy.101
  318.7 2.9 copy.100
  327.9 1.9 copy-done.3
  330.1 1.9 copy-done.4
  332.6 5.1 add.329
  340.2 3.3 fusion.31
  343.6 2.6 copy.81
  346.2 2.5 copy.80
  348.7 41.2 %all-reduce.2 = f32[4096]{0:T(1024)S(1)} all-reduce(f32[4096]{0:T(1024)S(1)} %slice.215), channel_id=3, replica_groups=mesh['dp'=16,'rep'=2] {'dp','rep'}, use_global_device_ids=true, to_apply=%region_41.42.clone | all-reduce | flops 4096 | bytes 32768
  390.5 188.1 %all-reduce.8.cloned.1.call-done = f32[3151872]{0:T(1024)} async-done(((f32[3151872]{0:T(1024)}), f32[3151872]{0:T(1024)}) %all-reduce.8.cloned.1.call-update) | async-done | bytes 12607504
  578.7 2.4 multiply_add_fusion.3
  (227 shorter events, 48.0 us)
Async XLA Ops:
  7.2 168.6 %all-reduce.6.cloned.1.call-start = ((), (), s32[]{:S(2)}) async-start(), calls=%async_computation | async-start | bytes 12607488
  11.3 4.5 copy-start.33
  11.3 5.5 copy-start.55
  184.1 9.2 %copy-start.5 = (bf16[512,2048]{1,0:T(8,128)(2,1)}, bf16[512,2048]{1,0:T(8,128)(2,1)S(1)}, u32[]{:S(2)}) copy-start(bf16[512,2048]{1,0:T(8,128)(2,1)S(1)} %slice.170) | copy-start | bytes 6291460
  186.2 3.3 copy-start.38
  187.7 3.2 copy-start
  202.9 2.9 copy-start.22
  218.4 2.8 copy-start.20
  225.3 2.7 copy-start.47
  228.0 4.4 copy-start.25
  232.4 3.8 copy-start.57
  238.5 11.1 %copy-start.11 = (f32[512,512]{0,1:T(8,128)}, f32[512,512]{0,1:T(8,128)S(1)}, u32[]{:S(2)}) copy-start(f32[512,512]{0,1:T(8,128)S(1)} %get-tuple-element.192) | copy-start | bytes 3145732
  242.0 2.9 copy-start.17
  245.9 3.8 copy-start.51
  247.3 2.4 copy-start.53
  247.3 2.4 copy-start.30
  249.7 3.4 copy-start.37
  251.5 5.4 copy-start.43
  251.5 8.0 %slice-start = ((s8[8388608]{0:T(1024)(128)(4,1)}), s8[4194304]{0:T(1024)(128)(4,1)S(1)}, s32[]{:S(2)}) async-start(s8[8388608]{0:T(1024)(128)(4,1)} %bitcast.145), calls=%async_computation.2 | async-start | bytes 8388608
  253.1 6.4 %slice-start.1 = ((s8[8388608]{0:T(1024)(128)(4,1)}), s8[4194304]{0:T(1024)(128)(4,1)S(1)}, s32[]{:S(2)}) async-start(s8[8388608]{0:T(1024)(128)(4,1)} %bitcast.145), calls=%async_computation.3 | async-start | bytes 8388608
  259.1 15.3 %copy-start.9 = (f32[512,512]{0,1:T(8,128)}, f32[512,512]{0,1:T(8,128)S(1)}, u32[]{:S(2)}) copy-start(f32[512,512]{0,1:T(8,128)S(1)} %get-tuple-element.188) | copy-start | bytes 3145732
  269.2 2.6 copy-start.16
  272.9 23.2 %copy-start.49 = (bf16[8,64,512]{2,1,0:T(8,128)(2,1)}, bf16[8,64,512]{2,1,0:T(8,128)(2,1)S(1)}, u32[]{:S(2)}) copy-start(bf16[8,64,512]{2,1,0:T(8,128)(2,1)S(1)} %get-tuple-element.237) | copy-start | bytes 1572868
  272.9 2.5 copy-start.24
  272.9 2.9 copy-start.44
  274.3 21.8 %copy-start.50 = (bf16[8,64,512]{2,1,0:T(8,128)(2,1)}, bf16[8,64,512]{2,1,0:T(8,128)(2,1)S(1)}, u32[]{:S(2)}) copy-start(bf16[8,64,512]{2,1,0:T(8,128)(2,1)S(1)} %fusion.37) | copy-start | bytes 1572868
  275.8 4.3 copy-start.26
  275.8 4.3 copy-start.58
  280.1 4.0 copy-start.41
  284.2 3.3 copy-start.31
  284.2 3.3 copy-start.52
  284.2 3.3 copy-start.54
  284.2 3.3 copy-start.65
  287.5 2.8 copy-start.12
  287.5 2.8 copy-start.48
  290.9 5.2 copy-start.34
  291.0 5.2 copy-start.63
  308.2 3.7 copy-start.27
  311.9 3.2 copy-start.62
  315.2 3.5 copy-start.1
  318.6 2.9 copy-start.32
  321.8 3.3 slice-start.4
  322.8 3.6 slice-start.5
  322.8 4.8 copy-start.2
  338.4 240.3 %all-reduce.8.cloned.1.call-start = ((), (), s32[]{:S(2)}) async-start(), calls=%async_computation.1 | async-start | bytes 25214976
  343.6 235.1 %copy-start.42 = (f32[98496]{0:T(1024)S(1)}, f32[98496]{0:T(1024)}, u32[]{:S(2)}) copy-start(f32[98496]{0:T(1024)} %param.9) | copy-start | bytes 1181956
  343.6 235.1 %copy-start.59 = (f32[98496]{0:T(1024)S(1)}, f32[98496]{0:T(1024)}, u32[]{:S(2)}) copy-start(f32[98496]{0:T(1024)} %param.11) | copy-start | bytes 1181956
  343.6 235.1 %copy-start.60 = (f32[98496]{0:T(1024)S(1)}, f32[98496]{0:T(1024)}, u32[]{:S(2)}) copy-start(f32[98496]{0:T(1024)} %param.10) | copy-start | bytes 1181956
  (26 other events, 47.9 us)
Sparse Core Ops, SparseCore 0:
  15.9 159.7 all-reduce.5
  345.5 233.1 all-reduce.7
where the time goes:
time: 597 us; the launch traced here: 588 us
  waiting for transfers between devices  347 us (58%)
  local copies, waits for them, and re-layouts  84.4 us (14%)
  matrix products  72.2 us (12%)
  blocking collectives  41.2 us (7%)
  other arithmetic  28.3 us (5%)
  between operations  15.5 us (3%)
    unnamed x4, waiting for transfers between devices  347 us
    unnamed x169, local copies, waits for them, and re-layouts  57.5 us
    unnamed x1, blocking collectives  41.2 us
  transfers between devices with their start and end apart: 2, of which 2 were waited for; matrix products, arithmetic and copies ran while one was open for 2% of the time, Pallas kernels for 0%

commit v1 on v0

v1 whole, which is shorter than its diff:
```python
import functools
import math

import jax
import jax.numpy as jnp
from jax import lax
from jax.experimental import pallas as pl
from jax.experimental.pallas import tpu as pltpu
from jax.sharding import PartitionSpec as P

FF = 2048
HEADS = 8
REC = 2
TILE = 16
LANES = 128

norm_eps = 1e-05
mom_decay = 0.9
avg_keep = 0.8
rate_base = 0.006

BF = jnp.bfloat16
F32 = jnp.float32


def dot(a, b):
    return lax.dot_general(a, b, (((1,), (0,)), ((), ())), preferred_element_type=F32)


def dot_t(a, b):
    return lax.dot_general(a, b, (((1,), (1,)), ((), ())), preferred_element_type=F32)


def t_dot(a, b):
    return lax.dot_general(a, b, (((0,), (0,)), ((), ())), preferred_element_type=F32)


def one_hot_swap(outer, inner):
    size = outer * inner
    row = lax.broadcasted_iota(jnp.int32, (size, size), 0)
    col = lax.broadcasted_iota(jnp.int32, (size, size), 1)
    shift = inner.bit_length() - 1
    want = (row & (inner - 1)) * outer + (row >> shift)
    return jnp.where(col == want, 1.0, 0.0).astype(F32).astype(BF)


def unpack_weights(flat, wa, wi, wo, b1, vec, width):
    per = 4 * width // LANES
    swap = one_hot_swap(per, 256 // per)
    groups = width * per // 512

    def wide(dst, base):
        def body(g, carry):
            first = flat[pl.ds(pl.multiple_of(base + g * 512, 256), 256), :]
            second = flat[pl.ds(pl.multiple_of(base + g * 512 + 256, 256), 256), :]
            out = dot(swap, jnp.concatenate([first, second], axis=1)).astype(BF)
            n = 256 // per
            for c in range(per):
                piece = out[c * n : (c + 1) * n]
                dst[pl.ds(pl.multiple_of(g * 2 * n, n), n), c * LANES : (c + 1) * LANES] = piece[:, :LANES]
                dst[pl.ds(pl.multiple_of(g * 2 * n + n, n), n), c * LANES : (c + 1) * LANES] = piece[:, LANES:]
            return carry

        lax.fori_loop(0, groups, body, 0, unroll=2)

    wide(wa, 0)
    wide(wi, width * per)
    per_out = width // LANES
    swap_out = one_hot_swap(per_out, 256 // per_out)
    base = 2 * width * per

    def narrow(g, carry):
        first = flat[pl.ds(pl.multiple_of(base + g * 512, 256), 256), :]
        second = flat[pl.ds(pl.multiple_of(base + g * 512 + 256, 256), 256), :]
        out = dot(swap_out, jnp.concatenate([first, second], axis=1)).astype(BF)
        n = 256 // per_out
        for c in range(per_out):
            piece = out[c * n : (c + 1) * n]
            wo[pl.ds(pl.multiple_of(g * 2 * n, n), n), c * LANES : (c + 1) * LANES] = piece[:, :LANES]
            wo[pl.ds(pl.multiple_of(g * 2 * n + n, n), n), c * LANES : (c + 1) * LANES] = piece[:, LANES:]
        return carry

    lax.fori_loop(0, FF * per_out // 512, narrow, 0, unroll=2)
    base = base + FF * per_out
    tail = flat[base : base + FF // LANES + 8 * per_out, :].astype(F32)
    for c in range(FF // LANES):
        b1[0:1, c * LANES : (c + 1) * LANES] = tail[c : c + 1]
    for r in range(8):
        for c in range(per_out):
            k = FF // LANES + r * per_out + c
            vec[r : r + 1, c * LANES : (c + 1) * LANES] = tail[k : k + 1]


def norm_stats(resid):
    center = resid - jnp.mean(resid, axis=-1, keepdims=True)
    variance = jnp.mean(center * center, axis=-1, keepdims=True)
    inv = lax.rsqrt(variance + norm_eps)
    return center * inv, inv


def norm_grad(upstream, normed, inv, gain):
    scaled = upstream * gain
    m0 = jnp.mean(scaled, axis=-1, keepdims=True)
    m1 = jnp.mean(scaled * normed, axis=-1, keepdims=True)
    return inv * (scaled - m0 - normed * m1)


def colsum(v):
    return jnp.sum(v, axis=0, keepdims=True)


def lane_mask(which, dtype):
    lane = lax.broadcasted_iota(jnp.int32, (1, LANES), 1)
    keep = (lane < 64) if which == 0 else (lane >= 64)
    return jnp.where(keep, 1.0, 0.0).astype(F32).astype(dtype)


C0 = math.sqrt(2.0 / math.pi)


def gelu_pair(u):
    u2 = u * u
    inner = u * (C0 + (C0 * 0.044715) * u2)
    half = 0.5 + 0.5 * jnp.tanh(inner)
    g = u * half
    slope = half + 2.0 * g * (1.0 - half) * (C0 + (3.0 * C0 * 0.044715) * u2)
    return g, slope


def window_starts(shards, tiles):
    return [i * tiles // shards for i in range(shards + 1)]


def own_index():
    return lax.axis_index("dp") * lax.axis_size("rep") + lax.axis_index("rep")


def load_windows(w_refs, pieces, flat, edge, sem, shards):
    tiles = flat.shape[0] // TILE
    rows = [ref.shape[-2] for ref in w_refs]
    half = rows[0]
    base = tiles // shards * TILE
    me = own_index()
    copies = []
    for ref, (part, entries) in zip(w_refs, pieces):
        for pos, rel in entries:
            src = ref
            for k in pos:
                src = src.at[k]
            owner = jnp.bitwise_xor(me, rel)
            start = pl.multiple_of((owner * tiles // shards) * TILE, TILE)
            if part == 0:
                moves = [(src, flat.at[pl.ds(start, half)])]
            else:
                moves = [
                    (src.at[pl.ds(0, base - half)], flat.at[pl.ds(pl.multiple_of(start + half, TILE), base - half)]),
                    (src.at[pl.ds(base - half, 2 * TILE)], edge.at[owner]),
                ]
            for a, b in moves:
                copies.append(pltpu.make_async_copy(a, b, sem.at[len(copies)]))
                copies[-1].start()
    for copy in copies:
        copy.wait()
    starts = window_starts(shards, tiles)
    for i in range(shards):
        nxt = starts[i + 1]
        low = edge[i, 0:TILE, :]
        if nxt - starts[i] == base // TILE:
            if i + 1 < shards:
                flat[nxt * TILE : (nxt + 1) * TILE, :] = flat[nxt * TILE : (nxt + 1) * TILE, :] + low
        else:
            flat[(nxt - 1) * TILE : nxt * TILE, :] = low
            if i + 1 < shards:
                flat[nxt * TILE : (nxt + 1) * TILE, :] = flat[nxt * TILE : (nxt + 1) * TILE, :] + edge[i, TILE : 2 * TILE, :]


def store_windows(g_refs, flat, edge, sem, shards, vec_rows):
    tiles = flat.shape[0] // TILE
    half = g_refs[0].shape[-2]
    whole = 2 * half
    starts = window_starts(shards, tiles)
    last = lax.broadcasted_iota(jnp.int32, (TILE, LANES), 0) == TILE - 1
    for i in range(shards):
        low = starts[i] * TILE + whole - TILE
        if low + TILE <= flat.shape[0]:
            tile = flat[low : low + TILE, :].astype(F32)
        else:
            tile = jnp.zeros((TILE, LANES), F32)
        edge[i, 0:TILE, :] = jnp.where(last, vec_rows[i : i + 1], tile).astype(BF)
    me = own_index()
    copies = []
    for part in range(2):
        for rc in range(2):
            ref = g_refs[2 * rc + part]
            for r0 in range(2):
                for r1 in range(2):
                    rx, ry = (r0, r1) if part == 0 else (r1, r0)
                    for rz in range(4):
                        owner = jnp.bitwise_xor(me, rz * 8 + rx * 4 + rc * 2 + ry)
                        start = pl.multiple_of((owner * tiles // shards) * TILE, TILE)
                        dst = ref.at[r0].at[r1].at[rz]
                        if part == 0:
                            moves = [(flat.at[pl.ds(start, half)], dst)]
                        else:
                            moves = [
                                (flat.at[pl.ds(pl.multiple_of(start + half, TILE), half - TILE)], dst.at[pl.ds(0, half - TILE)]),
                                (edge.at[owner].at[pl.ds(0, TILE)], dst.at[pl.ds(half - TILE, TILE)]),
                            ]
                        for a, b in moves:
                            copies.append(pltpu.make_async_copy(a, b, sem.at[len(copies)]))
                            copies[-1].start()
    for copy in copies:
        copy.wait()


def pack_kernel(x_ref, a_ref, b_ref):
    me = own_index()
    v = x_ref[...]
    rows = v.shape[0]
    lane = lax.broadcasted_iota(jnp.int32, v.shape, 1)
    turned = pltpu.roll(v, 64, 1)
    moved = jnp.where(lane >= 64, turned, pltpu.roll(turned, 1, 0))
    odd = (me & 1) == 1
    v = jnp.where(odd, moved, v)
    shift = ((me * 192) & 2047) >> 7
    v = pltpu.roll(v, shift, 0).astype(BF)
    a_ref[...] = v[: rows // 2]
    b_ref[...] = v[rows // 2 :]


def finish_kernel(*refs):
    parts = []
    for h in range(2):
        total = None
        for ref in refs[4 * h : 4 * h + 4]:
            v = ref[...].astype(F32)
            total = v if total is None else total + v
        parts.append(total)
    out_ref, vec_ref = refs[8:]
    v = jnp.concatenate(parts, axis=0)
    rows = v.shape[0]
    vec_ref[...] = v[rows - 8 :]
    me = own_index()
    shift = ((me * 192) & 2047) >> 7
    v = pltpu.roll(v, rows - shift, 0)
    lane = lax.broadcasted_iota(jnp.int32, v.shape, 1)
    turned = pltpu.roll(v, 64, 1)
    moved = jnp.where(lane < 64, turned, pltpu.roll(turned, rows - 1, 0))
    odd = (me & 1) == 1
    out_ref[...] = jnp.where(odd, moved, v)


ROWB = 256
CHUNK = 512


def core_kernel(*refs, width, length, shards, pieces):
    n_in = 1 if pieces is None else len(pieces)
    (x_ref, cot_ref, segr_ref, segc_ref) = refs[:4]
    w_refs = refs[4 : 4 + n_in]
    refs = refs[4 + n_in :]
    (y_ref, dx_ref) = refs[:2]
    n_out = 1 if pieces is None else 4
    g_refs = refs[2 : 2 + n_out]
    (flat, wa, wi, wo, b1, vec, xb, qkv, ab0, ctx, xh1, iv1, xh2, iv2, h1b, slope, hb, du, df, da, dqkv, dc, xs, dr1, edge,
     gb1, gvec, sem) = refs[2 + n_out :]
    D = width
    T = length
    nb = T // ROWB
    pairs = D // LANES

    if pieces is None:
        cp = pltpu.make_async_copy(w_refs[0], flat, sem.at[0])
        cp.start()
        cp.wait()
    else:
        load_windows(w_refs, pieces, flat, edge, sem, shards)
    unpack_weights(flat, wa, wi, wo, b1, vec, D)

    scale = 0.125

    def bq(v):
        return v.astype(F32).astype(BF)

    def ab_store(r, h, qb, val):
        if r == 0:
            ab0[h, pl.ds(qb * ROWB, ROWB), :] = val
        else:
            for c in range(T // LANES):
                flat[pl.ds((h * (T // LANES) + c) * T + qb * ROWB, ROWB), :] = val[:, c * LANES : (c + 1) * LANES]

    def ab_load(r, h, qb):
        if r == 0:
            return ab0[h, pl.ds(qb * ROWB, ROWB), :]
        return jnp.concatenate(
            [flat[pl.ds((h * (T // LANES) + c) * T + qb * ROWB, ROWB), :] for c in range(T // LANES)], axis=1
        )

    def forward(r):
        src = x_ref if r == 0 else xs

        def proj(tb, carry):
            rows = pl.ds(pl.multiple_of(tb * ROWB, ROWB), ROWB)
            x16 = src[rows, :].astype(BF)
            xb[r, rows, :] = x16
            for j in range(3):
                p = dot(x16, wa[:, j * D : (j + 1) * D])
                if j == 0:
                    p = p + vec[0:1, :]
                if j == 2:
                    p = p + vec[1:2, :]
                p = p.astype(BF)
                for c in range(pairs):
                    qkv[r, j * pairs + c, rows, :] = p[:, c * LANES : (c + 1) * LANES]
            return carry

        lax.fori_loop(0, nb, proj, 0)

        def attend(p, carry):
            k2 = qkv[r, pairs + p]
            v2 = qkv[r, 2 * pairs + p]
            for qb in range(nb):
                out = None
                q2 = qkv[r, p, pl.ds(qb * ROWB, ROWB), :]
                allowed = segc_ref[pl.ds(qb * ROWB, ROWB), :] == segr_ref[...]
                for e in range(2):
                    m = lane_mask(e, BF)
                    s = dot_t(q2 * (m * scale).astype(BF), k2)
                    s = jnp.where(allowed, s, -1e30)
                    peak = jnp.max(s, axis=-1, keepdims=True)
                    ex = jnp.exp(s - peak)
                    tot = jnp.sum(ex, axis=-1, keepdims=True)
                    prob = (ex * (1.0 / tot)).astype(BF)
                    ab_store(r, 2 * p + e, qb, prob)
                    part = dot(prob, v2 * m)
                    out = part if out is None else out + part
                ctx[r, p, pl.ds(qb * ROWB, ROWB), :] = out.astype(BF)
            return carry

        lax.fori_loop(0, pairs, attend, 0)

        def mlp(tb, carry):
            rows = pl.ds(pl.multiple_of(tb * ROWB, ROWB), ROWB)
            c16 = jnp.concatenate([ctx[r, c, rows, :] for c in range(pairs)], axis=1)
            a = dot(c16, wa[:, 3 * D : 4 * D]) + vec[2:3, :]
            hat, inv = norm_stats(src[rows, :].astype(F32) + a)
            xh1[r, rows, :] = hat
            iv1[r, rows, :] = jnp.broadcast_to(inv, (ROWB, LANES))
            h1 = hat * vec[4:5, :] + vec[5:6, :]
            h16 = h1.astype(BF)
            h1b[r, rows, :] = h16
            f = h1 + vec[3:4, :]
            for c in range(FF // CHUNK):
                cols = slice(c * CHUNK, (c + 1) * CHUNK)
                u = dot(h16, wi[:, cols]) + b1[:, cols]
                g, sl = gelu_pair(u)
                g16 = g.astype(BF)
                hb[r, rows, cols] = g16
                slope[r, rows, cols] = sl
                f = f + dot(g16, wo[cols, :])
            hat, inv = norm_stats(f)
            xh2[r, rows, :] = hat
            iv2[r, rows, :] = jnp.broadcast_to(inv, (ROWB, LANES))
            y = hat * vec[6:7, :] + vec[7:8, :]
            if r == REC - 1:
                y_ref[rows, :] = y
            else:
                xs[rows, :] = y
            return carry

        lax.fori_loop(0, nb, mlp, 0)

    def acc(ref, row, val):
        ref[row : row + 1, :] = ref[row : row + 1, :] + val

    def backward(r):
        src = cot_ref if r == REC - 1 else dx_ref

        def mlp(tb, carry):
            rows = pl.ds(pl.multiple_of(tb * ROWB, ROWB), ROWB)
            dy = src[rows, :].astype(F32)
            hat = xh2[r, rows, :]
            acc(gvec, 6, colsum(dy * hat))
            acc(gvec, 7, colsum(dy))
            dr2 = norm_grad(dy, hat, iv2[r, rows, 0:1], vec[6:7, :])
            d16 = dr2.astype(BF)
            df[r, rows, :] = d16
            acc(gvec, 3, colsum(d16.astype(F32)))
            dh = dr2
            for c in range(FF // CHUNK):
                cols = slice(c * CHUNK, (c + 1) * CHUNK)
                t = dot_t(d16, wo[cols, :]).astype(BF).astype(F32)
                g16 = (t * slope[r, rows, cols]).astype(BF)
                du[r, rows, cols] = g16
                gb1[0:1, cols] = gb1[0:1, cols] + colsum(g16.astype(F32))
                dh = dh + dot_t(g16, wi[:, cols])
            hat = xh1[r, rows, :]
            acc(gvec, 4, colsum(dh * hat))
            acc(gvec, 5, colsum(dh))
            d1 = norm_grad(dh, hat, iv1[r, rows, 0:1], vec[4:5, :])
            dr1[rows, :] = d1
            a16 = d1.astype(BF)
            da[r, rows, :] = a16
            acc(gvec, 2, colsum(a16.astype(F32)))
            c16 = dot_t(a16, wa[:, 3 * D : 4 * D]).astype(BF)
            for c in range(pairs):
                dc[c, rows, :] = c16[:, c * LANES : (c + 1) * LANES]
            return carry

        lax.fori_loop(0, nb, mlp, 0)

        def attend(p, carry):
            k2 = qkv[r, pairs + p]
            v2 = qkv[r, 2 * pairs + p]
            dk = jnp.zeros((T, LANES), F32)
            dv = jnp.zeros((T, LANES), F32)
            for qb in range(nb):
                rows = pl.ds(qb * ROWB, ROWB)
                q2 = qkv[r, p, rows, :]
                dc2 = dc[p, rows, :]
                dq = None
                for e in range(2):
                    m = lane_mask(e, BF)
                    p16 = ab_load(r, 2 * p + e, qb)
                    pf = p16.astype(F32)
                    dcm = dc2 * m
                    t = dot_t(dcm, v2) * pf
                    s16 = (t - pf * jnp.sum(t, axis=-1, keepdims=True)).astype(BF)
                    part = dot(s16, k2 * m)
                    dq = part if dq is None else dq + part
                    dk = dk + t_dot(s16, q2 * m)
                    dv = dv + t_dot(p16, dcm)
                dqkv[r, p, rows, :] = (dq * scale).astype(BF)
            dqkv[r, pairs + p, :, :] = (dk * scale).astype(BF)
            dqkv[r, 2 * pairs + p, :, :] = dv.astype(BF)
            return carry

        lax.fori_loop(0, pairs, attend, 0)
        for c in range(pairs):
            cols = slice(c * LANES, (c + 1) * LANES)
            gvec[0:1, cols] = gvec[0:1, cols] + colsum(dqkv[r, c].astype(F32))
            gvec[1:2, cols] = gvec[1:2, cols] + colsum(dqkv[r, 2 * pairs + c].astype(F32))

        def back(tb, carry):
            rows = pl.ds(pl.multiple_of(tb * ROWB, ROWB), ROWB)
            d3 = jnp.concatenate([dqkv[r, c, rows, :] for c in range(3 * pairs)], axis=1)
            dx_ref[rows, :] = dr1[rows, :] + dot_t(d3, wa[:, : 3 * D])
            return carry

        lax.fori_loop(0, nb, back, 0)

    gb1[...] = jnp.zeros_like(gb1)
    gvec[...] = jnp.zeros_like(gvec)
    for r in range(REC):
        forward(r)
    for r in reversed(range(REC)):
        backward(r)

    per = 4 * D // LANES
    n = 256 // per
    swap = one_hot_swap(n, per)

    def wide_rows(base, d0, vals):
        for k in range(256 // n):
            pieces = []
            for c in range(per):
                v = vals[c * LANES // 512]
                o = c * LANES % 512
                pieces.append(v[k * n : (k + 1) * n, o : o + LANES])
            out = dot(swap, jnp.concatenate(pieces, axis=0)).astype(BF)
            flat[pl.ds(base + d0 * per + k * 256, 256), :] = out

    for d0 in range(0, D, 256):
        xt = [jnp.transpose(xb[r, :, d0 : d0 + 256]) for r in range(REC)]
        vals = []
        for j in range(3):
            g = None
            for r in range(REC):
                d3 = jnp.concatenate([dqkv[r, j * pairs + c] for c in range(pairs)], axis=1)
                part = dot(xt[r], d3)
                g = part if g is None else g + part
            vals.append(g.astype(BF))
        g = None
        for r in range(REC):
            cc = jnp.concatenate([ctx[r, d0 // LANES + c] for c in range(256 // LANES)], axis=1)
            part = t_dot(cc, da[r])
            g = part if g is None else g + part
        vals.append(g.astype(BF))
        wide_rows(0, d0, vals)
    for d0 in range(0, D, 256):
        ht = [jnp.transpose(h1b[r, :, d0 : d0 + 256]) for r in range(REC)]
        vals = []
        for j in range(FF // 512):
            g = None
            for r in range(REC):
                part = dot(ht[r], du[r, :, j * 512 : (j + 1) * 512])
                g = part if g is None else g + part
            vals.append(g.astype(BF))
        wide_rows(D * per, d0, vals)
    per_out = D // LANES
    n_out = 256 // per_out
    swap_out = one_hot_swap(n_out, per_out)
    base = 2 * D * per

    def out_rows(fb, carry):
        cols = pl.ds(pl.multiple_of(fb * 256, 256), 256)
        g = None
        for r in range(REC):
            part = t_dot(hb[r, :, cols], df[r])
            g = part if g is None else g + part
        g = g.astype(BF)
        for k in range(256 // n_out):
            pieces = [g[k * n_out : (k + 1) * n_out, c * LANES : (c + 1) * LANES] for c in range(per_out)]
            out = dot(swap_out, jnp.concatenate(pieces, axis=0)).astype(BF)
            flat[pl.ds(pl.multiple_of(base + fb * (256 * per_out) + k * 256, 256), 256), :] = out
        return carry

    lax.fori_loop(0, FF // 256, out_rows, 0)
    base = base + FF * per_out
    rows = [gb1[0:1, c * LANES : (c + 1) * LANES] for c in range(FF // LANES)]
    for r in range(8):
        rows = rows + [gvec[r : r + 1, c * LANES : (c + 1) * LANES] for c in range(per_out)]
    tail = jnp.concatenate(rows, axis=0)
    flat[base : base + len(rows), :] = tail.astype(BF)
    if pieces is None:
        cp = pltpu.make_async_copy(flat, g_refs[0], sem.at[0])
        cp.start()
        cp.wait()
    else:
        store_windows(g_refs, flat, edge, sem, shards, tail[FF // LANES :])


def core(x, cot, seg, flats, pieces, shards, rows):
    T, D = x.shape
    vm = pltpu.VMEM
    pairs = D // LANES
    scratch = [
        vm((rows, LANES), BF),
        vm((D, 4 * D), BF), vm((D, FF), BF), vm((FF, D), BF), vm((1, FF), F32), vm((8, D), F32),
        vm((REC, T, D), BF), vm((REC, 3 * pairs, T, LANES), BF), vm((HEADS, T, T), BF), vm((REC, pairs, T, LANES), BF),
        vm((REC, T, D), F32), vm((REC, T, LANES), F32), vm((REC, T, D), F32), vm((REC, T, LANES), F32),
        vm((REC, T, D), BF), vm((REC, T, FF), F32), vm((REC, T, FF), BF), vm((REC, T, FF), BF),
        vm((REC, T, D), BF), vm((REC, T, D), BF), vm((REC, 3 * pairs, T, LANES), BF), vm((pairs, T, LANES), BF),
        vm((T, D), F32), vm((T, D), F32), vm((shards if pieces else 1, 2 * TILE, LANES), BF),
        vm((1, FF), F32), vm((8, D), F32),
        pltpu.SemaphoreType.DMA((96,)),
    ]
    if pieces is None:
        g_shapes = [jax.ShapeDtypeStruct((rows, LANES), BF)]
    else:
        half = flats[0].shape[-2]
        g_shapes = [jax.ShapeDtypeStruct((2, 2, 4, half, LANES), BF)] * 4
    in_vmem = pl.BlockSpec(memory_space=pltpu.VMEM)
    anywhere = pl.BlockSpec(memory_space=pl.ANY)
    return pl.pallas_call(
        functools.partial(core_kernel, width=D, length=T, shards=shards, pieces=pieces),
        out_shape=tuple([jax.ShapeDtypeStruct((T, D), F32)] * 2 + g_shapes),
        in_specs=[in_vmem] * 4 + [anywhere] * len(flats),
        out_specs=tuple([in_vmem] * 2 + [anywhere] * len(g_shapes)),
        scratch_shapes=scratch,
        compiler_params=pltpu.CompilerParams(vmem_limit_bytes=60 * 1024 * 1024),
        name="layer_core",
    )(x, cot, seg.reshape(1, T), seg.reshape(T, 1), *flats)


AXES = ("dp", "rep")


def exchange(v, rel):
    count = lax.axis_size("dp") * lax.axis_size("rep")
    return lax.ppermute(v, AXES, [(j, j ^ rel) for j in range(count)])


RZ, RX, RC, RY = 8, 4, 2, 1


def gather_windows(a, b):
    out, pieces = [], []
    for part, own in enumerate((a, b)):
        first, second = (RX, RY) if part == 0 else (RY, RX)
        stack = jnp.stack([own] + [exchange(own, k * RZ) for k in (1, 2, 3)])
        near = exchange(stack, first)
        far = exchange(jnp.stack([stack, near]), second)
        for rc in (0, RC):
            for v, dims in ((stack, (0,)), (near, (first,)), (far, (second,))):
                out.append(v if rc == 0 else exchange(v, rc))
                if v is far:
                    ent = [((n, k), k * RZ + second + n * first + rc) for n in range(2) for k in range(4)]
                else:
                    ent = [((k,), k * RZ + dims[0] + rc) for k in range(4)]
                pieces.append((part, ent))
    order = sorted(range(len(out)), key=lambda i: pieces[i][0])
    return [out[i] for i in order], [pieces[i] for i in order]


def sum_windows(keeps, sends):
    res = []
    for part in range(2):
        first, second = (RX, RY) if part == 0 else (RY, RX)
        got = exchange(sends[part], RC)
        keep = keeps[part]
        got1 = exchange(keep[1] + got[1], first)
        mine = keep[0] + got[0]
        got2 = exchange(mine[1] + got1[1], second)
        mine = mine[0] + got1[0]
        v = mine + got2
        res.append([v[0]] + [exchange(v[k], k * RZ) for k in (1, 2, 3)])
    return res


def shards_fn(block_input, segment_ids, cotangent, master_weights, momentum, weight_average):
    width = block_input.shape[2]
    length = block_input.shape[1]
    count = lax.axis_size("dp") * lax.axis_size("rep")
    share = master_weights.shape[0]
    rows = share * count // LANES
    tiles = rows // TILE
    vec_len = 8 * width // count
    args = (block_input[0], cotangent[0], segment_ids[0])
    in_vmem = pl.BlockSpec(memory_space=pltpu.VMEM)
    if count == 32:
        window = (tiles // count + 2) * TILE
        padded = jnp.pad(master_weights, (0, window * LANES - share)).reshape(window, LANES)
        half = jax.ShapeDtypeStruct((window // 2, LANES), BF)
        a, b = pl.pallas_call(
            pack_kernel, out_shape=(half, half), in_specs=[in_vmem], out_specs=(in_vmem, in_vmem), name="pack_shard"
        )(padded)
        flats, pieces = gather_windows(a, b)
        block_output, input_grad, ka, kb, sa, sb = core(*args, flats, pieces, count, rows)
        parts = sum_windows((ka, kb), (sa, sb))
        grad, tail = pl.pallas_call(
            finish_kernel,
            out_shape=(jax.ShapeDtypeStruct((window, LANES), F32), jax.ShapeDtypeStruct((8, LANES), F32)),
            in_specs=[in_vmem] * 8,
            out_specs=(in_vmem, in_vmem),
            name="finish_shard",
        )(*parts[0], *parts[1])
        weight_grad = grad.reshape(-1)[:share]
        vector_grad = tail[7]
    else:
        flat = lax.all_gather(master_weights.astype(BF), AXES, axis=0, tiled=True).reshape(rows, LANES)
        block_output, input_grad, grad = core(*args, [flat], None, count, rows)
        grad = grad.reshape(-1).astype(F32)
        weight_grad = lax.psum_scatter(grad, AXES, scatter_dimension=0, tiled=True)
        vector_grad = lax.psum_scatter(grad[grad.shape[0] - 8 * width :], AXES, scatter_dimension=0, tiled=True)
    token_count = block_input.shape[0] * length * count
    rate = rate_base / math.sqrt(token_count)
    new_momentum = mom_decay * momentum + weight_grad
    new_weights = master_weights - rate * (weight_grad + mom_decay * new_momentum)
    new_average = avg_keep * weight_average + (1.0 - avg_keep) * new_weights
    return (
        block_output[None],
        input_grad[None],
        weight_grad,
        vector_grad,
        new_momentum,
        new_average,
        new_weights,
    )


def solution(mesh):
    three = P(AXES, None, None)
    two = P(AXES, None)
    one = P(AXES)
    return jax.shard_map(
        shards_fn,
        mesh=mesh,
        in_specs=(three, two, three, one, one, one),
        out_specs=(three, three, one, one, one, one, one),
        check_vma=False,
    )
```

time: 597 us -> 209 us (0.35); the launches traced: 588 us -> 209 us
  waiting for transfers between devices: 347 us -> 68.4 us
  Pallas kernels: 0 us -> 88 us
  local copies, waits for them, and re-layouts: 84.4 us -> 6.83 us
  matrix products: 72.2 us -> 0 us
  blocking collectives: 41.2 us -> 0 us
  starting transfers between devices: 0.04 us -> 38.4 us
  other arithmetic: 28.3 us -> 6.41 us
  between operations: 15.5 us -> 0.81 us
    unnamed x4 -> x0, waiting for transfers between devices: 347 us -> none
    pallas_call x0 -> x3, Pallas kernels: none -> 88 us  [the longest x1 83.6 us: core(): pl.pallas_call(functools.partial(core_kernel, width=D, length=T, shards=s...]
    dot_general x36 -> x0, matrix products: 72.2 us -> none  [the longest x2 8.31 us: layer_backward(): jnp.einsum('tf,td->fd', hidden_b, branch_grad, preferred_element_type=jnp...]
    ppermute x0 -> x28, waiting for transfers between devices: none -> 68.4 us  [exchange(): return lax.ppermute(v, AXES, [(j, j ^ rel) for j in range(count)])]
    unnamed x169 -> x38, local copies, waits for them, and re-layouts: 57.5 us -> 1.66 us
    unnamed x1 -> x0, blocking collectives: 41.2 us -> none
    ppermute x0 -> x28, starting transfers between devices: none -> 38.4 us  [exchange(): return lax.ppermute(v, AXES, [(j, j ^ rel) for j in range(count)])]
    slice x10 -> x0, local copies, waits for them, and re-layouts: 21 us -> none  [the longest x2 8.41 us: unpack(): w_in = flat_vec[offset:offset + width * hidden].reshape(width, hidden)]
  transfers between devices with their start and end apart: 2 -> 28, of which waited for: 2 -> 14; matrix products, arithmetic and copies ran while one was open for 2% -> 3% of each run, Pallas kernels for 0% -> 0%
where the time goes in v1:
time: 209 us
  Pallas kernels  88 us (42%)
  waiting for transfers between devices  68.4 us (33%)
  starting transfers between devices  38.4 us (18%)
  local copies, waits for them, and re-layouts  6.83 us (3%)
  other arithmetic  6.41 us (3%)
    pallas_call x1, Pallas kernels, core(): pl.pallas_call(functools.partial(core_kernel, width=D, length=T, shards=s...  83.6 us
    ppermute x28, waiting for transfers between devices, exchange(): return lax.ppermute(v, AXES, [(j, j ^ rel) for j in range(count)])  68.4 us
    ppermute x28, starting transfers between devices, exchange(): return lax.ppermute(v, AXES, [(j, j ^ rel) for j in range(count)])  38.4 us
  transfers between devices with their start and end apart: 28, of which 14 were waited for; matrix products, arithmetic and copies ran while one was open for 3% of the time, Pallas kernels for 0%

profile of v1, /device:TPU:0, one launch (start us, length us, event | category | flops | bytes accessed | tf_op | source)
XLA Modules:
  0.0 208.9 jit_solution(3341524329956728499)
XLA Ops:
  0.6 1.8 pad_bitcast_fusion.x_ref
  2.4 2.0 pack_shard.1
  4.4 5.0 %collective-permute-start.10 = (bf16[400,128]{1,0:T(8,128)(2,1)}, bf16[400,128]{1,0:T(8,128)(2,1)S(1)}, u32[]{:S(2)}, u32[]{:S(2)}) collective-permute-start(bf16[400,128]{1,0:T(8,128)(2,1)} %get-tuple-element.18), channel_id=1, source_target_pairs={{0,24},{1,25},{2,26},{3,27},{4,28},{5,29},{6,30},{7,31},{8,16},{9,... | collective-permute-start | bytes 307208 | tf_op jit(solution)/shard_map/ppermute | solution.py:571
  9.4 0.6 collective-permute-start.8
  10.0 3.8 %collective-permute-start.2 = (bf16[400,128]{1,0:T(8,128)(2,1)}, bf16[400,128]{1,0:T(8,128)(2,1)S(1)}, u32[]{:S(2)}, u32[]{:S(2)}) collective-permute-start(bf16[400,128]{1,0:T(8,128)(2,1)} %get-tuple-element.17), channel_id=1, source_target_pairs={{0,24},{1,25},{2,26},{3,27},{4,28},{5,29},{6,30},{7,31},{8,16},{9,... | collective-permute-start | bytes 307208 | tf_op jit(solution)/shard_map/ppermute | solution.py:571
  13.8 4.6 %collective-permute-start = (bf16[400,128]{1,0:T(8,128)(2,1)}, bf16[400,128]{1,0:T(8,128)(2,1)S(1)}, u32[]{:S(2)}, u32[]{:S(2)}) collective-permute-start(bf16[400,128]{1,0:T(8,128)(2,1)} %get-tuple-element.17), channel_id=1, source_target_pairs={{0,8},{1,9},{2,10},{3,11},{4,12},{5,13},{6,14},{7,15},{8,0},{9,1},... | collective-permute-start | bytes 307208 | tf_op jit(solution)/shard_map/ppermute | solution.py:571
  18.4 5.2 %collective-permute-done.9 = bf16[400,128]{1,0:T(8,128)(2,1)S(1)} collective-permute-done((bf16[400,128]{1,0:T(8,128)(2,1)}, bf16[400,128]{1,0:T(8,128)(2,1)S(1)}, u32[]{:S(2)}, u32[]{:S(2)}) %collective-permute-start.9) | collective-permute-done | bytes 102432 | tf_op jit(solution)/shard_map/ppermute | solution.py:571
  23.6 1.0 fusion.8
  24.6 1.6 collective-permute-start.11
  26.2 0.9 collective-permute-done.1
  27.0 1.0 fusion.9
  28.0 1.6 collective-permute-start.3
  29.6 4.1 %collective-permute-done.11.refs_11_ = bf16[4,400,128]{2,1,0:T(8,128)(2,1)S(1)} collective-permute-done((bf16[4,400,128]{2,1,0:T(8,128)(2,1)S(1)}, bf16[4,400,128]{2,1,0:T(8,128)(2,1)S(1)}, u32[]{:S(2)}, u32[]{:S(2)}) %collective-permute-start.11) | collective-permute-done | bytes 409632 | tf_op jit(solution)/shard_map/ppermute | solution.py:571
  33.7 1.6 collective-permute-start.12
  35.3 5.2 %collective-permute-done.3.refs_5_ = bf16[4,400,128]{2,1,0:T(8,128)(2,1)S(1)} collective-permute-done((bf16[4,400,128]{2,1,0:T(8,128)(2,1)S(1)}, bf16[4,400,128]{2,1,0:T(8,128)(2,1)S(1)}, u32[]{:S(2)}, u32[]{:S(2)}) %collective-permute-start.3) | collective-permute-done | bytes 409632 | tf_op jit(solution)/shard_map/ppermute | solution.py:571
  40.6 1.6 collective-permute-start.4
  42.2 14.0 %collective-permute-done.12.refs_12_ = bf16[2,4,400,128]{3,2,1,0:T(8,128)(2,1)S(1)} collective-permute-done((bf16[2,4,400,128]{3,2,1,0:T(8,128)(2,1)S(1)}, bf16[2,4,400,128]{3,2,1,0:T(8,128)(2,1)S(1)}, u32[]{:S(2)}, u32[]{:S(2)}) %collective-permute-start.12) | collective-permute-done | bytes 819232 | tf_op jit(solution)/shard_map/ppermute | solution.py:571
  56.2 1.0 collective-permute-done.4.refs_6_
  57.1 0.5 collective-permute-start.13
  57.7 0.5 collective-permute-start.14
  58.2 0.3 copy-done.8
  58.5 0.9 copy.13.refs_3_
  59.3 1.6 collective-permute-done.13.refs_13_
  61.0 0.6 collective-permute-done.6.refs_8_
  61.6 0.7 copy-done.9
  62.3 83.6 %layer_core.1 = (f32[512,512]{1,0:T(8,128)}, f32[512,512]{1,0:T(8,128)}, bf16[2,2,4,400,128]{4,3,2,1,0:T(8,128)(2,1)}, bf16[2,2,4,400,128]{4,3,2,1,0:T(8,128)(2,...) custom-call(bf16[512,512]{1,0:T(8,128)(2,1)} %bitcast.74, bf16[512,512]{1,0:T(8,128)(2,1)} %bitcast.75, ...), custom_call_target="tpu_custom_call" | custom-call | tf_op jit(solution)/shard_map/layer_core/pallas_call | solution.py:555
  146.0 0.2 collective-permute-start.16
  146.1 0.4 collective-permute-start.22
  146.5 3.2 %collective-permute-done.16 = bf16[2,2,4,400,128]{4,3,2,1,0:T(8,128)(2,1)S(1)} collective-permute-done((bf16[2,2,4,400,128]{4,3,2,1,0:T(8,128)(2,1)}, bf16[2,2,4,400,128]{4,3,2,1,0:T(8,128)(2,1)S(1)}, u32[]{:S(2)}, u32[]{:S(2)}) %collective-permute-start.16) | collective-permute-done | bytes 1638432 | tf_op jit(solution)/shard_map/ppermute | solution.py:571
  149.7 1.7 slice_add_fusion.3
  151.5 1.6 collective-permute-start.17
  153.2 1.6 collective-permute-start.23
  154.8 17.0 %collective-permute-done.17 = bf16[2,4,400,128]{3,2,1,0:T(8,128)(2,1)S(1)} collective-permute-done((bf16[2,4,400,128]{3,2,1,0:T(8,128)(2,1)S(1)}, bf16[2,4,400,128]{3,2,1,0:T(8,128)(2,1)S(1)}, u32[]{:S(2)}, u32[]{:S(2)}) %collective-permute-start.17) | collective-permute-done | bytes 819232 | tf_op jit(solution)/shard_map/ppermute | solution.py:571
  171.9 1.6 collective-permute-start.18
  173.5 1.6 collective-permute-start.24
  175.1 7.5 %collective-permute-done.18 = bf16[4,400,128]{2,1,0:T(8,128)(2,1)S(1)} collective-permute-done((bf16[4,400,128]{2,1,0:T(8,128)(2,1)S(1)}, bf16[4,400,128]{2,1,0:T(8,128)(2,1)S(1)}, u32[]{:S(2)}, u32[]{:S(2)}) %collective-permute-start.18) | collective-permute-done | bytes 409632 | tf_op jit(solution)/shard_map/ppermute | solution.py:571
  182.7 0.7 slice_bitcast_fusion.8
  183.3 2.0 collective-permute-start.21
  185.3 2.4 %collective-permute-start.19 = (bf16[400,128]{1,0:T(8,128)(2,1)S(1)}, bf16[400,128]{1,0:T(8,128)(2,1)S(1)}, u32[]{:S(2)}, u32[]{:S(2)}) collective-permute-start(bf16[400,128]{1,0:T(8,128)(2,1)S(1)} %get-tuple-element.41), channel_id=1, source_target_pairs={{0,8},{1,9},{2,10},{3,11},{4,12},{5,13},{6,14},{7,15},{8,0},{9,1},... | collective-permute-start | bytes 307208 | tf_op jit(solution)/shard_map/ppermute | solution.py:571
  187.8 0.7 slice_bitcast_fusion.4
  188.5 2.0 collective-permute-start.27
  190.7 3.8 %collective-permute-start.25 = (bf16[400,128]{1,0:T(8,128)(2,1)S(1)}, bf16[400,128]{1,0:T(8,128)(2,1)S(1)}, u32[]{:S(2)}, u32[]{:S(2)}) collective-permute-start(bf16[400,128]{1,0:T(8,128)(2,1)S(1)} %get-tuple-element.37), channel_id=1, source_target_pairs={{0,8},{1,9},{2,10},{3,11},{4,12},{5,13},{6,14},{7,15},{8,0},{9,1},... | collective-permute-start | bytes 307208 | tf_op jit(solution)/shard_map/ppermute | solution.py:571
  194.5 4.3 %collective-permute-done.20.refs_2_ = bf16[400,128]{1,0:T(8,128)(2,1)S(1)} collective-permute-done((bf16[400,128]{1,0:T(8,128)(2,1)S(1)}, bf16[400,128]{1,0:T(8,128)(2,1)S(1)}, u32[]{:S(2)}, u32[]{:S(2)}) %collective-permute-start.20) | collective-permute-done | bytes 102432 | tf_op jit(solution)/shard_map/ppermute | solution.py:571
  198.8 3.6 %collective-permute-done.26.refs_6_ = bf16[400,128]{1,0:T(8,128)(2,1)S(1)} collective-permute-done((bf16[400,128]{1,0:T(8,128)(2,1)S(1)}, bf16[400,128]{1,0:T(8,128)(2,1)S(1)}, u32[]{:S(2)}, u32[]{:S(2)}) %collective-permute-start.26) | collective-permute-done | bytes 102432 | tf_op jit(solution)/shard_map/ppermute | solution.py:571
  202.4 0.6 copy-done.16
  203.1 2.4 %finish_shard.1 = (f32[800,128]{1,0:T(8,128)}, f32[8,128]{1,0:T(8,128)}) custom-call(bf16[400,128]{1,0:T(8,128)(2,1)} %get-tuple-element.42.refs_0_, bf16[400,128]{1,0:T(8,128)(2,1)} %copy-done.14, bf16[400,128]{1,0:T(8,128)(2,1)} %copy-done.13, bf16[400,128]{1,0:T(8,128)(2,1)} %copy-done.12, bf16[400,128]{1,0:T(8,128)(2,1)} %get-tuple-element.38.refs_4_, ...), custom_call_target="tpu_custom_call" | custom-call | tf_op jit(solution)/shard_map/finish_shard/pallas_call | solution.py:631
  205.5 1.2 slice_bitcast_fusion.12
  206.7 2.2 %multiply_add_fusion = (f32[98496]{0:T(1024)}, f32[98496]{0:T(1024)}, f32[98496]{0:T(1024)}, f32[98496]{0:T(1024)}) fusion(f32[98496]{0:T(1024)S(1)} %copy-done.10, f32[98496]{0:T(1024)S(1)} %copy-done.5, f32[98496]{0:T(1024)S(1)} %copy-done.11, f32[102400]{0:T(1024)} %bitcast.76), kind=kLoop, calls=%fused_computation.25 | loop fusion | flops 886464 | bytes 3151872 | tf_op jit(solution)/shard_map/add | solution.py:650
  (65 shorter events, 1.0 us)
Async XLA Ops:
  4.4 9.4 %collective-permute-start.10 = (bf16[400,128]{1,0:T(8,128)(2,1)}, bf16[400,128]{1,0:T(8,128)(2,1)S(1)}, u32[]{:S(2)}, u32[]{:S(2)}) collective-permute-start(bf16[400,128]{1,0:T(8,128)(2,1)} %get-tuple-element.18), channel_id=1, source_target_pairs={{0,24},{1,25},{2,26},{3,27},{4,28},{5,29},{6,30},{7,31},{8,16},{9,... | collective-permute-start | bytes 307208 | tf_op jit(solution)/shard_map/ppermute | solution.py:571
  9.4 14.2 %collective-permute-start.9 = (bf16[400,128]{1,0:T(8,128)(2,1)}, bf16[400,128]{1,0:T(8,128)(2,1)S(1)}, u32[]{:S(2)}, u32[]{:S(2)}) collective-permute-start(bf16[400,128]{1,0:T(8,128)(2,1)} %get-tuple-element.18), channel_id=1, source_target_pairs={{0,16},{1,17},{2,18},{3,19},{4,20},{5,21},{6,22},{7,23},{8,24},{9,... | collective-permute-start | bytes 307208 | tf_op jit(solution)/shard_map/ppermute | solution.py:571
  9.4 14.2 %collective-permute-start.8 = (bf16[400,128]{1,0:T(8,128)(2,1)}, bf16[400,128]{1,0:T(8,128)(2,1)S(1)}, u32[]{:S(2)}, u32[]{:S(2)}) collective-permute-start(bf16[400,128]{1,0:T(8,128)(2,1)} %get-tuple-element.18), channel_id=1, source_target_pairs={{0,8},{1,9},{2,10},{3,11},{4,12},{5,13},{6,14},{7,15},{8,0},{9,1},... | collective-permute-start | bytes 307208 | tf_op jit(solution)/shard_map/ppermute | solution.py:571
  10.0 16.2 %collective-permute-start.2 = (bf16[400,128]{1,0:T(8,128)(2,1)}, bf16[400,128]{1,0:T(8,128)(2,1)S(1)}, u32[]{:S(2)}, u32[]{:S(2)}) collective-permute-start(bf16[400,128]{1,0:T(8,128)(2,1)} %get-tuple-element.17), channel_id=1, source_target_pairs={{0,24},{1,25},{2,26},{3,27},{4,28},{5,29},{6,30},{7,31},{8,16},{9,... | collective-permute-start | bytes 307208 | tf_op jit(solution)/shard_map/ppermute | solution.py:571
  13.8 13.2 %collective-permute-start.1 = (bf16[400,128]{1,0:T(8,128)(2,1)}, bf16[400,128]{1,0:T(8,128)(2,1)S(1)}, u32[]{:S(2)}, u32[]{:S(2)}) collective-permute-start(bf16[400,128]{1,0:T(8,128)(2,1)} %get-tuple-element.17), channel_id=1, source_target_pairs={{0,16},{1,17},{2,18},{3,19},{4,20},{5,21},{6,22},{7,23},{8,24},{9,... | collective-permute-start | bytes 307208 | tf_op jit(solution)/shard_map/ppermute | solution.py:571
  13.8 13.2 %collective-permute-start = (bf16[400,128]{1,0:T(8,128)(2,1)}, bf16[400,128]{1,0:T(8,128)(2,1)S(1)}, u32[]{:S(2)}, u32[]{:S(2)}) collective-permute-start(bf16[400,128]{1,0:T(8,128)(2,1)} %get-tuple-element.17), channel_id=1, source_target_pairs={{0,8},{1,9},{2,10},{3,11},{4,12},{5,13},{6,14},{7,15},{8,0},{9,1},... | collective-permute-start | bytes 307208 | tf_op jit(solution)/shard_map/ppermute | solution.py:571
  24.6 32.6 %copy-start.1 = (bf16[4,400,128]{2,1,0:T(8,128)(2,1)}, bf16[4,400,128]{2,1,0:T(8,128)(2,1)S(1)}, u32[]{:S(2)}) copy-start(bf16[4,400,128]{2,1,0:T(8,128)(2,1)S(1)} %get-tuple-element.44.refs_10_) | copy-start | bytes 1228804
  24.6 9.1 %collective-permute-start.11 = (bf16[4,400,128]{2,1,0:T(8,128)(2,1)S(1)}, bf16[4,400,128]{2,1,0:T(8,128)(2,1)S(1)}, u32[]{:S(2)}, u32[]{:S(2)}) collective-permute-start(bf16[4,400,128]{2,1,0:T(8,128)(2,1)S(1)} %get-tuple-element.44.refs_10_), channel_id=1, source_target_pairs={{0,1},{1,0},{2,3},{3,2},{4,5},{5,4},{6,7},{7,6},{8,9},{9,8},{10,11... | collective-permute-start | bytes 1228808 | tf_op jit(solution)/shard_map/ppermute | solution.py:571
  28.0 14.1 %copy-start.3 = (bf16[4,400,128]{2,1,0:T(8,128)(2,1)}, bf16[4,400,128]{2,1,0:T(8,128)(2,1)S(1)}, u32[]{:S(2)}) copy-start(bf16[4,400,128]{2,1,0:T(8,128)(2,1)S(1)} %get-tuple-element.46.refs_4_) | copy-start | bytes 1228804
  28.0 12.5 %collective-permute-start.3 = (bf16[4,400,128]{2,1,0:T(8,128)(2,1)S(1)}, bf16[4,400,128]{2,1,0:T(8,128)(2,1)S(1)}, u32[]{:S(2)}, u32[]{:S(2)}) collective-permute-start(bf16[4,400,128]{2,1,0:T(8,128)(2,1)S(1)} %get-tuple-element.46.refs_4_), channel_id=1, source_target_pairs={{0,4},{1,5},{2,6},{3,7},{4,0},{5,1},{6,2},{7,3},{8,12},{9,13},{10,... | collective-permute-start | bytes 1228808 | tf_op jit(solution)/shard_map/ppermute | solution.py:571
  33.7 24.0 %copy-start.2 = (bf16[4,400,128]{2,1,0:T(8,128)(2,1)}, bf16[4,400,128]{2,1,0:T(8,128)(2,1)S(1)}, u32[]{:S(2)}) copy-start(bf16[4,400,128]{2,1,0:T(8,128)(2,1)S(1)} %collective-permute-done.11.refs_11_) | copy-start | bytes 1228804
  33.7 24.8 %copy-start.18 = (s32[1,512]{1,0:T(1,128)S(1)}, s32[1,512]{1,0:T(1,128)}, u32[]{:S(2)}) copy-start(s32[1,512]{1,0:T(1,128)} %refs_2_.1) | copy-start | bytes 6148
  33.7 22.4 %collective-permute-start.12 = (bf16[2,4,400,128]{3,2,1,0:T(8,128)(2,1)S(1)}, bf16[2,4,400,128]{3,2,1,0:T(8,128)(2,1)S(1)}, u32[]{:S(2)}, u32[]{:S(2)}) collective-permute-start(bf16[2,4,400,128]{3,2,1,0:T(8,128)(2,1)S(1)} %pad_maximum_fusion.1), channel_id=1, source_target_pairs={{0,4},{1,5},{2,6},{3,7},{4,0},{5,1},{6,2},{7,3},{8,12},{9,13},{10,... | collective-permute-start | bytes 2457608 | tf_op jit(solution)/shard_map/ppermute | solution.py:571
  40.5 21.1 %copy-start.4 = (bf16[4,400,128]{2,1,0:T(8,128)(2,1)}, bf16[4,400,128]{2,1,0:T(8,128)(2,1)S(1)}, u32[]{:S(2)}) copy-start(bf16[4,400,128]{2,1,0:T(8,128)(2,1)S(1)} %collective-permute-done.3.refs_5_) | copy-start | bytes 1228804
  40.6 16.6 %collective-permute-start.4 = (bf16[2,4,400,128]{3,2,1,0:T(8,128)(2,1)S(1)}, bf16[2,4,400,128]{3,2,1,0:T(8,128)(2,1)S(1)}, u32[]{:S(2)}, u32[]{:S(2)}) collective-permute-start(bf16[2,4,400,128]{3,2,1,0:T(8,128)(2,1)S(1)} %pad_maximum_fusion), channel_id=1, source_target_pairs={{0,1},{1,0},{2,3},{3,2},{4,5},{5,4},{6,7},{7,6},{8,9},{9,8},{10,11... | collective-permute-start | bytes 2457608 | tf_op jit(solution)/shard_map/ppermute | solution.py:571
  42.1 15.6 %collective-permute-start.5 = (bf16[4,400,128]{2,1,0:T(8,128)(2,1)S(1)}, bf16[4,400,128]{2,1,0:T(8,128)(2,1)S(1)}, u32[]{:S(2)}, u32[]{:S(2)}) collective-permute-start(bf16[4,400,128]{2,1,0:T(8,128)(2,1)S(1)} %get-tuple-element.46.refs_4_), channel_id=1, source_target_pairs={{0,2},{1,3},{2,0},{3,1},{4,6},{5,7},{6,4},{7,5},{8,10},{9,11},{10,... | collective-permute-start | bytes 1228808 | tf_op jit(solution)/shard_map/ppermute | solution.py:571
  56.2 5.4 %copy-start.6 = (bf16[2,4,400,128]{3,2,1,0:T(8,128)(2,1)}, bf16[2,4,400,128]{3,2,1,0:T(8,128)(2,1)S(1)}, u32[]{:S(2)}) copy-start(bf16[2,4,400,128]{3,2,1,0:T(8,128)(2,1)S(1)} %collective-permute-done.12.refs_12_) | copy-start | bytes 2457604
  56.2 5.4 %collective-permute-start.15 = (bf16[2,4,400,128]{3,2,1,0:T(8,128)(2,1)S(1)}, bf16[2,4,400,128]{3,2,1,0:T(8,128)(2,1)}, u32[]{:S(2)}, u32[]{:S(2)}) collective-permute-start(bf16[2,4,400,128]{3,2,1,0:T(8,128)(2,1)S(1)} %collective-permute-done.12.refs_12_), channel_id=1, source_target_pairs={{0,2},{1,3},{2,0},{3,1},{4,6},{5,7},{6,4},{7,5},{8,10},{9,11},{10,... | collective-permute-start | bytes 2457608 | tf_op jit(solution)/shard_map/ppermute | solution.py:571
  57.1 4.5 %copy-start.7 = (bf16[2,4,400,128]{3,2,1,0:T(8,128)(2,1)}, bf16[2,4,400,128]{3,2,1,0:T(8,128)(2,1)S(1)}, u32[]{:S(2)}) copy-start(bf16[2,4,400,128]{3,2,1,0:T(8,128)(2,1)S(1)} %collective-permute-done.4.refs_6_) | copy-start | bytes 2457604
  57.1 4.4 %collective-permute-start.7 = (bf16[2,4,400,128]{3,2,1,0:T(8,128)(2,1)S(1)}, bf16[2,4,400,128]{3,2,1,0:T(8,128)(2,1)}, u32[]{:S(2)}, u32[]{:S(2)}) collective-permute-start(bf16[2,4,400,128]{3,2,1,0:T(8,128)(2,1)S(1)} %collective-permute-done.4.refs_6_), channel_id=1, source_target_pairs={{0,2},{1,3},{2,0},{3,1},{4,6},{5,7},{6,4},{7,5},{8,10},{9,11},{10,... | collective-permute-start | bytes 2457608 | tf_op jit(solution)/shard_map/ppermute | solution.py:571
  57.1 3.8 %collective-permute-start.13 = (bf16[4,400,128]{2,1,0:T(8,128)(2,1)S(1)}, bf16[4,400,128]{2,1,0:T(8,128)(2,1)}, u32[]{:S(2)}, u32[]{:S(2)}) collective-permute-start(bf16[4,400,128]{2,1,0:T(8,128)(2,1)S(1)} %get-tuple-element.44.refs_10_), channel_id=1, source_target_pairs={{0,2},{1,3},{2,0},{3,1},{4,6},{5,7},{6,4},{7,5},{8,10},{9,11},{10,... | collective-permute-start | bytes 1228808 | tf_op jit(solution)/shard_map/ppermute | solution.py:571
  57.6 3.9 %collective-permute-start.6 = (bf16[4,400,128]{2,1,0:T(8,128)(2,1)S(1)}, bf16[4,400,128]{2,1,0:T(8,128)(2,1)}, u32[]{:S(2)}, u32[]{:S(2)}) collective-permute-start(bf16[4,400,128]{2,1,0:T(8,128)(2,1)S(1)} %collective-permute-done.3.refs_5_), channel_id=1, source_target_pairs={{0,2},{1,3},{2,0},{3,1},{4,6},{5,7},{6,4},{7,5},{8,10},{9,11},{10,... | collective-permute-start | bytes 1228808 | tf_op jit(solution)/shard_map/ppermute | solution.py:571
  57.7 0.8 copy-start.8
  57.7 3.8 %collective-permute-start.14 = (bf16[4,400,128]{2,1,0:T(8,128)(2,1)S(1)}, bf16[4,400,128]{2,1,0:T(8,128)(2,1)S(1)}, u32[]{:S(2)}, u32[]{:S(2)}) collective-permute-start(bf16[4,400,128]{2,1,0:T(8,128)(2,1)S(1)} %collective-permute-done.11.refs_11_), channel_id=1, source_target_pairs={{0,2},{1,3},{2,0},{3,1},{4,6},{5,7},{6,4},{7,5},{8,10},{9,11},{10,... | collective-permute-start | bytes 1228808 | tf_op jit(solution)/shard_map/ppermute | solution.py:571
  61.6 0.7 copy-start.9
  146.0 3.8 %collective-permute-start.16 = (bf16[2,2,4,400,128]{4,3,2,1,0:T(8,128)(2,1)}, bf16[2,2,4,400,128]{4,3,2,1,0:T(8,128)(2,1)S(1)}, u32[]{:S(2)}, u32[]{:S(2)}) collective-permute-start(bf16[2,2,4,400,128]{4,3,2,1,0:T(8,128)(2,1)} %get-tuple-element.22), channel_id=1, source_target_pairs={{0,2},{1,3},{2,0},{3,1},{4,6},{5,7},{6,4},{7,5},{8,10},{9,11},{10,... | collective-permute-start | bytes 4915208 | tf_op jit(solution)/shard_map/ppermute | solution.py:571
  146.1 6.9 %collective-permute-start.22 = (bf16[2,2,4,400,128]{4,3,2,1,0:T(8,128)(2,1)}, bf16[2,2,4,400,128]{4,3,2,1,0:T(8,128)(2,1)S(1)}, u32[]{:S(2)}, u32[]{:S(2)}) collective-permute-start(bf16[2,2,4,400,128]{4,3,2,1,0:T(8,128)(2,1)} %get-tuple-element.24), channel_id=1, source_target_pairs={{0,2},{1,3},{2,0},{3,1},{4,6},{5,7},{6,4},{7,5},{8,10},{9,11},{10,... | collective-permute-start | bytes 4915208 | tf_op jit(solution)/shard_map/ppermute | solution.py:571
  149.7 3.3 %copy-start = (bf16[2,2,4,400,128]{4,3,2,1,0:T(8,128)(2,1)S(1)}, bf16[2,2,4,400,128]{4,3,2,1,0:T(8,128)(2,1)}, u32[]{:S(2)}) copy-start(bf16[2,2,4,400,128]{4,3,2,1,0:T(8,128)(2,1)} %get-tuple-element.23) | copy-start | bytes 4915204
  151.5 20.4 %collective-permute-start.17 = (bf16[2,4,400,128]{3,2,1,0:T(8,128)(2,1)S(1)}, bf16[2,4,400,128]{3,2,1,0:T(8,128)(2,1)S(1)}, u32[]{:S(2)}, u32[]{:S(2)}) collective-permute-start(bf16[2,4,400,128]{3,2,1,0:T(8,128)(2,1)S(1)} %get-tuple-element.34), channel_id=1, source_target_pairs={{0,4},{1,5},{2,6},{3,7},{4,0},{5,1},{6,2},{7,3},{8,12},{9,13},{10,... | collective-permute-start | bytes 2457608 | tf_op jit(solution)/shard_map/ppermute | solution.py:571
  153.2 20.3 %collective-permute-start.23 = (bf16[2,4,400,128]{3,2,1,0:T(8,128)(2,1)S(1)}, bf16[2,4,400,128]{3,2,1,0:T(8,128)(2,1)S(1)}, u32[]{:S(2)}, u32[]{:S(2)}) collective-permute-start(bf16[2,4,400,128]{3,2,1,0:T(8,128)(2,1)S(1)} %get-tuple-element.32), channel_id=1, source_target_pairs={{0,1},{1,0},{2,3},{3,2},{4,5},{5,4},{6,7},{7,6},{8,9},{9,8},{10,11... | collective-permute-start | bytes 2457608 | tf_op jit(solution)/shard_map/ppermute | solution.py:571
  171.9 10.7 %collective-permute-start.18 = (bf16[4,400,128]{2,1,0:T(8,128)(2,1)S(1)}, bf16[4,400,128]{2,1,0:T(8,128)(2,1)S(1)}, u32[]{:S(2)}, u32[]{:S(2)}) collective-permute-start(bf16[4,400,128]{2,1,0:T(8,128)(2,1)S(1)} %fusion.5), channel_id=1, source_target_pairs={{0,1},{1,0},{2,3},{3,2},{4,5},{5,4},{6,7},{7,6},{8,9},{9,8},{10,11... | collective-permute-start | bytes 1228808 | tf_op jit(solution)/shard_map/ppermute | solution.py:571
  173.5 14.2 %collective-permute-start.24 = (bf16[4,400,128]{2,1,0:T(8,128)(2,1)S(1)}, bf16[4,400,128]{2,1,0:T(8,128)(2,1)S(1)}, u32[]{:S(2)}, u32[]{:S(2)}) collective-permute-start(bf16[4,400,128]{2,1,0:T(8,128)(2,1)S(1)} %fusion.2), channel_id=1, source_target_pairs={{0,4},{1,5},{2,6},{3,7},{4,0},{5,1},{6,2},{7,3},{8,12},{9,13},{10,... | collective-permute-start | bytes 1228808 | tf_op jit(solution)/shard_map/ppermute | solution.py:571
  183.3 7.3 %collective-permute-start.21 = (bf16[400,128]{1,0:T(8,128)(2,1)S(1)}, bf16[400,128]{1,0:T(8,128)(2,1)S(1)}, u32[]{:S(2)}, u32[]{:S(2)}) collective-permute-start(bf16[400,128]{1,0:T(8,128)(2,1)S(1)} %get-tuple-element.39), channel_id=1, source_target_pairs={{0,24},{1,25},{2,26},{3,27},{4,28},{5,29},{6,30},{7,31},{8,16},{9,... | collective-permute-start | bytes 307208 | tf_op jit(solution)/shard_map/ppermute | solution.py:571
  185.3 13.4 %collective-permute-start.20 = (bf16[400,128]{1,0:T(8,128)(2,1)S(1)}, bf16[400,128]{1,0:T(8,128)(2,1)S(1)}, u32[]{:S(2)}, u32[]{:S(2)}) collective-permute-start(bf16[400,128]{1,0:T(8,128)(2,1)S(1)} %get-tuple-element.40), channel_id=1, source_target_pairs={{0,16},{1,17},{2,18},{3,19},{4,20},{5,21},{6,22},{7,23},{8,24},{9,... | collective-permute-start | bytes 307208 | tf_op jit(solution)/shard_map/ppermute | solution.py:571
  185.3 21.4 %copy-start.5 = (f32[98496]{0:T(1024)S(1)}, f32[98496]{0:T(1024)}, u32[]{:S(2)}) copy-start(f32[98496]{0:T(1024)} %param.9) | copy-start | bytes 1181956
  185.3 21.4 %copy-start.10 = (f32[98496]{0:T(1024)S(1)}, f32[98496]{0:T(1024)}, u32[]{:S(2)}) copy-start(f32[98496]{0:T(1024)} %param.11) | copy-start | bytes 1181956
  185.3 21.4 %copy-start.11 = (f32[98496]{0:T(1024)S(1)}, f32[98496]{0:T(1024)}, u32[]{:S(2)}) copy-start(f32[98496]{0:T(1024)} %param.10) | copy-start | bytes 1181956
  185.3 13.4 %collective-permute-start.19 = (bf16[400,128]{1,0:T(8,128)(2,1)S(1)}, bf16[400,128]{1,0:T(8,128)(2,1)S(1)}, u32[]{:S(2)}, u32[]{:S(2)}) collective-permute-start(bf16[400,128]{1,0:T(8,128)(2,1)S(1)} %get-tuple-element.41), channel_id=1, source_target_pairs={{0,8},{1,9},{2,10},{3,11},{4,12},{5,13},{6,14},{7,15},{8,0},{9,1},... | collective-permute-start | bytes 307208 | tf_op jit(solution)/shard_map/ppermute | solution.py:571
  188.5 10.3 %collective-permute-start.27 = (bf16[400,128]{1,0:T(8,128)(2,1)S(1)}, bf16[400,128]{1,0:T(8,128)(2,1)S(1)}, u32[]{:S(2)}, u32[]{:S(2)}) collective-permute-start(bf16[400,128]{1,0:T(8,128)(2,1)S(1)} %get-tuple-element.35), channel_id=1, source_target_pairs={{0,24},{1,25},{2,26},{3,27},{4,28},{5,29},{6,30},{7,31},{8,16},{9,... | collective-permute-start | bytes 307208 | tf_op jit(solution)/shard_map/ppermute | solution.py:571
  190.5 11.9 %collective-permute-start.26 = (bf16[400,128]{1,0:T(8,128)(2,1)S(1)}, bf16[400,128]{1,0:T(8,128)(2,1)S(1)}, u32[]{:S(2)}, u32[]{:S(2)}) collective-permute-start(bf16[400,128]{1,0:T(8,128)(2,1)S(1)} %get-tuple-element.36), channel_id=1, source_target_pairs={{0,16},{1,17},{2,18},{3,19},{4,20},{5,21},{6,22},{7,23},{8,24},{9,... | collective-permute-start | bytes 307208 | tf_op jit(solution)/shard_map/ppermute | solution.py:571
  190.7 11.7 %copy-start.12 = (bf16[400,128]{1,0:T(8,128)(2,1)}, bf16[400,128]{1,0:T(8,128)(2,1)S(1)}, u32[]{:S(2)}) copy-start(bf16[400,128]{1,0:T(8,128)(2,1)S(1)} %collective-permute-done.21.refs_3_) | copy-start | bytes 307204
  190.7 11.7 %collective-permute-start.25 = (bf16[400,128]{1,0:T(8,128)(2,1)S(1)}, bf16[400,128]{1,0:T(8,128)(2,1)S(1)}, u32[]{:S(2)}, u32[]{:S(2)}) collective-permute-start(bf16[400,128]{1,0:T(8,128)(2,1)S(1)} %get-tuple-element.37), channel_id=1, source_target_pairs={{0,8},{1,9},{2,10},{3,11},{4,12},{5,13},{6,14},{7,15},{8,0},{9,1},... | collective-permute-start | bytes 307208 | tf_op jit(solution)/shard_map/ppermute | solution.py:571
  198.8 3.6 %copy-start.13 = (bf16[400,128]{1,0:T(8,128)(2,1)}, bf16[400,128]{1,0:T(8,128)(2,1)S(1)}, u32[]{:S(2)}) copy-start(bf16[400,128]{1,0:T(8,128)(2,1)S(1)} %collective-permute-done.20.refs_2_) | copy-start | bytes 307204
  198.8 3.6 %copy-start.14 = (bf16[400,128]{1,0:T(8,128)(2,1)}, bf16[400,128]{1,0:T(8,128)(2,1)S(1)}, u32[]{:S(2)}) copy-start(bf16[400,128]{1,0:T(8,128)(2,1)S(1)} %collective-permute-done.19.refs_1_) | copy-start | bytes 307204
  198.8 3.6 %copy-start.15 = (bf16[400,128]{1,0:T(8,128)(2,1)}, bf16[400,128]{1,0:T(8,128)(2,1)S(1)}, u32[]{:S(2)}) copy-start(bf16[400,128]{1,0:T(8,128)(2,1)S(1)} %collective-permute-done.27.refs_7_) | copy-start | bytes 307204
  202.4 0.6 copy-start.16
  202.4 0.7 copy-start.17

commit v2 on v1

v2 whole, which is shorter than its diff:
```python
import functools
import math

import jax
import jax.numpy as jnp
from jax import lax
from jax.experimental import pallas as pl
from jax.experimental.pallas import tpu as pltpu
from jax.sharding import PartitionSpec as P

FF = 2048
HEADS = 8
REC = 2
TILE = 16
LANES = 128

norm_eps = 1e-05
mom_decay = 0.9
avg_keep = 0.8
rate_base = 0.006

BF = jnp.bfloat16
F32 = jnp.float32


def dot(a, b):
    return lax.dot_general(a, b, (((1,), (0,)), ((), ())), preferred_element_type=F32)


def dot_t(a, b):
    return lax.dot_general(a, b, (((1,), (1,)), ((), ())), preferred_element_type=F32)


def t_dot(a, b):
    return lax.dot_general(a, b, (((0,), (0,)), ((), ())), preferred_element_type=F32)


def one_hot_swap(outer, inner):
    size = outer * inner
    row = lax.broadcasted_iota(jnp.int32, (size, size), 0)
    col = lax.broadcasted_iota(jnp.int32, (size, size), 1)
    shift = inner.bit_length() - 1
    want = (row & (inner - 1)) * outer + (row >> shift)
    return jnp.where(col == want, 1.0, 0.0).astype(F32).astype(BF)


def matrix_blocks(wa, wi, wo, width):
    per = 4 * width // LANES
    base = 0
    for ref, per in ((wa, per), (wi, FF // LANES), (wo, width // LANES)):
        yield ref, per, base
        base = base + ref.shape[0] * per


def unpack_weights(flat, wa, wi, wo, b1, vec, width):
    for ref, per, base in matrix_blocks(wa, wi, wo, width):
        n = 256 // per
        swap = one_hot_swap(per, n)

        def body(g, carry, ref=ref, per=per, base=base, n=n, swap=swap):
            first = flat[pl.ds(pl.multiple_of(base + g * 512, 512), 256), :]
            second = flat[pl.ds(pl.multiple_of(base + g * 512, 512) + 256, 256), :]
            out = dot(swap, jnp.concatenate([first, second], axis=1)).astype(BF)
            row = pl.multiple_of(g * 2 * n, 2 * n)
            for c in range(per):
                piece = out[c * n : (c + 1) * n]
                cols = slice(c * LANES, (c + 1) * LANES)
                ref[pl.ds(row, 2 * n), cols] = jnp.concatenate([piece[:, :LANES], piece[:, LANES:]], axis=0)
            return carry

        lax.fori_loop(0, ref.shape[0] * per // 512, body, 0, unroll=8)
    per_out = width // LANES
    tail = flat[flat.shape[0] - FF // LANES - 8 * per_out : flat.shape[0], :].astype(F32)
    for c in range(FF // LANES):
        b1[0:1, c * LANES : (c + 1) * LANES] = tail[c : c + 1]
    for r in range(8):
        for c in range(per_out):
            k = FF // LANES + r * per_out + c
            vec[r : r + 1, c * LANES : (c + 1) * LANES] = tail[k : k + 1]


def pack_weights(flat, wa, wi, wo, width):
    for ref, per, base in matrix_blocks(wa, wi, wo, width):
        n = 256 // per
        swap = one_hot_swap(n, per)

        def body(g, carry, ref=ref, per=per, base=base, n=n, swap=swap):
            row = pl.multiple_of(g * 2 * n, 2 * n)
            pieces = []
            for c in range(per):
                v = ref[pl.ds(row, 2 * n), c * LANES : (c + 1) * LANES]
                pieces.append(jnp.concatenate([v[:n], v[n:]], axis=1))
            out = dot(swap, jnp.concatenate(pieces, axis=0)).astype(BF)
            first = pl.multiple_of(base + g * 512, 512)
            flat[pl.ds(first, 256), :] = out[:, :LANES]
            flat[pl.ds(first + 256, 256), :] = out[:, LANES:]
            return carry

        lax.fori_loop(0, ref.shape[0] * per // 512, body, 0, unroll=8)


def norm_stats(resid):
    center = resid - jnp.mean(resid, axis=-1, keepdims=True)
    variance = jnp.mean(center * center, axis=-1, keepdims=True)
    inv = lax.rsqrt(variance + norm_eps)
    return center * inv, inv


def norm_grad(upstream, normed, inv, gain):
    scaled = upstream * gain
    m0 = jnp.mean(scaled, axis=-1, keepdims=True)
    m1 = jnp.mean(scaled * normed, axis=-1, keepdims=True)
    return inv * (scaled - m0 - normed * m1)


def colsum(v):
    return jnp.sum(v, axis=0, keepdims=True)


def lane_mask(which, dtype):
    lane = lax.broadcasted_iota(jnp.int32, (1, LANES), 1)
    keep = (lane < 64) if which == 0 else (lane >= 64)
    return jnp.where(keep, 1.0, 0.0).astype(F32).astype(dtype)


C0 = math.sqrt(2.0 / math.pi)


def gelu_pair(u):
    u2 = u * u
    inner = u * (C0 + (C0 * 0.044715) * u2)
    half = 0.5 + 0.5 * jnp.tanh(inner)
    g = u * half
    slope = half + 2.0 * g * (1.0 - half) * (C0 + (3.0 * C0 * 0.044715) * u2)
    return g, slope


def window_starts(shards, tiles):
    return [i * tiles // shards for i in range(shards + 1)]


def own_index():
    return lax.axis_index("dp") * lax.axis_size("rep") + lax.axis_index("rep")


def load_windows(w_refs, pieces, flat, edge, sem, shards):
    tiles = flat.shape[0] // TILE
    rows = [ref.shape[-2] for ref in w_refs]
    half = rows[0]
    base = tiles // shards * TILE
    me = own_index()
    copies = []
    for ref, (part, entries) in zip(w_refs, pieces):
        for pos, rel in entries:
            src = ref
            for k in pos:
                src = src.at[k]
            owner = jnp.bitwise_xor(me, rel)
            start = pl.multiple_of((owner * tiles // shards) * TILE, TILE)
            if part == 0:
                moves = [(src, flat.at[pl.ds(start, half)])]
            else:
                moves = [
                    (src.at[pl.ds(0, base - half)], flat.at[pl.ds(pl.multiple_of(start + half, TILE), base - half)]),
                    (src.at[pl.ds(base - half, 2 * TILE)], edge.at[owner]),
                ]
            for a, b in moves:
                copies.append(pltpu.make_async_copy(a, b, sem.at[len(copies)]))
                copies[-1].start()
    for copy in copies:
        copy.wait()
    starts = window_starts(shards, tiles)
    for i in range(shards):
        nxt = starts[i + 1]
        low = edge[i, 0:TILE, :]
        if nxt - starts[i] == base // TILE:
            if i + 1 < shards:
                flat[nxt * TILE : (nxt + 1) * TILE, :] = flat[nxt * TILE : (nxt + 1) * TILE, :] + low
        else:
            flat[(nxt - 1) * TILE : nxt * TILE, :] = low
            if i + 1 < shards:
                flat[nxt * TILE : (nxt + 1) * TILE, :] = flat[nxt * TILE : (nxt + 1) * TILE, :] + edge[i, TILE : 2 * TILE, :]


def store_windows(g_refs, flat, edge, sem, shards, vec_rows):
    tiles = flat.shape[0] // TILE
    half = g_refs[0].shape[-2]
    whole = 2 * half
    starts = window_starts(shards, tiles)
    last = lax.broadcasted_iota(jnp.int32, (TILE, LANES), 0) == TILE - 1
    for i in range(shards):
        low = starts[i] * TILE + whole - TILE
        if low + TILE <= flat.shape[0]:
            tile = flat[low : low + TILE, :].astype(F32)
        else:
            tile = jnp.zeros((TILE, LANES), F32)
        edge[i, 0:TILE, :] = jnp.where(last, vec_rows[i : i + 1], tile).astype(BF)
    me = own_index()
    copies = []
    for part in range(2):
        for rc in range(2):
            ref = g_refs[2 * rc + part]
            for r0 in range(2):
                for r1 in range(2):
                    rx, ry = (r0, r1) if part == 0 else (r1, r0)
                    for rz in range(4):
                        owner = jnp.bitwise_xor(me, rz * 8 + rx * 4 + rc * 2 + ry)
                        start = pl.multiple_of((owner * tiles // shards) * TILE, TILE)
                        dst = ref.at[r0].at[r1].at[rz]
                        if part == 0:
                            moves = [(flat.at[pl.ds(start, half)], dst)]
                        else:
                            moves = [
                                (flat.at[pl.ds(pl.multiple_of(start + half, TILE), half - TILE)], dst.at[pl.ds(0, half - TILE)]),
                                (edge.at[owner].at[pl.ds(0, TILE)], dst.at[pl.ds(half - TILE, TILE)]),
                            ]
                        for a, b in moves:
                            copies.append(pltpu.make_async_copy(a, b, sem.at[len(copies)]))
                            copies[-1].start()
    for copy in copies:
        copy.wait()


def pack_kernel(x_ref, a_ref, b_ref):
    me = own_index()
    v = x_ref[...]
    rows = v.shape[0]
    lane = lax.broadcasted_iota(jnp.int32, v.shape, 1)
    turned = pltpu.roll(v, 64, 1)
    moved = jnp.where(lane >= 64, turned, pltpu.roll(turned, 1, 0))
    odd = (me & 1) == 1
    v = jnp.where(odd, moved, v)
    shift = ((me * 192) & 2047) >> 7
    v = pltpu.roll(v, shift, 0).astype(BF)
    a_ref[...] = v[: rows // 2]
    b_ref[...] = v[rows // 2 :]


def finish_kernel(*refs):
    parts = []
    for h in range(2):
        total = None
        for ref in refs[4 * h : 4 * h + 4]:
            v = ref[...].astype(F32)
            total = v if total is None else total + v
        parts.append(total)
    out_ref, vec_ref = refs[8:]
    v = jnp.concatenate(parts, axis=0)
    rows = v.shape[0]
    vec_ref[...] = v[rows - 8 :]
    me = own_index()
    shift = ((me * 192) & 2047) >> 7
    v = pltpu.roll(v, rows - shift, 0)
    lane = lax.broadcasted_iota(jnp.int32, v.shape, 1)
    turned = pltpu.roll(v, 64, 1)
    moved = jnp.where(lane < 64, turned, pltpu.roll(turned, rows - 1, 0))
    odd = (me & 1) == 1
    out_ref[...] = jnp.where(odd, moved, v)


CHUNK = 512
STEP = 32
GSTEP = 16
AHEAD = 2


def core_kernel(*refs, width, length, shards, pieces, flat_rows):
    n_in = 1 if pieces is None else len(pieces)
    (x_ref, cot_ref, segr_ref, segc_ref) = refs[:4]
    w_refs = refs[4 : 4 + n_in]
    refs = refs[4 + n_in :]
    (y_ref, dx_ref) = refs[:2]
    n_out = 1 if pieces is None else 4
    g_refs = refs[2 : 2 + n_out]
    (wide, wa, wi, wo, b1, vec, xb, qkv, ab, ctx, xh1, iv1, xh2, iv2, h1b, slope, df, da, dqkv, dc, dr1, edge,
     bias, gb1, gvec, count_ref, sem) = refs[2 + n_out :]
    D = width
    T = length
    pairs = D // LANES
    flat = wide.at[pl.ds(0, flat_rows)]

    if pieces is None:
        cp = pltpu.make_async_copy(w_refs[0], flat, sem.at[0])
        cp.start()
        cp.wait()
    else:
        load_windows(w_refs, pieces, flat, edge, sem, shards)
    unpack_weights(flat, wa, wi, wo, b1, vec, D)

    scale = 0.125
    bias[...] = jnp.where(segc_ref[...] == segr_ref[...], 0.0, -1e30).astype(F32)

    count_ref[0] = 1
    single = count_ref[0]

    def phase(body):
        def step(_, carry):
            body()
            return carry

        lax.fori_loop(0, single, step, 0)

    hidden = FF * REC * T // LANES

    def put(which, chunk, row, val):
        for j in range(CHUNK // LANES):
            at = which * hidden + (chunk * (CHUNK // LANES) + j) * REC * T
            wide[pl.ds(row + at, val.shape[0]), :] = val[:, j * LANES : (j + 1) * LANES]

    def get(which, chunk, row, n):
        at = [which * hidden + (chunk * (CHUNK // LANES) + j) * REC * T for j in range(CHUNK // LANES)]
        return jnp.concatenate([wide[pl.ds(row + k, n), :] for k in at], axis=1)

    def project(r):
        rows = pl.ds(pl.multiple_of(r * T, T), T)
        x16 = dx_ref[...].astype(BF)
        xb[rows, :] = x16
        for j in range(3):
            p = dot(x16, wa[:, j * D : (j + 1) * D])
            if j == 0:
                p = p + vec[0:1, :]
            if j == 2:
                p = p + vec[1:2, :]
            p = p.astype(BF)
            for c in range(pairs):
                qkv[r, j * pairs + c] = p[:, c * LANES : (c + 1) * LANES]

    def attend(r):
        rows = pl.ds(pl.multiple_of(r * T, T), T)

        def score(h):
            return dot_t(qkv[r, h // 2] * (lane_mask(h % 2, BF) * scale).astype(BF), qkv[r, pairs + h // 2])

        pend = [score(h) for h in range(AHEAD)]
        left = None
        for h in range(HEADS):
            if h + AHEAD < HEADS:
                pend.append(score(h + AHEAD))
            full = pend.pop(0)
            parts = []
            for i in range(0, T, STEP):
                sc = full[i : i + STEP] + bias[i : i + STEP, :]
                ex = jnp.exp(sc - jnp.max(sc, axis=-1, keepdims=True))
                tot = jnp.sum(ex, axis=-1, keepdims=True)
                parts.append((ex * (1.0 / tot)).astype(BF))
                ab[r * HEADS + h, pl.ds(i, STEP), :] = parts[-1]
            out = dot(jnp.concatenate(parts, axis=0), qkv[r, 2 * pairs + h // 2] * lane_mask(h % 2, BF))
            if h % 2 == 0:
                left = out
            else:
                ctx[h // 2, rows, :] = (left + out).astype(BF)

    def feed(r):
        rows = pl.ds(pl.multiple_of(r * T, T), T)
        a = dot(jnp.concatenate([ctx[c, rows, :] for c in range(pairs)], axis=1), wa[:, 3 * D : 4 * D])
        for i in range(0, T, STEP):
            sub = pl.ds(i, STEP)
            hat, inv = norm_stats(dx_ref[sub, :] + (a[i : i + STEP] + vec[2:3, :]))
            xh1[r, sub, :] = hat
            iv1[r, sub, :] = jnp.broadcast_to(inv, (STEP, LANES))
            h1b[pl.ds(pl.multiple_of(r * T, T) + i, STEP), :] = (hat * vec[4:5, :] + vec[5:6, :]).astype(BF)
        h16 = h1b[rows, :]

        def up(c):
            return dot(h16, wi[:, c * CHUNK : (c + 1) * CHUNK])

        pend = [up(0)]
        f = None
        for c in range(FF // CHUNK):
            cols = slice(c * CHUNK, (c + 1) * CHUNK)
            if c + 1 < FF // CHUNK:
                pend.append(up(c + 1))
            u = pend.pop(0)
            parts = []
            for i in range(0, T, GSTEP):
                g, sl = gelu_pair(u[i : i + GSTEP] + b1[:, cols])
                parts.append(g.astype(BF))
                put(0, c, pl.multiple_of(r * T, T) + i, parts[-1])
                slope[r, pl.ds(i, GSTEP), cols] = sl
            part = dot(jnp.concatenate(parts, axis=0), wo[cols, :])
            f = part if f is None else f + part
        for i in range(0, T, STEP):
            sub = pl.ds(i, STEP)
            h1 = xh1[r, sub, :] * vec[4:5, :] + vec[5:6, :]
            hat, inv = norm_stats(h1 + (f[i : i + STEP] + vec[3:4, :]))
            xh2[r, sub, :] = hat
            iv2[r, sub, :] = jnp.broadcast_to(inv, (STEP, LANES))
            y = hat * vec[6:7, :] + vec[7:8, :]
            dx_ref[sub, :] = y

    def acc(ref, row, val):
        ref[row : row + 1, :] = ref[row : row + 1, :] + val

    def feed_back(r):
        rows = pl.ds(pl.multiple_of(r * T, T), T)
        sums = [jnp.zeros((8, D), F32) for _ in range(6)]

        def add(k, val):
            sums[k] = sums[k] + jnp.sum(val.reshape(STEP // 8, 8, D), axis=0)

        for i in range(0, T, STEP):
            sub = pl.ds(i, STEP)
            dy = dx_ref[sub, :]
            hat = xh2[r, sub, :]
            add(0, dy * hat)
            add(1, dy)
            dr2 = norm_grad(dy, hat, iv2[r, sub, 0:1], vec[6:7, :])
            dr1[sub, :] = dr2
            d16 = dr2.astype(BF)
            df[pl.ds(pl.multiple_of(r * T, T) + i, STEP), :] = d16
            add(2, d16.astype(F32))
        d16 = df[rows, :]

        def down(c):
            return dot_t(d16, wo[c * CHUNK : (c + 1) * CHUNK, :])

        pend = [down(0)]
        dh = None
        for c in range(FF // CHUNK):
            cols = slice(c * CHUNK, (c + 1) * CHUNK)
            if c + 1 < FF // CHUNK:
                pend.append(down(c + 1))
            t = pend.pop(0)
            tot = jnp.zeros((8, CHUNK), F32)
            parts = []
            for i in range(0, T, GSTEP):
                g16 = (t[i : i + GSTEP].astype(BF).astype(F32) * slope[r, pl.ds(i, GSTEP), cols]).astype(BF)
                parts.append(g16)
                put(1, c, pl.multiple_of(r * T, T) + i, g16)
                tot = tot + jnp.sum(g16.astype(F32).reshape(GSTEP // 8, 8, CHUNK), axis=0)
            gb1[0:1, cols] = gb1[0:1, cols] + colsum(tot)
            part = dot_t(jnp.concatenate(parts, axis=0), wi[:, cols])
            dh = part if dh is None else dh + part
        for i in range(0, T, STEP):
            sub = pl.ds(i, STEP)
            hat = xh1[r, sub, :]
            upstream = dr1[sub, :] + dh[i : i + STEP]
            add(3, upstream * hat)
            add(4, upstream)
            d1 = norm_grad(upstream, hat, iv1[r, sub, 0:1], vec[4:5, :])
            dr1[sub, :] = d1
            a16 = d1.astype(BF)
            da[pl.ds(pl.multiple_of(r * T, T) + i, STEP), :] = a16
            add(5, a16.astype(F32))
        for row, k in ((6, 0), (7, 1), (3, 2), (4, 3), (5, 4), (2, 5)):
            acc(gvec, row, colsum(sums[k]))
        c16 = dot_t(da[rows, :], wa[:, 3 * D : 4 * D]).astype(BF)
        for c in range(pairs):
            dc[c] = c16[:, c * LANES : (c + 1) * LANES]

    def attend_back(r):
        rows = pl.ds(pl.multiple_of(r * T, T), T)

        def rise(h):
            return dot_t(dc[h // 2] * lane_mask(h % 2, BF), qkv[r, 2 * pairs + h // 2])

        pend = [rise(h) for h in range(AHEAD)]
        for h in range(HEADS):
            if h + AHEAD < HEADS:
                pend.append(rise(h + AHEAD))
            full = pend.pop(0)
            p, e = h // 2, h % 2
            half = slice(64 * e, 64 * e + 64)
            if e == 0:
                qt = jnp.transpose(qkv[r, p])
                ct = jnp.transpose(dc[p])
                dkt, dvt = [], []
            p16 = ab[r * HEADS + h]
            parts = []
            for i in range(0, T, STEP):
                pf = p16[i : i + STEP].astype(F32)
                t = full[i : i + STEP] * pf
                parts.append((t - pf * jnp.sum(t, axis=-1, keepdims=True)).astype(BF))
            s16 = jnp.concatenate(parts, axis=0)
            part = dot(s16, qkv[r, pairs + p] * lane_mask(e, BF))
            dkt.append(dot(qt[half], s16))
            dvt.append(dot(ct[half], p16))
            if e == 0:
                dq = part
            else:
                dqkv[p, rows, :] = ((dq + part) * scale).astype(BF)
                dqkv[pairs + p, rows, :] = jnp.transpose((jnp.concatenate(dkt, axis=0) * scale).astype(BF))
                dqkv[2 * pairs + p, rows, :] = jnp.transpose(jnp.concatenate(dvt, axis=0).astype(BF))
    def project_back(r):
        rows = pl.ds(pl.multiple_of(r * T, T), T)
        for c in range(pairs):
            cols = slice(c * LANES, (c + 1) * LANES)
            gvec[0:1, cols] = gvec[0:1, cols] + colsum(dqkv[c, rows, :].astype(F32))
            gvec[1:2, cols] = gvec[1:2, cols] + colsum(dqkv[2 * pairs + c, rows, :].astype(F32))
        d3 = jnp.concatenate([dqkv[c, rows, :] for c in range(3 * pairs)], axis=1)
        dx_ref[...] = dr1[...] + dot_t(d3, wa[:, : 3 * D])

    gb1[...] = jnp.zeros_like(gb1)
    gvec[...] = jnp.zeros_like(gvec)
    dx_ref[...] = x_ref[...].astype(F32)

    def forward(r, carry):
        for part in (project, attend, feed):
            phase(functools.partial(part, r))
        return carry

    def backward(i, carry):
        for part in (feed_back, attend_back, project_back):
            phase(functools.partial(part, REC - 1 - i))
        return carry

    lax.fori_loop(0, REC, forward, 0)
    y_ref[...] = dx_ref[...]
    dx_ref[...] = cot_ref[...].astype(F32)
    lax.fori_loop(0, REC, backward, 0)

    def grad_qkvo():
        xt = jnp.transpose(xb[...])
        for j in range(3):
            d3 = jnp.concatenate([dqkv[j * pairs + c] for c in range(pairs)], axis=1)
            wa[:, j * D : (j + 1) * D] = dot(xt, d3).astype(BF)
        for c in range(pairs):
            wa[c * LANES : (c + 1) * LANES, 3 * D : 4 * D] = t_dot(ctx[c], da[...]).astype(BF)

    def grad_in():
        ht = jnp.transpose(h1b[...])
        for c in range(FF // CHUNK):
            cols = slice(c * CHUNK, (c + 1) * CHUNK)
            wi[:, cols] = dot(ht, get(1, c, 0, REC * T)).astype(BF)

    def grad_out():
        for c in range(FF // CHUNK):
            cols = slice(c * CHUNK, (c + 1) * CHUNK)
            wo[cols, :] = t_dot(get(0, c, 0, REC * T), df[...]).astype(BF)

    phase(grad_qkvo)
    phase(grad_in)
    phase(grad_out)
    pack_weights(flat, wa, wi, wo, D)
    per_out = D // LANES
    rows = [gb1[0:1, c * LANES : (c + 1) * LANES] for c in range(FF // LANES)]
    for r in range(8):
        rows = rows + [gvec[r : r + 1, c * LANES : (c + 1) * LANES] for c in range(per_out)]
    tail = jnp.concatenate(rows, axis=0)
    flat[flat.shape[0] - len(rows) : flat.shape[0], :] = tail.astype(BF)
    if pieces is None:
        cp = pltpu.make_async_copy(flat, g_refs[0], sem.at[0])
        cp.start()
        cp.wait()
    else:
        store_windows(g_refs, flat, edge, sem, shards, tail[FF // LANES :])


def core(x, cot, seg, flats, pieces, shards, rows):
    T, D = x.shape
    vm = pltpu.VMEM
    pairs = D // LANES
    scratch = [
        vm((max(2 * FF * REC * T // LANES, rows), LANES), BF),
        vm((D, 4 * D), BF), vm((D, FF), BF), vm((FF, D), BF), vm((1, FF), F32), vm((8, D), F32),
        vm((REC * T, D), BF), vm((REC, 3 * pairs, T, LANES), BF), vm((REC * HEADS, T, T), BF), vm((pairs, REC * T, LANES), BF),
        vm((REC, T, D), F32), vm((REC, T, LANES), F32), vm((REC, T, D), F32), vm((REC, T, LANES), F32),
        vm((REC * T, D), BF), vm((REC, T, FF), F32),
        vm((REC * T, D), BF), vm((REC * T, D), BF), vm((3 * pairs, REC * T, LANES), BF), vm((pairs, T, LANES), BF),
        vm((T, D), F32), vm((shards if pieces else 1, 2 * TILE, LANES), BF), vm((T, T), F32),
        vm((1, FF), F32), vm((8, D), F32),
        pltpu.SMEM((1,), jnp.int32), pltpu.SemaphoreType.DMA((96,)),
    ]
    if pieces is None:
        g_shapes = [jax.ShapeDtypeStruct((rows, LANES), BF)]
    else:
        half = flats[0].shape[-2]
        g_shapes = [jax.ShapeDtypeStruct((2, 2, 4, half, LANES), BF)] * 4
    in_vmem = pl.BlockSpec(memory_space=pltpu.VMEM)
    anywhere = pl.BlockSpec(memory_space=pl.ANY)
    return pl.pallas_call(
        functools.partial(core_kernel, width=D, length=T, shards=shards, pieces=pieces, flat_rows=rows),
        out_shape=tuple([jax.ShapeDtypeStruct((T, D), F32)] * 2 + g_shapes),
        in_specs=[in_vmem] * 4 + [anywhere] * len(flats),
        out_specs=tuple([in_vmem] * 2 + [anywhere] * len(g_shapes)),
        scratch_shapes=scratch,
        compiler_params=pltpu.CompilerParams(vmem_limit_bytes=59 * 1024 * 1024),
        name="layer_core",
    )(x, cot, seg.reshape(1, T), seg.reshape(T, 1), *flats)


AXES = ("dp", "rep")


def exchange(v, rel):
    count = lax.axis_size("dp") * lax.axis_size("rep")
    return lax.ppermute(v, AXES, [(j, j ^ rel) for j in range(count)])


RZ, RX, RC, RY = 8, 4, 2, 1


def gather_windows(a, b):
    out, pieces = [], []
    for part, own in enumerate((a, b)):
        first, second = (RX, RY) if part == 0 else (RY, RX)
        stack = jnp.stack([own] + [exchange(own, k * RZ) for k in (1, 2, 3)])
        near = exchange(stack, first)
        far = exchange(jnp.stack([stack, near]), second)
        for rc in (0, RC):
            for v, dims in ((stack, (0,)), (near, (first,)), (far, (second,))):
                out.append(v if rc == 0 else exchange(v, rc))
                if v is far:
                    ent = [((n, k), k * RZ + second + n * first + rc) for n in range(2) for k in range(4)]
                else:
                    ent = [((k,), k * RZ + dims[0] + rc) for k in range(4)]
                pieces.append((part, ent))
    order = sorted(range(len(out)), key=lambda i: pieces[i][0])
    return [out[i] for i in order], [pieces[i] for i in order]


def sum_windows(keeps, sends):
    res = []
    for part in range(2):
        first, second = (RX, RY) if part == 0 else (RY, RX)
        got = exchange(sends[part], RC)
        keep = keeps[part]
        got1 = exchange(keep[1] + got[1], first)
        mine = keep[0] + got[0]
        got2 = exchange(mine[1] + got1[1], second)
        mine = mine[0] + got1[0]
        v = mine + got2
        res.append([v[0]] + [exchange(v[k], k * RZ) for k in (1, 2, 3)])
    return res


def shards_fn(block_input, segment_ids, cotangent, master_weights, momentum, weight_average):
    width = block_input.shape[2]
    length = block_input.shape[1]
    count = lax.axis_size("dp") * lax.axis_size("rep")
    share = master_weights.shape[0]
    rows = share * count // LANES
    tiles = rows // TILE
    vec_len = 8 * width // count
    args = (block_input[0], cotangent[0], segment_ids[0])
    in_vmem = pl.BlockSpec(memory_space=pltpu.VMEM)
    if count == 32:
        window = (tiles // count + 2) * TILE
        padded = jnp.pad(master_weights, (0, window * LANES - share)).reshape(window, LANES)
        half = jax.ShapeDtypeStruct((window // 2, LANES), BF)
        a, b = pl.pallas_call(
            pack_kernel, out_shape=(half, half), in_specs=[in_vmem], out_specs=(in_vmem, in_vmem), name="pack_shard"
        )(padded)
        flats, pieces = gather_windows(a, b)
        block_output, input_grad, ka, kb, sa, sb = core(*args, flats, pieces, count, rows)
        parts = sum_windows((ka, kb), (sa, sb))
        grad, tail = pl.pallas_call(
            finish_kernel,
            out_shape=(jax.ShapeDtypeStruct((window, LANES), F32), jax.ShapeDtypeStruct((8, LANES), F32)),
            in_specs=[in_vmem] * 8,
            out_specs=(in_vmem, in_vmem),
            name="finish_shard",
        )(*parts[0], *parts[1])
        weight_grad = grad.reshape(-1)[:share]
        vector_grad = tail[7]
    else:
        flat = lax.all_gather(master_weights.astype(BF), AXES, axis=0, tiled=True).reshape(rows, LANES)
        block_output, input_grad, grad = core(*args, [flat], None, count, rows)
        grad = grad.reshape(-1).astype(F32)
        weight_grad = lax.psum_scatter(grad, AXES, scatter_dimension=0, tiled=True)
        vector_grad = lax.psum_scatter(grad[grad.shape[0] - 8 * width :], AXES, scatter_dimension=0, tiled=True)
    token_count = block_input.shape[0] * length * count
    rate = rate_base / math.sqrt(token_count)
    new_momentum = mom_decay * momentum + weight_grad
    new_weights = master_weights - rate * (weight_grad + mom_decay * new_momentum)
    new_average = avg_keep * weight_average + (1.0 - avg_keep) * new_weights
    return (
        block_output[None],
        input_grad[None],
        weight_grad,
        vector_grad,
        new_momentum,
        new_average,
        new_weights,
    )


def solution(mesh):
    three = P(AXES, None, None)
    two = P(AXES, None)
    one = P(AXES)
    return jax.shard_map(
        shards_fn,
        mesh=mesh,
        in_specs=(three, two, three, one, one, one),
        out_specs=(three, three, one, one, one, one, one),
        check_vma=False,
    )
```

time: 209 us -> 189 us (0.904)
  Pallas kernels: 88 us -> 67.6 us
    pallas_call x1, Pallas kernels: 83.6 us -> 63.1 us  [core(): pl.pallas_call(functools.partial(core_kernel, width=D, length=T, shards=s...]
where the time goes in v2:
time: 189 us; the launch traced here: 188 us
  waiting for transfers between devices  68.4 us (36%)
  Pallas kernels  67.6 us (36%)
  starting transfers between devices  38.5 us (20%)
  local copies, waits for them, and re-layouts  6.83 us (4%)
  other arithmetic  6.39 us (3%)
    ppermute x28, waiting for transfers between devices, exchange(): return lax.ppermute(v, AXES, [(j, j ^ rel) for j in range(count)])  68.4 us
    pallas_call x1, Pallas kernels, core(): pl.pallas_call(functools.partial(core_kernel, width=D, length=T, shards=s...  63.1 us
    ppermute x28, starting transfers between devices, exchange(): return lax.ppermute(v, AXES, [(j, j ^ rel) for j in range(count)])  38.5 us
  transfers between devices with their start and end apart: 28, of which 14 were waited for; matrix products, arithmetic and copies ran while one was open for 3% of the time, Pallas kernels for 0%

profile of v2, /device:TPU:0, one launch (start us, length us, event | category | flops | bytes accessed | tf_op | source)
XLA Modules:
  0.0 188.4 jit_solution(16873789232045718575)
XLA Ops:
  0.6 1.8 pad_bitcast_fusion.x_ref
  2.4 2.0 %pack_shard.1 = (bf16[400,128]{1,0:T(8,128)(2,1)}, bf16[400,128]{1,0:T(8,128)(2,1)}) custom-call(f32[800,128]{1,0:T(8,128)} %pad_bitcast_fusion.x_ref), custom_call_target="tpu_custom_call" | custom-call | tf_op jit(solution)/shard_map/pack_shard/pallas_call | solution.py:641
  4.4 5.0 %collective-permute-start.10 = (bf16[400,128]{1,0:T(8,128)(2,1)}, bf16[400,128]{1,0:T(8,128)(2,1)S(1)}, u32[]{:S(2)}, u32[]{:S(2)}) collective-permute-start(bf16[400,128]{1,0:T(8,128)(2,1)} %get-tuple-element.18), channel_id=1, source_target_pairs={{0,24},{1,25},{2,26},{3,27},{4,28},{5,29},{6,30},{7,31},{8,16},{9,... | collective-permute-start | bytes 307208 | tf_op jit(solution)/shard_map/ppermute | solution.py:587
  9.4 0.6 collective-permute-start.8
  10.0 3.8 %collective-permute-start.2 = (bf16[400,128]{1,0:T(8,128)(2,1)}, bf16[400,128]{1,0:T(8,128)(2,1)S(1)}, u32[]{:S(2)}, u32[]{:S(2)}) collective-permute-start(bf16[400,128]{1,0:T(8,128)(2,1)} %get-tuple-element.17), channel_id=1, source_target_pairs={{0,24},{1,25},{2,26},{3,27},{4,28},{5,29},{6,30},{7,31},{8,16},{9,... | collective-permute-start | bytes 307208 | tf_op jit(solution)/shard_map/ppermute | solution.py:587
  13.8 4.6 %collective-permute-start = (bf16[400,128]{1,0:T(8,128)(2,1)}, bf16[400,128]{1,0:T(8,128)(2,1)S(1)}, u32[]{:S(2)}, u32[]{:S(2)}) collective-permute-start(bf16[400,128]{1,0:T(8,128)(2,1)} %get-tuple-element.17), channel_id=1, source_target_pairs={{0,8},{1,9},{2,10},{3,11},{4,12},{5,13},{6,14},{7,15},{8,0},{9,1},... | collective-permute-start | bytes 307208 | tf_op jit(solution)/shard_map/ppermute | solution.py:587
  18.4 5.2 %collective-permute-done.9 = bf16[400,128]{1,0:T(8,128)(2,1)S(1)} collective-permute-done((bf16[400,128]{1,0:T(8,128)(2,1)}, bf16[400,128]{1,0:T(8,128)(2,1)S(1)}, u32[]{:S(2)}, u32[]{:S(2)}) %collective-permute-start.9) | collective-permute-done | bytes 102432 | tf_op jit(solution)/shard_map/ppermute | solution.py:587
  23.6 1.0 fusion.8
  24.6 1.6 collective-permute-start.11
  26.2 0.9 collective-permute-done.1
  27.0 1.0 fusion.9
  28.0 1.6 collective-permute-start.3
  29.6 4.1 %collective-permute-done.11.refs_11_ = bf16[4,400,128]{2,1,0:T(8,128)(2,1)S(1)} collective-permute-done((bf16[4,400,128]{2,1,0:T(8,128)(2,1)S(1)}, bf16[4,400,128]{2,1,0:T(8,128)(2,1)S(1)}, u32[]{:S(2)}, u32[]{:S(2)}) %collective-permute-start.11) | collective-permute-done | bytes 409632 | tf_op jit(solution)/shard_map/ppermute | solution.py:587
  33.7 1.6 collective-permute-start.12
  35.3 5.2 %collective-permute-done.3.refs_5_ = bf16[4,400,128]{2,1,0:T(8,128)(2,1)S(1)} collective-permute-done((bf16[4,400,128]{2,1,0:T(8,128)(2,1)S(1)}, bf16[4,400,128]{2,1,0:T(8,128)(2,1)S(1)}, u32[]{:S(2)}, u32[]{:S(2)}) %collective-permute-start.3) | collective-permute-done | bytes 409632 | tf_op jit(solution)/shard_map/ppermute | solution.py:587
  40.6 1.6 collective-permute-start.4
  42.2 14.0 %collective-permute-done.12.refs_12_ = bf16[2,4,400,128]{3,2,1,0:T(8,128)(2,1)S(1)} collective-permute-done((bf16[2,4,400,128]{3,2,1,0:T(8,128)(2,1)S(1)}, bf16[2,4,400,128]{3,2,1,0:T(8,128)(2,1)S(1)}, u32[]{:S(2)}, u32[]{:S(2)}) %collective-permute-start.12) | collective-permute-done | bytes 819232 | tf_op jit(solution)/shard_map/ppermute | solution.py:587
  56.2 1.0 collective-permute-done.4.refs_6_
  57.1 0.5 collective-permute-start.13
  57.7 0.5 collective-permute-start.14
  58.2 0.3 copy-done.8
  58.5 0.9 copy.13.refs_3_
  59.3 1.6 collective-permute-done.13.refs_13_
  61.0 0.6 collective-permute-done.6.refs_8_
  61.6 0.7 copy-done.9
  62.3 63.1 %layer_core.1 = (f32[512,512]{1,0:T(8,128)}, f32[512,512]{1,0:T(8,128)}, bf16[2,2,4,400,128]{4,3,2,1,0:T(8,128)(2,1)}, bf16[2,2,4,400,128]{4,3,2,1,0:T(8,128)(2,...) custom-call(bf16[512,512]{1,0:T(8,128)(2,1)} %bitcast.74, bf16[512,512]{1,0:T(8,128)(2,1)} %bitcast.75, ...), custom_call_target="tpu_custom_call" | custom-call | tf_op jit(solution)/shard_map/layer_core/pallas_call | solution.py:571
  125.7 0.4 collective-permute-start.22
  126.0 3.2 %collective-permute-done.16 = bf16[2,2,4,400,128]{4,3,2,1,0:T(8,128)(2,1)S(1)} collective-permute-done((bf16[2,2,4,400,128]{4,3,2,1,0:T(8,128)(2,1)}, bf16[2,2,4,400,128]{4,3,2,1,0:T(8,128)(2,1)S(1)}, u32[]{:S(2)}, u32[]{:S(2)}) %collective-permute-start.16) | collective-permute-done | bytes 1638432 | tf_op jit(solution)/shard_map/ppermute | solution.py:587
  129.2 1.7 slice_add_fusion.3
  131.0 1.6 collective-permute-start.17
  132.7 1.6 collective-permute-start.23
  134.3 17.0 %collective-permute-done.17 = bf16[2,4,400,128]{3,2,1,0:T(8,128)(2,1)S(1)} collective-permute-done((bf16[2,4,400,128]{3,2,1,0:T(8,128)(2,1)S(1)}, bf16[2,4,400,128]{3,2,1,0:T(8,128)(2,1)S(1)}, u32[]{:S(2)}, u32[]{:S(2)}) %collective-permute-start.17) | collective-permute-done | bytes 819232 | tf_op jit(solution)/shard_map/ppermute | solution.py:587
  151.4 1.6 collective-permute-start.18
  153.0 1.6 collective-permute-start.24
  154.6 7.5 %collective-permute-done.18 = bf16[4,400,128]{2,1,0:T(8,128)(2,1)S(1)} collective-permute-done((bf16[4,400,128]{2,1,0:T(8,128)(2,1)S(1)}, bf16[4,400,128]{2,1,0:T(8,128)(2,1)S(1)}, u32[]{:S(2)}, u32[]{:S(2)}) %collective-permute-start.18) | collective-permute-done | bytes 409632 | tf_op jit(solution)/shard_map/ppermute | solution.py:587
  162.2 0.7 slice_bitcast_fusion.8
  162.8 2.0 %collective-permute-start.21 = (bf16[400,128]{1,0:T(8,128)(2,1)S(1)}, bf16[400,128]{1,0:T(8,128)(2,1)S(1)}, u32[]{:S(2)}, u32[]{:S(2)}) collective-permute-start(bf16[400,128]{1,0:T(8,128)(2,1)S(1)} %get-tuple-element.39), channel_id=1, source_target_pairs={{0,24},{1,25},{2,26},{3,27},{4,28},{5,29},{6,30},{7,31},{8,16},{9,... | collective-permute-start | bytes 307208 | tf_op jit(solution)/shard_map/ppermute | solution.py:587
  164.9 2.4 %collective-permute-start.19 = (bf16[400,128]{1,0:T(8,128)(2,1)S(1)}, bf16[400,128]{1,0:T(8,128)(2,1)S(1)}, u32[]{:S(2)}, u32[]{:S(2)}) collective-permute-start(bf16[400,128]{1,0:T(8,128)(2,1)S(1)} %get-tuple-element.41), channel_id=1, source_target_pairs={{0,8},{1,9},{2,10},{3,11},{4,12},{5,13},{6,14},{7,15},{8,0},{9,1},... | collective-permute-start | bytes 307208 | tf_op jit(solution)/shard_map/ppermute | solution.py:587
  167.3 0.7 slice_bitcast_fusion.4
  168.0 2.0 %collective-permute-start.27 = (bf16[400,128]{1,0:T(8,128)(2,1)S(1)}, bf16[400,128]{1,0:T(8,128)(2,1)S(1)}, u32[]{:S(2)}, u32[]{:S(2)}) collective-permute-start(bf16[400,128]{1,0:T(8,128)(2,1)S(1)} %get-tuple-element.35), channel_id=1, source_target_pairs={{0,24},{1,25},{2,26},{3,27},{4,28},{5,29},{6,30},{7,31},{8,16},{9,... | collective-permute-start | bytes 307208 | tf_op jit(solution)/shard_map/ppermute | solution.py:587
  170.0 0.2 collective-permute-done.21.refs_3_
  170.2 3.8 %collective-permute-start.25 = (bf16[400,128]{1,0:T(8,128)(2,1)S(1)}, bf16[400,128]{1,0:T(8,128)(2,1)S(1)}, u32[]{:S(2)}, u32[]{:S(2)}) collective-permute-start(bf16[400,128]{1,0:T(8,128)(2,1)S(1)} %get-tuple-element.37), channel_id=1, source_target_pairs={{0,8},{1,9},{2,10},{3,11},{4,12},{5,13},{6,14},{7,15},{8,0},{9,1},... | collective-permute-start | bytes 307208 | tf_op jit(solution)/shard_map/ppermute | solution.py:587
  174.0 4.3 %collective-permute-done.20.refs_2_ = bf16[400,128]{1,0:T(8,128)(2,1)S(1)} collective-permute-done((bf16[400,128]{1,0:T(8,128)(2,1)S(1)}, bf16[400,128]{1,0:T(8,128)(2,1)S(1)}, u32[]{:S(2)}, u32[]{:S(2)}) %collective-permute-start.20) | collective-permute-done | bytes 102432 | tf_op jit(solution)/shard_map/ppermute | solution.py:587
  178.3 3.6 %collective-permute-done.26.refs_6_ = bf16[400,128]{1,0:T(8,128)(2,1)S(1)} collective-permute-done((bf16[400,128]{1,0:T(8,128)(2,1)S(1)}, bf16[400,128]{1,0:T(8,128)(2,1)S(1)}, u32[]{:S(2)}, u32[]{:S(2)}) %collective-permute-start.26) | collective-permute-done | bytes 102432 | tf_op jit(solution)/shard_map/ppermute | solution.py:587
  181.9 0.6 copy-done.16
  182.6 2.4 %finish_shard.1 = (f32[800,128]{1,0:T(8,128)}, f32[8,128]{1,0:T(8,128)}) custom-call(bf16[400,128]{1,0:T(8,128)(2,1)} %get-tuple-element.42.refs_0_, bf16[400,128]{1,0:T(8,128)(2,1)} %copy-done.14, bf16[400,128]{1,0:T(8,128)(2,1)} %copy-done.13, bf16[400,128]{1,0:T(8,128)(2,1)} %copy-done.12, bf16[400,128]{1,0:T(8,128)(2,1)} %get-tuple-element.38.refs_4_, ...), custom_call_target="tpu_custom_call" | custom-call | tf_op jit(solution)/shard_map/finish_shard/pallas_call | solution.py:647
  185.0 1.2 slice_bitcast_fusion.12
  186.2 2.2 %multiply_add_fusion = (f32[98496]{0:T(1024)}, f32[98496]{0:T(1024)}, f32[98496]{0:T(1024)}, f32[98496]{0:T(1024)}) fusion(f32[98496]{0:T(1024)S(1)} %copy-done.10, f32[98496]{0:T(1024)S(1)} %copy-done.5, f32[98496]{0:T(1024)S(1)} %copy-done.11, f32[102400]{0:T(1024)} %bitcast.76), kind=kLoop, calls=%fused_computation.25 | loop fusion | flops 886464 | bytes 3151872 | tf_op jit(solution)/shard_map/add | solution.py:666
  (65 shorter events, 1.0 us)
Async XLA Ops:
  4.4 9.4 %collective-permute-start.10 = (bf16[400,128]{1,0:T(8,128)(2,1)}, bf16[400,128]{1,0:T(8,128)(2,1)S(1)}, u32[]{:S(2)}, u32[]{:S(2)}) collective-permute-start(bf16[400,128]{1,0:T(8,128)(2,1)} %get-tuple-element.18), channel_id=1, source_target_pairs={{0,24},{1,25},{2,26},{3,27},{4,28},{5,29},{6,30},{7,31},{8,16},{9,... | collective-permute-start | bytes 307208 | tf_op jit(solution)/shard_map/ppermute | solution.py:587
  9.4 14.2 %collective-permute-start.9 = (bf16[400,128]{1,0:T(8,128)(2,1)}, bf16[400,128]{1,0:T(8,128)(2,1)S(1)}, u32[]{:S(2)}, u32[]{:S(2)}) collective-permute-start(bf16[400,128]{1,0:T(8,128)(2,1)} %get-tuple-element.18), channel_id=1, source_target_pairs={{0,16},{1,17},{2,18},{3,19},{4,20},{5,21},{6,22},{7,23},{8,24},{9,... | collective-permute-start | bytes 307208 | tf_op jit(solution)/shard_map/ppermute | solution.py:587
  9.4 14.2 %collective-permute-start.8 = (bf16[400,128]{1,0:T(8,128)(2,1)}, bf16[400,128]{1,0:T(8,128)(2,1)S(1)}, u32[]{:S(2)}, u32[]{:S(2)}) collective-permute-start(bf16[400,128]{1,0:T(8,128)(2,1)} %get-tuple-element.18), channel_id=1, source_target_pairs={{0,8},{1,9},{2,10},{3,11},{4,12},{5,13},{6,14},{7,15},{8,0},{9,1},... | collective-permute-start | bytes 307208 | tf_op jit(solution)/shard_map/ppermute | solution.py:587
  10.0 16.2 %collective-permute-start.2 = (bf16[400,128]{1,0:T(8,128)(2,1)}, bf16[400,128]{1,0:T(8,128)(2,1)S(1)}, u32[]{:S(2)}, u32[]{:S(2)}) collective-permute-start(bf16[400,128]{1,0:T(8,128)(2,1)} %get-tuple-element.17), channel_id=1, source_target_pairs={{0,24},{1,25},{2,26},{3,27},{4,28},{5,29},{6,30},{7,31},{8,16},{9,... | collective-permute-start | bytes 307208 | tf_op jit(solution)/shard_map/ppermute | solution.py:587
  13.8 13.2 %collective-permute-start.1 = (bf16[400,128]{1,0:T(8,128)(2,1)}, bf16[400,128]{1,0:T(8,128)(2,1)S(1)}, u32[]{:S(2)}, u32[]{:S(2)}) collective-permute-start(bf16[400,128]{1,0:T(8,128)(2,1)} %get-tuple-element.17), channel_id=1, source_target_pairs={{0,16},{1,17},{2,18},{3,19},{4,20},{5,21},{6,22},{7,23},{8,24},{9,... | collective-permute-start | bytes 307208 | tf_op jit(solution)/shard_map/ppermute | solution.py:587
  13.8 13.2 %collective-permute-start = (bf16[400,128]{1,0:T(8,128)(2,1)}, bf16[400,128]{1,0:T(8,128)(2,1)S(1)}, u32[]{:S(2)}, u32[]{:S(2)}) collective-permute-start(bf16[400,128]{1,0:T(8,128)(2,1)} %get-tuple-element.17), channel_id=1, source_target_pairs={{0,8},{1,9},{2,10},{3,11},{4,12},{5,13},{6,14},{7,15},{8,0},{9,1},... | collective-permute-start | bytes 307208 | tf_op jit(solution)/shard_map/ppermute | solution.py:587
  24.6 32.6 %copy-start.1 = (bf16[4,400,128]{2,1,0:T(8,128)(2,1)}, bf16[4,400,128]{2,1,0:T(8,128)(2,1)S(1)}, u32[]{:S(2)}) copy-start(bf16[4,400,128]{2,1,0:T(8,128)(2,1)S(1)} %get-tuple-element.44.refs_10_) | copy-start | bytes 1228804
  24.6 9.1 %collective-permute-start.11 = (bf16[4,400,128]{2,1,0:T(8,128)(2,1)S(1)}, bf16[4,400,128]{2,1,0:T(8,128)(2,1)S(1)}, u32[]{:S(2)}, u32[]{:S(2)}) collective-permute-start(bf16[4,400,128]{2,1,0:T(8,128)(2,1)S(1)} %get-tuple-element.44.refs_10_), channel_id=1, source_target_pairs={{0,1},{1,0},{2,3},{3,2},{4,5},{5,4},{6,7},{7,6},{8,9},{9,8},{10,11... | collective-permute-start | bytes 1228808 | tf_op jit(solution)/shard_map/ppermute | solution.py:587
  28.0 14.1 %copy-start.3 = (bf16[4,400,128]{2,1,0:T(8,128)(2,1)}, bf16[4,400,128]{2,1,0:T(8,128)(2,1)S(1)}, u32[]{:S(2)}) copy-start(bf16[4,400,128]{2,1,0:T(8,128)(2,1)S(1)} %get-tuple-element.46.refs_4_) | copy-start | bytes 1228804
  28.0 12.5 %collective-permute-start.3 = (bf16[4,400,128]{2,1,0:T(8,128)(2,1)S(1)}, bf16[4,400,128]{2,1,0:T(8,128)(2,1)S(1)}, u32[]{:S(2)}, u32[]{:S(2)}) collective-permute-start(bf16[4,400,128]{2,1,0:T(8,128)(2,1)S(1)} %get-tuple-element.46.refs_4_), channel_id=1, source_target_pairs={{0,4},{1,5},{2,6},{3,7},{4,0},{5,1},{6,2},{7,3},{8,12},{9,13},{10,... | collective-permute-start | bytes 1228808 | tf_op jit(solution)/shard_map/ppermute | solution.py:587
  33.7 24.1 %copy-start.2 = (bf16[4,400,128]{2,1,0:T(8,128)(2,1)}, bf16[4,400,128]{2,1,0:T(8,128)(2,1)S(1)}, u32[]{:S(2)}) copy-start(bf16[4,400,128]{2,1,0:T(8,128)(2,1)S(1)} %collective-permute-done.11.refs_11_) | copy-start | bytes 1228804
  33.7 24.8 %copy-start.18 = (s32[1,512]{1,0:T(1,128)S(1)}, s32[1,512]{1,0:T(1,128)}, u32[]{:S(2)}) copy-start(s32[1,512]{1,0:T(1,128)} %refs_2_.1) | copy-start | bytes 6148
  33.7 22.4 %collective-permute-start.12 = (bf16[2,4,400,128]{3,2,1,0:T(8,128)(2,1)S(1)}, bf16[2,4,400,128]{3,2,1,0:T(8,128)(2,1)S(1)}, u32[]{:S(2)}, u32[]{:S(2)}) collective-permute-start(bf16[2,4,400,128]{3,2,1,0:T(8,128)(2,1)S(1)} %pad_maximum_fusion.1), channel_id=1, source_target_pairs={{0,4},{1,5},{2,6},{3,7},{4,0},{5,1},{6,2},{7,3},{8,12},{9,13},{10,... | collective-permute-start | bytes 2457608 | tf_op jit(solution)/shard_map/ppermute | solution.py:587
  40.5 21.1 %copy-start.4 = (bf16[4,400,128]{2,1,0:T(8,128)(2,1)}, bf16[4,400,128]{2,1,0:T(8,128)(2,1)S(1)}, u32[]{:S(2)}) copy-start(bf16[4,400,128]{2,1,0:T(8,128)(2,1)S(1)} %collective-permute-done.3.refs_5_) | copy-start | bytes 1228804
  40.6 16.6 %collective-permute-start.4 = (bf16[2,4,400,128]{3,2,1,0:T(8,128)(2,1)S(1)}, bf16[2,4,400,128]{3,2,1,0:T(8,128)(2,1)S(1)}, u32[]{:S(2)}, u32[]{:S(2)}) collective-permute-start(bf16[2,4,400,128]{3,2,1,0:T(8,128)(2,1)S(1)} %pad_maximum_fusion), channel_id=1, source_target_pairs={{0,1},{1,0},{2,3},{3,2},{4,5},{5,4},{6,7},{7,6},{8,9},{9,8},{10,11... | collective-permute-start | bytes 2457608 | tf_op jit(solution)/shard_map/ppermute | solution.py:587
  42.1 15.6 %collective-permute-start.5 = (bf16[4,400,128]{2,1,0:T(8,128)(2,1)S(1)}, bf16[4,400,128]{2,1,0:T(8,128)(2,1)S(1)}, u32[]{:S(2)}, u32[]{:S(2)}) collective-permute-start(bf16[4,400,128]{2,1,0:T(8,128)(2,1)S(1)} %get-tuple-element.46.refs_4_), channel_id=1, source_target_pairs={{0,2},{1,3},{2,0},{3,1},{4,6},{5,7},{6,4},{7,5},{8,10},{9,11},{10,... | collective-permute-start | bytes 1228808 | tf_op jit(solution)/shard_map/ppermute | solution.py:587
  56.2 5.4 %copy-start.6 = (bf16[2,4,400,128]{3,2,1,0:T(8,128)(2,1)}, bf16[2,4,400,128]{3,2,1,0:T(8,128)(2,1)S(1)}, u32[]{:S(2)}) copy-start(bf16[2,4,400,128]{3,2,1,0:T(8,128)(2,1)S(1)} %collective-permute-done.12.refs_12_) | copy-start | bytes 2457604
  56.2 5.4 %collective-permute-start.15 = (bf16[2,4,400,128]{3,2,1,0:T(8,128)(2,1)S(1)}, bf16[2,4,400,128]{3,2,1,0:T(8,128)(2,1)}, u32[]{:S(2)}, u32[]{:S(2)}) collective-permute-start(bf16[2,4,400,128]{3,2,1,0:T(8,128)(2,1)S(1)} %collective-permute-done.12.refs_12_), channel_id=1, source_target_pairs={{0,2},{1,3},{2,0},{3,1},{4,6},{5,7},{6,4},{7,5},{8,10},{9,11},{10,... | collective-permute-start | bytes 2457608 | tf_op jit(solution)/shard_map/ppermute | solution.py:587
  57.1 4.5 %copy-start.7 = (bf16[2,4,400,128]{3,2,1,0:T(8,128)(2,1)}, bf16[2,4,400,128]{3,2,1,0:T(8,128)(2,1)S(1)}, u32[]{:S(2)}) copy-start(bf16[2,4,400,128]{3,2,1,0:T(8,128)(2,1)S(1)} %collective-permute-done.4.refs_6_) | copy-start | bytes 2457604
  57.1 4.4 %collective-permute-start.7 = (bf16[2,4,400,128]{3,2,1,0:T(8,128)(2,1)S(1)}, bf16[2,4,400,128]{3,2,1,0:T(8,128)(2,1)}, u32[]{:S(2)}, u32[]{:S(2)}) collective-permute-start(bf16[2,4,400,128]{3,2,1,0:T(8,128)(2,1)S(1)} %collective-permute-done.4.refs_6_), channel_id=1, source_target_pairs={{0,2},{1,3},{2,0},{3,1},{4,6},{5,7},{6,4},{7,5},{8,10},{9,11},{10,... | collective-permute-start | bytes 2457608 | tf_op jit(solution)/shard_map/ppermute | solution.py:587
  57.1 3.8 %collective-permute-start.13 = (bf16[4,400,128]{2,1,0:T(8,128)(2,1)S(1)}, bf16[4,400,128]{2,1,0:T(8,128)(2,1)}, u32[]{:S(2)}, u32[]{:S(2)}) collective-permute-start(bf16[4,400,128]{2,1,0:T(8,128)(2,1)S(1)} %get-tuple-element.44.refs_10_), channel_id=1, source_target_pairs={{0,2},{1,3},{2,0},{3,1},{4,6},{5,7},{6,4},{7,5},{8,10},{9,11},{10,... | collective-permute-start | bytes 1228808 | tf_op jit(solution)/shard_map/ppermute | solution.py:587
  57.6 3.9 %collective-permute-start.6 = (bf16[4,400,128]{2,1,0:T(8,128)(2,1)S(1)}, bf16[4,400,128]{2,1,0:T(8,128)(2,1)}, u32[]{:S(2)}, u32[]{:S(2)}) collective-permute-start(bf16[4,400,128]{2,1,0:T(8,128)(2,1)S(1)} %collective-permute-done.3.refs_5_), channel_id=1, source_target_pairs={{0,2},{1,3},{2,0},{3,1},{4,6},{5,7},{6,4},{7,5},{8,10},{9,11},{10,... | collective-permute-start | bytes 1228808 | tf_op jit(solution)/shard_map/ppermute | solution.py:587
  57.7 0.8 copy-start.8
  57.7 3.8 %collective-permute-start.14 = (bf16[4,400,128]{2,1,0:T(8,128)(2,1)S(1)}, bf16[4,400,128]{2,1,0:T(8,128)(2,1)S(1)}, u32[]{:S(2)}, u32[]{:S(2)}) collective-permute-start(bf16[4,400,128]{2,1,0:T(8,128)(2,1)S(1)} %collective-permute-done.11.refs_11_), channel_id=1, source_target_pairs={{0,2},{1,3},{2,0},{3,1},{4,6},{5,7},{6,4},{7,5},{8,10},{9,11},{10,... | collective-permute-start | bytes 1228808 | tf_op jit(solution)/shard_map/ppermute | solution.py:587
  61.6 0.7 copy-start.9
  125.5 3.8 %collective-permute-start.16 = (bf16[2,2,4,400,128]{4,3,2,1,0:T(8,128)(2,1)}, bf16[2,2,4,400,128]{4,3,2,1,0:T(8,128)(2,1)S(1)}, u32[]{:S(2)}, u32[]{:S(2)}) collective-permute-start(bf16[2,2,4,400,128]{4,3,2,1,0:T(8,128)(2,1)} %get-tuple-element.22), channel_id=1, source_target_pairs={{0,2},{1,3},{2,0},{3,1},{4,6},{5,7},{6,4},{7,5},{8,10},{9,11},{10,... | collective-permute-start | bytes 4915208 | tf_op jit(solution)/shard_map/ppermute | solution.py:587
  125.7 6.9 %collective-permute-start.22 = (bf16[2,2,4,400,128]{4,3,2,1,0:T(8,128)(2,1)}, bf16[2,2,4,400,128]{4,3,2,1,0:T(8,128)(2,1)S(1)}, u32[]{:S(2)}, u32[]{:S(2)}) collective-permute-start(bf16[2,2,4,400,128]{4,3,2,1,0:T(8,128)(2,1)} %get-tuple-element.24), channel_id=1, source_target_pairs={{0,2},{1,3},{2,0},{3,1},{4,6},{5,7},{6,4},{7,5},{8,10},{9,11},{10,... | collective-permute-start | bytes 4915208 | tf_op jit(solution)/shard_map/ppermute | solution.py:587
  129.2 3.3 %copy-start = (bf16[2,2,4,400,128]{4,3,2,1,0:T(8,128)(2,1)S(1)}, bf16[2,2,4,400,128]{4,3,2,1,0:T(8,128)(2,1)}, u32[]{:S(2)}) copy-start(bf16[2,2,4,400,128]{4,3,2,1,0:T(8,128)(2,1)} %get-tuple-element.23) | copy-start | bytes 4915204
  131.0 20.4 %collective-permute-start.17 = (bf16[2,4,400,128]{3,2,1,0:T(8,128)(2,1)S(1)}, bf16[2,4,400,128]{3,2,1,0:T(8,128)(2,1)S(1)}, u32[]{:S(2)}, u32[]{:S(2)}) collective-permute-start(bf16[2,4,400,128]{3,2,1,0:T(8,128)(2,1)S(1)} %get-tuple-element.34), channel_id=1, source_target_pairs={{0,4},{1,5},{2,6},{3,7},{4,0},{5,1},{6,2},{7,3},{8,12},{9,13},{10,... | collective-permute-start | bytes 2457608 | tf_op jit(solution)/shard_map/ppermute | solution.py:587
  132.7 20.3 %collective-permute-start.23 = (bf16[2,4,400,128]{3,2,1,0:T(8,128)(2,1)S(1)}, bf16[2,4,400,128]{3,2,1,0:T(8,128)(2,1)S(1)}, u32[]{:S(2)}, u32[]{:S(2)}) collective-permute-start(bf16[2,4,400,128]{3,2,1,0:T(8,128)(2,1)S(1)} %get-tuple-element.32), channel_id=1, source_target_pairs={{0,1},{1,0},{2,3},{3,2},{4,5},{5,4},{6,7},{7,6},{8,9},{9,8},{10,11... | collective-permute-start | bytes 2457608 | tf_op jit(solution)/shard_map/ppermute | solution.py:587
  151.4 10.7 %collective-permute-start.18 = (bf16[4,400,128]{2,1,0:T(8,128)(2,1)S(1)}, bf16[4,400,128]{2,1,0:T(8,128)(2,1)S(1)}, u32[]{:S(2)}, u32[]{:S(2)}) collective-permute-start(bf16[4,400,128]{2,1,0:T(8,128)(2,1)S(1)} %fusion.5), channel_id=1, source_target_pairs={{0,1},{1,0},{2,3},{3,2},{4,5},{5,4},{6,7},{7,6},{8,9},{9,8},{10,11... | collective-permute-start | bytes 1228808 | tf_op jit(solution)/shard_map/ppermute | solution.py:587
  153.0 14.2 %collective-permute-start.24 = (bf16[4,400,128]{2,1,0:T(8,128)(2,1)S(1)}, bf16[4,400,128]{2,1,0:T(8,128)(2,1)S(1)}, u32[]{:S(2)}, u32[]{:S(2)}) collective-permute-start(bf16[4,400,128]{2,1,0:T(8,128)(2,1)S(1)} %fusion.2), channel_id=1, source_target_pairs={{0,4},{1,5},{2,6},{3,7},{4,0},{5,1},{6,2},{7,3},{8,12},{9,13},{10,... | collective-permute-start | bytes 1228808 | tf_op jit(solution)/shard_map/ppermute | solution.py:587
  162.8 7.3 %collective-permute-start.21 = (bf16[400,128]{1,0:T(8,128)(2,1)S(1)}, bf16[400,128]{1,0:T(8,128)(2,1)S(1)}, u32[]{:S(2)}, u32[]{:S(2)}) collective-permute-start(bf16[400,128]{1,0:T(8,128)(2,1)S(1)} %get-tuple-element.39), channel_id=1, source_target_pairs={{0,24},{1,25},{2,26},{3,27},{4,28},{5,29},{6,30},{7,31},{8,16},{9,... | collective-permute-start | bytes 307208 | tf_op jit(solution)/shard_map/ppermute | solution.py:587
  164.8 13.4 %collective-permute-start.20 = (bf16[400,128]{1,0:T(8,128)(2,1)S(1)}, bf16[400,128]{1,0:T(8,128)(2,1)S(1)}, u32[]{:S(2)}, u32[]{:S(2)}) collective-permute-start(bf16[400,128]{1,0:T(8,128)(2,1)S(1)} %get-tuple-element.40), channel_id=1, source_target_pairs={{0,16},{1,17},{2,18},{3,19},{4,20},{5,21},{6,22},{7,23},{8,24},{9,... | collective-permute-start | bytes 307208 | tf_op jit(solution)/shard_map/ppermute | solution.py:587
  164.8 21.4 %copy-start.5 = (f32[98496]{0:T(1024)S(1)}, f32[98496]{0:T(1024)}, u32[]{:S(2)}) copy-start(f32[98496]{0:T(1024)} %param.9) | copy-start | bytes 1181956
  164.8 21.4 %copy-start.10 = (f32[98496]{0:T(1024)S(1)}, f32[98496]{0:T(1024)}, u32[]{:S(2)}) copy-start(f32[98496]{0:T(1024)} %param.11) | copy-start | bytes 1181956
  164.8 21.4 %copy-start.11 = (f32[98496]{0:T(1024)S(1)}, f32[98496]{0:T(1024)}, u32[]{:S(2)}) copy-start(f32[98496]{0:T(1024)} %param.10) | copy-start | bytes 1181956
  164.9 13.4 %collective-permute-start.19 = (bf16[400,128]{1,0:T(8,128)(2,1)S(1)}, bf16[400,128]{1,0:T(8,128)(2,1)S(1)}, u32[]{:S(2)}, u32[]{:S(2)}) collective-permute-start(bf16[400,128]{1,0:T(8,128)(2,1)S(1)} %get-tuple-element.41), channel_id=1, source_target_pairs={{0,8},{1,9},{2,10},{3,11},{4,12},{5,13},{6,14},{7,15},{8,0},{9,1},... | collective-permute-start | bytes 307208 | tf_op jit(solution)/shard_map/ppermute | solution.py:587
  168.0 10.3 %collective-permute-start.27 = (bf16[400,128]{1,0:T(8,128)(2,1)S(1)}, bf16[400,128]{1,0:T(8,128)(2,1)S(1)}, u32[]{:S(2)}, u32[]{:S(2)}) collective-permute-start(bf16[400,128]{1,0:T(8,128)(2,1)S(1)} %get-tuple-element.35), channel_id=1, source_target_pairs={{0,24},{1,25},{2,26},{3,27},{4,28},{5,29},{6,30},{7,31},{8,16},{9,... | collective-permute-start | bytes 307208 | tf_op jit(solution)/shard_map/ppermute | solution.py:587
  170.0 11.9 %collective-permute-start.26 = (bf16[400,128]{1,0:T(8,128)(2,1)S(1)}, bf16[400,128]{1,0:T(8,128)(2,1)S(1)}, u32[]{:S(2)}, u32[]{:S(2)}) collective-permute-start(bf16[400,128]{1,0:T(8,128)(2,1)S(1)} %get-tuple-element.36), channel_id=1, source_target_pairs={{0,16},{1,17},{2,18},{3,19},{4,20},{5,21},{6,22},{7,23},{8,24},{9,... | collective-permute-start | bytes 307208 | tf_op jit(solution)/shard_map/ppermute | solution.py:587
  170.2 11.7 %copy-start.12 = (bf16[400,128]{1,0:T(8,128)(2,1)}, bf16[400,128]{1,0:T(8,128)(2,1)S(1)}, u32[]{:S(2)}) copy-start(bf16[400,128]{1,0:T(8,128)(2,1)S(1)} %collective-permute-done.21.refs_3_) | copy-start | bytes 307204
  170.2 11.7 %collective-permute-start.25 = (bf16[400,128]{1,0:T(8,128)(2,1)S(1)}, bf16[400,128]{1,0:T(8,128)(2,1)S(1)}, u32[]{:S(2)}, u32[]{:S(2)}) collective-permute-start(bf16[400,128]{1,0:T(8,128)(2,1)S(1)} %get-tuple-element.37), channel_id=1, source_target_pairs={{0,8},{1,9},{2,10},{3,11},{4,12},{5,13},{6,14},{7,15},{8,0},{9,1},... | collective-permute-start | bytes 307208 | tf_op jit(solution)/shard_map/ppermute | solution.py:587
  178.3 3.6 %copy-start.13 = (bf16[400,128]{1,0:T(8,128)(2,1)}, bf16[400,128]{1,0:T(8,128)(2,1)S(1)}, u32[]{:S(2)}) copy-start(bf16[400,128]{1,0:T(8,128)(2,1)S(1)} %collective-permute-done.20.refs_2_) | copy-start | bytes 307204
  178.3 3.6 %copy-start.14 = (bf16[400,128]{1,0:T(8,128)(2,1)}, bf16[400,128]{1,0:T(8,128)(2,1)S(1)}, u32[]{:S(2)}) copy-start(bf16[400,128]{1,0:T(8,128)(2,1)S(1)} %collective-permute-done.19.refs_1_) | copy-start | bytes 307204
  178.3 3.6 %copy-start.15 = (bf16[400,128]{1,0:T(8,128)(2,1)}, bf16[400,128]{1,0:T(8,128)(2,1)S(1)}, u32[]{:S(2)}) copy-start(bf16[400,128]{1,0:T(8,128)(2,1)S(1)} %collective-permute-done.27.refs_7_) | copy-start | bytes 307204
  181.9 0.6 copy-start.16
  181.9 0.7 copy-start.17

commit v3 on v2

--- a/solution.py
+++ b/solution.py
@@ -143,112 +143,114 @@
     return lax.axis_index("dp") * lax.axis_size("rep") + lax.axis_index("rep")
 
 
-def load_windows(w_refs, pieces, flat, edge, sem, shards):
+RZ, RX, RC, RY = 8, 4, 2, 1
+STEPS = ((RX, RY), (RY, RX), (2 * RZ, RZ), (RZ, 2 * RZ))
+SLOTS = 1 << len(STEPS)
+
+
+def own_core(me):
+    return (me // RC) & 1
+
+
+def slot_owner(base, core, slot):
+    owner = base
+    for k, (zero, one) in enumerate(STEPS):
+        if slot >> (len(STEPS) - 1 - k) & 1:
+            owner = jnp.bitwise_xor(owner, jnp.where(core == 0, zero, one))
+    return owner
+
+
+def settle(ref, rows, sem):
+    pltpu.make_async_copy(ref.at[pl.ds(0, rows)], ref.at[pl.ds(0, rows)], sem).wait()
+
+
+def window_moves(owner, height, tiles, shards, edge_row):
+    start = pl.multiple_of((owner * tiles // shards) * TILE, TILE)
+    edge = pl.multiple_of(edge_row + owner * 2 * TILE, TILE)
+    body = height - 2 * TILE
+    return [(0, start, body), (body, edge, 2 * TILE)]
+
+
+def load_windows(w_refs, wide, flat, sem, shards):
     tiles = flat.shape[0] // TILE
-    rows = [ref.shape[-2] for ref in w_refs]
-    half = rows[0]
+    height = w_refs[0].shape[0]
+    edge_row = flat.shape[0] + TILE
     base = tiles // shards * TILE
     me = own_index()
-    copies = []
-    for ref, (part, entries) in zip(w_refs, pieces):
-        for pos, rel in entries:
-            src = ref
-            for k in pos:
-                src = src.at[k]
-            owner = jnp.bitwise_xor(me, rel)
-            start = pl.multiple_of((owner * tiles // shards) * TILE, TILE)
-            if part == 0:
-                moves = [(src, flat.at[pl.ds(start, half)])]
-            else:
-                moves = [
-                    (src.at[pl.ds(0, base - half)], flat.at[pl.ds(pl.multiple_of(start + half, TILE), base - half)]),
-                    (src.at[pl.ds(base - half, 2 * TILE)], edge.at[owner]),
-                ]
-            for a, b in moves:
-                copies.append(pltpu.make_async_copy(a, b, sem.at[len(copies)]))
-                copies[-1].start()
-    for copy in copies:
-        copy.wait()
+    core = own_core(me)
+    for n, ref in enumerate(w_refs):
+        side, origin = (core, me) if n < SLOTS else (1 - core, jnp.bitwise_xor(me, RC))
+        owner = slot_owner(origin, side, n % SLOTS)
+        for at, to, rows in window_moves(owner, height, tiles, shards, edge_row):
+            pltpu.make_async_copy(ref.at[pl.ds(at, rows)], wide.at[pl.ds(to, rows)], sem.at[0]).start()
+    settle(wide, height * len(w_refs), sem.at[0])
     starts = window_starts(shards, tiles)
+
+    def tile(row):
+        return wide[row : row + TILE, :]
+
     for i in range(shards):
         nxt = starts[i + 1]
-        low = edge[i, 0:TILE, :]
-        if nxt - starts[i] == base // TILE:
-            if i + 1 < shards:
-                flat[nxt * TILE : (nxt + 1) * TILE, :] = flat[nxt * TILE : (nxt + 1) * TILE, :] + low
-        else:
-            flat[(nxt - 1) * TILE : nxt * TILE, :] = low
-            if i + 1 < shards:
-                flat[nxt * TILE : (nxt + 1) * TILE, :] = flat[nxt * TILE : (nxt + 1) * TILE, :] + edge[i, TILE : 2 * TILE, :]
-
-
-def store_windows(g_refs, flat, edge, sem, shards, vec_rows):
+        row = edge_row + i * 2 * TILE
+        if nxt - starts[i] != base // TILE:
+            wide[(nxt - 1) * TILE : nxt * TILE, :] = tile(row)
+            row = row + TILE
+        if i + 1 < shards:
+            wide[nxt * TILE : (nxt + 1) * TILE, :] = tile(nxt * TILE) + tile(row)
+
+
+def store_windows(g_refs, wide, flat, sem, shards, vec_rows):
     tiles = flat.shape[0] // TILE
-    half = g_refs[0].shape[-2]
-    whole = 2 * half
+    height = g_refs[0].shape[1]
+    edge_row = flat.shape[0] + TILE
     starts = window_starts(shards, tiles)
     last = lax.broadcasted_iota(jnp.int32, (TILE, LANES), 0) == TILE - 1
     for i in range(shards):
-        low = starts[i] * TILE + whole - TILE
-        if low + TILE <= flat.shape[0]:
-            tile = flat[low : low + TILE, :].astype(F32)
-        else:
-            tile = jnp.zeros((TILE, LANES), F32)
-        edge[i, 0:TILE, :] = jnp.where(last, vec_rows[i : i + 1], tile).astype(BF)
+        low = starts[i] * TILE + height - 2 * TILE
+        row = edge_row + i * 2 * TILE
+        for k in range(2):
+            at = low + k * TILE
+            if at + TILE <= flat.shape[0]:
+                tile = wide[at : at + TILE, :]
+            else:
+                tile = jnp.zeros((TILE, LANES), BF)
+            if k == 1:
+                tile = jnp.where(last, vec_rows[i : i + 1], tile.astype(F32)).astype(BF)
+            wide[row + k * TILE : row + (k + 1) * TILE, :] = tile
     me = own_index()
-    copies = []
-    for part in range(2):
-        for rc in range(2):
-            ref = g_refs[2 * rc + part]
-            for r0 in range(2):
-                for r1 in range(2):
-                    rx, ry = (r0, r1) if part == 0 else (r1, r0)
-                    for rz in range(4):
-                        owner = jnp.bitwise_xor(me, rz * 8 + rx * 4 + rc * 2 + ry)
-                        start = pl.multiple_of((owner * tiles // shards) * TILE, TILE)
-                        dst = ref.at[r0].at[r1].at[rz]
-                        if part == 0:
-                            moves = [(flat.at[pl.ds(start, half)], dst)]
-                        else:
-                            moves = [
-                                (flat.at[pl.ds(pl.multiple_of(start + half, TILE), half - TILE)], dst.at[pl.ds(0, half - TILE)]),
-                                (edge.at[owner].at[pl.ds(0, TILE)], dst.at[pl.ds(half - TILE, TILE)]),
-                            ]
-                        for a, b in moves:
-                            copies.append(pltpu.make_async_copy(a, b, sem.at[len(copies)]))
-                            copies[-1].start()
-    for copy in copies:
-        copy.wait()
-
-
-def pack_kernel(x_ref, a_ref, b_ref):
+    core = own_core(me)
+    for n, ref in enumerate(g_refs):
+        side, origin = (core, me) if n == 0 else (1 - core, jnp.bitwise_xor(me, RC))
+        first = SLOTS // 2 if n == 1 else 0
+        for k in range(ref.shape[0]):
+            owner = slot_owner(origin, side, first + k)
+            for at, to, rows in window_moves(owner, height, tiles, shards, edge_row):
+                pltpu.make_async_copy(wide.at[pl.ds(to, rows)], ref.at[k].at[pl.ds(at, rows)], sem.at[n]).start()
+    for n, ref in enumerate(g_refs):
+        settle(wide, ref.shape[0] * ref.shape[1], sem.at[n])
+
+
+def pack_kernel(x_ref, out_ref):
     me = own_index()
     v = x_ref[...]
-    rows = v.shape[0]
     lane = lax.broadcasted_iota(jnp.int32, v.shape, 1)
     turned = pltpu.roll(v, 64, 1)
     moved = jnp.where(lane >= 64, turned, pltpu.roll(turned, 1, 0))
     odd = (me & 1) == 1
     v = jnp.where(odd, moved, v)
     shift = ((me * 192) & 2047) >> 7
-    v = pltpu.roll(v, shift, 0).astype(BF)
-    a_ref[...] = v[: rows // 2]
-    b_ref[...] = v[rows // 2 :]
+    out_ref[...] = pltpu.roll(v, shift, 0).astype(BF)
 
 
 def finish_kernel(*refs):
-    parts = []
-    for h in range(2):
-        total = None
-        for ref in refs[4 * h : 4 * h + 4]:
-            v = ref[...].astype(F32)
-            total = v if total is None else total + v
-        parts.append(total)
-    out_ref, vec_ref = refs[8:]
-    v = jnp.concatenate(parts, axis=0)
+    out_ref, vec_ref = refs[-2:]
+    me = own_index()
+    v = None
+    for ref in refs[:-2]:
+        part = ref[...].astype(F32)
+        v = part if v is None else v + part
     rows = v.shape[0]
     vec_ref[...] = v[rows - 8 :]
-    me = own_index()
     shift = ((me * 192) & 2047) >> 7
     v = pltpu.roll(v, rows - shift, 0)
     lane = lax.broadcasted_iota(jnp.int32, v.shape, 1)
@@ -264,27 +266,27 @@
 AHEAD = 2
 
 
-def core_kernel(*refs, width, length, shards, pieces, flat_rows):
-    n_in = 1 if pieces is None else len(pieces)
+def core_kernel(*refs, width, length, shards, windows, flat_rows):
+    n_in = 2 * SLOTS if windows else 1
     (x_ref, cot_ref, segr_ref, segc_ref) = refs[:4]
     w_refs = refs[4 : 4 + n_in]
     refs = refs[4 + n_in :]
     (y_ref, dx_ref) = refs[:2]
-    n_out = 1 if pieces is None else 4
+    n_out = 3 if windows else 1
     g_refs = refs[2 : 2 + n_out]
-    (wide, wa, wi, wo, b1, vec, xb, qkv, ab, ctx, xh1, iv1, xh2, iv2, h1b, slope, df, da, dqkv, dc, dr1, edge,
+    (wide, wa, wi, wo, b1, vec, xb, qkv, ab, ctx, xh1, iv1, xh2, iv2, h1b, slope, df, da, dqkv, dc, dr1,
      bias, gb1, gvec, count_ref, sem) = refs[2 + n_out :]
     D = width
     T = length
     pairs = D // LANES
     flat = wide.at[pl.ds(0, flat_rows)]
 
-    if pieces is None:
+    if windows:
+        load_windows(w_refs, wide, flat, sem, shards)
+    else:
         cp = pltpu.make_async_copy(w_refs[0], flat, sem.at[0])
         cp.start()
         cp.wait()
-    else:
-        load_windows(w_refs, pieces, flat, edge, sem, shards)
     unpack_weights(flat, wa, wi, wo, b1, vec, D)
 
     scale = 0.125
@@ -538,38 +540,37 @@
         rows = rows + [gvec[r : r + 1, c * LANES : (c + 1) * LANES] for c in range(per_out)]
     tail = jnp.concatenate(rows, axis=0)
     flat[flat.shape[0] - len(rows) : flat.shape[0], :] = tail.astype(BF)
-    if pieces is None:
+    if windows:
+        store_windows(g_refs, wide, flat, sem, shards, tail[FF // LANES :])
+    else:
         cp = pltpu.make_async_copy(flat, g_refs[0], sem.at[0])
         cp.start()
         cp.wait()
-    else:
-        store_windows(g_refs, flat, edge, sem, shards, tail[FF // LANES :])
-
-
-def core(x, cot, seg, flats, pieces, shards, rows):
+
+
+def core(x, cot, seg, flats, windows, shards, rows):
     T, D = x.shape
     vm = pltpu.VMEM
     pairs = D // LANES
     scratch = [
-        vm((max(2 * FF * REC * T // LANES, rows), LANES), BF),
+        vm((max(2 * FF * REC * T // LANES, rows + TILE + 2 * TILE * shards), LANES), BF),
         vm((D, 4 * D), BF), vm((D, FF), BF), vm((FF, D), BF), vm((1, FF), F32), vm((8, D), F32),
         vm((REC * T, D), BF), vm((REC, 3 * pairs, T, LANES), BF), vm((REC * HEADS, T, T), BF), vm((pairs, REC * T, LANES), BF),
         vm((REC, T, D), F32), vm((REC, T, LANES), F32), vm((REC, T, D), F32), vm((REC, T, LANES), F32),
         vm((REC * T, D), BF), vm((REC, T, FF), F32),
         vm((REC * T, D), BF), vm((REC * T, D), BF), vm((3 * pairs, REC * T, LANES), BF), vm((pairs, T, LANES), BF),
-        vm((T, D), F32), vm((shards if pieces else 1, 2 * TILE, LANES), BF), vm((T, T), F32),
+        vm((T, D), F32), vm((T, T), F32),
         vm((1, FF), F32), vm((8, D), F32),
-        pltpu.SMEM((1,), jnp.int32), pltpu.SemaphoreType.DMA((96,)),
+        pltpu.SMEM((1,), jnp.int32), pltpu.SemaphoreType.DMA((8,)),
     ]
-    if pieces is None:
+    if windows:
+        g_shapes = [jax.ShapeDtypeStruct((n, flats[0].shape[0], LANES), BF) for n in (SLOTS, SLOTS // 2, SLOTS // 2)]
+    else:
         g_shapes = [jax.ShapeDtypeStruct((rows, LANES), BF)]
-    else:
-        half = flats[0].shape[-2]
-        g_shapes = [jax.ShapeDtypeStruct((2, 2, 4, half, LANES), BF)] * 4
     in_vmem = pl.BlockSpec(memory_space=pltpu.VMEM)
     anywhere = pl.BlockSpec(memory_space=pl.ANY)
     return pl.pallas_call(
-        functools.partial(core_kernel, width=D, length=T, shards=shards, pieces=pieces, flat_rows=rows),
+        functools.partial(core_kernel, width=D, length=T, shards=shards, windows=windows, flat_rows=rows),
         out_shape=tuple([jax.ShapeDtypeStruct((T, D), F32)] * 2 + g_shapes),
         in_specs=[in_vmem] * 4 + [anywhere] * len(flats),
         out_specs=tuple([in_vmem] * 2 + [anywhere] * len(g_shapes)),
@@ -582,46 +583,42 @@
 AXES = ("dp", "rep")
 
 
-def exchange(v, rel):
+def exchange(v, step):
     count = lax.axis_size("dp") * lax.axis_size("rep")
-    return lax.ppermute(v, AXES, [(j, j ^ rel) for j in range(count)])
-
-
-RZ, RX, RC, RY = 8, 4, 2, 1
-
-
-def gather_windows(a, b):
-    out, pieces = [], []
-    for part, own in enumerate((a, b)):
-        first, second = (RX, RY) if part == 0 else (RY, RX)
-        stack = jnp.stack([own] + [exchange(own, k * RZ) for k in (1, 2, 3)])
-        near = exchange(stack, first)
-        far = exchange(jnp.stack([stack, near]), second)
-        for rc in (0, RC):
-            for v, dims in ((stack, (0,)), (near, (first,)), (far, (second,))):
-                out.append(v if rc == 0 else exchange(v, rc))
-                if v is far:
-                    ent = [((n, k), k * RZ + second + n * first + rc) for n in range(2) for k in range(4)]
-                else:
-                    ent = [((k,), k * RZ + dims[0] + rc) for k in range(4)]
-                pieces.append((part, ent))
-    order = sorted(range(len(out)), key=lambda i: pieces[i][0])
-    return [out[i] for i in order], [pieces[i] for i in order]
-
-
-def sum_windows(keeps, sends):
-    res = []
-    for part in range(2):
-        first, second = (RX, RY) if part == 0 else (RY, RX)
-        got = exchange(sends[part], RC)
-        keep = keeps[part]
-        got1 = exchange(keep[1] + got[1], first)
-        mine = keep[0] + got[0]
-        got2 = exchange(mine[1] + got1[1], second)
-        mine = mine[0] + got1[0]
-        v = mine + got2
-        res.append([v[0]] + [exchange(v[k], k * RZ) for k in (1, 2, 3)])
-    return res
+    zero, one = STEPS[step] if step < len(STEPS) else (RC, RC)
+    return lax.ppermute(v, AXES, [(j, j ^ (one if j // RC & 1 else zero)) for j in range(count)])
+
+
+def gather_windows(own):
+    planes = [own, exchange(own, 3), exchange(own, 2)]
+    planes.append(exchange(planes[1], 2))
+    near = [None] * SLOTS
+    for m, v in enumerate(planes):
+        side = exchange(v, 0)
+        near[m], near[8 + m], near[4 + m], near[12 + m] = v, side, exchange(v, 1), exchange(side, 1)
+    return near + [exchange(v, 4) for v in near]
+
+
+def total(*parts):
+    v = parts[0].astype(F32)
+    for part in parts[1:]:
+        v = v + part.astype(F32)
+    return v.astype(BF)
+
+
+def sum_windows(keep, sent_first, sent_last):
+    half = SLOTS // 2
+    first, last = exchange(sent_first, 4), exchange(sent_last, 4)
+    sums = {}
+    for m in (3, 1, 2, 0):
+        far = exchange(total(keep[half + 4 + m], first[4 + m]), 0)
+        side = exchange(total(keep[half + m], first[m]), 0)
+        far = exchange(total(keep[4 + m], last[4 + m], far), 1)
+        sums[m] = (keep[m], last[m], side, far)
+    turn = exchange(total(*sums[3]), 2)
+    one = exchange(total(*sums[1], turn), 3)
+    two = exchange(total(*sums[2]), 2)
+    return (*sums[0], one, two)
 
 
 def shards_fn(block_input, segment_ids, cotangent, master_weights, momentum, weight_average):
@@ -637,25 +634,23 @@
     if count == 32:
         window = (tiles // count + 2) * TILE
         padded = jnp.pad(master_weights, (0, window * LANES - share)).reshape(window, LANES)
-        half = jax.ShapeDtypeStruct((window // 2, LANES), BF)
-        a, b = pl.pallas_call(
-            pack_kernel, out_shape=(half, half), in_specs=[in_vmem], out_specs=(in_vmem, in_vmem), name="pack_shard"
+        packed = pl.pallas_call(
+            pack_kernel, out_shape=jax.ShapeDtypeStruct((window, LANES), BF), in_specs=[in_vmem], out_specs=in_vmem, name="pack_shard"
         )(padded)
-        flats, pieces = gather_windows(a, b)
-        block_output, input_grad, ka, kb, sa, sb = core(*args, flats, pieces, count, rows)
-        parts = sum_windows((ka, kb), (sa, sb))
+        block_output, input_grad, *sums = core(*args, gather_windows(packed), True, count, rows)
+        addends = sum_windows(*sums)
         grad, tail = pl.pallas_call(
             finish_kernel,
             out_shape=(jax.ShapeDtypeStruct((window, LANES), F32), jax.ShapeDtypeStruct((8, LANES), F32)),
-            in_specs=[in_vmem] * 8,
+            in_specs=[in_vmem] * len(addends),
             out_specs=(in_vmem, in_vmem),
             name="finish_shard",
-        )(*parts[0], *parts[1])
+        )(*addends)
         weight_grad = grad.reshape(-1)[:share]
         vector_grad = tail[7]
     else:
         flat = lax.all_gather(master_weights.astype(BF), AXES, axis=0, tiled=True).reshape(rows, LANES)
-        block_output, input_grad, grad = core(*args, [flat], None, count, rows)
+        block_output, input_grad, grad = core(*args, [flat], False, count, rows)
         grad = grad.reshape(-1).astype(F32)
         weight_grad = lax.psum_scatter(grad, AXES, scatter_dimension=0, tiled=True)
         vector_grad = lax.psum_scatter(grad[grad.shape[0] - 8 * width :], AXES, scatter_dimension=0, tiled=True)

time: 189 us -> 174 us (0.921)
  waiting for transfers between devices: 68.4 us -> 59.5 us
  starting transfers between devices: 38.5 us -> 34.7 us
    ppermute x28 -> x48, waiting for transfers between devices: 68.4 us -> 59.5 us  [exchange(): lax.ppermute(v, AXES, [(j, j ^ (one if j // RC & 1 else zero)) for j in r...]
    ppermute x28 -> x48, starting transfers between devices: 38.5 us -> 34.7 us  [exchange(): lax.ppermute(v, AXES, [(j, j ^ (one if j // RC & 1 else zero)) for j in r...]
    convert_element_type x0 -> x5, other arithmetic: none -> 2.85 us  [total(): return v.astype(BF)]
    add x6 -> x0, other arithmetic: 2.09 us -> none  [the longest x2 1.89 us: sum_windows(): mine = keep[0] + got[0]]
    another operation x4 -> x0, other arithmetic: 2.08 us -> none  [gather_windows(): far = exchange(jnp.stack([stack, near]), second)]
  transfers between devices with their start and end apart: 28 -> 48, of which waited for: 14 -> 20; matrix products, arithmetic and copies ran while one was open for 3% -> 3% of each run, Pallas kernels for 0% -> 0%
where the time goes in v3:
time: 174 us
  Pallas kernels  67.1 us (39%)
  waiting for transfers between devices  59.5 us (34%)
  starting transfers between devices  34.7 us (20%)
  local copies, waits for them, and re-layouts  6.66 us (4%)
  other arithmetic  5.05 us (3%)
    pallas_call x1, Pallas kernels, core(): pl.pallas_call(functools.partial(core_kernel, width=D, length=T, shards=s...  62.5 us
    ppermute x48, waiting for transfers between devices, exchange(): lax.ppermute(v, AXES, [(j, j ^ (one if j // RC & 1 else zero)) for j in r...  59.5 us
    ppermute x48, starting transfers between devices, exchange(): lax.ppermute(v, AXES, [(j, j ^ (one if j // RC & 1 else zero)) for j in r...  34.7 us
  transfers between devices with their start and end apart: 48, of which 20 were waited for; matrix products, arithmetic and copies ran while one was open for 3% of the time, Pallas kernels for 0%

profile of v3, /device:TPU:0, one launch (start us, length us, event | category | flops | bytes accessed | tf_op | source)
XLA Modules:
  0.0 174.0 jit_solution(11451688813475887653)
XLA Ops:
  0.6 1.8 %pad_bitcast_fusion.x_ref = f32[800,128]{1,0:T(8,128)} fusion(f32[98496]{0:T(1024)} %param.9), kind=kLoop, calls=%fused_computation.26 | loop fusion | bytes 803584 | tf_op jit(solution)/shard_map/reshape | solution.py:636
  2.4 2.0 %pack_shard.1.refs_4_ = bf16[800,128]{1,0:T(8,128)(2,1)} custom-call(f32[800,128]{1,0:T(8,128)} %pad_bitcast_fusion.x_ref), custom_call_target="tpu_custom_call" | custom-call | tf_op jit(solution)/shard_map/pack_shard/pallas_call | solution.py:637
  4.4 2.9 %collective-permute-start.7 = (bf16[800,128]{1,0:T(8,128)(2,1)}, bf16[800,128]{1,0:T(8,128)(2,1)S(1)}, u32[]{:S(2)}, u32[]{:S(2)}) collective-permute-start(bf16[800,128]{1,0:T(8,128)(2,1)} %pack_shard.1.refs_4_), channel_id=1, source_target_pairs={{0,4},{1,5},{2,3},{3,2},{4,0},{5,1},{6,7},{7,6},{8,12},{9,13},{10,... | collective-permute-start | bytes 614408 | tf_op jit(solution)/shard_map/ppermute | solution.py:589
  7.3 1.5 collective-permute-start.3
  8.8 2.6 %collective-permute-start.1 = (bf16[800,128]{1,0:T(8,128)(2,1)}, bf16[800,128]{1,0:T(8,128)(2,1)S(1)}, u32[]{:S(2)}, u32[]{:S(2)}) collective-permute-start(bf16[800,128]{1,0:T(8,128)(2,1)} %pack_shard.1.refs_4_), channel_id=1, source_target_pairs={{0,16},{1,17},{2,10},{3,11},{4,20},{5,21},{6,14},{7,15},{8,24},{9,... | collective-permute-start | bytes 614408 | tf_op jit(solution)/shard_map/ppermute | solution.py:589
  11.4 1.6 collective-permute-start
  13.0 1.6 collective-permute-start.11
  14.6 1.0 collective-permute-start.19
  15.6 6.3 %collective-permute-done.1.refs_6_ = bf16[800,128]{1,0:T(8,128)(2,1)S(1)} collective-permute-done((bf16[800,128]{1,0:T(8,128)(2,1)}, bf16[800,128]{1,0:T(8,128)(2,1)S(1)}, u32[]{:S(2)}, u32[]{:S(2)}) %collective-permute-start.1) | collective-permute-done | bytes 204832 | tf_op jit(solution)/shard_map/ppermute | solution.py:589
  22.6 1.7 collective-permute-start.8
  24.3 1.9 %collective-permute-start.4 = (bf16[800,128]{1,0:T(8,128)(2,1)S(1)}, bf16[800,128]{1,0:T(8,128)(2,1)S(1)}, u32[]{:S(2)}, u32[]{:S(2)}) collective-permute-start(bf16[800,128]{1,0:T(8,128)(2,1)S(1)} %collective-permute-done.refs_5_), channel_id=1, source_target_pairs={{0,1},{1,0},{2,6},{3,7},{4,5},{5,4},{6,2},{7,3},{8,9},{9,8},{10,14... | collective-permute-start | bytes 614408 | tf_op jit(solution)/shard_map/ppermute | solution.py:589
  26.2 3.7 %collective-permute-done.9.refs_14_ = bf16[800,128]{1,0:T(8,128)(2,1)S(1)} collective-permute-done((bf16[800,128]{1,0:T(8,128)(2,1)S(1)}, bf16[800,128]{1,0:T(8,128)(2,1)S(1)}, u32[]{:S(2)}, u32[]{:S(2)}) %collective-permute-start.9) | collective-permute-done | bytes 204832 | tf_op jit(solution)/shard_map/ppermute | solution.py:589
  30.8 3.1 %collective-permute-done.8.refs_13_ = bf16[800,128]{1,0:T(8,128)(2,1)S(1)} collective-permute-done((bf16[800,128]{1,0:T(8,128)(2,1)S(1)}, bf16[800,128]{1,0:T(8,128)(2,1)S(1)}, u32[]{:S(2)}, u32[]{:S(2)}) %collective-permute-start.8) | collective-permute-done | bytes 204832 | tf_op jit(solution)/shard_map/ppermute | solution.py:589
  34.0 3.8 %collective-permute-done.2.refs_7_ = bf16[800,128]{1,0:T(8,128)(2,1)S(1)} collective-permute-done((bf16[800,128]{1,0:T(8,128)(2,1)S(1)}, bf16[800,128]{1,0:T(8,128)(2,1)S(1)}, u32[]{:S(2)}, u32[]{:S(2)}) %collective-permute-start.2) | collective-permute-done | bytes 204832 | tf_op jit(solution)/shard_map/ppermute | solution.py:589
  37.8 1.3 collective-permute-start.10
  39.1 0.6 collective-permute-done.13.refs_18_
  40.3 1.4 collective-permute-start.6
  41.7 4.2 %collective-permute-done.10.refs_15_ = bf16[800,128]{1,0:T(8,128)(2,1)} collective-permute-done((bf16[800,128]{1,0:T(8,128)(2,1)S(1)}, bf16[800,128]{1,0:T(8,128)(2,1)}, u32[]{:S(2)}, u32[]{:S(2)}) %collective-permute-start.10) | collective-permute-done | bytes 204832 | tf_op jit(solution)/shard_map/ppermute | solution.py:589
  46.5 1.1 collective-permute-done.6.refs_11_
  47.7 4.2 %collective-permute-done.14.refs_19_ = bf16[800,128]{1,0:T(8,128)(2,1)} collective-permute-done((bf16[800,128]{1,0:T(8,128)(2,1)}, bf16[800,128]{1,0:T(8,128)(2,1)}, u32[]{:S(2)}, u32[]{:S(2)}) %collective-permute-start.14) | collective-permute-done | bytes 204832 | tf_op jit(solution)/shard_map/ppermute | solution.py:589
  51.9 1.5 copy.13.refs_3_
  53.9 62.5 %layer_core.1 = (f32[512,512]{1,0:T(8,128)}, f32[512,512]{1,0:T(8,128)}, bf16[16,800,128]{2,1,0:T(8,128)(2,1)}, bf16[8,800,128]{2,1,0:T(8,128)(2,1)}, bf16[8,800,128]{2,1,0:T(8,128)(2,1)}) custom-call(bf16[512,512]{1,0:T(8,128)(2,1)} %bitcast.66, bf16[512,512]{1,0:T(8,128)(2,1)} %bitcast.67, s32[1,512]{1,0:T(1,128)} %refs_2_.1, s32[512,1]{1,0:T(8,128)} %copy.13.refs_3_, ...), custom_call_target="tpu_custom_call" | custom-call | tf_op jit(solution)/shard_map/layer_core/pallas_call | solution.py:572
  116.9 3.2 %collective-permute-done.32 = bf16[8,800,128]{2,1,0:T(8,128)(2,1)S(1)} collective-permute-done((bf16[8,800,128]{2,1,0:T(8,128)(2,1)}, bf16[8,800,128]{2,1,0:T(8,128)(2,1)S(1)}, u32[]{:S(2)}, u32[]{:S(2)}) %collective-permute-start.32) | collective-permute-done | bytes 1638432 | tf_op jit(solution)/shard_map/ppermute | solution.py:589
  120.1 2.2 %fusion.17 = (bf16[800,128]{1,0:T(8,128)(2,1)S(1)}, bf16[800,128]{1,0:T(8,128)(2,1)S(1)}, bf16[800,128]{1,0:T(8,128)(2,1)S(1)}, bf16[800,128]{1,0:T(8,128)(2,1)S...) fusion(bf16[8,800,128]{2,1,0:T(8,128)(2,1)S(1)} %collective-per, ...), kind=kLoop, calls=%fused_computation.36 | loop fusion | flops 3276800 | bytes 4915200 | tf_op jit(solution)/shard_map/convert_element_type | solution.py:606
  122.3 1.3 collective-permute-start.45
  123.6 0.8 collective-permute-start.44
  124.4 1.2 collective-permute-start.40
  125.6 0.8 collective-permute-start.37
  126.4 1.2 collective-permute-start.34
  128.3 2.0 %collective-permute-done.44 = bf16[800,128]{1,0:T(8,128)(2,1)S(1)} collective-permute-done((bf16[800,128]{1,0:T(8,128)(2,1)S(1)}, bf16[800,128]{1,0:T(8,128)(2,1)S(1)}, u32[]{:S(2)}, u32[]{:S(2)}) %collective-permute-start.44) | collective-permute-done | bytes 204832 | tf_op jit(solution)/shard_map/ppermute | solution.py:589
  130.3 1.2 collective-permute-start.39
  131.6 3.1 %collective-permute-done.40 = bf16[800,128]{1,0:T(8,128)(2,1)S(1)} collective-permute-done((bf16[800,128]{1,0:T(8,128)(2,1)S(1)}, bf16[800,128]{1,0:T(8,128)(2,1)S(1)}, u32[]{:S(2)}, u32[]{:S(2)}) %collective-permute-start.40) | collective-permute-done | bytes 204832 | tf_op jit(solution)/shard_map/ppermute | solution.py:589
  134.6 2.3 %collective-permute-done.37 = bf16[800,128]{1,0:T(8,128)(2,1)S(1)} collective-permute-done((bf16[800,128]{1,0:T(8,128)(2,1)S(1)}, bf16[800,128]{1,0:T(8,128)(2,1)S(1)}, u32[]{:S(2)}, u32[]{:S(2)}) %collective-permute-start.37) | collective-permute-done | bytes 204832 | tf_op jit(solution)/shard_map/ppermute | solution.py:589
  136.9 2.2 %collective-permute-done.34 = bf16[800,128]{1,0:T(8,128)(2,1)S(1)} collective-permute-done((bf16[800,128]{1,0:T(8,128)(2,1)S(1)}, bf16[800,128]{1,0:T(8,128)(2,1)S(1)}, u32[]{:S(2)}, u32[]{:S(2)}) %collective-permute-start.34) | collective-permute-done | bytes 204832 | tf_op jit(solution)/shard_map/ppermute | solution.py:589
  139.5 1.3 collective-permute-start.36
  140.8 1.9 %collective-permute-start.38 = (bf16[800,128]{1,0:T(8,128)(2,1)S(1)}, bf16[800,128]{1,0:T(8,128)(2,1)S(1)}, u32[]{:S(2)}, u32[]{:S(2)}) collective-permute-start(bf16[800,128]{1,0:T(8,128)(2,1)S(1)} %get-tuple-element.27), channel_id=1, source_target_pairs={{0,1},{1,0},{2,6},{3,7},{4,5},{5,4},{6,2},{7,3},{8,9},{9,8},{10,14... | collective-permute-start | bytes 614408 | tf_op jit(solution)/shard_map/ppermute | solution.py:589
  142.8 4.1 %collective-permute-done.41 = bf16[800,128]{1,0:T(8,128)(2,1)S(1)} collective-permute-done((bf16[800,128]{1,0:T(8,128)(2,1)S(1)}, bf16[800,128]{1,0:T(8,128)(2,1)S(1)}, u32[]{:S(2)}, u32[]{:S(2)}) %collective-permute-start.41) | collective-permute-done | bytes 204832 | tf_op jit(solution)/shard_map/ppermute | solution.py:589
  147.2 0.7 slice_bitcast_fusion.1.refs_0_
  147.9 0.8 collective-permute-start.33
  148.6 2.9 %collective-permute-start.47 = (bf16[800,128]{1,0:T(8,128)(2,1)S(1)}, bf16[800,128]{1,0:T(8,128)(2,1)S(1)}, u32[]{:S(2)}, u32[]{:S(2)}) collective-permute-start(bf16[800,128]{1,0:T(8,128)(2,1)S(1)} %get-tuple-element.25), channel_id=1, source_target_pairs={{0,16},{1,17},{2,10},{3,11},{4,20},{5,21},{6,14},{7,15},{8,24},{9,... | collective-permute-start | bytes 614408 | tf_op jit(solution)/shard_map/ppermute | solution.py:589
  151.8 9.4 %collective-permute-done.42 = bf16[800,128]{1,0:T(8,128)(2,1)S(1)} collective-permute-done((bf16[800,128]{1,0:T(8,128)(2,1)S(1)}, bf16[800,128]{1,0:T(8,128)(2,1)S(1)}, u32[]{:S(2)}, u32[]{:S(2)}) %collective-permute-start.42) | collective-permute-done | bytes 204832 | tf_op jit(solution)/shard_map/ppermute | solution.py:589
  161.5 0.7 slice_bitcast_fusion.refs_1_
  162.2 2.1 %collective-permute-done.47.refs_5_ = bf16[800,128]{1,0:T(8,128)(2,1)S(1)} collective-permute-done((bf16[800,128]{1,0:T(8,128)(2,1)S(1)}, bf16[800,128]{1,0:T(8,128)(2,1)S(1)}, u32[]{:S(2)}, u32[]{:S(2)}) %collective-permute-start.47) | collective-permute-done | bytes 204832 | tf_op jit(solution)/shard_map/ppermute | solution.py:589
  164.3 2.9 %collective-permute-done.43.refs_4_ = bf16[800,128]{1,0:T(8,128)(2,1)S(1)} collective-permute-done((bf16[800,128]{1,0:T(8,128)(2,1)S(1)}, bf16[800,128]{1,0:T(8,128)(2,1)S(1)}, u32[]{:S(2)}, u32[]{:S(2)}) %collective-permute-start.43) | collective-permute-done | bytes 204832 | tf_op jit(solution)/shard_map/ppermute | solution.py:589
  167.3 0.7 copy-done.7
  167.9 2.7 %finish_shard.1 = (f32[800,128]{1,0:T(8,128)}, f32[8,128]{1,0:T(8,128)}) custom-call(bf16[800,128]{1,0:T(8,128)(2,1)} %slice_bitcast_fusion.1.refs_0_, bf16[800,128]{1,0:T(8,128)(2,1)} %slice_bitcast_fusion.refs_1_, bf16[800,128]{1,0:T(8,128)(2,1)} %copy-done.4, bf16[800,128]{1,0:T(8,128)(2,1)} %copy-done.6, bf16[800,128]{1,0:T(8,128)(2,1)} %copy-done.7, ...), custom_call_target="tpu_custom_call" | custom-call | tf_op jit(solution)/shard_map/finish_shard/pallas_call | solution.py:642
  170.6 1.2 slice_bitcast_fusion.2
  171.8 2.2 %multiply_add_fusion = (f32[98496]{0:T(1024)}, f32[98496]{0:T(1024)}, f32[98496]{0:T(1024)}, f32[98496]{0:T(1024)}) fusion(f32[98496]{0:T(1024)S(1)} %copy-done.2, f32[98496]{0:T(1024)S(1)} %copy-done.1, f32[98496]{0:T(1024)S(1)} %copy-done.3, f32[102400]{0:T(1024)} %bitcast.68), kind=kLoop, calls=%fused_computation.27 | loop fusion | flops 886464 | bytes 3151872 | tf_op jit(solution)/shard_map/add | solution.py:661
  (120 shorter events, 5.5 us)
Async XLA Ops:
  4.4 8.6 %collective-permute-start.7 = (bf16[800,128]{1,0:T(8,128)(2,1)}, bf16[800,128]{1,0:T(8,128)(2,1)S(1)}, u32[]{:S(2)}, u32[]{:S(2)}) collective-permute-start(bf16[800,128]{1,0:T(8,128)(2,1)} %pack_shard.1.refs_4_), channel_id=1, source_target_pairs={{0,4},{1,5},{2,3},{3,2},{4,0},{5,1},{6,7},{7,6},{8,12},{9,13},{10,... | collective-permute-start | bytes 614408 | tf_op jit(solution)/shard_map/ppermute | solution.py:589
  7.3 5.7 %collective-permute-start.15 = (bf16[800,128]{1,0:T(8,128)(2,1)}, bf16[800,128]{1,0:T(8,128)(2,1)S(1)}, u32[]{:S(2)}, u32[]{:S(2)}) collective-permute-start(bf16[800,128]{1,0:T(8,128)(2,1)} %pack_shard.1.refs_4_), channel_id=1, source_target_pairs={{0,2},{1,3},{2,0},{3,1},{4,6},{5,7},{6,4},{7,5},{8,10},{9,11},{10,... | collective-permute-start | bytes 614408 | tf_op jit(solution)/shard_map/ppermute | solution.py:589
  7.3 7.3 %collective-permute-start.3 = (bf16[800,128]{1,0:T(8,128)(2,1)}, bf16[800,128]{1,0:T(8,128)(2,1)S(1)}, u32[]{:S(2)}, u32[]{:S(2)}) collective-permute-start(bf16[800,128]{1,0:T(8,128)(2,1)} %pack_shard.1.refs_4_), channel_id=1, source_target_pairs={{0,1},{1,0},{2,6},{3,7},{4,5},{5,4},{6,2},{7,3},{8,9},{9,8},{10,14... | collective-permute-start | bytes 614408 | tf_op jit(solution)/shard_map/ppermute | solution.py:589
  8.8 13.1 %collective-permute-start.1 = (bf16[800,128]{1,0:T(8,128)(2,1)}, bf16[800,128]{1,0:T(8,128)(2,1)S(1)}, u32[]{:S(2)}, u32[]{:S(2)}) collective-permute-start(bf16[800,128]{1,0:T(8,128)(2,1)} %pack_shard.1.refs_4_), channel_id=1, source_target_pairs={{0,16},{1,17},{2,10},{3,11},{4,20},{5,21},{6,14},{7,15},{8,24},{9,... | collective-permute-start | bytes 614408 | tf_op jit(solution)/shard_map/ppermute | solution.py:589
  11.4 10.5 %collective-permute-start = (bf16[800,128]{1,0:T(8,128)(2,1)}, bf16[800,128]{1,0:T(8,128)(2,1)S(1)}, u32[]{:S(2)}, u32[]{:S(2)}) collective-permute-start(bf16[800,128]{1,0:T(8,128)(2,1)} %pack_shard.1.refs_4_), channel_id=1, source_target_pairs={{0,8},{1,9},{2,18},{3,19},{4,12},{5,13},{6,22},{7,23},{8,0},{9,1},... | collective-permute-start | bytes 614408 | tf_op jit(solution)/shard_map/ppermute | solution.py:589
  13.0 9.3 %collective-permute-start.23 = (bf16[800,128]{1,0:T(8,128)(2,1)S(1)}, bf16[800,128]{1,0:T(8,128)(2,1)S(1)}, u32[]{:S(2)}, u32[]{:S(2)}) collective-permute-start(bf16[800,128]{1,0:T(8,128)(2,1)S(1)} %collective-permute-done.7.refs_12_), channel_id=1, source_target_pairs={{0,2},{1,3},{2,0},{3,1},{4,6},{5,7},{6,4},{7,5},{8,10},{9,11},{10,... | collective-permute-start | bytes 614408 | tf_op jit(solution)/shard_map/ppermute | solution.py:589
  13.0 9.3 %collective-permute-start.11 = (bf16[800,128]{1,0:T(8,128)(2,1)S(1)}, bf16[800,128]{1,0:T(8,128)(2,1)S(1)}, u32[]{:S(2)}, u32[]{:S(2)}) collective-permute-start(bf16[800,128]{1,0:T(8,128)(2,1)S(1)} %collective-permute-done.7.refs_12_), channel_id=1, source_target_pairs={{0,1},{1,0},{2,6},{3,7},{4,5},{5,4},{6,2},{7,3},{8,9},{9,8},{10,14... | collective-permute-start | bytes 614408 | tf_op jit(solution)/shard_map/ppermute | solution.py:589
  14.6 8.0 %collective-permute-start.19 = (bf16[800,128]{1,0:T(8,128)(2,1)S(1)}, bf16[800,128]{1,0:T(8,128)(2,1)S(1)}, u32[]{:S(2)}, u32[]{:S(2)}) collective-permute-start(bf16[800,128]{1,0:T(8,128)(2,1)S(1)} %collective-permute-done.3.refs_8_), channel_id=1, source_target_pairs={{0,2},{1,3},{2,0},{3,1},{4,6},{5,7},{6,4},{7,5},{8,10},{9,11},{10,... | collective-permute-start | bytes 614408 | tf_op jit(solution)/shard_map/ppermute | solution.py:589
  21.9 2.4 %collective-permute-start.17 = (bf16[800,128]{1,0:T(8,128)(2,1)S(1)}, bf16[800,128]{1,0:T(8,128)(2,1)S(1)}, u32[]{:S(2)}, u32[]{:S(2)}) collective-permute-start(bf16[800,128]{1,0:T(8,128)(2,1)S(1)} %collective-permute-done.1.refs_6_), channel_id=1, source_target_pairs={{0,2},{1,3},{2,0},{3,1},{4,6},{5,7},{6,4},{7,5},{8,10},{9,11},{10,... | collective-permute-start | bytes 614408 | tf_op jit(solution)/shard_map/ppermute | solution.py:589
  21.9 7.9 %collective-permute-start.9 = (bf16[800,128]{1,0:T(8,128)(2,1)S(1)}, bf16[800,128]{1,0:T(8,128)(2,1)S(1)}, u32[]{:S(2)}, u32[]{:S(2)}) collective-permute-start(bf16[800,128]{1,0:T(8,128)(2,1)S(1)} %collective-permute-done.1.refs_6_), channel_id=1, source_target_pairs={{0,4},{1,5},{2,3},{3,2},{4,0},{5,1},{6,7},{7,6},{8,12},{9,13},{10,... | collective-permute-start | bytes 614408 | tf_op jit(solution)/shard_map/ppermute | solution.py:589
  22.3 7.9 %collective-permute-start.5 = (bf16[800,128]{1,0:T(8,128)(2,1)S(1)}, bf16[800,128]{1,0:T(8,128)(2,1)S(1)}, u32[]{:S(2)}, u32[]{:S(2)}) collective-permute-start(bf16[800,128]{1,0:T(8,128)(2,1)S(1)} %collective-permute-done.1.refs_6_), channel_id=1, source_target_pairs={{0,1},{1,0},{2,6},{3,7},{4,5},{5,4},{6,2},{7,3},{8,9},{9,8},{10,14... | collective-permute-start | bytes 614408 | tf_op jit(solution)/shard_map/ppermute | solution.py:589
  22.3 7.9 %collective-permute-start.16 = (bf16[800,128]{1,0:T(8,128)(2,1)S(1)}, bf16[800,128]{1,0:T(8,128)(2,1)S(1)}, u32[]{:S(2)}, u32[]{:S(2)}) collective-permute-start(bf16[800,128]{1,0:T(8,128)(2,1)S(1)} %collective-permute-done.refs_5_), channel_id=1, source_target_pairs={{0,2},{1,3},{2,0},{3,1},{4,6},{5,7},{6,4},{7,5},{8,10},{9,11},{10,... | collective-permute-start | bytes 614408 | tf_op jit(solution)/shard_map/ppermute | solution.py:589
  22.6 11.3 %collective-permute-start.8 = (bf16[800,128]{1,0:T(8,128)(2,1)S(1)}, bf16[800,128]{1,0:T(8,128)(2,1)S(1)}, u32[]{:S(2)}, u32[]{:S(2)}) collective-permute-start(bf16[800,128]{1,0:T(8,128)(2,1)S(1)} %collective-permute-done.refs_5_), channel_id=1, source_target_pairs={{0,4},{1,5},{2,3},{3,2},{4,0},{5,1},{6,7},{7,6},{8,12},{9,13},{10,... | collective-permute-start | bytes 614408 | tf_op jit(solution)/shard_map/ppermute | solution.py:589
  24.3 9.6 %collective-permute-start.4 = (bf16[800,128]{1,0:T(8,128)(2,1)S(1)}, bf16[800,128]{1,0:T(8,128)(2,1)S(1)}, u32[]{:S(2)}, u32[]{:S(2)}) collective-permute-start(bf16[800,128]{1,0:T(8,128)(2,1)S(1)} %collective-permute-done.refs_5_), channel_id=1, source_target_pairs={{0,1},{1,0},{2,6},{3,7},{4,5},{5,4},{6,2},{7,3},{8,9},{9,8},{10,14... | collective-permute-start | bytes 614408 | tf_op jit(solution)/shard_map/ppermute | solution.py:589
  29.9 7.9 %collective-permute-start.2 = (bf16[800,128]{1,0:T(8,128)(2,1)S(1)}, bf16[800,128]{1,0:T(8,128)(2,1)S(1)}, u32[]{:S(2)}, u32[]{:S(2)}) collective-permute-start(bf16[800,128]{1,0:T(8,128)(2,1)S(1)} %collective-permute-done.refs_5_), channel_id=1, source_target_pairs={{0,16},{1,17},{2,10},{3,11},{4,20},{5,21},{6,14},{7,15},{8,24},{9,... | collective-permute-start | bytes 614408 | tf_op jit(solution)/shard_map/ppermute | solution.py:589
  30.2 7.6 %collective-permute-start.27 = (bf16[800,128]{1,0:T(8,128)(2,1)S(1)}, bf16[800,128]{1,0:T(8,128)(2,1)S(1)}, u32[]{:S(2)}, u32[]{:S(2)}) collective-permute-start(bf16[800,128]{1,0:T(8,128)(2,1)S(1)} %collective-permute-done.11.refs_16_), channel_id=1, source_target_pairs={{0,2},{1,3},{2,0},{3,1},{4,6},{5,7},{6,4},{7,5},{8,10},{9,11},{10,... | collective-permute-start | bytes 614408 | tf_op jit(solution)/shard_map/ppermute | solution.py:589
  30.3 8.9 %collective-permute-start.25 = (bf16[800,128]{1,0:T(8,128)(2,1)S(1)}, bf16[800,128]{1,0:T(8,128)(2,1)S(1)}, u32[]{:S(2)}, u32[]{:S(2)}) collective-permute-start(bf16[800,128]{1,0:T(8,128)(2,1)S(1)} %collective-permute-done.9.refs_14_), channel_id=1, source_target_pairs={{0,2},{1,3},{2,0},{3,1},{4,6},{5,7},{6,4},{7,5},{8,10},{9,11},{10,... | collective-permute-start | bytes 614408 | tf_op jit(solution)/shard_map/ppermute | solution.py:589
  33.9 5.9 %collective-permute-start.13 = (bf16[800,128]{1,0:T(8,128)(2,1)S(1)}, bf16[800,128]{1,0:T(8,128)(2,1)}, u32[]{:S(2)}, u32[]{:S(2)}) collective-permute-start(bf16[800,128]{1,0:T(8,128)(2,1)S(1)} %collective-permute-done.9.refs_14_), channel_id=1, source_target_pairs={{0,1},{1,0},{2,6},{3,7},{4,5},{5,4},{6,2},{7,3},{8,9},{9,8},{10,14... | collective-permute-start | bytes 614408 | tf_op jit(solution)/shard_map/ppermute | solution.py:589
  33.9 5.9 %collective-permute-start.21 = (bf16[800,128]{1,0:T(8,128)(2,1)S(1)}, bf16[800,128]{1,0:T(8,128)(2,1)S(1)}, u32[]{:S(2)}, u32[]{:S(2)}) collective-permute-start(bf16[800,128]{1,0:T(8,128)(2,1)S(1)} %collective-permute-done.5.refs_10_), channel_id=1, source_target_pairs={{0,2},{1,3},{2,0},{3,1},{4,6},{5,7},{6,4},{7,5},{8,10},{9,11},{10,... | collective-permute-start | bytes 614408 | tf_op jit(solution)/shard_map/ppermute | solution.py:589
  37.8 2.5 %collective-permute-start.24 = (bf16[800,128]{1,0:T(8,128)(2,1)S(1)}, bf16[800,128]{1,0:T(8,128)(2,1)S(1)}, u32[]{:S(2)}, u32[]{:S(2)}) collective-permute-start(bf16[800,128]{1,0:T(8,128)(2,1)S(1)} %collective-permute-done.8.refs_13_), channel_id=1, source_target_pairs={{0,2},{1,3},{2,0},{3,1},{4,6},{5,7},{6,4},{7,5},{8,10},{9,11},{10,... | collective-permute-start | bytes 614408 | tf_op jit(solution)/shard_map/ppermute | solution.py:589
  37.8 8.0 %collective-permute-start.10 = (bf16[800,128]{1,0:T(8,128)(2,1)S(1)}, bf16[800,128]{1,0:T(8,128)(2,1)}, u32[]{:S(2)}, u32[]{:S(2)}) collective-permute-start(bf16[800,128]{1,0:T(8,128)(2,1)S(1)} %collective-permute-done.2.refs_7_), channel_id=1, source_target_pairs={{0,4},{1,5},{2,3},{3,2},{4,0},{5,1},{6,7},{7,6},{8,12},{9,13},{10,... | collective-permute-start | bytes 614408 | tf_op jit(solution)/shard_map/ppermute | solution.py:589
  39.1 6.7 %collective-permute-start.12 = (bf16[800,128]{1,0:T(8,128)(2,1)S(1)}, bf16[800,128]{1,0:T(8,128)(2,1)}, u32[]{:S(2)}, u32[]{:S(2)}) collective-permute-start(bf16[800,128]{1,0:T(8,128)(2,1)S(1)} %collective-permute-done.8.refs_13_), channel_id=1, source_target_pairs={{0,1},{1,0},{2,6},{3,7},{4,5},{5,4},{6,2},{7,3},{8,9},{9,8},{10,14... | collective-permute-start | bytes 614408 | tf_op jit(solution)/shard_map/ppermute | solution.py:589
  39.8 6.1 %collective-permute-start.20 = (bf16[800,128]{1,0:T(8,128)(2,1)S(1)}, bf16[800,128]{1,0:T(8,128)(2,1)S(1)}, u32[]{:S(2)}, u32[]{:S(2)}) collective-permute-start(bf16[800,128]{1,0:T(8,128)(2,1)S(1)} %collective-permute-done.4.refs_9_), channel_id=1, source_target_pairs={{0,2},{1,3},{2,0},{3,1},{4,6},{5,7},{6,4},{7,5},{8,10},{9,11},{10,... | collective-permute-start | bytes 614408 | tf_op jit(solution)/shard_map/ppermute | solution.py:589
  39.8 6.6 %collective-permute-start.18 = (bf16[800,128]{1,0:T(8,128)(2,1)S(1)}, bf16[800,128]{1,0:T(8,128)(2,1)S(1)}, u32[]{:S(2)}, u32[]{:S(2)}) collective-permute-start(bf16[800,128]{1,0:T(8,128)(2,1)S(1)} %collective-permute-done.2.refs_7_), channel_id=1, source_target_pairs={{0,2},{1,3},{2,0},{3,1},{4,6},{5,7},{6,4},{7,5},{8,10},{9,11},{10,... | collective-permute-start | bytes 614408 | tf_op jit(solution)/shard_map/ppermute | solution.py:589
  40.3 7.3 %collective-permute-start.6 = (bf16[800,128]{1,0:T(8,128)(2,1)S(1)}, bf16[800,128]{1,0:T(8,128)(2,1)}, u32[]{:S(2)}, u32[]{:S(2)}) collective-permute-start(bf16[800,128]{1,0:T(8,128)(2,1)S(1)} %collective-permute-done.2.refs_7_), channel_id=1, source_target_pairs={{0,1},{1,0},{2,6},{3,7},{4,5},{5,4},{6,2},{7,3},{8,9},{9,8},{10,14... | collective-permute-start | bytes 614408 | tf_op jit(solution)/shard_map/ppermute | solution.py:589
  45.9 6.1 %collective-permute-start.14 = (bf16[800,128]{1,0:T(8,128)(2,1)}, bf16[800,128]{1,0:T(8,128)(2,1)}, u32[]{:S(2)}, u32[]{:S(2)}) collective-permute-start(bf16[800,128]{1,0:T(8,128)(2,1)} %collective-permute-done.10.refs_15_), channel_id=1, source_target_pairs={{0,1},{1,0},{2,6},{3,7},{4,5},{5,4},{6,2},{7,3},{8,9},{9,8},{10,14... | collective-permute-start | bytes 614408 | tf_op jit(solution)/shard_map/ppermute | solution.py:589
  45.9 7.6 %collective-permute-start.26 = (bf16[800,128]{1,0:T(8,128)(2,1)}, bf16[800,128]{1,0:T(8,128)(2,1)}, u32[]{:S(2)}, u32[]{:S(2)}) collective-permute-start(bf16[800,128]{1,0:T(8,128)(2,1)} %collective-permute-done.10.refs_15_), channel_id=1, source_target_pairs={{0,2},{1,3},{2,0},{3,1},{4,6},{5,7},{6,4},{7,5},{8,10},{9,11},{10,... | collective-permute-start | bytes 614408 | tf_op jit(solution)/shard_map/ppermute | solution.py:589
  45.9 7.6 %collective-permute-start.29 = (bf16[800,128]{1,0:T(8,128)(2,1)}, bf16[800,128]{1,0:T(8,128)(2,1)}, u32[]{:S(2)}, u32[]{:S(2)}) collective-permute-start(bf16[800,128]{1,0:T(8,128)(2,1)} %collective-permute-done.13.refs_18_), channel_id=1, source_target_pairs={{0,2},{1,3},{2,0},{3,1},{4,6},{5,7},{6,4},{7,5},{8,10},{9,11},{10,... | collective-permute-start | bytes 614408 | tf_op jit(solution)/shard_map/ppermute | solution.py:589
  46.4 7.1 %collective-permute-start.28 = (bf16[800,128]{1,0:T(8,128)(2,1)}, bf16[800,128]{1,0:T(8,128)(2,1)}, u32[]{:S(2)}, u32[]{:S(2)}) collective-permute-start(bf16[800,128]{1,0:T(8,128)(2,1)} %collective-permute-done.12.refs_17_), channel_id=1, source_target_pairs={{0,2},{1,3},{2,0},{3,1},{4,6},{5,7},{6,4},{7,5},{8,10},{9,11},{10,... | collective-permute-start | bytes 614408 | tf_op jit(solution)/shard_map/ppermute | solution.py:589
  47.6 5.9 %collective-permute-start.22 = (bf16[800,128]{1,0:T(8,128)(2,1)}, bf16[800,128]{1,0:T(8,128)(2,1)}, u32[]{:S(2)}, u32[]{:S(2)}) collective-permute-start(bf16[800,128]{1,0:T(8,128)(2,1)} %collective-permute-done.6.refs_11_), channel_id=1, source_target_pairs={{0,2},{1,3},{2,0},{3,1},{4,6},{5,7},{6,4},{7,5},{8,10},{9,11},{10,... | collective-permute-start | bytes 614408 | tf_op jit(solution)/shard_map/ppermute | solution.py:589
  51.9 1.8 %collective-permute-start.30 = (bf16[800,128]{1,0:T(8,128)(2,1)}, bf16[800,128]{1,0:T(8,128)(2,1)}, u32[]{:S(2)}, u32[]{:S(2)}) collective-permute-start(bf16[800,128]{1,0:T(8,128)(2,1)} %collective-permute-done.14.refs_19_), channel_id=1, source_target_pairs={{0,2},{1,3},{2,0},{3,1},{4,6},{5,7},{6,4},{7,5},{8,10},{9,11},{10,... | collective-permute-start | bytes 614408 | tf_op jit(solution)/shard_map/ppermute | solution.py:589
  116.4 3.8 %collective-permute-start.32 = (bf16[8,800,128]{2,1,0:T(8,128)(2,1)}, bf16[8,800,128]{2,1,0:T(8,128)(2,1)S(1)}, u32[]{:S(2)}, u32[]{:S(2)}) collective-permute-start(bf16[8,800,128]{2,1,0:T(8,128)(2,1)} %get-tuple-element.18), channel_id=1, source_target_pairs={{0,2},{1,3},{2,0},{3,1},{4,6},{5,7},{6,4},{7,5},{8,10},{9,11},{10,... | collective-permute-start | bytes 4915208 | tf_op jit(solution)/shard_map/ppermute | solution.py:589
  116.7 9.7 %collective-permute-start.31 = (bf16[8,800,128]{2,1,0:T(8,128)(2,1)}, bf16[8,800,128]{2,1,0:T(8,128)(2,1)S(1)}, u32[]{:S(2)}, u32[]{:S(2)}) collective-permute-start(bf16[8,800,128]{2,1,0:T(8,128)(2,1)} %get-tuple-element.17), channel_id=1, source_target_pairs={{0,2},{1,3},{2,0},{3,1},{4,6},{5,7},{6,4},{7,5},{8,10},{9,11},{10,... | collective-permute-start | bytes 4915208 | tf_op jit(solution)/shard_map/ppermute | solution.py:589
  122.3 5.8 %collective-permute-start.45 = (bf16[800,128]{1,0:T(8,128)(2,1)S(1)}, bf16[800,128]{1,0:T(8,128)(2,1)S(1)}, u32[]{:S(2)}, u32[]{:S(2)}) collective-permute-start(bf16[800,128]{1,0:T(8,128)(2,1)S(1)} %get-tuple-element.30), channel_id=1, source_target_pairs={{0,4},{1,5},{2,3},{3,2},{4,0},{5,1},{6,7},{7,6},{8,12},{9,13},{10,... | collective-permute-start | bytes 614408 | tf_op jit(solution)/shard_map/ppermute | solution.py:589
  123.6 6.7 %collective-permute-start.44 = (bf16[800,128]{1,0:T(8,128)(2,1)S(1)}, bf16[800,128]{1,0:T(8,128)(2,1)S(1)}, u32[]{:S(2)}, u32[]{:S(2)}) collective-permute-start(bf16[800,128]{1,0:T(8,128)(2,1)S(1)} %get-tuple-element.29), channel_id=1, source_target_pairs={{0,4},{1,5},{2,3},{3,2},{4,0},{5,1},{6,7},{7,6},{8,12},{9,13},{10,... | collective-permute-start | bytes 614408 | tf_op jit(solution)/shard_map/ppermute | solution.py:589
  124.4 10.2 %collective-permute-start.40 = (bf16[800,128]{1,0:T(8,128)(2,1)S(1)}, bf16[800,128]{1,0:T(8,128)(2,1)S(1)}, u32[]{:S(2)}, u32[]{:S(2)}) collective-permute-start(bf16[800,128]{1,0:T(8,128)(2,1)S(1)} %get-tuple-element.31), channel_id=1, source_target_pairs={{0,4},{1,5},{2,3},{3,2},{4,0},{5,1},{6,7},{7,6},{8,12},{9,13},{10,... | collective-permute-start | bytes 614408 | tf_op jit(solution)/shard_map/ppermute | solution.py:589
  125.6 11.3 %collective-permute-start.37 = (bf16[800,128]{1,0:T(8,128)(2,1)S(1)}, bf16[800,128]{1,0:T(8,128)(2,1)S(1)}, u32[]{:S(2)}, u32[]{:S(2)}) collective-permute-start(bf16[800,128]{1,0:T(8,128)(2,1)S(1)} %get-tuple-element.33), channel_id=1, source_target_pairs={{0,4},{1,5},{2,3},{3,2},{4,0},{5,1},{6,7},{7,6},{8,12},{9,13},{10,... | collective-permute-start | bytes 614408 | tf_op jit(solution)/shard_map/ppermute | solution.py:589
  126.4 12.7 %collective-permute-start.34 = (bf16[800,128]{1,0:T(8,128)(2,1)S(1)}, bf16[800,128]{1,0:T(8,128)(2,1)S(1)}, u32[]{:S(2)}, u32[]{:S(2)}) collective-permute-start(bf16[800,128]{1,0:T(8,128)(2,1)S(1)} %get-tuple-element.35), channel_id=1, source_target_pairs={{0,4},{1,5},{2,3},{3,2},{4,0},{5,1},{6,7},{7,6},{8,12},{9,13},{10,... | collective-permute-start | bytes 614408 | tf_op jit(solution)/shard_map/ppermute | solution.py:589
  128.2 10.9 %collective-permute-start.46 = (bf16[800,128]{1,0:T(8,128)(2,1)S(1)}, bf16[800,128]{1,0:T(8,128)(2,1)S(1)}, u32[]{:S(2)}, u32[]{:S(2)}) collective-permute-start(bf16[800,128]{1,0:T(8,128)(2,1)S(1)} %fusion), channel_id=1, source_target_pairs={{0,1},{1,0},{2,6},{3,7},{4,5},{5,4},{6,2},{7,3},{8,9},{9,8},{10,14... | collective-permute-start | bytes 614408 | tf_op jit(solution)/shard_map/ppermute | solution.py:589
  130.3 12.5 %collective-permute-start.39 = (bf16[800,128]{1,0:T(8,128)(2,1)S(1)}, bf16[800,128]{1,0:T(8,128)(2,1)S(1)}, u32[]{:S(2)}, u32[]{:S(2)}) collective-permute-start(bf16[800,128]{1,0:T(8,128)(2,1)S(1)} %get-tuple-element.32), channel_id=1, source_target_pairs={{0,4},{1,5},{2,3},{3,2},{4,0},{5,1},{6,7},{7,6},{8,12},{9,13},{10,... | collective-permute-start | bytes 614408 | tf_op jit(solution)/shard_map/ppermute | solution.py:589
  139.5 7.5 %collective-permute-start.41 = (bf16[800,128]{1,0:T(8,128)(2,1)S(1)}, bf16[800,128]{1,0:T(8,128)(2,1)S(1)}, u32[]{:S(2)}, u32[]{:S(2)}) collective-permute-start(bf16[800,128]{1,0:T(8,128)(2,1)S(1)} %get-tuple-element.26), channel_id=1, source_target_pairs={{0,1},{1,0},{2,6},{3,7},{4,5},{5,4},{6,2},{7,3},{8,9},{9,8},{10,14... | collective-permute-start | bytes 614408 | tf_op jit(solution)/shard_map/ppermute | solution.py:589
  139.5 12.0 %collective-permute-start.36 = (bf16[800,128]{1,0:T(8,128)(2,1)S(1)}, bf16[800,128]{1,0:T(8,128)(2,1)S(1)}, u32[]{:S(2)}, u32[]{:S(2)}) collective-permute-start(bf16[800,128]{1,0:T(8,128)(2,1)S(1)} %get-tuple-element.34), channel_id=1, source_target_pairs={{0,4},{1,5},{2,3},{3,2},{4,0},{5,1},{6,7},{7,6},{8,12},{9,13},{10,... | collective-permute-start | bytes 614408 | tf_op jit(solution)/shard_map/ppermute | solution.py:589
  140.8 11.0 %collective-permute-start.38 = (bf16[800,128]{1,0:T(8,128)(2,1)S(1)}, bf16[800,128]{1,0:T(8,128)(2,1)S(1)}, u32[]{:S(2)}, u32[]{:S(2)}) collective-permute-start(bf16[800,128]{1,0:T(8,128)(2,1)S(1)} %get-tuple-element.27), channel_id=1, source_target_pairs={{0,1},{1,0},{2,6},{3,7},{4,5},{5,4},{6,2},{7,3},{8,9},{9,8},{10,14... | collective-permute-start | bytes 614408 | tf_op jit(solution)/shard_map/ppermute | solution.py:589
  147.1 14.2 %collective-permute-start.42 = (bf16[800,128]{1,0:T(8,128)(2,1)S(1)}, bf16[800,128]{1,0:T(8,128)(2,1)S(1)}, u32[]{:S(2)}, u32[]{:S(2)}) collective-permute-start(bf16[800,128]{1,0:T(8,128)(2,1)S(1)} %fusion.5), channel_id=1, source_target_pairs={{0,16},{1,17},{2,10},{3,11},{4,20},{5,21},{6,14},{7,15},{8,24},{9,... | collective-permute-start | bytes 614408 | tf_op jit(solution)/shard_map/ppermute | solution.py:589
  147.9 14.3 %collective-permute-start.33 = (bf16[800,128]{1,0:T(8,128)(2,1)S(1)}, bf16[800,128]{1,0:T(8,128)(2,1)S(1)}, u32[]{:S(2)}, u32[]{:S(2)}) collective-permute-start(bf16[800,128]{1,0:T(8,128)(2,1)S(1)} %get-tuple-element.36), channel_id=1, source_target_pairs={{0,4},{1,5},{2,3},{3,2},{4,0},{5,1},{6,7},{7,6},{8,12},{9,13},{10,... | collective-permute-start | bytes 614408 | tf_op jit(solution)/shard_map/ppermute | solution.py:589
  148.6 15.7 %collective-permute-start.47 = (bf16[800,128]{1,0:T(8,128)(2,1)S(1)}, bf16[800,128]{1,0:T(8,128)(2,1)S(1)}, u32[]{:S(2)}, u32[]{:S(2)}) collective-permute-start(bf16[800,128]{1,0:T(8,128)(2,1)S(1)} %get-tuple-element.25), channel_id=1, source_target_pairs={{0,16},{1,17},{2,10},{3,11},{4,20},{5,21},{6,14},{7,15},{8,24},{9,... | collective-permute-start | bytes 614408 | tf_op jit(solution)/shard_map/ppermute | solution.py:589
  151.5 12.8 %collective-permute-start.35 = (bf16[800,128]{1,0:T(8,128)(2,1)S(1)}, bf16[800,128]{1,0:T(8,128)(2,1)S(1)}, u32[]{:S(2)}, u32[]{:S(2)}) collective-permute-start(bf16[800,128]{1,0:T(8,128)(2,1)S(1)} %get-tuple-element.28), channel_id=1, source_target_pairs={{0,1},{1,0},{2,6},{3,7},{4,5},{5,4},{6,2},{7,3},{8,9},{9,8},{10,14... | collective-permute-start | bytes 614408 | tf_op jit(solution)/shard_map/ppermute | solution.py:589
  161.4 5.8 %collective-permute-start.43 = (bf16[800,128]{1,0:T(8,128)(2,1)S(1)}, bf16[800,128]{1,0:T(8,128)(2,1)S(1)}, u32[]{:S(2)}, u32[]{:S(2)}) collective-permute-start(bf16[800,128]{1,0:T(8,128)(2,1)S(1)} %fusion.9), channel_id=1, source_target_pairs={{0,8},{1,9},{2,18},{3,19},{4,12},{5,13},{6,22},{7,23},{8,0},{9,1},... | collective-permute-start | bytes 614408 | tf_op jit(solution)/shard_map/ppermute | solution.py:589
  (29 other events, 586.1 us)

commit v4 on v3

--- a/solution.py
+++ b/solution.py
@@ -146,6 +146,7 @@
 RZ, RX, RC, RY = 8, 4, 2, 1
 STEPS = ((RX, RY), (RY, RX), (2 * RZ, RZ), (RZ, 2 * RZ))
 SLOTS = 1 << len(STEPS)
+PLANES = (3, 2, 1, 0)
 
 
 def own_core(me):
@@ -183,7 +184,7 @@
         owner = slot_owner(origin, side, n % SLOTS)
         for at, to, rows in window_moves(owner, height, tiles, shards, edge_row):
             pltpu.make_async_copy(ref.at[pl.ds(at, rows)], wide.at[pl.ds(to, rows)], sem.at[0]).start()
-    settle(wide, height * len(w_refs), sem.at[0])
+    settle(wide, height * shards, sem.at[0])
     starts = window_starts(shards, tiles)
 
     def tile(row):
@@ -221,45 +222,15 @@
     core = own_core(me)
     for n, ref in enumerate(g_refs):
         side, origin = (core, me) if n == 0 else (1 - core, jnp.bitwise_xor(me, RC))
-        first = SLOTS // 2 if n == 1 else 0
         for k in range(ref.shape[0]):
-            owner = slot_owner(origin, side, first + k)
+            slot = k if n == 0 else 4 * k + PLANES[n - 1]
+            owner = slot_owner(origin, side, slot)
             for at, to, rows in window_moves(owner, height, tiles, shards, edge_row):
                 pltpu.make_async_copy(wide.at[pl.ds(to, rows)], ref.at[k].at[pl.ds(at, rows)], sem.at[n]).start()
     for n, ref in enumerate(g_refs):
         settle(wide, ref.shape[0] * ref.shape[1], sem.at[n])
 
 
-def pack_kernel(x_ref, out_ref):
-    me = own_index()
-    v = x_ref[...]
-    lane = lax.broadcasted_iota(jnp.int32, v.shape, 1)
-    turned = pltpu.roll(v, 64, 1)
-    moved = jnp.where(lane >= 64, turned, pltpu.roll(turned, 1, 0))
-    odd = (me & 1) == 1
-    v = jnp.where(odd, moved, v)
-    shift = ((me * 192) & 2047) >> 7
-    out_ref[...] = pltpu.roll(v, shift, 0).astype(BF)
-
-
-def finish_kernel(*refs):
-    out_ref, vec_ref = refs[-2:]
-    me = own_index()
-    v = None
-    for ref in refs[:-2]:
-        part = ref[...].astype(F32)
-        v = part if v is None else v + part
-    rows = v.shape[0]
-    vec_ref[...] = v[rows - 8 :]
-    shift = ((me * 192) & 2047) >> 7
-    v = pltpu.roll(v, rows - shift, 0)
-    lane = lax.broadcasted_iota(jnp.int32, v.shape, 1)
-    turned = pltpu.roll(v, 64, 1)
-    moved = jnp.where(lane < 64, turned, pltpu.roll(turned, rows - 1, 0))
-    odd = (me & 1) == 1
-    out_ref[...] = jnp.where(odd, moved, v)
-
-
 CHUNK = 512
 STEP = 32
 GSTEP = 16
@@ -268,11 +239,11 @@
 
 def core_kernel(*refs, width, length, shards, windows, flat_rows):
     n_in = 2 * SLOTS if windows else 1
-    (x_ref, cot_ref, segr_ref, segc_ref) = refs[:4]
-    w_refs = refs[4 : 4 + n_in]
-    refs = refs[4 + n_in :]
+    (x_ref, cot_ref, seg_ref) = refs[:3]
+    w_refs = refs[3 : 3 + n_in]
+    refs = refs[3 + n_in :]
     (y_ref, dx_ref) = refs[:2]
-    n_out = 3 if windows else 1
+    n_out = 1 + len(PLANES) if windows else 1
     g_refs = refs[2 : 2 + n_out]
     (wide, wa, wi, wo, b1, vec, xb, qkv, ab, ctx, xh1, iv1, xh2, iv2, h1b, slope, df, da, dqkv, dc, dr1,
      bias, gb1, gvec, count_ref, sem) = refs[2 + n_out :]
@@ -290,7 +261,9 @@
     unpack_weights(flat, wa, wi, wo, b1, vec, D)
 
     scale = 0.125
-    bias[...] = jnp.where(segc_ref[...] == segr_ref[...], 0.0, -1e30).astype(F32)
+    seg = seg_ref[...].astype(F32)
+    column = jnp.transpose(jnp.broadcast_to(seg, (LANES, T)))[:, 0:1]
+    bias[...] = jnp.where(column == seg, 0.0, -1e30).astype(F32)
 
     count_ref[0] = 1
     single = count_ref[0]
@@ -564,7 +537,7 @@
         pltpu.SMEM((1,), jnp.int32), pltpu.SemaphoreType.DMA((8,)),
     ]
     if windows:
-        g_shapes = [jax.ShapeDtypeStruct((n, flats[0].shape[0], LANES), BF) for n in (SLOTS, SLOTS // 2, SLOTS // 2)]
+        g_shapes = [jax.ShapeDtypeStruct((n, flats[0].shape[0], LANES), BF) for n in (SLOTS, 4, 4, 4, 4)]
     else:
         g_shapes = [jax.ShapeDtypeStruct((rows, LANES), BF)]
     in_vmem = pl.BlockSpec(memory_space=pltpu.VMEM)
@@ -572,12 +545,12 @@
     return pl.pallas_call(
         functools.partial(core_kernel, width=D, length=T, shards=shards, windows=windows, flat_rows=rows),
         out_shape=tuple([jax.ShapeDtypeStruct((T, D), F32)] * 2 + g_shapes),
-        in_specs=[in_vmem] * 4 + [anywhere] * len(flats),
+        in_specs=[in_vmem] * 3 + [anywhere] * len(flats),
         out_specs=tuple([in_vmem] * 2 + [anywhere] * len(g_shapes)),
         scratch_shapes=scratch,
         compiler_params=pltpu.CompilerParams(vmem_limit_bytes=59 * 1024 * 1024),
         name="layer_core",
-    )(x, cot, seg.reshape(1, T), seg.reshape(T, 1), *flats)
+    )(x, cot, seg, *flats)
 
 
 AXES = ("dp", "rep")
@@ -589,10 +562,14 @@
     return lax.ppermute(v, AXES, [(j, j ^ (one if j // RC & 1 else zero)) for j in range(count)])
 
 
+def after(v, earlier):
+    return lax.optimization_barrier((v, earlier))[0]
+
+
 def gather_windows(own):
-    planes = [own, exchange(own, 3), exchange(own, 2)]
-    planes.append(exchange(planes[1], 2))
+    next_plane = exchange(own, 3)
     near = [None] * SLOTS
+    planes = [own, next_plane, exchange(after(own, next_plane), 2), exchange(next_plane, 2)]
     for m, v in enumerate(planes):
         side = exchange(v, 0)
         near[m], near[8 + m], near[4 + m], near[12 + m] = v, side, exchange(v, 1), exchange(side, 1)
@@ -606,19 +583,38 @@
     return v.astype(BF)
 
 
-def sum_windows(keep, sent_first, sent_last):
-    half = SLOTS // 2
-    first, last = exchange(sent_first, 4), exchange(sent_last, 4)
-    sums = {}
-    for m in (3, 1, 2, 0):
-        far = exchange(total(keep[half + 4 + m], first[4 + m]), 0)
-        side = exchange(total(keep[half + m], first[m]), 0)
-        far = exchange(total(keep[4 + m], last[4 + m], far), 1)
-        sums[m] = (keep[m], last[m], side, far)
-    turn = exchange(total(*sums[3]), 2)
-    one = exchange(total(*sums[1], turn), 3)
-    two = exchange(total(*sums[2]), 2)
-    return (*sums[0], one, two)
+def sum_windows(keep, *sent):
+    got = {m: exchange(v, 4) for m, v in zip(PLANES, sent)}
+    far, side, back, last = {}, {}, {}, [None]
+
+    def add(*parts):
+        if last[0] is not None:
+            parts = (*parts[:-1], after(parts[-1], last[0]))
+        last[0] = total(*parts)
+        return last[0]
+
+    def near_far(m):
+        far[m] = exchange(add(keep[12 + m], got[m][3]), 0)
+        side[m] = exchange(add(keep[8 + m], got[m][2]), 0)
+
+    def second(m):
+        back[m] = exchange(add(keep[4 + m], got[m][1], far[m]), 1)
+
+    def plane(m):
+        return (keep[m], got[m][0], side[m], back[m])
+
+    near_far(3)
+    near_far(2)
+    second(3)
+    second(2)
+    near_far(1)
+    turn = exchange(add(*plane(3)), 2)
+    two = exchange(add(*plane(2)), 2)
+    near_far(0)
+    second(1)
+    second(0)
+    one = exchange(add(*plane(1), turn), 3)
+    return (*plane(0), one, two)
 
 
 def shards_fn(block_input, segment_ids, cotangent, master_weights, momentum, weight_average):
@@ -628,26 +624,19 @@
     share = master_weights.shape[0]
     rows = share * count // LANES
     tiles = rows // TILE
-    vec_len = 8 * width // count
-    args = (block_input[0], cotangent[0], segment_ids[0])
-    in_vmem = pl.BlockSpec(memory_space=pltpu.VMEM)
+    args = (block_input[0], cotangent[0], segment_ids)
     if count == 32:
         window = (tiles // count + 2) * TILE
-        padded = jnp.pad(master_weights, (0, window * LANES - share)).reshape(window, LANES)
-        packed = pl.pallas_call(
-            pack_kernel, out_shape=jax.ShapeDtypeStruct((window, LANES), BF), in_specs=[in_vmem], out_specs=in_vmem, name="pack_shard"
-        )(padded)
-        block_output, input_grad, *sums = core(*args, gather_windows(packed), True, count, rows)
+        first = (own_index() * share) % (TILE * LANES)
+        padded = jnp.pad(master_weights, (TILE * LANES, window * LANES - share))
+        own = lax.dynamic_slice(padded, (TILE * LANES - first,), (window * LANES,)).astype(BF).reshape(window, LANES)
+        block_output, input_grad, *sums = core(*args, gather_windows(own), True, count, rows)
         addends = sum_windows(*sums)
-        grad, tail = pl.pallas_call(
-            finish_kernel,
-            out_shape=(jax.ShapeDtypeStruct((window, LANES), F32), jax.ShapeDtypeStruct((8, LANES), F32)),
-            in_specs=[in_vmem] * len(addends),
-            out_specs=(in_vmem, in_vmem),
-            name="finish_shard",
-        )(*addends)
-        weight_grad = grad.reshape(-1)[:share]
-        vector_grad = tail[7]
+        grad = addends[0].astype(F32)
+        for addend in addends[1:]:
+            grad = grad + addend.astype(F32)
+        weight_grad = lax.dynamic_slice(grad.reshape(-1), (first,), (share,))
+        vector_grad = grad[window - 1]
     else:
         flat = lax.all_gather(master_weights.astype(BF), AXES, axis=0, tiled=True).reshape(rows, LANES)
         block_output, input_grad, grad = core(*args, [flat], False, count, rows)

time: 174 us -> 161 us (0.925)
  waiting for transfers between devices: 59.5 us -> 39.8 us
  starting transfers between devices: 34.7 us -> 43.1 us
  other arithmetic: 5.05 us -> 11.6 us
  Pallas kernels: 67.1 us -> 62.5 us
  local copies, waits for them, and re-layouts: 6.66 us -> 2.6 us
    ppermute x48 -> x50, waiting for transfers between devices: 59.5 us -> 39.8 us  [exchange(): lax.ppermute(v, AXES, [(j, j ^ (one if j // RC & 1 else zero)) for j in r...]
    ppermute x48 -> x50, starting transfers between devices: 34.7 us -> 43.1 us  [exchange(): lax.ppermute(v, AXES, [(j, j ^ (one if j // RC & 1 else zero)) for j in r...]
    convert_element_type x5 -> x15, other arithmetic: 2.85 us -> 7.6 us  [total(): return v.astype(BF)]
    pallas_call x2 -> x0, Pallas kernels: 4.66 us -> none  [the longest x1 2.69 us: shards_fn(): pl.pallas_call(finish_kernel, out_shape=(jax.ShapeDtypeStruct((window, LA...]
    squeeze x3 -> x5, local copies, waits for them, and re-layouts: 2.57 us -> 0.61 us  [the longest x1 0.51 us: shards_fn(): vector_grad = grad[window - 1]]
  transfers between devices with their start and end apart: 48 -> 50, of which waited for: 20 -> 18; matrix products, arithmetic and copies ran while one was open for 3% -> 5% of each run, Pallas kernels for 0% -> 0%
where the time goes in v4:
time: 161 us
  Pallas kernels  62.5 us (39%)
  starting transfers between devices  43.1 us (27%)
  waiting for transfers between devices  39.8 us (25%)
  other arithmetic  11.6 us (7%)
  local copies, waits for them, and re-layouts  2.6 us (2%)
    pallas_call x1, Pallas kernels, core(): pl.pallas_call(functools.partial(core_kernel, width=D, length=T, shards=s...  62.5 us
    ppermute x50, starting transfers between devices, exchange(): lax.ppermute(v, AXES, [(j, j ^ (one if j // RC & 1 else zero)) for j in r...  43.1 us
    ppermute x50, waiting for transfers between devices, exchange(): lax.ppermute(v, AXES, [(j, j ^ (one if j // RC & 1 else zero)) for j in r...  39.8 us
    convert_element_type x15, other arithmetic, total(): return v.astype(BF)  7.6 us
  transfers between devices with their start and end apart: 50, of which 18 were waited for; matrix products, arithmetic and copies ran while one was open for 5% of the time, Pallas kernels for 0%

profile of v4, /device:TPU:0, one launch (start us, length us, event | category | flops | bytes accessed | tf_op | source)
XLA Modules:
  0.0 160.8 jit_solution(17913261680922091911)
XLA Ops:
  0.7 1.2 fusion.23.refs_3_
  1.9 3.0 %collective-permute-start.7 = (bf16[800,128]{1,0:T(8,128)(2,1)S(1)}, bf16[800,128]{1,0:T(8,128)(2,1)S(1)}, u32[]{:S(2)}, u32[]{:S(2)}) collective-permute-start(bf16[800,128]{1,0:T(8,128)(2,1)S(1)} %fusion.23.refs_3_), channel_id=1, source_target_pairs={{0,4},{1,5},{2,3},{3,2},{4,0},{5,1},{6,7},{7,6},{8,12},{9,13},{10,... | collective-permute-start | bytes 614408 | tf_op jit(solution)/shard_map/ppermute | solution.py:562
  4.9 1.6 collective-permute-start
  6.4 1.5 collective-permute-start.3
  8.6 2.8 %collective-permute-start.11 = (bf16[800,128]{1,0:T(8,128)(2,1)S(1)}, bf16[800,128]{1,0:T(8,128)(2,1)S(1)}, u32[]{:S(2)}, u32[]{:S(2)}) collective-permute-start(bf16[800,128]{1,0:T(8,128)(2,1)S(1)} %collective-permute-done.7.refs_11_), channel_id=1, source_target_pairs={{0,1},{1,0},{2,6},{3,7},{4,5},{5,4},{6,2},{7,3},{8,9},{9,8},{10,14... | collective-permute-start | bytes 614408 | tf_op jit(solution)/shard_map/ppermute | solution.py:562
  12.2 3.3 %collective-permute-start.1 = (bf16[800,128]{1,0:T(8,128)(2,1)S(1)}, bf16[800,128]{1,0:T(8,128)(2,1)S(1)}, u32[]{:S(2)}, u32[]{:S(2)}) collective-permute-start(bf16[800,128]{1,0:T(8,128)(2,1)S(1)} %fusion.23.refs_3_), channel_id=1, source_target_pairs={{0,16},{1,17},{2,10},{3,11},{4,20},{5,21},{6,14},{7,15},{8,24},{9,... | collective-permute-start | bytes 614408 | tf_op jit(solution)/shard_map/ppermute | solution.py:562
  15.6 0.7 collective-permute-start.8
  16.4 1.2 collective-permute-start.4
  17.6 2.8 %collective-permute-start.2 = (bf16[800,128]{1,0:T(8,128)(2,1)S(1)}, bf16[800,128]{1,0:T(8,128)(2,1)S(1)}, u32[]{:S(2)}, u32[]{:S(2)}) collective-permute-start(bf16[800,128]{1,0:T(8,128)(2,1)S(1)} %collective-permute-done.refs_4_), channel_id=1, source_target_pairs={{0,16},{1,17},{2,10},{3,11},{4,20},{5,21},{6,14},{7,15},{8,24},{9,... | collective-permute-start | bytes 614408 | tf_op jit(solution)/shard_map/ppermute | solution.py:562
  21.2 2.4 %collective-permute-done.8.refs_12_ = bf16[800,128]{1,0:T(8,128)(2,1)S(1)} collective-permute-done((bf16[800,128]{1,0:T(8,128)(2,1)S(1)}, bf16[800,128]{1,0:T(8,128)(2,1)S(1)}, u32[]{:S(2)}, u32[]{:S(2)}) %collective-permute-start.8) | collective-permute-done | bytes 204832 | tf_op jit(solution)/shard_map/ppermute | solution.py:562
  24.0 1.5 collective-permute-start.5
  25.6 1.0 collective-permute-start.12
  26.6 1.5 collective-permute-start.20
  28.1 3.5 %collective-permute-done.9.refs_13_ = bf16[800,128]{1,0:T(8,128)(2,1)S(1)} collective-permute-done((bf16[800,128]{1,0:T(8,128)(2,1)S(1)}, bf16[800,128]{1,0:T(8,128)(2,1)S(1)}, u32[]{:S(2)}, u32[]{:S(2)}) %collective-permute-start.9) | collective-permute-done | bytes 204832 | tf_op jit(solution)/shard_map/ppermute | solution.py:562
  32.0 1.5 collective-permute-start.6
  34.4 5.2 %collective-permute-done.10.refs_14_ = bf16[800,128]{1,0:T(8,128)(2,1)S(1)} collective-permute-done((bf16[800,128]{1,0:T(8,128)(2,1)S(1)}, bf16[800,128]{1,0:T(8,128)(2,1)S(1)}, u32[]{:S(2)}, u32[]{:S(2)}) %collective-permute-start.10) | collective-permute-done | bytes 204832 | tf_op jit(solution)/shard_map/ppermute | solution.py:562
  40.2 1.1 collective-permute-done.13.refs_17_
  41.7 3.6 %collective-permute-done.14.refs_18_ = bf16[800,128]{1,0:T(8,128)(2,1)S(1)} collective-permute-done((bf16[800,128]{1,0:T(8,128)(2,1)S(1)}, bf16[800,128]{1,0:T(8,128)(2,1)S(1)}, u32[]{:S(2)}, u32[]{:S(2)}) %collective-permute-start.14) | collective-permute-done | bytes 204832 | tf_op jit(solution)/shard_map/ppermute | solution.py:562
  45.4 1.4 collective-permute-done.30.refs_34_
  47.7 62.5 %layer_core.1 = (f32[512,512]{1,0:T(8,128)}, f32[512,512]{1,0:T(8,128)}, bf16[16,800,128]{2,1,0:T(8,128)(2,1)}, bf16[4,800,128]{2,1,0:T(8,128)(2,1)}, bf16[4,800...) custom-call(bf16[512,512]{1,0:T(8,128)(2,1)} %bitcast.91, ...), custom_call_target="tpu_custom_call" | custom-call | tf_op jit(solution)/shard_map/layer_core/pallas_call | solution.py:545
  111.3 1.5 collective-permute-done.33
  112.8 1.0 fusion.22
  113.9 1.0 fusion.3
  114.9 2.1 %collective-permute-start.38 = (bf16[800,128]{1,0:T(8,128)(2,1)S(1)}, bf16[800,128]{1,0:T(8,128)(2,1)S(1)}, u32[]{:S(2)}, u32[]{:S(2)}) collective-permute-start(bf16[800,128]{1,0:T(8,128)(2,1)S(1)} %fusion.3), channel_id=1, source_target_pairs={{0,4},{1,5},{2,3},{3,2},{4,0},{5,1},{6,7},{7,6},{8,12},{9,13},{10,... | collective-permute-start | bytes 614408 | tf_op jit(solution)/shard_map/ppermute | solution.py:562
  117.0 1.0 fusion.4
  118.0 1.0 fusion.5
  119.1 2.1 %collective-permute-start.34 = (bf16[800,128]{1,0:T(8,128)(2,1)S(1)}, bf16[800,128]{1,0:T(8,128)(2,1)S(1)}, u32[]{:S(2)}, u32[]{:S(2)}) collective-permute-start(bf16[800,128]{1,0:T(8,128)(2,1)S(1)} %fusion.5), channel_id=1, source_target_pairs={{0,4},{1,5},{2,3},{3,2},{4,0},{5,1},{6,7},{7,6},{8,12},{9,13},{10,... | collective-permute-start | bytes 614408 | tf_op jit(solution)/shard_map/ppermute | solution.py:562
  121.4 3.5 %collective-permute-done.35 = bf16[800,128]{1,0:T(8,128)(2,1)S(1)} collective-permute-done((bf16[800,128]{1,0:T(8,128)(2,1)S(1)}, bf16[800,128]{1,0:T(8,128)(2,1)S(1)}, u32[]{:S(2)}, u32[]{:S(2)}) %collective-permute-start.35) | collective-permute-done | bytes 204832 | tf_op jit(solution)/shard_map/ppermute | solution.py:562
  125.0 1.3 collective-permute-start.37
  126.3 0.7 collective-permute-start.43
  127.1 1.6 collective-permute-done.39
  128.8 1.5 collective-permute-start.47
  130.3 2.8 %collective-permute-done.37 = bf16[800,128]{1,0:T(8,128)(2,1)S(1)} collective-permute-done((bf16[800,128]{1,0:T(8,128)(2,1)S(1)}, bf16[800,128]{1,0:T(8,128)(2,1)S(1)}, u32[]{:S(2)}, u32[]{:S(2)}) %collective-permute-start.37) | collective-permute-done | bytes 204832 | tf_op jit(solution)/shard_map/ppermute | solution.py:562
  133.1 0.8 fusion.18
  133.9 1.4 collective-permute-start.49
  135.3 0.9 collective-permute-start.42
  136.2 0.7 fusion.7
  136.9 1.2 collective-permute-start.41
  138.3 3.2 %collective-permute-done.42 = bf16[800,128]{1,0:T(8,128)(2,1)S(1)} collective-permute-done((bf16[800,128]{1,0:T(8,128)(2,1)S(1)}, bf16[800,128]{1,0:T(8,128)(2,1)S(1)}, u32[]{:S(2)}, u32[]{:S(2)}) %collective-permute-start.42) | collective-permute-done | bytes 204832 | tf_op jit(solution)/shard_map/ppermute | solution.py:562
  141.4 1.2 collective-permute-start.46
  142.7 0.8 fusion.12
  143.4 0.8 collective-permute-start.44
  144.3 3.0 %collective-permute-done.46 = bf16[800,128]{1,0:T(8,128)(2,1)S(1)} collective-permute-done((bf16[800,128]{1,0:T(8,128)(2,1)S(1)}, bf16[800,128]{1,0:T(8,128)(2,1)S(1)}, u32[]{:S(2)}, u32[]{:S(2)}) %collective-permute-start.46) | collective-permute-done | bytes 204832 | tf_op jit(solution)/shard_map/ppermute | solution.py:562
  147.2 0.8 fusion.10
  148.0 2.9 %collective-permute-start.48 = (bf16[800,128]{1,0:T(8,128)(2,1)}, bf16[800,128]{1,0:T(8,128)(2,1)}, u32[]{:S(2)}, u32[]{:S(2)}) collective-permute-start(bf16[800,128]{1,0:T(8,128)(2,1)} %fusion.10), channel_id=1, source_target_pairs={{0,8},{1,9},{2,18},{3,19},{4,12},{5,13},{6,22},{7,23},{8,0},{9,1},... | collective-permute-start | bytes 614408 | tf_op jit(solution)/shard_map/ppermute | solution.py:562
  150.9 5.3 %collective-permute-done.48 = bf16[800,128]{1,0:T(8,128)(2,1)} collective-permute-done((bf16[800,128]{1,0:T(8,128)(2,1)}, bf16[800,128]{1,0:T(8,128)(2,1)}, u32[]{:S(2)}, u32[]{:S(2)}) %collective-permute-start.48) | collective-permute-done | bytes 204832 | tf_op jit(solution)/shard_map/ppermute | solution.py:562
  156.3 1.4 fusion.21
  158.2 2.6 %multiply_add_fusion = (f32[98496]{0:T(1024)}, f32[98496]{0:T(1024)}, f32[98496]{0:T(1024)}, f32[98496]{0:T(1024)}) fusion(f32[98496]{0:T(1024)} %param.11, f32[98496]{0:T(1024)} %param.9, f32[98496]{0:T(1024)} %param.10, f32[102400]{0:T(1024)S(1)} %bitcast.90, s32[]{:T(128)S(6)} %select_n.15), kind=kLoop, calls=%fused_computation.39 | loop fusion | flops 886464 | bytes 3151876 | tf_op jit(solution)/shard_map/add | solution.py:650
  (144 shorter events, 8.5 us)
Async XLA Ops:
  1.9 6.7 %collective-permute-start.7 = (bf16[800,128]{1,0:T(8,128)(2,1)S(1)}, bf16[800,128]{1,0:T(8,128)(2,1)S(1)}, u32[]{:S(2)}, u32[]{:S(2)}) collective-permute-start(bf16[800,128]{1,0:T(8,128)(2,1)S(1)} %fusion.23.refs_3_), channel_id=1, source_target_pairs={{0,4},{1,5},{2,3},{3,2},{4,0},{5,1},{6,7},{7,6},{8,12},{9,13},{10,... | collective-permute-start | bytes 614408 | tf_op jit(solution)/shard_map/ppermute | solution.py:562
  4.9 7.0 %collective-permute-start = (bf16[800,128]{1,0:T(8,128)(2,1)S(1)}, bf16[800,128]{1,0:T(8,128)(2,1)S(1)}, u32[]{:S(2)}, u32[]{:S(2)}) collective-permute-start(bf16[800,128]{1,0:T(8,128)(2,1)S(1)} %fusion.23.refs_3_), channel_id=1, source_target_pairs={{0,8},{1,9},{2,18},{3,19},{4,12},{5,13},{6,22},{7,23},{8,0},{9,1},... | collective-permute-start | bytes 614408 | tf_op jit(solution)/shard_map/ppermute | solution.py:562
  6.4 5.8 %collective-permute-start.3 = (bf16[800,128]{1,0:T(8,128)(2,1)S(1)}, bf16[800,128]{1,0:T(8,128)(2,1)S(1)}, u32[]{:S(2)}, u32[]{:S(2)}) collective-permute-start(bf16[800,128]{1,0:T(8,128)(2,1)S(1)} %fusion.23.refs_3_), channel_id=1, source_target_pairs={{0,1},{1,0},{2,6},{3,7},{4,5},{5,4},{6,2},{7,3},{8,9},{9,8},{10,14... | collective-permute-start | bytes 614408 | tf_op jit(solution)/shard_map/ppermute | solution.py:562
  8.0 7.6 %collective-permute-start.15 = (bf16[800,128]{1,0:T(8,128)(2,1)S(1)}, bf16[800,128]{1,0:T(8,128)(2,1)S(1)}, u32[]{:S(2)}, u32[]{:S(2)}) collective-permute-start(bf16[800,128]{1,0:T(8,128)(2,1)S(1)} %fusion.23.refs_3_), channel_id=1, source_target_pairs={{0,2},{1,3},{2,0},{3,1},{4,6},{5,7},{6,4},{7,5},{8,10},{9,11},{10,... | collective-permute-start | bytes 614408 | tf_op jit(solution)/shard_map/ppermute | solution.py:562
  8.6 7.0 %collective-permute-start.23 = (bf16[800,128]{1,0:T(8,128)(2,1)S(1)}, bf16[800,128]{1,0:T(8,128)(2,1)S(1)}, u32[]{:S(2)}, u32[]{:S(2)}) collective-permute-start(bf16[800,128]{1,0:T(8,128)(2,1)S(1)} %collective-permute-done.7.refs_11_), channel_id=1, source_target_pairs={{0,2},{1,3},{2,0},{3,1},{4,6},{5,7},{6,4},{7,5},{8,10},{9,11},{10,... | collective-permute-start | bytes 614408 | tf_op jit(solution)/shard_map/ppermute | solution.py:562
  8.6 7.7 %collective-permute-start.11 = (bf16[800,128]{1,0:T(8,128)(2,1)S(1)}, bf16[800,128]{1,0:T(8,128)(2,1)S(1)}, u32[]{:S(2)}, u32[]{:S(2)}) collective-permute-start(bf16[800,128]{1,0:T(8,128)(2,1)S(1)} %collective-permute-done.7.refs_11_), channel_id=1, source_target_pairs={{0,1},{1,0},{2,6},{3,7},{4,5},{5,4},{6,2},{7,3},{8,9},{9,8},{10,14... | collective-permute-start | bytes 614408 | tf_op jit(solution)/shard_map/ppermute | solution.py:562
  12.2 5.3 %collective-permute-start.19 = (bf16[800,128]{1,0:T(8,128)(2,1)S(1)}, bf16[800,128]{1,0:T(8,128)(2,1)S(1)}, u32[]{:S(2)}, u32[]{:S(2)}) collective-permute-start(bf16[800,128]{1,0:T(8,128)(2,1)S(1)} %collective-permute-done.3.refs_7_), channel_id=1, source_target_pairs={{0,2},{1,3},{2,0},{3,1},{4,6},{5,7},{6,4},{7,5},{8,10},{9,11},{10,... | collective-permute-start | bytes 614408 | tf_op jit(solution)/shard_map/ppermute | solution.py:562
  12.2 8.4 %collective-permute-start.1 = (bf16[800,128]{1,0:T(8,128)(2,1)S(1)}, bf16[800,128]{1,0:T(8,128)(2,1)S(1)}, u32[]{:S(2)}, u32[]{:S(2)}) collective-permute-start(bf16[800,128]{1,0:T(8,128)(2,1)S(1)} %fusion.23.refs_3_), channel_id=1, source_target_pairs={{0,16},{1,17},{2,10},{3,11},{4,20},{5,21},{6,14},{7,15},{8,24},{9,... | collective-permute-start | bytes 614408 | tf_op jit(solution)/shard_map/ppermute | solution.py:562
  15.6 5.1 %collective-permute-start.16 = (bf16[800,128]{1,0:T(8,128)(2,1)S(1)}, bf16[800,128]{1,0:T(8,128)(2,1)S(1)}, u32[]{:S(2)}, u32[]{:S(2)}) collective-permute-start(bf16[800,128]{1,0:T(8,128)(2,1)S(1)} %collective-permute-done.refs_4_), channel_id=1, source_target_pairs={{0,2},{1,3},{2,0},{3,1},{4,6},{5,7},{6,4},{7,5},{8,10},{9,11},{10,... | collective-permute-start | bytes 614408 | tf_op jit(solution)/shard_map/ppermute | solution.py:562
  15.6 8.0 %collective-permute-start.8 = (bf16[800,128]{1,0:T(8,128)(2,1)S(1)}, bf16[800,128]{1,0:T(8,128)(2,1)S(1)}, u32[]{:S(2)}, u32[]{:S(2)}) collective-permute-start(bf16[800,128]{1,0:T(8,128)(2,1)S(1)} %collective-permute-done.refs_4_), channel_id=1, source_target_pairs={{0,4},{1,5},{2,3},{3,2},{4,0},{5,1},{6,7},{7,6},{8,12},{9,13},{10,... | collective-permute-start | bytes 614408 | tf_op jit(solution)/shard_map/ppermute | solution.py:562
  16.4 7.7 %collective-permute-start.4 = (bf16[800,128]{1,0:T(8,128)(2,1)S(1)}, bf16[800,128]{1,0:T(8,128)(2,1)S(1)}, u32[]{:S(2)}, u32[]{:S(2)}) collective-permute-start(bf16[800,128]{1,0:T(8,128)(2,1)S(1)} %collective-permute-done.refs_4_), channel_id=1, source_target_pairs={{0,1},{1,0},{2,6},{3,7},{4,5},{5,4},{6,2},{7,3},{8,9},{9,8},{10,14... | collective-permute-start | bytes 614408 | tf_op jit(solution)/shard_map/ppermute | solution.py:562
  17.6 8.0 %collective-permute-start.2 = (bf16[800,128]{1,0:T(8,128)(2,1)S(1)}, bf16[800,128]{1,0:T(8,128)(2,1)S(1)}, u32[]{:S(2)}, u32[]{:S(2)}) collective-permute-start(bf16[800,128]{1,0:T(8,128)(2,1)S(1)} %collective-permute-done.refs_4_), channel_id=1, source_target_pairs={{0,16},{1,17},{2,10},{3,11},{4,20},{5,21},{6,14},{7,15},{8,24},{9,... | collective-permute-start | bytes 614408 | tf_op jit(solution)/shard_map/ppermute | solution.py:562
  20.7 4.9 %collective-permute-start.27 = (bf16[800,128]{1,0:T(8,128)(2,1)S(1)}, bf16[800,128]{1,0:T(8,128)(2,1)S(1)}, u32[]{:S(2)}, u32[]{:S(2)}) collective-permute-start(bf16[800,128]{1,0:T(8,128)(2,1)S(1)} %collective-permute-done.11.refs_15_), channel_id=1, source_target_pairs={{0,2},{1,3},{2,0},{3,1},{4,6},{5,7},{6,4},{7,5},{8,10},{9,11},{10,... | collective-permute-start | bytes 614408 | tf_op jit(solution)/shard_map/ppermute | solution.py:562
  20.7 5.9 %collective-permute-start.17 = (bf16[800,128]{1,0:T(8,128)(2,1)S(1)}, bf16[800,128]{1,0:T(8,128)(2,1)S(1)}, u32[]{:S(2)}, u32[]{:S(2)}) collective-permute-start(bf16[800,128]{1,0:T(8,128)(2,1)S(1)} %collective-permute-done.1.refs_5_), channel_id=1, source_target_pairs={{0,2},{1,3},{2,0},{3,1},{4,6},{5,7},{6,4},{7,5},{8,10},{9,11},{10,... | collective-permute-start | bytes 614408 | tf_op jit(solution)/shard_map/ppermute | solution.py:562
  23.6 7.9 %collective-permute-start.9 = (bf16[800,128]{1,0:T(8,128)(2,1)S(1)}, bf16[800,128]{1,0:T(8,128)(2,1)S(1)}, u32[]{:S(2)}, u32[]{:S(2)}) collective-permute-start(bf16[800,128]{1,0:T(8,128)(2,1)S(1)} %collective-permute-done.1.refs_5_), channel_id=1, source_target_pairs={{0,4},{1,5},{2,3},{3,2},{4,0},{5,1},{6,7},{7,6},{8,12},{9,13},{10,... | collective-permute-start | bytes 614408 | tf_op jit(solution)/shard_map/ppermute | solution.py:562
  24.0 7.5 %collective-permute-start.5 = (bf16[800,128]{1,0:T(8,128)(2,1)S(1)}, bf16[800,128]{1,0:T(8,128)(2,1)S(1)}, u32[]{:S(2)}, u32[]{:S(2)}) collective-permute-start(bf16[800,128]{1,0:T(8,128)(2,1)S(1)} %collective-permute-done.1.refs_5_), channel_id=1, source_target_pairs={{0,1},{1,0},{2,6},{3,7},{4,5},{5,4},{6,2},{7,3},{8,9},{9,8},{10,14... | collective-permute-start | bytes 614408 | tf_op jit(solution)/shard_map/ppermute | solution.py:562
  25.6 6.4 %collective-permute-start.24 = (bf16[800,128]{1,0:T(8,128)(2,1)S(1)}, bf16[800,128]{1,0:T(8,128)(2,1)S(1)}, u32[]{:S(2)}, u32[]{:S(2)}) collective-permute-start(bf16[800,128]{1,0:T(8,128)(2,1)S(1)} %collective-permute-done.8.refs_12_), channel_id=1, source_target_pairs={{0,2},{1,3},{2,0},{3,1},{4,6},{5,7},{6,4},{7,5},{8,10},{9,11},{10,... | collective-permute-start | bytes 614408 | tf_op jit(solution)/shard_map/ppermute | solution.py:562
  25.6 7.9 %collective-permute-start.12 = (bf16[800,128]{1,0:T(8,128)(2,1)S(1)}, bf16[800,128]{1,0:T(8,128)(2,1)S(1)}, u32[]{:S(2)}, u32[]{:S(2)}) collective-permute-start(bf16[800,128]{1,0:T(8,128)(2,1)S(1)} %collective-permute-done.8.refs_12_), channel_id=1, source_target_pairs={{0,1},{1,0},{2,6},{3,7},{4,5},{5,4},{6,2},{7,3},{8,9},{9,8},{10,14... | collective-permute-start | bytes 614408 | tf_op jit(solution)/shard_map/ppermute | solution.py:562
  26.6 6.9 %collective-permute-start.20 = (bf16[800,128]{1,0:T(8,128)(2,1)S(1)}, bf16[800,128]{1,0:T(8,128)(2,1)S(1)}, u32[]{:S(2)}, u32[]{:S(2)}) collective-permute-start(bf16[800,128]{1,0:T(8,128)(2,1)S(1)} %collective-permute-done.4.refs_8_), channel_id=1, source_target_pairs={{0,2},{1,3},{2,0},{3,1},{4,6},{5,7},{6,4},{7,5},{8,10},{9,11},{10,... | collective-permute-start | bytes 614408 | tf_op jit(solution)/shard_map/ppermute | solution.py:562
  31.5 8.0 %collective-permute-start.10 = (bf16[800,128]{1,0:T(8,128)(2,1)S(1)}, bf16[800,128]{1,0:T(8,128)(2,1)S(1)}, u32[]{:S(2)}, u32[]{:S(2)}) collective-permute-start(bf16[800,128]{1,0:T(8,128)(2,1)S(1)} %collective-permute-done.2.refs_6_), channel_id=1, source_target_pairs={{0,4},{1,5},{2,3},{3,2},{4,0},{5,1},{6,7},{7,6},{8,12},{9,13},{10,... | collective-permute-start | bytes 614408 | tf_op jit(solution)/shard_map/ppermute | solution.py:562
  32.0 7.6 %collective-permute-start.6 = (bf16[800,128]{1,0:T(8,128)(2,1)S(1)}, bf16[800,128]{1,0:T(8,128)(2,1)S(1)}, u32[]{:S(2)}, u32[]{:S(2)}) collective-permute-start(bf16[800,128]{1,0:T(8,128)(2,1)S(1)} %collective-permute-done.2.refs_6_), channel_id=1, source_target_pairs={{0,1},{1,0},{2,6},{3,7},{4,5},{5,4},{6,2},{7,3},{8,9},{9,8},{10,14... | collective-permute-start | bytes 614408 | tf_op jit(solution)/shard_map/ppermute | solution.py:562
  33.5 6.2 %collective-permute-start.25 = (bf16[800,128]{1,0:T(8,128)(2,1)S(1)}, bf16[800,128]{1,0:T(8,128)(2,1)S(1)}, u32[]{:S(2)}, u32[]{:S(2)}) collective-permute-start(bf16[800,128]{1,0:T(8,128)(2,1)S(1)} %collective-permute-done.9.refs_13_), channel_id=1, source_target_pairs={{0,2},{1,3},{2,0},{3,1},{4,6},{5,7},{6,4},{7,5},{8,10},{9,11},{10,... | collective-permute-start | bytes 614408 | tf_op jit(solution)/shard_map/ppermute | solution.py:562
  33.5 7.7 %collective-permute-start.13 = (bf16[800,128]{1,0:T(8,128)(2,1)S(1)}, bf16[800,128]{1,0:T(8,128)(2,1)S(1)}, u32[]{:S(2)}, u32[]{:S(2)}) collective-permute-start(bf16[800,128]{1,0:T(8,128)(2,1)S(1)} %collective-permute-done.9.refs_13_), channel_id=1, source_target_pairs={{0,1},{1,0},{2,6},{3,7},{4,5},{5,4},{6,2},{7,3},{8,9},{9,8},{10,14... | collective-permute-start | bytes 614408 | tf_op jit(solution)/shard_map/ppermute | solution.py:562
  34.1 7.2 %collective-permute-start.21 = (bf16[800,128]{1,0:T(8,128)(2,1)S(1)}, bf16[800,128]{1,0:T(8,128)(2,1)S(1)}, u32[]{:S(2)}, u32[]{:S(2)}) collective-permute-start(bf16[800,128]{1,0:T(8,128)(2,1)S(1)} %collective-permute-done.5.refs_9_), channel_id=1, source_target_pairs={{0,2},{1,3},{2,0},{3,1},{4,6},{5,7},{6,4},{7,5},{8,10},{9,11},{10,... | collective-permute-start | bytes 614408 | tf_op jit(solution)/shard_map/ppermute | solution.py:562
  39.6 5.8 %collective-permute-start.14 = (bf16[800,128]{1,0:T(8,128)(2,1)S(1)}, bf16[800,128]{1,0:T(8,128)(2,1)S(1)}, u32[]{:S(2)}, u32[]{:S(2)}) collective-permute-start(bf16[800,128]{1,0:T(8,128)(2,1)S(1)} %collective-permute-done.10.refs_14_), channel_id=1, source_target_pairs={{0,1},{1,0},{2,6},{3,7},{4,5},{5,4},{6,2},{7,3},{8,9},{9,8},{10,14... | collective-permute-start | bytes 614408 | tf_op jit(solution)/shard_map/ppermute | solution.py:562
  39.6 5.8 %collective-permute-start.26 = (bf16[800,128]{1,0:T(8,128)(2,1)S(1)}, bf16[800,128]{1,0:T(8,128)(2,1)S(1)}, u32[]{:S(2)}, u32[]{:S(2)}) collective-permute-start(bf16[800,128]{1,0:T(8,128)(2,1)S(1)} %collective-permute-done.10.refs_14_), channel_id=1, source_target_pairs={{0,2},{1,3},{2,0},{3,1},{4,6},{5,7},{6,4},{7,5},{8,10},{9,11},{10,... | collective-permute-start | bytes 614408 | tf_op jit(solution)/shard_map/ppermute | solution.py:562
  39.7 5.6 %collective-permute-start.28 = (bf16[800,128]{1,0:T(8,128)(2,1)S(1)}, bf16[800,128]{1,0:T(8,128)(2,1)S(1)}, u32[]{:S(2)}, u32[]{:S(2)}) collective-permute-start(bf16[800,128]{1,0:T(8,128)(2,1)S(1)} %collective-permute-done.12.refs_16_), channel_id=1, source_target_pairs={{0,2},{1,3},{2,0},{3,1},{4,6},{5,7},{6,4},{7,5},{8,10},{9,11},{10,... | collective-permute-start | bytes 614408 | tf_op jit(solution)/shard_map/ppermute | solution.py:562
  41.2 4.1 %collective-permute-start.22 = (bf16[800,128]{1,0:T(8,128)(2,1)S(1)}, bf16[800,128]{1,0:T(8,128)(2,1)S(1)}, u32[]{:S(2)}, u32[]{:S(2)}) collective-permute-start(bf16[800,128]{1,0:T(8,128)(2,1)S(1)} %collective-permute-done.6.refs_10_), channel_id=1, source_target_pairs={{0,2},{1,3},{2,0},{3,1},{4,6},{5,7},{6,4},{7,5},{8,10},{9,11},{10,... | collective-permute-start | bytes 614408 | tf_op jit(solution)/shard_map/ppermute | solution.py:562
  41.3 4.0 %collective-permute-start.29 = (bf16[800,128]{1,0:T(8,128)(2,1)S(1)}, bf16[800,128]{1,0:T(8,128)(2,1)S(1)}, u32[]{:S(2)}, u32[]{:S(2)}) collective-permute-start(bf16[800,128]{1,0:T(8,128)(2,1)S(1)} %collective-permute-done.13.refs_17_), channel_id=1, source_target_pairs={{0,2},{1,3},{2,0},{3,1},{4,6},{5,7},{6,4},{7,5},{8,10},{9,11},{10,... | collective-permute-start | bytes 614408 | tf_op jit(solution)/shard_map/ppermute | solution.py:562
  110.2 2.6 %collective-permute-start.33 = (bf16[4,800,128]{2,1,0:T(8,128)(2,1)}, bf16[4,800,128]{2,1,0:T(8,128)(2,1)S(1)}, u32[]{:S(2)}, u32[]{:S(2)}) collective-permute-start(bf16[4,800,128]{2,1,0:T(8,128)(2,1)} %get-tuple-element.35), channel_id=1, source_target_pairs={{0,2},{1,3},{2,0},{3,1},{4,6},{5,7},{6,4},{7,5},{8,10},{9,11},{10,... | collective-permute-start | bytes 2457608 | tf_op jit(solution)/shard_map/ppermute | solution.py:562
  110.4 6.6 %collective-permute-start.32 = (bf16[4,800,128]{2,1,0:T(8,128)(2,1)}, bf16[4,800,128]{2,1,0:T(8,128)(2,1)S(1)}, u32[]{:S(2)}, u32[]{:S(2)}) collective-permute-start(bf16[4,800,128]{2,1,0:T(8,128)(2,1)} %get-tuple-element.34), channel_id=1, source_target_pairs={{0,2},{1,3},{2,0},{3,1},{4,6},{5,7},{6,4},{7,5},{8,10},{9,11},{10,... | collective-permute-start | bytes 2457608 | tf_op jit(solution)/shard_map/ppermute | solution.py:562
  110.7 8.3 %collective-permute-start.31 = (bf16[4,800,128]{2,1,0:T(8,128)(2,1)}, bf16[4,800,128]{2,1,0:T(8,128)(2,1)S(1)}, u32[]{:S(2)}, u32[]{:S(2)}) collective-permute-start(bf16[4,800,128]{2,1,0:T(8,128)(2,1)} %get-tuple-element.33), channel_id=1, source_target_pairs={{0,2},{1,3},{2,0},{3,1},{4,6},{5,7},{6,4},{7,5},{8,10},{9,11},{10,... | collective-permute-start | bytes 2457608 | tf_op jit(solution)/shard_map/ppermute | solution.py:562
  110.9 10.3 %collective-permute-start.40 = (bf16[4,800,128]{2,1,0:T(8,128)(2,1)}, bf16[4,800,128]{2,1,0:T(8,128)(2,1)S(1)}, u32[]{:S(2)}, u32[]{:S(2)}) collective-permute-start(bf16[4,800,128]{2,1,0:T(8,128)(2,1)} %get-tuple-element.41), channel_id=1, source_target_pairs={{0,2},{1,3},{2,0},{3,1},{4,6},{5,7},{6,4},{7,5},{8,10},{9,11},{10,... | collective-permute-start | bytes 2457608 | tf_op jit(solution)/shard_map/ppermute | solution.py:562
  113.8 7.4 %collective-permute-start.36 = (bf16[800,128]{1,0:T(8,128)(2,1)S(1)}, bf16[800,128]{1,0:T(8,128)(2,1)S(1)}, u32[]{:S(2)}, u32[]{:S(2)}) collective-permute-start(bf16[800,128]{1,0:T(8,128)(2,1)S(1)} %fusion.22), channel_id=1, source_target_pairs={{0,4},{1,5},{2,3},{3,2},{4,0},{5,1},{6,7},{7,6},{8,12},{9,13},{10,... | collective-permute-start | bytes 614408 | tf_op jit(solution)/shard_map/ppermute | solution.py:562
  114.9 13.8 %collective-permute-start.38 = (bf16[800,128]{1,0:T(8,128)(2,1)S(1)}, bf16[800,128]{1,0:T(8,128)(2,1)S(1)}, u32[]{:S(2)}, u32[]{:S(2)}) collective-permute-start(bf16[800,128]{1,0:T(8,128)(2,1)S(1)} %fusion.3), channel_id=1, source_target_pairs={{0,4},{1,5},{2,3},{3,2},{4,0},{5,1},{6,7},{7,6},{8,12},{9,13},{10,... | collective-permute-start | bytes 614408 | tf_op jit(solution)/shard_map/ppermute | solution.py:562
  118.0 6.9 %collective-permute-start.35 = (bf16[800,128]{1,0:T(8,128)(2,1)S(1)}, bf16[800,128]{1,0:T(8,128)(2,1)S(1)}, u32[]{:S(2)}, u32[]{:S(2)}) collective-permute-start(bf16[800,128]{1,0:T(8,128)(2,1)S(1)} %fusion.4), channel_id=1, source_target_pairs={{0,4},{1,5},{2,3},{3,2},{4,0},{5,1},{6,7},{7,6},{8,12},{9,13},{10,... | collective-permute-start | bytes 614408 | tf_op jit(solution)/shard_map/ppermute | solution.py:562
  119.1 14.0 %collective-permute-start.34 = (bf16[800,128]{1,0:T(8,128)(2,1)S(1)}, bf16[800,128]{1,0:T(8,128)(2,1)S(1)}, u32[]{:S(2)}, u32[]{:S(2)}) collective-permute-start(bf16[800,128]{1,0:T(8,128)(2,1)S(1)} %fusion.5), channel_id=1, source_target_pairs={{0,4},{1,5},{2,3},{3,2},{4,0},{5,1},{6,7},{7,6},{8,12},{9,13},{10,... | collective-permute-start | bytes 614408 | tf_op jit(solution)/shard_map/ppermute | solution.py:562
  121.3 7.4 %collective-permute-start.39 = (bf16[800,128]{1,0:T(8,128)(2,1)S(1)}, bf16[800,128]{1,0:T(8,128)(2,1)S(1)}, u32[]{:S(2)}, u32[]{:S(2)}) collective-permute-start(bf16[800,128]{1,0:T(8,128)(2,1)S(1)} %fusion.15), channel_id=1, source_target_pairs={{0,1},{1,0},{2,6},{3,7},{4,5},{5,4},{6,2},{7,3},{8,9},{9,8},{10,14... | collective-permute-start | bytes 614408 | tf_op jit(solution)/shard_map/ppermute | solution.py:562
  125.0 8.1 %collective-permute-start.37 = (bf16[800,128]{1,0:T(8,128)(2,1)S(1)}, bf16[800,128]{1,0:T(8,128)(2,1)S(1)}, u32[]{:S(2)}, u32[]{:S(2)}) collective-permute-start(bf16[800,128]{1,0:T(8,128)(2,1)S(1)} %fusion.16), channel_id=1, source_target_pairs={{0,1},{1,0},{2,6},{3,7},{4,5},{5,4},{6,2},{7,3},{8,9},{9,8},{10,14... | collective-permute-start | bytes 614408 | tf_op jit(solution)/shard_map/ppermute | solution.py:562
  126.3 10.6 %collective-permute-start.43 = (bf16[800,128]{1,0:T(8,128)(2,1)S(1)}, bf16[800,128]{1,0:T(8,128)(2,1)S(1)}, u32[]{:S(2)}, u32[]{:S(2)}) collective-permute-start(bf16[800,128]{1,0:T(8,128)(2,1)S(1)} %fusion.1), channel_id=1, source_target_pairs={{0,4},{1,5},{2,3},{3,2},{4,0},{5,1},{6,7},{7,6},{8,12},{9,13},{10,... | collective-permute-start | bytes 614408 | tf_op jit(solution)/shard_map/ppermute | solution.py:562
  128.7 15.6 %collective-permute-start.45 = (bf16[800,128]{1,0:T(8,128)(2,1)S(1)}, bf16[800,128]{1,0:T(8,128)(2,1)S(1)}, u32[]{:S(2)}, u32[]{:S(2)}) collective-permute-start(bf16[800,128]{1,0:T(8,128)(2,1)S(1)} %fusion.2), channel_id=1, source_target_pairs={{0,4},{1,5},{2,3},{3,2},{4,0},{5,1},{6,7},{7,6},{8,12},{9,13},{10,... | collective-permute-start | bytes 614408 | tf_op jit(solution)/shard_map/ppermute | solution.py:562
  128.8 14.6 %collective-permute-start.47 = (bf16[800,128]{1,0:T(8,128)(2,1)S(1)}, bf16[800,128]{1,0:T(8,128)(2,1)S(1)}, u32[]{:S(2)}, u32[]{:S(2)}) collective-permute-start(bf16[800,128]{1,0:T(8,128)(2,1)S(1)} %fusion.14), channel_id=1, source_target_pairs={{0,16},{1,17},{2,10},{3,11},{4,20},{5,21},{6,14},{7,15},{8,24},{9,... | collective-permute-start | bytes 614408 | tf_op jit(solution)/shard_map/ppermute | solution.py:562
  133.9 17.1 %collective-permute-start.49 = (bf16[800,128]{1,0:T(8,128)(2,1)}, bf16[800,128]{1,0:T(8,128)(2,1)S(1)}, u32[]{:S(2)}, u32[]{:S(2)}) collective-permute-start(bf16[800,128]{1,0:T(8,128)(2,1)} %fusion.18), channel_id=1, source_target_pairs={{0,16},{1,17},{2,10},{3,11},{4,20},{5,21},{6,14},{7,15},{8,24},{9,... | collective-permute-start | bytes 614408 | tf_op jit(solution)/shard_map/ppermute | solution.py:562
  135.3 6.1 %collective-permute-start.42 = (bf16[800,128]{1,0:T(8,128)(2,1)S(1)}, bf16[800,128]{1,0:T(8,128)(2,1)S(1)}, u32[]{:S(2)}, u32[]{:S(2)}) collective-permute-start(bf16[800,128]{1,0:T(8,128)(2,1)S(1)} %fusion.6), channel_id=1, source_target_pairs={{0,4},{1,5},{2,3},{3,2},{4,0},{5,1},{6,7},{7,6},{8,12},{9,13},{10,... | collective-permute-start | bytes 614408 | tf_op jit(solution)/shard_map/ppermute | solution.py:562
  136.9 14.0 %collective-permute-start.41 = (bf16[800,128]{1,0:T(8,128)(2,1)}, bf16[800,128]{1,0:T(8,128)(2,1)}, u32[]{:S(2)}, u32[]{:S(2)}) collective-permute-start(bf16[800,128]{1,0:T(8,128)(2,1)} %fusion.7), channel_id=1, source_target_pairs={{0,4},{1,5},{2,3},{3,2},{4,0},{5,1},{6,7},{7,6},{8,12},{9,13},{10,... | collective-permute-start | bytes 614408 | tf_op jit(solution)/shard_map/ppermute | solution.py:562
  141.4 5.8 %collective-permute-start.46 = (bf16[800,128]{1,0:T(8,128)(2,1)S(1)}, bf16[800,128]{1,0:T(8,128)(2,1)S(1)}, u32[]{:S(2)}, u32[]{:S(2)}) collective-permute-start(bf16[800,128]{1,0:T(8,128)(2,1)S(1)} %fusion.11), channel_id=1, source_target_pairs={{0,1},{1,0},{2,6},{3,7},{4,5},{5,4},{6,2},{7,3},{8,9},{9,8},{10,14... | collective-permute-start | bytes 614408 | tf_op jit(solution)/shard_map/ppermute | solution.py:562
  143.4 7.5 %collective-permute-start.44 = (bf16[800,128]{1,0:T(8,128)(2,1)}, bf16[800,128]{1,0:T(8,128)(2,1)}, u32[]{:S(2)}, u32[]{:S(2)}) collective-permute-start(bf16[800,128]{1,0:T(8,128)(2,1)} %fusion.12), channel_id=1, source_target_pairs={{0,1},{1,0},{2,6},{3,7},{4,5},{5,4},{6,2},{7,3},{8,9},{9,8},{10,14... | collective-permute-start | bytes 614408 | tf_op jit(solution)/shard_map/ppermute | solution.py:562
  148.0 8.3 %collective-permute-start.48 = (bf16[800,128]{1,0:T(8,128)(2,1)}, bf16[800,128]{1,0:T(8,128)(2,1)}, u32[]{:S(2)}, u32[]{:S(2)}) collective-permute-start(bf16[800,128]{1,0:T(8,128)(2,1)} %fusion.10), channel_id=1, source_target_pairs={{0,8},{1,9},{2,18},{3,19},{4,12},{5,13},{6,22},{7,23},{8,0},{9,1},... | collective-permute-start | bytes 614408 | tf_op jit(solution)/shard_map/ppermute | solution.py:562
  (36 other events, 617.2 us)

commit v5 on v4

--- a/solution.py
+++ b/solution.py
@@ -11,7 +11,7 @@
 FF = 2048
 HEADS = 8
 REC = 2
-TILE = 16
+TILE = 8
 LANES = 128
 
 norm_eps = 1e-05
@@ -172,7 +172,7 @@
     return [(0, start, body), (body, edge, 2 * TILE)]
 
 
-def load_windows(w_refs, wide, flat, sem, shards):
+def load_windows(w_refs, wide, flat, sem, shards, prepare):
     tiles = flat.shape[0] // TILE
     height = w_refs[0].shape[0]
     edge_row = flat.shape[0] + TILE
@@ -184,6 +184,7 @@
         owner = slot_owner(origin, side, n % SLOTS)
         for at, to, rows in window_moves(owner, height, tiles, shards, edge_row):
             pltpu.make_async_copy(ref.at[pl.ds(at, rows)], wide.at[pl.ds(to, rows)], sem.at[0]).start()
+    prepare()
     settle(wide, height * shards, sem.at[0])
     starts = window_starts(shards, tiles)
 
@@ -223,7 +224,8 @@
     for n, ref in enumerate(g_refs):
         side, origin = (core, me) if n == 0 else (1 - core, jnp.bitwise_xor(me, RC))
         for k in range(ref.shape[0]):
-            slot = k if n == 0 else 4 * k + PLANES[n - 1]
+            plane = k // 4 if n == 0 else PLANES[n - 1]
+            slot = 4 * (k % 4) + plane
             owner = slot_owner(origin, side, slot)
             for at, to, rows in window_moves(owner, height, tiles, shards, edge_row):
                 pltpu.make_async_copy(wide.at[pl.ds(to, rows)], ref.at[k].at[pl.ds(at, rows)], sem.at[n]).start()
@@ -252,21 +254,25 @@
     pairs = D // LANES
     flat = wide.at[pl.ds(0, flat_rows)]
 
+    count_ref[0] = 1
+    single = count_ref[0]
+    scale = 0.125
+
+    def prepare():
+        seg = seg_ref[...].astype(F32)
+        column = jnp.transpose(jnp.broadcast_to(seg, (LANES, T)))[:, 0:1]
+        bias[...] = jnp.where(column == seg, 0.0, -1e30).astype(F32)
+        dx_ref[...] = x_ref[...].astype(F32)
+        gvec[...] = jnp.zeros_like(gvec)
+
     if windows:
-        load_windows(w_refs, wide, flat, sem, shards)
+        load_windows(w_refs, wide, flat, sem, shards, prepare)
     else:
         cp = pltpu.make_async_copy(w_refs[0], flat, sem.at[0])
         cp.start()
+        prepare()
         cp.wait()
     unpack_weights(flat, wa, wi, wo, b1, vec, D)
-
-    scale = 0.125
-    seg = seg_ref[...].astype(F32)
-    column = jnp.transpose(jnp.broadcast_to(seg, (LANES, T)))[:, 0:1]
-    bias[...] = jnp.where(column == seg, 0.0, -1e30).astype(F32)
-
-    count_ref[0] = 1
-    single = count_ref[0]
 
     def phase(body):
         def step(_, carry):
@@ -339,19 +345,19 @@
         def up(c):
             return dot(h16, wi[:, c * CHUNK : (c + 1) * CHUNK])
 
-        pend = [up(0)]
+        pend = [up(c) for c in range(AHEAD)]
         f = None
         for c in range(FF // CHUNK):
             cols = slice(c * CHUNK, (c + 1) * CHUNK)
-            if c + 1 < FF // CHUNK:
-                pend.append(up(c + 1))
+            if c + AHEAD < FF // CHUNK:
+                pend.append(up(c + AHEAD))
             u = pend.pop(0)
             parts = []
             for i in range(0, T, GSTEP):
                 g, sl = gelu_pair(u[i : i + GSTEP] + b1[:, cols])
                 parts.append(g.astype(BF))
                 put(0, c, pl.multiple_of(r * T, T) + i, parts[-1])
-                slope[r, pl.ds(i, GSTEP), cols] = sl
+                slope[r, pl.ds(i, GSTEP), cols] = sl.astype(BF)
             part = dot(jnp.concatenate(parts, axis=0), wo[cols, :])
             f = part if f is None else f + part
         for i in range(0, T, STEP):
@@ -389,21 +395,18 @@
         def down(c):
             return dot_t(d16, wo[c * CHUNK : (c + 1) * CHUNK, :])
 
-        pend = [down(0)]
+        pend = [down(c) for c in range(AHEAD)]
         dh = None
         for c in range(FF // CHUNK):
             cols = slice(c * CHUNK, (c + 1) * CHUNK)
-            if c + 1 < FF // CHUNK:
-                pend.append(down(c + 1))
+            if c + AHEAD < FF // CHUNK:
+                pend.append(down(c + AHEAD))
             t = pend.pop(0)
-            tot = jnp.zeros((8, CHUNK), F32)
             parts = []
             for i in range(0, T, GSTEP):
-                g16 = (t[i : i + GSTEP].astype(BF).astype(F32) * slope[r, pl.ds(i, GSTEP), cols]).astype(BF)
+                g16 = t[i : i + GSTEP].astype(BF) * slope[r, pl.ds(i, GSTEP), cols]
                 parts.append(g16)
                 put(1, c, pl.multiple_of(r * T, T) + i, g16)
-                tot = tot + jnp.sum(g16.astype(F32).reshape(GSTEP // 8, 8, CHUNK), axis=0)
-            gb1[0:1, cols] = gb1[0:1, cols] + colsum(tot)
             part = dot_t(jnp.concatenate(parts, axis=0), wi[:, cols])
             dh = part if dh is None else dh + part
         for i in range(0, T, STEP):
@@ -465,10 +468,6 @@
         d3 = jnp.concatenate([dqkv[c, rows, :] for c in range(3 * pairs)], axis=1)
         dx_ref[...] = dr1[...] + dot_t(d3, wa[:, : 3 * D])
 
-    gb1[...] = jnp.zeros_like(gb1)
-    gvec[...] = jnp.zeros_like(gvec)
-    dx_ref[...] = x_ref[...].astype(F32)
-
     def forward(r, carry):
         for part in (project, attend, feed):
             phase(functools.partial(part, r))
@@ -493,10 +492,12 @@
             wa[c * LANES : (c + 1) * LANES, 3 * D : 4 * D] = t_dot(ctx[c], da[...]).astype(BF)
 
     def grad_in():
-        ht = jnp.transpose(h1b[...])
+        ht = jnp.concatenate([jnp.transpose(h1b[...]), jnp.ones((16, REC * T), BF)], axis=0)
         for c in range(FF // CHUNK):
             cols = slice(c * CHUNK, (c + 1) * CHUNK)
-            wi[:, cols] = dot(ht, get(1, c, 0, REC * T)).astype(BF)
+            grad = dot(ht, get(1, c, 0, REC * T))
+            wi[:, cols] = grad[:D].astype(BF)
+            gb1[0:1, cols] = grad[D : D + 1]
 
     def grad_out():
         for c in range(FF // CHUNK):
@@ -530,7 +531,7 @@
         vm((D, 4 * D), BF), vm((D, FF), BF), vm((FF, D), BF), vm((1, FF), F32), vm((8, D), F32),
         vm((REC * T, D), BF), vm((REC, 3 * pairs, T, LANES), BF), vm((REC * HEADS, T, T), BF), vm((pairs, REC * T, LANES), BF),
         vm((REC, T, D), F32), vm((REC, T, LANES), F32), vm((REC, T, D), F32), vm((REC, T, LANES), F32),
-        vm((REC * T, D), BF), vm((REC, T, FF), F32),
+        vm((REC * T, D), BF), vm((REC, T, FF), BF),
         vm((REC * T, D), BF), vm((REC * T, D), BF), vm((3 * pairs, REC * T, LANES), BF), vm((pairs, T, LANES), BF),
         vm((T, D), F32), vm((T, T), F32),
         vm((1, FF), F32), vm((8, D), F32),
@@ -548,7 +549,7 @@
         in_specs=[in_vmem] * 3 + [anywhere] * len(flats),
         out_specs=tuple([in_vmem] * 2 + [anywhere] * len(g_shapes)),
         scratch_shapes=scratch,
-        compiler_params=pltpu.CompilerParams(vmem_limit_bytes=59 * 1024 * 1024),
+        compiler_params=pltpu.CompilerParams(vmem_limit_bytes=54 * 1024 * 1024),
         name="layer_core",
     )(x, cot, seg, *flats)
 
@@ -585,7 +586,7 @@
 
 def sum_windows(keep, *sent):
     got = {m: exchange(v, 4) for m, v in zip(PLANES, sent)}
-    far, side, back, last = {}, {}, {}, [None]
+    side, back, last = {}, {}, [None]
 
     def add(*parts):
         if last[0] is not None:
@@ -593,25 +594,24 @@
         last[0] = total(*parts)
         return last[0]
 
-    def near_far(m):
-        far[m] = exchange(add(keep[12 + m], got[m][3]), 0)
-        side[m] = exchange(add(keep[8 + m], got[m][2]), 0)
+    def pair(m):
+        side[m] = exchange(add(keep[4 * m + 2 : 4 * m + 4], got[m][2:]), 0)
 
     def second(m):
-        back[m] = exchange(add(keep[4 + m], got[m][1], far[m]), 1)
+        back[m] = exchange(add(keep[4 * m + 1], got[m][1], side[m][1]), 1)
 
     def plane(m):
-        return (keep[m], got[m][0], side[m], back[m])
-
-    near_far(3)
-    near_far(2)
+        return (keep[4 * m], got[m][0], side[m][0], back[m])
+
+    pair(3)
+    pair(2)
+    pair(1)
     second(3)
     second(2)
-    near_far(1)
+    pair(0)
     turn = exchange(add(*plane(3)), 2)
+    second(1)
     two = exchange(add(*plane(2)), 2)
-    near_far(0)
-    second(1)
     second(0)
     one = exchange(add(*plane(1), turn), 3)
     return (*plane(0), one, two)

time: 161 us -> 159 us (0.988)
  waiting for transfers between devices: 39.8 us -> 49.9 us
  starting transfers between devices: 43.1 us -> 34 us
  other arithmetic: 11.6 us -> 9.14 us
    ppermute x50 -> x46, waiting for transfers between devices: 39.8 us -> 49.9 us  [exchange(): lax.ppermute(v, AXES, [(j, j ^ (one if j // RC & 1 else zero)) for j in r...]
    ppermute x50 -> x46, starting transfers between devices: 43.1 us -> 34 us  [exchange(): lax.ppermute(v, AXES, [(j, j ^ (one if j // RC & 1 else zero)) for j in r...]
    convert_element_type x15 -> x11, other arithmetic: 7.6 us -> 5.17 us  [total(): return v.astype(BF)]
  transfers between devices with their start and end apart: 50 -> 46, of which waited for: 18 -> 18; matrix products, arithmetic and copies ran while one was open for 5% -> 3% of each run, Pallas kernels for 0% -> 0%
where the time goes in v5:
time: 159 us; the launch traced here: 158 us
  Pallas kernels  61.6 us (39%)
  waiting for transfers between devices  49.9 us (31%)
  starting transfers between devices  34 us (21%)
  other arithmetic  9.14 us (6%)
  local copies, waits for them, and re-layouts  2.37 us (1%)
    pallas_call x1, Pallas kernels, core(): pl.pallas_call(functools.partial(core_kernel, width=D, length=T, shards=s...  61.6 us
    ppermute x46, waiting for transfers between devices, exchange(): lax.ppermute(v, AXES, [(j, j ^ (one if j // RC & 1 else zero)) for j in r...  49.9 us
    ppermute x46, starting transfers between devices, exchange(): lax.ppermute(v, AXES, [(j, j ^ (one if j // RC & 1 else zero)) for j in r...  34 us
    convert_element_type x11, other arithmetic, total(): return v.astype(BF)  5.17 us
  transfers between devices with their start and end apart: 46, of which 18 were waited for; matrix products, arithmetic and copies ran while one was open for 3% of the time, Pallas kernels for 0%

profile of v5, /device:TPU:0, one launch (start us, length us, event | category | flops | bytes accessed | tf_op | source)
XLA Modules:
  0.0 158.3 jit_solution(8146235513392229579)
XLA Ops:
  0.7 1.2 fusion.11.refs_3_
  1.9 3.0 %collective-permute-start.7 = (bf16[784,128]{1,0:T(8,128)(2,1)S(1)}, bf16[784,128]{1,0:T(8,128)(2,1)S(1)}, u32[]{:S(2)}, u32[]{:S(2)}) collective-permute-start(bf16[784,128]{1,0:T(8,128)(2,1)S(1)} %fusion.11.refs_3_), channel_id=1, source_target_pairs={{0,4},{1,5},{2,3},{3,2},{4,0},{5,1},{6,7},{7,6},{8,12},{9,13},{10,... | collective-permute-start | bytes 602120 | tf_op jit(solution)/shard_map/ppermute | solution.py:563
  4.9 1.6 collective-permute-start
  6.4 1.5 collective-permute-start.3
  8.0 0.6 collective-permute-done.7.refs_11_
  8.6 2.7 %collective-permute-start.11 = (bf16[784,128]{1,0:T(8,128)(2,1)S(1)}, bf16[784,128]{1,0:T(8,128)(2,1)S(1)}, u32[]{:S(2)}, u32[]{:S(2)}) collective-permute-start(bf16[784,128]{1,0:T(8,128)(2,1)S(1)} %collective-permute-done.7.refs_11_), channel_id=1, source_target_pairs={{0,1},{1,0},{2,6},{3,7},{4,5},{5,4},{6,2},{7,3},{8,9},{9,8},{10,14... | collective-permute-start | bytes 602120 | tf_op jit(solution)/shard_map/ppermute | solution.py:563
  11.3 0.5 collective-permute-done.refs_4_
  12.2 3.3 %collective-permute-start.1 = (bf16[784,128]{1,0:T(8,128)(2,1)S(1)}, bf16[784,128]{1,0:T(8,128)(2,1)S(1)}, u32[]{:S(2)}, u32[]{:S(2)}) collective-permute-start(bf16[784,128]{1,0:T(8,128)(2,1)S(1)} %fusion.11.refs_3_), channel_id=1, source_target_pairs={{0,16},{1,17},{2,10},{3,11},{4,20},{5,21},{6,14},{7,15},{8,24},{9,... | collective-permute-start | bytes 602120 | tf_op jit(solution)/shard_map/ppermute | solution.py:563
  15.5 0.7 collective-permute-start.8
  16.3 1.2 collective-permute-start.4
  17.5 2.7 %collective-permute-start.2 = (bf16[784,128]{1,0:T(8,128)(2,1)S(1)}, bf16[784,128]{1,0:T(8,128)(2,1)S(1)}, u32[]{:S(2)}, u32[]{:S(2)}) collective-permute-start(bf16[784,128]{1,0:T(8,128)(2,1)S(1)} %collective-permute-done.refs_4_), channel_id=1, source_target_pairs={{0,16},{1,17},{2,10},{3,11},{4,20},{5,21},{6,14},{7,15},{8,24},{9,... | collective-permute-start | bytes 602120 | tf_op jit(solution)/shard_map/ppermute | solution.py:563
  20.5 0.5 collective-permute-start.17
  21.0 2.4 %collective-permute-done.8.refs_12_ = bf16[784,128]{1,0:T(8,128)(2,1)S(1)} collective-permute-done((bf16[784,128]{1,0:T(8,128)(2,1)S(1)}, bf16[784,128]{1,0:T(8,128)(2,1)S(1)}, u32[]{:S(2)}, u32[]{:S(2)}) %collective-permute-start.8) | collective-permute-done | bytes 200736 | tf_op jit(solution)/shard_map/ppermute | solution.py:563
  23.4 0.4 collective-permute-start.9
  23.8 1.5 collective-permute-start.5
  25.4 1.0 collective-permute-start.12
  26.4 1.5 collective-permute-start.20
  27.9 3.4 %collective-permute-done.9.refs_13_ = bf16[784,128]{1,0:T(8,128)(2,1)S(1)} collective-permute-done((bf16[784,128]{1,0:T(8,128)(2,1)S(1)}, bf16[784,128]{1,0:T(8,128)(2,1)S(1)}, u32[]{:S(2)}, u32[]{:S(2)}) %collective-permute-start.9) | collective-permute-done | bytes 200736 | tf_op jit(solution)/shard_map/ppermute | solution.py:563
  31.6 1.6 %collective-permute-start.6 = (bf16[784,128]{1,0:T(8,128)(2,1)S(1)}, bf16[784,128]{1,0:T(8,128)(2,1)S(1)}, u32[]{:S(2)}, u32[]{:S(2)}) collective-permute-start(bf16[784,128]{1,0:T(8,128)(2,1)S(1)} %collective-permute-done.2.refs_6_), channel_id=1, source_target_pairs={{0,1},{1,0},{2,6},{3,7},{4,5},{5,4},{6,2},{7,3},{8,9},{9,8},{10,14... | collective-permute-start | bytes 602120 | tf_op jit(solution)/shard_map/ppermute | solution.py:563
  33.3 0.5 collective-permute-start.13
  33.8 0.4 collective-permute-start.21
  34.1 5.1 %collective-permute-done.10.refs_14_ = bf16[784,128]{1,0:T(8,128)(2,1)S(1)} collective-permute-done((bf16[784,128]{1,0:T(8,128)(2,1)S(1)}, bf16[784,128]{1,0:T(8,128)(2,1)S(1)}, u32[]{:S(2)}, u32[]{:S(2)}) %collective-permute-start.10) | collective-permute-done | bytes 200736 | tf_op jit(solution)/shard_map/ppermute | solution.py:563
  39.3 0.5 collective-permute-start.28
  39.8 1.0 collective-permute-done.13.refs_17_
  40.9 0.4 collective-permute-start.29
  41.3 3.6 %collective-permute-done.14.refs_18_ = bf16[784,128]{1,0:T(8,128)(2,1)S(1)} collective-permute-done((bf16[784,128]{1,0:T(8,128)(2,1)S(1)}, bf16[784,128]{1,0:T(8,128)(2,1)S(1)}, u32[]{:S(2)}, u32[]{:S(2)}) %collective-permute-start.14) | collective-permute-done | bytes 200736 | tf_op jit(solution)/shard_map/ppermute | solution.py:563
  45.0 1.4 collective-permute-done.30.refs_34_
  47.1 61.6 %layer_core.1 = (f32[512,512]{1,0:T(8,128)}, f32[512,512]{1,0:T(8,128)}, bf16[16,784,128]{2,1,0:T(8,128)(2,1)}, bf16[4,784,128]{2,1,0:T(8,128)(2,1)}, bf16[4,784...) custom-call(bf16[512,512]{1,0:T(8,128)(2,1)} %bitcast.54, ...), custom_call_target="tpu_custom_call" | custom-call | tf_op jit(solution)/shard_map/layer_core/pallas_call | solution.py:546
  109.8 1.5 collective-permute-done.33
  111.3 1.1 add_convert_fusion.3
  112.5 1.1 add_convert_fusion.2
  113.6 2.1 %collective-permute-start.34 = (bf16[2,784,128]{2,1,0:T(8,128)(2,1)S(1)}, bf16[2,784,128]{2,1,0:T(8,128)(2,1)S(1)}, u32[]{:S(2)}, u32[]{:S(2)}) collective-permute-start(bf16[2,784,128]{2,1,0:T(8,128)(2,1)S(1)} %add_convert_fusion.2), channel_id=1, source_target_pairs={{0,4},{1,5},{2,3},{3,2},{4,0},{5,1},{6,7},{7,6},{8,12},{9,13},{10,... | collective-permute-start | bytes 1204232 | tf_op jit(solution)/shard_map/ppermute | solution.py:563
  116.0 4.3 %collective-permute-done.35 = bf16[2,784,128]{2,1,0:T(8,128)(2,1)S(1)} collective-permute-done((bf16[2,784,128]{2,1,0:T(8,128)(2,1)S(1)}, bf16[2,784,128]{2,1,0:T(8,128)(2,1)S(1)}, u32[]{:S(2)}, u32[]{:S(2)}) %collective-permute-start.35) | collective-permute-done | bytes 401440 | tf_op jit(solution)/shard_map/ppermute | solution.py:563
  120.5 6.3 %collective-permute-done.34 = bf16[2,784,128]{2,1,0:T(8,128)(2,1)S(1)} collective-permute-done((bf16[2,784,128]{2,1,0:T(8,128)(2,1)S(1)}, bf16[2,784,128]{2,1,0:T(8,128)(2,1)S(1)}, u32[]{:S(2)}, u32[]{:S(2)}) %collective-permute-start.34) | collective-permute-done | bytes 401440 | tf_op jit(solution)/shard_map/ppermute | solution.py:563
  127.1 1.8 %collective-permute-start.37 = (bf16[2,784,128]{2,1,0:T(8,128)(2,1)S(1)}, bf16[2,784,128]{2,1,0:T(8,128)(2,1)S(1)}, u32[]{:S(2)}, u32[]{:S(2)}) collective-permute-start(bf16[2,784,128]{2,1,0:T(8,128)(2,1)S(1)} %add_convert_fusion), channel_id=1, source_target_pairs={{0,4},{1,5},{2,3},{3,2},{4,0},{5,1},{6,7},{7,6},{8,12},{9,13},{10,... | collective-permute-start | bytes 1204232 | tf_op jit(solution)/shard_map/ppermute | solution.py:563
  129.0 4.3 %collective-permute-done.39 = bf16[2,784,128]{2,1,0:T(8,128)(2,1)S(1)} collective-permute-done((bf16[2,784,128]{2,1,0:T(8,128)(2,1)S(1)}, bf16[2,784,128]{2,1,0:T(8,128)(2,1)S(1)}, u32[]{:S(2)}, u32[]{:S(2)}) %collective-permute-start.39) | collective-permute-done | bytes 401440 | tf_op jit(solution)/shard_map/ppermute | solution.py:563
  133.4 0.8 collective-permute-start.43
  134.2 2.1 %collective-permute-start.42 = (bf16[784,128]{1,0:T(8,128)(2,1)S(1)}, bf16[784,128]{1,0:T(8,128)(2,1)S(1)}, u32[]{:S(2)}, u32[]{:S(2)}) collective-permute-start(bf16[784,128]{1,0:T(8,128)(2,1)S(1)} %fusion.4), channel_id=1, source_target_pairs={{0,1},{1,0},{2,6},{3,7},{4,5},{5,4},{6,2},{7,3},{8,9},{9,8},{10,14... | collective-permute-start | bytes 602120 | tf_op jit(solution)/shard_map/ppermute | solution.py:563
  136.3 0.8 fusion.5
  137.3 2.4 %collective-permute-done.37 = bf16[2,784,128]{2,1,0:T(8,128)(2,1)S(1)} collective-permute-done((bf16[2,784,128]{2,1,0:T(8,128)(2,1)S(1)}, bf16[2,784,128]{2,1,0:T(8,128)(2,1)S(1)}, u32[]{:S(2)}, u32[]{:S(2)}) %collective-permute-start.37) | collective-permute-done | bytes 401440 | tf_op jit(solution)/shard_map/ppermute | solution.py:563
  139.7 0.8 fusion.6
  140.5 6.4 %collective-permute-done.43 = bf16[784,128]{1,0:T(8,128)(2,1)S(1)} collective-permute-done((bf16[784,128]{1,0:T(8,128)(2,1)S(1)}, bf16[784,128]{1,0:T(8,128)(2,1)S(1)}, u32[]{:S(2)}, u32[]{:S(2)}) %collective-permute-start.43) | collective-permute-done | bytes 200736 | tf_op jit(solution)/shard_map/ppermute | solution.py:563
  146.9 0.8 fusion.2
  147.8 3.0 %collective-permute-done.45 = bf16[784,128]{1,0:T(8,128)(2,1)S(1)} collective-permute-done((bf16[784,128]{1,0:T(8,128)(2,1)}, bf16[784,128]{1,0:T(8,128)(2,1)S(1)}, u32[]{:S(2)}, u32[]{:S(2)}) %collective-permute-start.45) | collective-permute-done | bytes 200736 | tf_op jit(solution)/shard_map/ppermute | solution.py:563
  150.8 3.0 %collective-permute-done.44 = bf16[784,128]{1,0:T(8,128)(2,1)} collective-permute-done((bf16[784,128]{1,0:T(8,128)(2,1)}, bf16[784,128]{1,0:T(8,128)(2,1)}, u32[]{:S(2)}, u32[]{:S(2)}) %collective-permute-start.44) | collective-permute-done | bytes 200736 | tf_op jit(solution)/shard_map/ppermute | solution.py:563
  153.8 1.4 fusion.8
  155.2 0.5 slice_bitcast_fusion.4
  155.7 2.6 %multiply_add_fusion = (f32[98496]{0:T(1024)}, f32[98496]{0:T(1024)}, f32[98496]{0:T(1024)}, f32[98496]{0:T(1024)}) fusion(f32[98496]{0:T(1024)} %param.11, f32[98496]{0:T(1024)} %param.9, f32[98496]{0:T(1024)} %param.10, f32[100352]{0:T(1024)S(1)} %bitcast.53, s32[]{:T(128)S(6)} %select_n.15), kind=kLoop, calls=%fused_computation.24 | loop fusion | flops 886464 | bytes 3151876 | tf_op jit(solution)/shard_map/add | solution.py:650
  (137 shorter events, 4.2 us)
Async XLA Ops:
  1.9 44.5 %copy-start.2 = (bf16[784,128]{1,0:T(8,128)(2,1)}, bf16[784,128]{1,0:T(8,128)(2,1)S(1)}, u32[]{:S(2)}) copy-start(bf16[784,128]{1,0:T(8,128)(2,1)S(1)} %fusion.11.refs_3_) | copy-start | bytes 602116
  1.9 6.7 %collective-permute-start.7 = (bf16[784,128]{1,0:T(8,128)(2,1)S(1)}, bf16[784,128]{1,0:T(8,128)(2,1)S(1)}, u32[]{:S(2)}, u32[]{:S(2)}) collective-permute-start(bf16[784,128]{1,0:T(8,128)(2,1)S(1)} %fusion.11.refs_3_), channel_id=1, source_target_pairs={{0,4},{1,5},{2,3},{3,2},{4,0},{5,1},{6,7},{7,6},{8,12},{9,13},{10,... | collective-permute-start | bytes 602120 | tf_op jit(solution)/shard_map/ppermute | solution.py:563
  4.9 6.9 %collective-permute-start = (bf16[784,128]{1,0:T(8,128)(2,1)S(1)}, bf16[784,128]{1,0:T(8,128)(2,1)S(1)}, u32[]{:S(2)}, u32[]{:S(2)}) collective-permute-start(bf16[784,128]{1,0:T(8,128)(2,1)S(1)} %fusion.11.refs_3_), channel_id=1, source_target_pairs={{0,8},{1,9},{2,18},{3,19},{4,12},{5,13},{6,22},{7,23},{8,0},{9,1},... | collective-permute-start | bytes 602120 | tf_op jit(solution)/shard_map/ppermute | solution.py:563
  6.4 5.7 %collective-permute-start.3 = (bf16[784,128]{1,0:T(8,128)(2,1)S(1)}, bf16[784,128]{1,0:T(8,128)(2,1)S(1)}, u32[]{:S(2)}, u32[]{:S(2)}) collective-permute-start(bf16[784,128]{1,0:T(8,128)(2,1)S(1)} %fusion.11.refs_3_), channel_id=1, source_target_pairs={{0,1},{1,0},{2,6},{3,7},{4,5},{5,4},{6,2},{7,3},{8,9},{9,8},{10,14... | collective-permute-start | bytes 602120 | tf_op jit(solution)/shard_map/ppermute | solution.py:563
  8.0 7.5 %collective-permute-start.15 = (bf16[784,128]{1,0:T(8,128)(2,1)S(1)}, bf16[784,128]{1,0:T(8,128)(2,1)S(1)}, u32[]{:S(2)}, u32[]{:S(2)}) collective-permute-start(bf16[784,128]{1,0:T(8,128)(2,1)S(1)} %fusion.11.refs_3_), channel_id=1, source_target_pairs={{0,2},{1,3},{2,0},{3,1},{4,6},{5,7},{6,4},{7,5},{8,10},{9,11},{10,... | collective-permute-start | bytes 602120 | tf_op jit(solution)/shard_map/ppermute | solution.py:563
  8.6 37.8 %copy-start.4 = (bf16[784,128]{1,0:T(8,128)(2,1)}, bf16[784,128]{1,0:T(8,128)(2,1)S(1)}, u32[]{:S(2)}) copy-start(bf16[784,128]{1,0:T(8,128)(2,1)S(1)} %collective-permute-done.7.refs_11_) | copy-start | bytes 602116
  8.6 6.9 %collective-permute-start.23 = (bf16[784,128]{1,0:T(8,128)(2,1)S(1)}, bf16[784,128]{1,0:T(8,128)(2,1)S(1)}, u32[]{:S(2)}, u32[]{:S(2)}) collective-permute-start(bf16[784,128]{1,0:T(8,128)(2,1)S(1)} %collective-permute-done.7.refs_11_), channel_id=1, source_target_pairs={{0,2},{1,3},{2,0},{3,1},{4,6},{5,7},{6,4},{7,5},{8,10},{9,11},{10,... | collective-permute-start | bytes 602120 | tf_op jit(solution)/shard_map/ppermute | solution.py:563
  8.6 7.7 %collective-permute-start.11 = (bf16[784,128]{1,0:T(8,128)(2,1)S(1)}, bf16[784,128]{1,0:T(8,128)(2,1)S(1)}, u32[]{:S(2)}, u32[]{:S(2)}) collective-permute-start(bf16[784,128]{1,0:T(8,128)(2,1)S(1)} %collective-permute-done.7.refs_11_), channel_id=1, source_target_pairs={{0,1},{1,0},{2,6},{3,7},{4,5},{5,4},{6,2},{7,3},{8,9},{9,8},{10,14... | collective-permute-start | bytes 602120 | tf_op jit(solution)/shard_map/ppermute | solution.py:563
  12.2 5.3 %collective-permute-start.19 = (bf16[784,128]{1,0:T(8,128)(2,1)S(1)}, bf16[784,128]{1,0:T(8,128)(2,1)S(1)}, u32[]{:S(2)}, u32[]{:S(2)}) collective-permute-start(bf16[784,128]{1,0:T(8,128)(2,1)S(1)} %collective-permute-done.3.refs_7_), channel_id=1, source_target_pairs={{0,2},{1,3},{2,0},{3,1},{4,6},{5,7},{6,4},{7,5},{8,10},{9,11},{10,... | collective-permute-start | bytes 602120 | tf_op jit(solution)/shard_map/ppermute | solution.py:563
  12.2 8.3 %collective-permute-start.1 = (bf16[784,128]{1,0:T(8,128)(2,1)S(1)}, bf16[784,128]{1,0:T(8,128)(2,1)S(1)}, u32[]{:S(2)}, u32[]{:S(2)}) collective-permute-start(bf16[784,128]{1,0:T(8,128)(2,1)S(1)} %fusion.11.refs_3_), channel_id=1, source_target_pairs={{0,16},{1,17},{2,10},{3,11},{4,20},{5,21},{6,14},{7,15},{8,24},{9,... | collective-permute-start | bytes 602120 | tf_op jit(solution)/shard_map/ppermute | solution.py:563
  15.5 5.0 %collective-permute-start.16 = (bf16[784,128]{1,0:T(8,128)(2,1)S(1)}, bf16[784,128]{1,0:T(8,128)(2,1)S(1)}, u32[]{:S(2)}, u32[]{:S(2)}) collective-permute-start(bf16[784,128]{1,0:T(8,128)(2,1)S(1)} %collective-permute-done.refs_4_), channel_id=1, source_target_pairs={{0,2},{1,3},{2,0},{3,1},{4,6},{5,7},{6,4},{7,5},{8,10},{9,11},{10,... | collective-permute-start | bytes 602120 | tf_op jit(solution)/shard_map/ppermute | solution.py:563
  15.5 7.9 %collective-permute-start.8 = (bf16[784,128]{1,0:T(8,128)(2,1)S(1)}, bf16[784,128]{1,0:T(8,128)(2,1)S(1)}, u32[]{:S(2)}, u32[]{:S(2)}) collective-permute-start(bf16[784,128]{1,0:T(8,128)(2,1)S(1)} %collective-permute-done.refs_4_), channel_id=1, source_target_pairs={{0,4},{1,5},{2,3},{3,2},{4,0},{5,1},{6,7},{7,6},{8,12},{9,13},{10,... | collective-permute-start | bytes 602120 | tf_op jit(solution)/shard_map/ppermute | solution.py:563
  16.3 7.6 %collective-permute-start.4 = (bf16[784,128]{1,0:T(8,128)(2,1)S(1)}, bf16[784,128]{1,0:T(8,128)(2,1)S(1)}, u32[]{:S(2)}, u32[]{:S(2)}) collective-permute-start(bf16[784,128]{1,0:T(8,128)(2,1)S(1)} %collective-permute-done.refs_4_), channel_id=1, source_target_pairs={{0,1},{1,0},{2,6},{3,7},{4,5},{5,4},{6,2},{7,3},{8,9},{9,8},{10,14... | collective-permute-start | bytes 602120 | tf_op jit(solution)/shard_map/ppermute | solution.py:563
  17.5 7.9 %collective-permute-start.2 = (bf16[784,128]{1,0:T(8,128)(2,1)S(1)}, bf16[784,128]{1,0:T(8,128)(2,1)S(1)}, u32[]{:S(2)}, u32[]{:S(2)}) collective-permute-start(bf16[784,128]{1,0:T(8,128)(2,1)S(1)} %collective-permute-done.refs_4_), channel_id=1, source_target_pairs={{0,16},{1,17},{2,10},{3,11},{4,20},{5,21},{6,14},{7,15},{8,24},{9,... | collective-permute-start | bytes 602120 | tf_op jit(solution)/shard_map/ppermute | solution.py:563
  20.5 4.9 %collective-permute-start.27 = (bf16[784,128]{1,0:T(8,128)(2,1)S(1)}, bf16[784,128]{1,0:T(8,128)(2,1)S(1)}, u32[]{:S(2)}, u32[]{:S(2)}) collective-permute-start(bf16[784,128]{1,0:T(8,128)(2,1)S(1)} %collective-permute-done.11.refs_15_), channel_id=1, source_target_pairs={{0,2},{1,3},{2,0},{3,1},{4,6},{5,7},{6,4},{7,5},{8,10},{9,11},{10,... | collective-permute-start | bytes 602120 | tf_op jit(solution)/shard_map/ppermute | solution.py:563
  20.5 5.9 %collective-permute-start.17 = (bf16[784,128]{1,0:T(8,128)(2,1)S(1)}, bf16[784,128]{1,0:T(8,128)(2,1)S(1)}, u32[]{:S(2)}, u32[]{:S(2)}) collective-permute-start(bf16[784,128]{1,0:T(8,128)(2,1)S(1)} %collective-permute-done.1.refs_5_), channel_id=1, source_target_pairs={{0,2},{1,3},{2,0},{3,1},{4,6},{5,7},{6,4},{7,5},{8,10},{9,11},{10,... | collective-permute-start | bytes 602120 | tf_op jit(solution)/shard_map/ppermute | solution.py:563
  23.4 7.8 %collective-permute-start.9 = (bf16[784,128]{1,0:T(8,128)(2,1)S(1)}, bf16[784,128]{1,0:T(8,128)(2,1)S(1)}, u32[]{:S(2)}, u32[]{:S(2)}) collective-permute-start(bf16[784,128]{1,0:T(8,128)(2,1)S(1)} %collective-permute-done.1.refs_5_), channel_id=1, source_target_pairs={{0,4},{1,5},{2,3},{3,2},{4,0},{5,1},{6,7},{7,6},{8,12},{9,13},{10,... | collective-permute-start | bytes 602120 | tf_op jit(solution)/shard_map/ppermute | solution.py:563
  23.8 7.4 %collective-permute-start.5 = (bf16[784,128]{1,0:T(8,128)(2,1)S(1)}, bf16[784,128]{1,0:T(8,128)(2,1)S(1)}, u32[]{:S(2)}, u32[]{:S(2)}) collective-permute-start(bf16[784,128]{1,0:T(8,128)(2,1)S(1)} %collective-permute-done.1.refs_5_), channel_id=1, source_target_pairs={{0,1},{1,0},{2,6},{3,7},{4,5},{5,4},{6,2},{7,3},{8,9},{9,8},{10,14... | collective-permute-start | bytes 602120 | tf_op jit(solution)/shard_map/ppermute | solution.py:563
  25.3 6.3 %collective-permute-start.24 = (bf16[784,128]{1,0:T(8,128)(2,1)S(1)}, bf16[784,128]{1,0:T(8,128)(2,1)S(1)}, u32[]{:S(2)}, u32[]{:S(2)}) collective-permute-start(bf16[784,128]{1,0:T(8,128)(2,1)S(1)} %collective-permute-done.8.refs_12_), channel_id=1, source_target_pairs={{0,2},{1,3},{2,0},{3,1},{4,6},{5,7},{6,4},{7,5},{8,10},{9,11},{10,... | collective-permute-start | bytes 602120 | tf_op jit(solution)/shard_map/ppermute | solution.py:563
  25.4 7.9 %collective-permute-start.12 = (bf16[784,128]{1,0:T(8,128)(2,1)S(1)}, bf16[784,128]{1,0:T(8,128)(2,1)S(1)}, u32[]{:S(2)}, u32[]{:S(2)}) collective-permute-start(bf16[784,128]{1,0:T(8,128)(2,1)S(1)} %collective-permute-done.8.refs_12_), channel_id=1, source_target_pairs={{0,1},{1,0},{2,6},{3,7},{4,5},{5,4},{6,2},{7,3},{8,9},{9,8},{10,14... | collective-permute-start | bytes 602120 | tf_op jit(solution)/shard_map/ppermute | solution.py:563
  26.4 6.8 %collective-permute-start.20 = (bf16[784,128]{1,0:T(8,128)(2,1)S(1)}, bf16[784,128]{1,0:T(8,128)(2,1)S(1)}, u32[]{:S(2)}, u32[]{:S(2)}) collective-permute-start(bf16[784,128]{1,0:T(8,128)(2,1)S(1)} %collective-permute-done.4.refs_8_), channel_id=1, source_target_pairs={{0,2},{1,3},{2,0},{3,1},{4,6},{5,7},{6,4},{7,5},{8,10},{9,11},{10,... | collective-permute-start | bytes 602120 | tf_op jit(solution)/shard_map/ppermute | solution.py:563
  31.3 2.5 %collective-permute-start.18 = (bf16[784,128]{1,0:T(8,128)(2,1)S(1)}, bf16[784,128]{1,0:T(8,128)(2,1)S(1)}, u32[]{:S(2)}, u32[]{:S(2)}) collective-permute-start(bf16[784,128]{1,0:T(8,128)(2,1)S(1)} %collective-permute-done.2.refs_6_), channel_id=1, source_target_pairs={{0,2},{1,3},{2,0},{3,1},{4,6},{5,7},{6,4},{7,5},{8,10},{9,11},{10,... | collective-permute-start | bytes 602120 | tf_op jit(solution)/shard_map/ppermute | solution.py:563
  31.3 7.9 %collective-permute-start.10 = (bf16[784,128]{1,0:T(8,128)(2,1)S(1)}, bf16[784,128]{1,0:T(8,128)(2,1)S(1)}, u32[]{:S(2)}, u32[]{:S(2)}) collective-permute-start(bf16[784,128]{1,0:T(8,128)(2,1)S(1)} %collective-permute-done.2.refs_6_), channel_id=1, source_target_pairs={{0,4},{1,5},{2,3},{3,2},{4,0},{5,1},{6,7},{7,6},{8,12},{9,13},{10,... | collective-permute-start | bytes 602120 | tf_op jit(solution)/shard_map/ppermute | solution.py:563
  31.6 7.6 %collective-permute-start.6 = (bf16[784,128]{1,0:T(8,128)(2,1)S(1)}, bf16[784,128]{1,0:T(8,128)(2,1)S(1)}, u32[]{:S(2)}, u32[]{:S(2)}) collective-permute-start(bf16[784,128]{1,0:T(8,128)(2,1)S(1)} %collective-permute-done.2.refs_6_), channel_id=1, source_target_pairs={{0,1},{1,0},{2,6},{3,7},{4,5},{5,4},{6,2},{7,3},{8,9},{9,8},{10,14... | collective-permute-start | bytes 602120 | tf_op jit(solution)/shard_map/ppermute | solution.py:563
  33.2 6.1 %collective-permute-start.25 = (bf16[784,128]{1,0:T(8,128)(2,1)S(1)}, bf16[784,128]{1,0:T(8,128)(2,1)S(1)}, u32[]{:S(2)}, u32[]{:S(2)}) collective-permute-start(bf16[784,128]{1,0:T(8,128)(2,1)S(1)} %collective-permute-done.9.refs_13_), channel_id=1, source_target_pairs={{0,2},{1,3},{2,0},{3,1},{4,6},{5,7},{6,4},{7,5},{8,10},{9,11},{10,... | collective-permute-start | bytes 602120 | tf_op jit(solution)/shard_map/ppermute | solution.py:563
  33.3 7.6 %collective-permute-start.13 = (bf16[784,128]{1,0:T(8,128)(2,1)S(1)}, bf16[784,128]{1,0:T(8,128)(2,1)S(1)}, u32[]{:S(2)}, u32[]{:S(2)}) collective-permute-start(bf16[784,128]{1,0:T(8,128)(2,1)S(1)} %collective-permute-done.9.refs_13_), channel_id=1, source_target_pairs={{0,1},{1,0},{2,6},{3,7},{4,5},{5,4},{6,2},{7,3},{8,9},{9,8},{10,14... | collective-permute-start | bytes 602120 | tf_op jit(solution)/shard_map/ppermute | solution.py:563
  33.8 7.2 %collective-permute-start.21 = (bf16[784,128]{1,0:T(8,128)(2,1)S(1)}, bf16[784,128]{1,0:T(8,128)(2,1)S(1)}, u32[]{:S(2)}, u32[]{:S(2)}) collective-permute-start(bf16[784,128]{1,0:T(8,128)(2,1)S(1)} %collective-permute-done.5.refs_9_), channel_id=1, source_target_pairs={{0,2},{1,3},{2,0},{3,1},{4,6},{5,7},{6,4},{7,5},{8,10},{9,11},{10,... | collective-permute-start | bytes 602120 | tf_op jit(solution)/shard_map/ppermute | solution.py:563
  39.2 5.7 %collective-permute-start.14 = (bf16[784,128]{1,0:T(8,128)(2,1)S(1)}, bf16[784,128]{1,0:T(8,128)(2,1)S(1)}, u32[]{:S(2)}, u32[]{:S(2)}) collective-permute-start(bf16[784,128]{1,0:T(8,128)(2,1)S(1)} %collective-permute-done.10.refs_14_), channel_id=1, source_target_pairs={{0,1},{1,0},{2,6},{3,7},{4,5},{5,4},{6,2},{7,3},{8,9},{9,8},{10,14... | collective-permute-start | bytes 602120 | tf_op jit(solution)/shard_map/ppermute | solution.py:563
  39.2 5.7 %collective-permute-start.26 = (bf16[784,128]{1,0:T(8,128)(2,1)S(1)}, bf16[784,128]{1,0:T(8,128)(2,1)S(1)}, u32[]{:S(2)}, u32[]{:S(2)}) collective-permute-start(bf16[784,128]{1,0:T(8,128)(2,1)S(1)} %collective-permute-done.10.refs_14_), channel_id=1, source_target_pairs={{0,2},{1,3},{2,0},{3,1},{4,6},{5,7},{6,4},{7,5},{8,10},{9,11},{10,... | collective-permute-start | bytes 602120 | tf_op jit(solution)/shard_map/ppermute | solution.py:563
  39.3 5.6 %collective-permute-start.28 = (bf16[784,128]{1,0:T(8,128)(2,1)S(1)}, bf16[784,128]{1,0:T(8,128)(2,1)S(1)}, u32[]{:S(2)}, u32[]{:S(2)}) collective-permute-start(bf16[784,128]{1,0:T(8,128)(2,1)S(1)} %collective-permute-done.12.refs_16_), channel_id=1, source_target_pairs={{0,2},{1,3},{2,0},{3,1},{4,6},{5,7},{6,4},{7,5},{8,10},{9,11},{10,... | collective-permute-start | bytes 602120 | tf_op jit(solution)/shard_map/ppermute | solution.py:563
  40.8 4.1 %collective-permute-start.22 = (bf16[784,128]{1,0:T(8,128)(2,1)S(1)}, bf16[784,128]{1,0:T(8,128)(2,1)S(1)}, u32[]{:S(2)}, u32[]{:S(2)}) collective-permute-start(bf16[784,128]{1,0:T(8,128)(2,1)S(1)} %collective-permute-done.6.refs_10_), channel_id=1, source_target_pairs={{0,2},{1,3},{2,0},{3,1},{4,6},{5,7},{6,4},{7,5},{8,10},{9,11},{10,... | collective-permute-start | bytes 602120 | tf_op jit(solution)/shard_map/ppermute | solution.py:563
  40.9 4.0 %collective-permute-start.29 = (bf16[784,128]{1,0:T(8,128)(2,1)S(1)}, bf16[784,128]{1,0:T(8,128)(2,1)S(1)}, u32[]{:S(2)}, u32[]{:S(2)}) collective-permute-start(bf16[784,128]{1,0:T(8,128)(2,1)S(1)} %collective-permute-done.13.refs_17_), channel_id=1, source_target_pairs={{0,2},{1,3},{2,0},{3,1},{4,6},{5,7},{6,4},{7,5},{8,10},{9,11},{10,... | collective-permute-start | bytes 602120 | tf_op jit(solution)/shard_map/ppermute | solution.py:563
  44.9 1.4 collective-permute-start.30
  108.7 2.6 %collective-permute-start.33 = (bf16[4,784,128]{2,1,0:T(8,128)(2,1)}, bf16[4,784,128]{2,1,0:T(8,128)(2,1)S(1)}, u32[]{:S(2)}, u32[]{:S(2)}) collective-permute-start(bf16[4,784,128]{2,1,0:T(8,128)(2,1)} %get-tuple-element.31), channel_id=1, source_target_pairs={{0,2},{1,3},{2,0},{3,1},{4,6},{5,7},{6,4},{7,5},{8,10},{9,11},{10,... | collective-permute-start | bytes 2408456 | tf_op jit(solution)/shard_map/ppermute | solution.py:563
  108.9 3.6 %collective-permute-start.32 = (bf16[4,784,128]{2,1,0:T(8,128)(2,1)}, bf16[4,784,128]{2,1,0:T(8,128)(2,1)S(1)}, u32[]{:S(2)}, u32[]{:S(2)}) collective-permute-start(bf16[4,784,128]{2,1,0:T(8,128)(2,1)} %get-tuple-element.30), channel_id=1, source_target_pairs={{0,2},{1,3},{2,0},{3,1},{4,6},{5,7},{6,4},{7,5},{8,10},{9,11},{10,... | collective-permute-start | bytes 2408456 | tf_op jit(solution)/shard_map/ppermute | solution.py:563
  109.3 6.4 %collective-permute-start.36 = (bf16[4,784,128]{2,1,0:T(8,128)(2,1)}, bf16[4,784,128]{2,1,0:T(8,128)(2,1)S(1)}, u32[]{:S(2)}, u32[]{:S(2)}) collective-permute-start(bf16[4,784,128]{2,1,0:T(8,128)(2,1)} %get-tuple-element.33), channel_id=1, source_target_pairs={{0,2},{1,3},{2,0},{3,1},{4,6},{5,7},{6,4},{7,5},{8,10},{9,11},{10,... | collective-permute-start | bytes 2408456 | tf_op jit(solution)/shard_map/ppermute | solution.py:563
  109.4 6.5 %collective-permute-start.31 = (bf16[4,784,128]{2,1,0:T(8,128)(2,1)}, bf16[4,784,128]{2,1,0:T(8,128)(2,1)S(1)}, u32[]{:S(2)}, u32[]{:S(2)}) collective-permute-start(bf16[4,784,128]{2,1,0:T(8,128)(2,1)} %get-tuple-element.29), channel_id=1, source_target_pairs={{0,2},{1,3},{2,0},{3,1},{4,6},{5,7},{6,4},{7,5},{8,10},{9,11},{10,... | collective-permute-start | bytes 2408456 | tf_op jit(solution)/shard_map/ppermute | solution.py:563
  112.4 7.9 %collective-permute-start.35 = (bf16[2,784,128]{2,1,0:T(8,128)(2,1)S(1)}, bf16[2,784,128]{2,1,0:T(8,128)(2,1)S(1)}, u32[]{:S(2)}, u32[]{:S(2)}) collective-permute-start(bf16[2,784,128]{2,1,0:T(8,128)(2,1)S(1)} %add_convert_fusion.3), channel_id=1, source_target_pairs={{0,4},{1,5},{2,3},{3,2},{4,0},{5,1},{6,7},{7,6},{8,12},{9,13},{10,... | collective-permute-start | bytes 1204232 | tf_op jit(solution)/shard_map/ppermute | solution.py:563
  113.6 13.2 %collective-permute-start.34 = (bf16[2,784,128]{2,1,0:T(8,128)(2,1)S(1)}, bf16[2,784,128]{2,1,0:T(8,128)(2,1)S(1)}, u32[]{:S(2)}, u32[]{:S(2)}) collective-permute-start(bf16[2,784,128]{2,1,0:T(8,128)(2,1)S(1)} %add_convert_fusion.2), channel_id=1, source_target_pairs={{0,4},{1,5},{2,3},{3,2},{4,0},{5,1},{6,7},{7,6},{8,12},{9,13},{10,... | collective-permute-start | bytes 1204232 | tf_op jit(solution)/shard_map/ppermute | solution.py:563
  115.9 17.4 %collective-permute-start.39 = (bf16[2,784,128]{2,1,0:T(8,128)(2,1)S(1)}, bf16[2,784,128]{2,1,0:T(8,128)(2,1)S(1)}, u32[]{:S(2)}, u32[]{:S(2)}) collective-permute-start(bf16[2,784,128]{2,1,0:T(8,128)(2,1)S(1)} %add_convert_fusion.1), channel_id=1, source_target_pairs={{0,4},{1,5},{2,3},{3,2},{4,0},{5,1},{6,7},{7,6},{8,12},{9,13},{10,... | collective-permute-start | bytes 1204232 | tf_op jit(solution)/shard_map/ppermute | solution.py:563
  120.4 12.8 %collective-permute-start.40 = (bf16[784,128]{1,0:T(8,128)(2,1)S(1)}, bf16[784,128]{1,0:T(8,128)(2,1)S(1)}, u32[]{:S(2)}, u32[]{:S(2)}) collective-permute-start(bf16[784,128]{1,0:T(8,128)(2,1)S(1)} %fusion.9), channel_id=1, source_target_pairs={{0,1},{1,0},{2,6},{3,7},{4,5},{5,4},{6,2},{7,3},{8,9},{9,8},{10,14... | collective-permute-start | bytes 602120 | tf_op jit(solution)/shard_map/ppermute | solution.py:563
  126.9 9.4 %collective-permute-start.38 = (bf16[784,128]{1,0:T(8,128)(2,1)S(1)}, bf16[784,128]{1,0:T(8,128)(2,1)S(1)}, u32[]{:S(2)}, u32[]{:S(2)}) collective-permute-start(bf16[784,128]{1,0:T(8,128)(2,1)S(1)} %fusion.10), channel_id=1, source_target_pairs={{0,1},{1,0},{2,6},{3,7},{4,5},{5,4},{6,2},{7,3},{8,9},{9,8},{10,14... | collective-permute-start | bytes 602120 | tf_op jit(solution)/shard_map/ppermute | solution.py:563
  127.1 12.6 %collective-permute-start.37 = (bf16[2,784,128]{2,1,0:T(8,128)(2,1)S(1)}, bf16[2,784,128]{2,1,0:T(8,128)(2,1)S(1)}, u32[]{:S(2)}, u32[]{:S(2)}) collective-permute-start(bf16[2,784,128]{2,1,0:T(8,128)(2,1)S(1)} %add_convert_fusion), channel_id=1, source_target_pairs={{0,4},{1,5},{2,3},{3,2},{4,0},{5,1},{6,7},{7,6},{8,12},{9,13},{10,... | collective-permute-start | bytes 1204232 | tf_op jit(solution)/shard_map/ppermute | solution.py:563
  133.4 13.6 %collective-permute-start.43 = (bf16[784,128]{1,0:T(8,128)(2,1)S(1)}, bf16[784,128]{1,0:T(8,128)(2,1)S(1)}, u32[]{:S(2)}, u32[]{:S(2)}) collective-permute-start(bf16[784,128]{1,0:T(8,128)(2,1)S(1)} %fusion.3), channel_id=1, source_target_pairs={{0,16},{1,17},{2,10},{3,11},{4,20},{5,21},{6,14},{7,15},{8,24},{9,... | collective-permute-start | bytes 602120 | tf_op jit(solution)/shard_map/ppermute | solution.py:563
  134.2 12.7 %collective-permute-start.42 = (bf16[784,128]{1,0:T(8,128)(2,1)S(1)}, bf16[784,128]{1,0:T(8,128)(2,1)S(1)}, u32[]{:S(2)}, u32[]{:S(2)}) collective-permute-start(bf16[784,128]{1,0:T(8,128)(2,1)S(1)} %fusion.4), channel_id=1, source_target_pairs={{0,1},{1,0},{2,6},{3,7},{4,5},{5,4},{6,2},{7,3},{8,9},{9,8},{10,14... | collective-permute-start | bytes 602120 | tf_op jit(solution)/shard_map/ppermute | solution.py:563
  137.1 13.7 %collective-permute-start.45 = (bf16[784,128]{1,0:T(8,128)(2,1)}, bf16[784,128]{1,0:T(8,128)(2,1)S(1)}, u32[]{:S(2)}, u32[]{:S(2)}) collective-permute-start(bf16[784,128]{1,0:T(8,128)(2,1)} %fusion.5), channel_id=1, source_target_pairs={{0,16},{1,17},{2,10},{3,11},{4,20},{5,21},{6,14},{7,15},{8,24},{9,... | collective-permute-start | bytes 602120 | tf_op jit(solution)/shard_map/ppermute | solution.py:563
  140.5 10.3 %collective-permute-start.41 = (bf16[784,128]{1,0:T(8,128)(2,1)}, bf16[784,128]{1,0:T(8,128)(2,1)}, u32[]{:S(2)}, u32[]{:S(2)}) collective-permute-start(bf16[784,128]{1,0:T(8,128)(2,1)} %fusion.6), channel_id=1, source_target_pairs={{0,1},{1,0},{2,6},{3,7},{4,5},{5,4},{6,2},{7,3},{8,9},{9,8},{10,14... | collective-permute-start | bytes 602120 | tf_op jit(solution)/shard_map/ppermute | solution.py:563
  147.8 6.0 %collective-permute-start.44 = (bf16[784,128]{1,0:T(8,128)(2,1)}, bf16[784,128]{1,0:T(8,128)(2,1)}, u32[]{:S(2)}, u32[]{:S(2)}) collective-permute-start(bf16[784,128]{1,0:T(8,128)(2,1)} %fusion.2), channel_id=1, source_target_pairs={{0,8},{1,9},{2,18},{3,19},{4,12},{5,13},{6,22},{7,23},{8,0},{9,1},... | collective-permute-start | bytes 602120 | tf_op jit(solution)/shard_map/ppermute | solution.py:563
  (33 other events, 516.0 us)

commit v6 on v5

--- a/solution.py
+++ b/solution.py
@@ -574,7 +574,8 @@
     for m, v in enumerate(planes):
         side = exchange(v, 0)
         near[m], near[8 + m], near[4 + m], near[12 + m] = v, side, exchange(v, 1), exchange(side, 1)
-    return near + [exchange(v, 4) for v in near]
+    late = near[8 + 2]
+    return near + [exchange(after(v, late) if n % 4 < 2 else v, 4) for n, v in enumerate(near)]
 
 
 def total(*parts):
@@ -594,6 +595,10 @@
         last[0] = total(*parts)
         return last[0]
 
+    def single(m):
+        far = exchange(add(keep[4 * m + 3], got[m][3]), 0)
+        side[m] = (exchange(add(keep[4 * m + 2], got[m][2]), 0), far)
+
     def pair(m):
         side[m] = exchange(add(keep[4 * m + 2 : 4 * m + 4], got[m][2:]), 0)
 
@@ -603,17 +608,17 @@
     def plane(m):
         return (keep[4 * m], got[m][0], side[m][0], back[m])
 
-    pair(3)
-    pair(2)
-    pair(1)
+    single(3)
+    single(2)
     second(3)
     second(2)
+    pair(1)
     pair(0)
     turn = exchange(add(*plane(3)), 2)
     second(1)
     two = exchange(add(*plane(2)), 2)
+    one = exchange(add(*plane(1), turn), 3)
     second(0)
-    one = exchange(add(*plane(1), turn), 3)
     return (*plane(0), one, two)
 
 

time: 159 us -> 152 us (0.956)
  waiting for transfers between devices: 49.9 us -> 26.2 us
  starting transfers between devices: 34 us -> 49.8 us
  other arithmetic: 9.14 us -> 10.9 us
    ppermute x46 -> x48, waiting for transfers between devices: 49.9 us -> 26.2 us  [exchange(): lax.ppermute(v, AXES, [(j, j ^ (one if j // RC & 1 else zero)) for j in r...]
    ppermute x46 -> x48, starting transfers between devices: 34 us -> 49.8 us  [exchange(): lax.ppermute(v, AXES, [(j, j ^ (one if j // RC & 1 else zero)) for j in r...]
    convert_element_type x11 -> x13, other arithmetic: 5.17 us -> 6.89 us  [total(): return v.astype(BF)]
  transfers between devices with their start and end apart: 46 -> 48, of which waited for: 18 -> 15; matrix products, arithmetic and copies ran while one was open for 3% -> 5% of each run, Pallas kernels for 0% -> 0%
where the time goes in v6:
time: 152 us
  Pallas kernels  61.6 us (41%)
  starting transfers between devices  49.8 us (33%)
  waiting for transfers between devices  26.2 us (17%)
  other arithmetic  10.9 us (7%)
  local copies, waits for them, and re-layouts  2.36 us (2%)
    pallas_call x1, Pallas kernels, core(): pl.pallas_call(functools.partial(core_kernel, width=D, length=T, shards=s...  61.6 us
    ppermute x48, starting transfers between devices, exchange(): lax.ppermute(v, AXES, [(j, j ^ (one if j // RC & 1 else zero)) for j in r...  49.8 us
    ppermute x48, waiting for transfers between devices, exchange(): lax.ppermute(v, AXES, [(j, j ^ (one if j // RC & 1 else zero)) for j in r...  26.2 us
    convert_element_type x13, other arithmetic, total(): return v.astype(BF)  6.89 us
  transfers between devices with their start and end apart: 48, of which 15 were waited for; matrix products, arithmetic and copies ran while one was open for 5% of the time, Pallas kernels for 0%

profile of v6, /device:TPU:0, one launch (start us, length us, event | category | flops | bytes accessed | tf_op | source)
XLA Modules:
  0.0 152.0 jit_solution(17150453838134501074)
XLA Ops:
  0.7 1.2 fusion.17.refs_3_
  1.9 3.1 %collective-permute-start = (bf16[784,128]{1,0:T(8,128)(2,1)S(1)}, bf16[784,128]{1,0:T(8,128)(2,1)S(1)}, u32[]{:S(2)}, u32[]{:S(2)}) collective-permute-start(bf16[784,128]{1,0:T(8,128)(2,1)S(1)} %fusion.17.refs_3_), channel_id=1, source_target_pairs={{0,8},{1,9},{2,18},{3,19},{4,12},{5,13},{6,22},{7,23},{8,0},{9,1},... | collective-permute-start | bytes 602120 | tf_op jit(solution)/shard_map/ppermute | solution.py:563
  5.0 1.5 collective-permute-start.7
  6.4 1.5 collective-permute-start.3
  8.0 2.5 %collective-permute-done.refs_4_ = bf16[784,128]{1,0:T(8,128)(2,1)S(1)} collective-permute-done((bf16[784,128]{1,0:T(8,128)(2,1)S(1)}, bf16[784,128]{1,0:T(8,128)(2,1)S(1)}, u32[]{:S(2)}, u32[]{:S(2)}) %collective-permute-start) | collective-permute-done | bytes 200736 | tf_op jit(solution)/shard_map/ppermute | solution.py:563
  10.4 2.3 %collective-permute-start.1 = (bf16[784,128]{1,0:T(8,128)(2,1)S(1)}, bf16[784,128]{1,0:T(8,128)(2,1)S(1)}, u32[]{:S(2)}, u32[]{:S(2)}) collective-permute-start(bf16[784,128]{1,0:T(8,128)(2,1)S(1)} %fusion.17.refs_3_), channel_id=1, source_target_pairs={{0,16},{1,17},{2,10},{3,11},{4,20},{5,21},{6,14},{7,15},{8,24},{9,... | collective-permute-start | bytes 602120 | tf_op jit(solution)/shard_map/ppermute | solution.py:563
  12.7 1.5 collective-permute-start.11
  14.3 1.5 collective-permute-start.8
  16.3 1.3 collective-permute-start.2
  17.5 2.3 %collective-permute-start.9 = (bf16[784,128]{1,0:T(8,128)(2,1)S(1)}, bf16[784,128]{1,0:T(8,128)(2,1)S(1)}, u32[]{:S(2)}, u32[]{:S(2)}) collective-permute-start(bf16[784,128]{1,0:T(8,128)(2,1)S(1)} %collective-permute-done.1.refs_5_), channel_id=1, source_target_pairs={{0,4},{1,5},{2,3},{3,2},{4,0},{5,1},{6,7},{7,6},{8,12},{9,13},{10,... | collective-permute-start | bytes 602120 | tf_op jit(solution)/shard_map/ppermute | solution.py:563
  19.8 1.1 collective-permute-done.8.refs_12_
  21.0 1.1 collective-permute-start.5
  22.1 1.2 collective-permute-done.4.refs_8_
  23.2 2.1 %collective-permute-start.12 = (bf16[784,128]{1,0:T(8,128)(2,1)S(1)}, bf16[784,128]{1,0:T(8,128)(2,1)S(1)}, u32[]{:S(2)}, u32[]{:S(2)}) collective-permute-start(bf16[784,128]{1,0:T(8,128)(2,1)S(1)} %collective-permute-done.8.refs_12_), channel_id=1, source_target_pairs={{0,1},{1,0},{2,6},{3,7},{4,5},{5,4},{6,2},{7,3},{8,9},{9,8},{10,14... | collective-permute-start | bytes 602120 | tf_op jit(solution)/shard_map/ppermute | solution.py:563
  25.4 2.3 %collective-permute-start.10 = (bf16[784,128]{1,0:T(8,128)(2,1)S(1)}, bf16[784,128]{1,0:T(8,128)(2,1)S(1)}, u32[]{:S(2)}, u32[]{:S(2)}) collective-permute-start(bf16[784,128]{1,0:T(8,128)(2,1)S(1)} %collective-permute-done.2.refs_6_), channel_id=1, source_target_pairs={{0,4},{1,5},{2,3},{3,2},{4,0},{5,1},{6,7},{7,6},{8,12},{9,13},{10,... | collective-permute-start | bytes 602120 | tf_op jit(solution)/shard_map/ppermute | solution.py:563
  27.7 1.4 collective-permute-start.6
  29.1 0.9 collective-permute-done.12.refs_16_
  30.6 2.8 %collective-permute-done.10.refs_14_ = bf16[784,128]{1,0:T(8,128)(2,1)S(1)} collective-permute-done((bf16[784,128]{1,0:T(8,128)(2,1)S(1)}, bf16[784,128]{1,0:T(8,128)(2,1)S(1)}, u32[]{:S(2)}, u32[]{:S(2)}) %collective-permute-start.10) | collective-permute-done | bytes 200736 | tf_op jit(solution)/shard_map/ppermute | solution.py:563
  34.0 1.9 %collective-permute-start.13 = (bf16[784,128]{1,0:T(8,128)(2,1)S(1)}, bf16[784,128]{1,0:T(8,128)(2,1)S(1)}, u32[]{:S(2)}, u32[]{:S(2)}) collective-permute-start(bf16[784,128]{1,0:T(8,128)(2,1)S(1)} %collective-permute-done.9.refs_13_), channel_id=1, source_target_pairs={{0,1},{1,0},{2,6},{3,7},{4,5},{5,4},{6,2},{7,3},{8,9},{9,8},{10,14... | collective-permute-start | bytes 602120 | tf_op jit(solution)/shard_map/ppermute | solution.py:563
  37.1 2.6 %collective-permute-done.13.refs_17_ = bf16[784,128]{1,0:T(8,128)(2,1)S(1)} collective-permute-done((bf16[784,128]{1,0:T(8,128)(2,1)S(1)}, bf16[784,128]{1,0:T(8,128)(2,1)S(1)}, u32[]{:S(2)}, u32[]{:S(2)}) %collective-permute-start.13) | collective-permute-done | bytes 200736 | tf_op jit(solution)/shard_map/ppermute | solution.py:563
  40.8 1.5 collective-permute-done.14.refs_18_
  42.3 1.4 collective-permute-done.30.refs_34_
  44.4 61.6 %layer_core.1 = (f32[512,512]{1,0:T(8,128)}, f32[512,512]{1,0:T(8,128)}, bf16[16,784,128]{2,1,0:T(8,128)(2,1)}, bf16[4,784,128]{2,1,0:T(8,128)(2,1)}, bf16[4,784...) custom-call(bf16[512,512]{1,0:T(8,128)(2,1)} %bitcast.71, ...), custom_call_target="tpu_custom_call" | custom-call | tf_op jit(solution)/shard_map/layer_core/pallas_call | solution.py:546
  107.1 1.5 collective-permute-done.34
  108.6 1.0 fusion.16
  109.6 1.0 collective-permute-start.36
  110.6 1.0 fusion.2
  111.6 1.1 collective-permute-start.39
  112.8 1.0 fusion.3
  113.8 1.0 collective-permute-start.35
  114.8 1.0 fusion.1
  115.8 1.1 collective-permute-start.43
  117.1 1.6 %collective-permute-start.40 = (bf16[784,128]{1,0:T(8,128)(2,1)S(1)}, bf16[784,128]{1,0:T(8,128)(2,1)S(1)}, u32[]{:S(2)}, u32[]{:S(2)}) collective-permute-start(bf16[784,128]{1,0:T(8,128)(2,1)S(1)} %fusion.14), channel_id=1, source_target_pairs={{0,1},{1,0},{2,6},{3,7},{4,5},{5,4},{6,2},{7,3},{8,9},{9,8},{10,14... | collective-permute-start | bytes 602120 | tf_op jit(solution)/shard_map/ppermute | solution.py:563
  118.7 1.7 %collective-permute-done.35 = bf16[784,128]{1,0:T(8,128)(2,1)S(1)} collective-permute-done((bf16[784,128]{1,0:T(8,128)(2,1)S(1)}, bf16[784,128]{1,0:T(8,128)(2,1)S(1)}, u32[]{:S(2)}, u32[]{:S(2)}) %collective-permute-start.35) | collective-permute-done | bytes 200736 | tf_op jit(solution)/shard_map/ppermute | solution.py:563
  120.5 1.6 %collective-permute-start.44 = (bf16[784,128]{1,0:T(8,128)(2,1)S(1)}, bf16[784,128]{1,0:T(8,128)(2,1)S(1)}, u32[]{:S(2)}, u32[]{:S(2)}) collective-permute-start(bf16[784,128]{1,0:T(8,128)(2,1)S(1)} %fusion.15), channel_id=1, source_target_pairs={{0,1},{1,0},{2,6},{3,7},{4,5},{5,4},{6,2},{7,3},{8,9},{9,8},{10,14... | collective-permute-start | bytes 602120 | tf_op jit(solution)/shard_map/ppermute | solution.py:563
  122.2 1.5 collective-permute-start.38
  124.6 3.7 %collective-permute-start.42 = (bf16[784,128]{1,0:T(8,128)(2,1)S(1)}, bf16[784,128]{1,0:T(8,128)(2,1)S(1)}, u32[]{:S(2)}, u32[]{:S(2)}) collective-permute-start(bf16[784,128]{1,0:T(8,128)(2,1)S(1)} %fusion.7), channel_id=1, source_target_pairs={{0,16},{1,17},{2,10},{3,11},{4,20},{5,21},{6,14},{7,15},{8,24},{9,... | collective-permute-start | bytes 602120 | tf_op jit(solution)/shard_map/ppermute | solution.py:563
  128.4 2.0 %collective-permute-done.38 = bf16[2,784,128]{2,1,0:T(8,128)(2,1)S(1)} collective-permute-done((bf16[2,784,128]{2,1,0:T(8,128)(2,1)S(1)}, bf16[2,784,128]{2,1,0:T(8,128)(2,1)S(1)}, u32[]{:S(2)}, u32[]{:S(2)}) %collective-permute-start.38) | collective-permute-done | bytes 401440 | tf_op jit(solution)/shard_map/ppermute | solution.py:563
  130.5 1.6 %collective-permute-start.41 = (bf16[784,128]{1,0:T(8,128)(2,1)S(1)}, bf16[784,128]{1,0:T(8,128)(2,1)S(1)}, u32[]{:S(2)}, u32[]{:S(2)}) collective-permute-start(bf16[784,128]{1,0:T(8,128)(2,1)S(1)} %fusion.8), channel_id=1, source_target_pairs={{0,1},{1,0},{2,6},{3,7},{4,5},{5,4},{6,2},{7,3},{8,9},{9,8},{10,14... | collective-permute-start | bytes 602120 | tf_op jit(solution)/shard_map/ppermute | solution.py:563
  132.9 2.3 %collective-permute-start.47 = (bf16[784,128]{1,0:T(8,128)(2,1)}, bf16[784,128]{1,0:T(8,128)(2,1)S(1)}, u32[]{:S(2)}, u32[]{:S(2)}) collective-permute-start(bf16[784,128]{1,0:T(8,128)(2,1)} %fusion.5), channel_id=1, source_target_pairs={{0,16},{1,17},{2,10},{3,11},{4,20},{5,21},{6,14},{7,15},{8,24},{9,... | collective-permute-start | bytes 602120 | tf_op jit(solution)/shard_map/ppermute | solution.py:563
  135.2 1.5 %collective-permute-done.37 = bf16[2,784,128]{2,1,0:T(8,128)(2,1)S(1)} collective-permute-done((bf16[2,784,128]{2,1,0:T(8,128)(2,1)S(1)}, bf16[2,784,128]{2,1,0:T(8,128)(2,1)S(1)}, u32[]{:S(2)}, u32[]{:S(2)}) %collective-permute-start.37) | collective-permute-done | bytes 401440 | tf_op jit(solution)/shard_map/ppermute | solution.py:563
  136.7 0.8 fusion.10
  138.3 1.7 %collective-permute-start.45 = (bf16[784,128]{1,0:T(8,128)(2,1)}, bf16[784,128]{1,0:T(8,128)(2,1)}, u32[]{:S(2)}, u32[]{:S(2)}) collective-permute-start(bf16[784,128]{1,0:T(8,128)(2,1)} %fusion.11), channel_id=1, source_target_pairs={{0,1},{1,0},{2,6},{3,7},{4,5},{5,4},{6,2},{7,3},{8,9},{9,8},{10,14... | collective-permute-start | bytes 602120 | tf_op jit(solution)/shard_map/ppermute | solution.py:563
  140.0 2.3 %collective-permute-start.46 = (bf16[784,128]{1,0:T(8,128)(2,1)}, bf16[784,128]{1,0:T(8,128)(2,1)}, u32[]{:S(2)}, u32[]{:S(2)}) collective-permute-start(bf16[784,128]{1,0:T(8,128)(2,1)} %fusion.10), channel_id=1, source_target_pairs={{0,8},{1,9},{2,18},{3,19},{4,12},{5,13},{6,22},{7,23},{8,0},{9,1},... | collective-permute-start | bytes 602120 | tf_op jit(solution)/shard_map/ppermute | solution.py:563
  142.3 2.1 %collective-permute-done.45 = bf16[784,128]{1,0:T(8,128)(2,1)} collective-permute-done((bf16[784,128]{1,0:T(8,128)(2,1)}, bf16[784,128]{1,0:T(8,128)(2,1)}, u32[]{:S(2)}, u32[]{:S(2)}) %collective-permute-start.45) | collective-permute-done | bytes 200736 | tf_op jit(solution)/shard_map/ppermute | solution.py:563
  144.4 3.2 %collective-permute-done.46 = bf16[784,128]{1,0:T(8,128)(2,1)} collective-permute-done((bf16[784,128]{1,0:T(8,128)(2,1)}, bf16[784,128]{1,0:T(8,128)(2,1)}, u32[]{:S(2)}, u32[]{:S(2)}) %collective-permute-start.46) | collective-permute-done | bytes 200736 | tf_op jit(solution)/shard_map/ppermute | solution.py:563
  147.5 1.4 fusion.13
  149.4 2.6 %multiply_add_fusion = (f32[98496]{0:T(1024)}, f32[98496]{0:T(1024)}, f32[98496]{0:T(1024)}, f32[98496]{0:T(1024)}) fusion(f32[98496]{0:T(1024)} %param.11, f32[98496]{0:T(1024)} %param.9, f32[98496]{0:T(1024)} %param.10, f32[100352]{0:T(1024)S(1)} %bitcast.70, s32[]{:T(128)S(6)} %select_n.15), kind=kLoop, calls=%fused_computation.31 | loop fusion | flops 886464 | bytes 3151876 | tf_op jit(solution)/shard_map/add | solution.py:655
  (142 shorter events, 8.9 us)
Async XLA Ops:
  1.9 8.6 %collective-permute-start = (bf16[784,128]{1,0:T(8,128)(2,1)S(1)}, bf16[784,128]{1,0:T(8,128)(2,1)S(1)}, u32[]{:S(2)}, u32[]{:S(2)}) collective-permute-start(bf16[784,128]{1,0:T(8,128)(2,1)S(1)} %fusion.17.refs_3_), channel_id=1, source_target_pairs={{0,8},{1,9},{2,18},{3,19},{4,12},{5,13},{6,22},{7,23},{8,0},{9,1},... | collective-permute-start | bytes 602120 | tf_op jit(solution)/shard_map/ppermute | solution.py:563
  5.0 7.8 %collective-permute-start.7 = (bf16[784,128]{1,0:T(8,128)(2,1)S(1)}, bf16[784,128]{1,0:T(8,128)(2,1)S(1)}, u32[]{:S(2)}, u32[]{:S(2)}) collective-permute-start(bf16[784,128]{1,0:T(8,128)(2,1)S(1)} %fusion.17.refs_3_), channel_id=1, source_target_pairs={{0,4},{1,5},{2,3},{3,2},{4,0},{5,1},{6,7},{7,6},{8,12},{9,13},{10,... | collective-permute-start | bytes 602120 | tf_op jit(solution)/shard_map/ppermute | solution.py:563
  6.4 9.8 %collective-permute-start.3 = (bf16[784,128]{1,0:T(8,128)(2,1)S(1)}, bf16[784,128]{1,0:T(8,128)(2,1)S(1)}, u32[]{:S(2)}, u32[]{:S(2)}) collective-permute-start(bf16[784,128]{1,0:T(8,128)(2,1)S(1)} %fusion.17.refs_3_), channel_id=1, source_target_pairs={{0,1},{1,0},{2,6},{3,7},{4,5},{5,4},{6,2},{7,3},{8,9},{9,8},{10,14... | collective-permute-start | bytes 602120 | tf_op jit(solution)/shard_map/ppermute | solution.py:563
  10.4 7.1 %collective-permute-start.1 = (bf16[784,128]{1,0:T(8,128)(2,1)S(1)}, bf16[784,128]{1,0:T(8,128)(2,1)S(1)}, u32[]{:S(2)}, u32[]{:S(2)}) collective-permute-start(bf16[784,128]{1,0:T(8,128)(2,1)S(1)} %fusion.17.refs_3_), channel_id=1, source_target_pairs={{0,16},{1,17},{2,10},{3,11},{4,20},{5,21},{6,14},{7,15},{8,24},{9,... | collective-permute-start | bytes 602120 | tf_op jit(solution)/shard_map/ppermute | solution.py:563
  12.7 7.1 %collective-permute-start.11 = (bf16[784,128]{1,0:T(8,128)(2,1)S(1)}, bf16[784,128]{1,0:T(8,128)(2,1)S(1)}, u32[]{:S(2)}, u32[]{:S(2)}) collective-permute-start(bf16[784,128]{1,0:T(8,128)(2,1)S(1)} %collective-permute-done.7.refs_11_), channel_id=1, source_target_pairs={{0,1},{1,0},{2,6},{3,7},{4,5},{5,4},{6,2},{7,3},{8,9},{9,8},{10,14... | collective-permute-start | bytes 602120 | tf_op jit(solution)/shard_map/ppermute | solution.py:563
  14.3 6.7 %collective-permute-start.8 = (bf16[784,128]{1,0:T(8,128)(2,1)S(1)}, bf16[784,128]{1,0:T(8,128)(2,1)S(1)}, u32[]{:S(2)}, u32[]{:S(2)}) collective-permute-start(bf16[784,128]{1,0:T(8,128)(2,1)S(1)} %collective-permute-done.refs_4_), channel_id=1, source_target_pairs={{0,4},{1,5},{2,3},{3,2},{4,0},{5,1},{6,7},{7,6},{8,12},{9,13},{10,... | collective-permute-start | bytes 602120 | tf_op jit(solution)/shard_map/ppermute | solution.py:563
  15.8 7.5 %collective-permute-start.4 = (bf16[784,128]{1,0:T(8,128)(2,1)S(1)}, bf16[784,128]{1,0:T(8,128)(2,1)S(1)}, u32[]{:S(2)}, u32[]{:S(2)}) collective-permute-start(bf16[784,128]{1,0:T(8,128)(2,1)S(1)} %collective-permute-done.refs_4_), channel_id=1, source_target_pairs={{0,1},{1,0},{2,6},{3,7},{4,5},{5,4},{6,2},{7,3},{8,9},{9,8},{10,14... | collective-permute-start | bytes 602120 | tf_op jit(solution)/shard_map/ppermute | solution.py:563
  16.3 9.1 %collective-permute-start.2 = (bf16[784,128]{1,0:T(8,128)(2,1)S(1)}, bf16[784,128]{1,0:T(8,128)(2,1)S(1)}, u32[]{:S(2)}, u32[]{:S(2)}) collective-permute-start(bf16[784,128]{1,0:T(8,128)(2,1)S(1)} %collective-permute-done.refs_4_), channel_id=1, source_target_pairs={{0,16},{1,17},{2,10},{3,11},{4,20},{5,21},{6,14},{7,15},{8,24},{9,... | collective-permute-start | bytes 602120 | tf_op jit(solution)/shard_map/ppermute | solution.py:563
  17.5 7.8 %collective-permute-start.9 = (bf16[784,128]{1,0:T(8,128)(2,1)S(1)}, bf16[784,128]{1,0:T(8,128)(2,1)S(1)}, u32[]{:S(2)}, u32[]{:S(2)}) collective-permute-start(bf16[784,128]{1,0:T(8,128)(2,1)S(1)} %collective-permute-done.1.refs_5_), channel_id=1, source_target_pairs={{0,4},{1,5},{2,3},{3,2},{4,0},{5,1},{6,7},{7,6},{8,12},{9,13},{10,... | collective-permute-start | bytes 602120 | tf_op jit(solution)/shard_map/ppermute | solution.py:563
  19.8 7.9 %collective-permute-start.17 = (bf16[784,128]{1,0:T(8,128)(2,1)S(1)}, bf16[784,128]{1,0:T(8,128)(2,1)S(1)}, u32[]{:S(2)}, u32[]{:S(2)}) collective-permute-start(bf16[784,128]{1,0:T(8,128)(2,1)S(1)} %collective-permute-done.1.refs_5_), channel_id=1, source_target_pairs={{0,2},{1,3},{2,0},{3,1},{4,6},{5,7},{6,4},{7,5},{8,10},{9,11},{10,... | collective-permute-start | bytes 602120 | tf_op jit(solution)/shard_map/ppermute | solution.py:563
  21.0 8.2 %collective-permute-start.5 = (bf16[784,128]{1,0:T(8,128)(2,1)S(1)}, bf16[784,128]{1,0:T(8,128)(2,1)S(1)}, u32[]{:S(2)}, u32[]{:S(2)}) collective-permute-start(bf16[784,128]{1,0:T(8,128)(2,1)S(1)} %collective-permute-done.1.refs_5_), channel_id=1, source_target_pairs={{0,1},{1,0},{2,6},{3,7},{4,5},{5,4},{6,2},{7,3},{8,9},{9,8},{10,14... | collective-permute-start | bytes 602120 | tf_op jit(solution)/shard_map/ppermute | solution.py:563
  23.2 6.8 %collective-permute-start.12 = (bf16[784,128]{1,0:T(8,128)(2,1)S(1)}, bf16[784,128]{1,0:T(8,128)(2,1)S(1)}, u32[]{:S(2)}, u32[]{:S(2)}) collective-permute-start(bf16[784,128]{1,0:T(8,128)(2,1)S(1)} %collective-permute-done.8.refs_12_), channel_id=1, source_target_pairs={{0,1},{1,0},{2,6},{3,7},{4,5},{5,4},{6,2},{7,3},{8,9},{9,8},{10,14... | collective-permute-start | bytes 602120 | tf_op jit(solution)/shard_map/ppermute | solution.py:563
  25.4 4.7 %collective-permute-start.18 = (bf16[784,128]{1,0:T(8,128)(2,1)S(1)}, bf16[784,128]{1,0:T(8,128)(2,1)S(1)}, u32[]{:S(2)}, u32[]{:S(2)}) collective-permute-start(bf16[784,128]{1,0:T(8,128)(2,1)S(1)} %collective-permute-done.2.refs_6_), channel_id=1, source_target_pairs={{0,2},{1,3},{2,0},{3,1},{4,6},{5,7},{6,4},{7,5},{8,10},{9,11},{10,... | collective-permute-start | bytes 602120 | tf_op jit(solution)/shard_map/ppermute | solution.py:563
  25.4 8.0 %collective-permute-start.10 = (bf16[784,128]{1,0:T(8,128)(2,1)S(1)}, bf16[784,128]{1,0:T(8,128)(2,1)S(1)}, u32[]{:S(2)}, u32[]{:S(2)}) collective-permute-start(bf16[784,128]{1,0:T(8,128)(2,1)S(1)} %collective-permute-done.2.refs_6_), channel_id=1, source_target_pairs={{0,4},{1,5},{2,3},{3,2},{4,0},{5,1},{6,7},{7,6},{8,12},{9,13},{10,... | collective-permute-start | bytes 602120 | tf_op jit(solution)/shard_map/ppermute | solution.py:563
  27.7 5.7 %collective-permute-start.6 = (bf16[784,128]{1,0:T(8,128)(2,1)S(1)}, bf16[784,128]{1,0:T(8,128)(2,1)S(1)}, u32[]{:S(2)}, u32[]{:S(2)}) collective-permute-start(bf16[784,128]{1,0:T(8,128)(2,1)S(1)} %collective-permute-done.2.refs_6_), channel_id=1, source_target_pairs={{0,1},{1,0},{2,6},{3,7},{4,5},{5,4},{6,2},{7,3},{8,9},{9,8},{10,14... | collective-permute-start | bytes 602120 | tf_op jit(solution)/shard_map/ppermute | solution.py:563
  29.1 4.8 %collective-permute-start.15 = (bf16[784,128]{1,0:T(8,128)(2,1)S(1)}, bf16[784,128]{1,0:T(8,128)(2,1)S(1)}, u32[]{:S(2)}, u32[]{:S(2)}) collective-permute-start(bf16[784,128]{1,0:T(8,128)(2,1)S(1)} %fusion.17.refs_3_), channel_id=1, source_target_pairs={{0,2},{1,3},{2,0},{3,1},{4,6},{5,7},{6,4},{7,5},{8,10},{9,11},{10,... | collective-permute-start | bytes 602120 | tf_op jit(solution)/shard_map/ppermute | solution.py:563
  30.0 3.9 %collective-permute-start.16 = (bf16[784,128]{1,0:T(8,128)(2,1)S(1)}, bf16[784,128]{1,0:T(8,128)(2,1)S(1)}, u32[]{:S(2)}, u32[]{:S(2)}) collective-permute-start(bf16[784,128]{1,0:T(8,128)(2,1)S(1)} %collective-permute-done.refs_4_), channel_id=1, source_target_pairs={{0,2},{1,3},{2,0},{3,1},{4,6},{5,7},{6,4},{7,5},{8,10},{9,11},{10,... | collective-permute-start | bytes 602120 | tf_op jit(solution)/shard_map/ppermute | solution.py:563
  30.1 5.8 %collective-permute-start.19 = (bf16[784,128]{1,0:T(8,128)(2,1)S(1)}, bf16[784,128]{1,0:T(8,128)(2,1)S(1)}, u32[]{:S(2)}, u32[]{:S(2)}) collective-permute-start(bf16[784,128]{1,0:T(8,128)(2,1)S(1)} %collective-permute-done.3.refs_7_), channel_id=1, source_target_pairs={{0,2},{1,3},{2,0},{3,1},{4,6},{5,7},{6,4},{7,5},{8,10},{9,11},{10,... | collective-permute-start | bytes 602120 | tf_op jit(solution)/shard_map/ppermute | solution.py:563
  33.4 2.5 %collective-permute-start.23 = (bf16[784,128]{1,0:T(8,128)(2,1)S(1)}, bf16[784,128]{1,0:T(8,128)(2,1)S(1)}, u32[]{:S(2)}, u32[]{:S(2)}) collective-permute-start(bf16[784,128]{1,0:T(8,128)(2,1)S(1)} %collective-permute-done.7.refs_11_), channel_id=1, source_target_pairs={{0,2},{1,3},{2,0},{3,1},{4,6},{5,7},{6,4},{7,5},{8,10},{9,11},{10,... | collective-permute-start | bytes 602120 | tf_op jit(solution)/shard_map/ppermute | solution.py:563
  33.4 3.0 %collective-permute-start.27 = (bf16[784,128]{1,0:T(8,128)(2,1)S(1)}, bf16[784,128]{1,0:T(8,128)(2,1)S(1)}, u32[]{:S(2)}, u32[]{:S(2)}) collective-permute-start(bf16[784,128]{1,0:T(8,128)(2,1)S(1)} %collective-permute-done.11.refs_15_), channel_id=1, source_target_pairs={{0,2},{1,3},{2,0},{3,1},{4,6},{5,7},{6,4},{7,5},{8,10},{9,11},{10,... | collective-permute-start | bytes 602120 | tf_op jit(solution)/shard_map/ppermute | solution.py:563
  33.9 2.6 %collective-permute-start.25 = (bf16[784,128]{1,0:T(8,128)(2,1)S(1)}, bf16[784,128]{1,0:T(8,128)(2,1)S(1)}, u32[]{:S(2)}, u32[]{:S(2)}) collective-permute-start(bf16[784,128]{1,0:T(8,128)(2,1)S(1)} %collective-permute-done.9.refs_13_), channel_id=1, source_target_pairs={{0,2},{1,3},{2,0},{3,1},{4,6},{5,7},{6,4},{7,5},{8,10},{9,11},{10,... | collective-permute-start | bytes 602120 | tf_op jit(solution)/shard_map/ppermute | solution.py:563
  34.0 5.7 %collective-permute-start.13 = (bf16[784,128]{1,0:T(8,128)(2,1)S(1)}, bf16[784,128]{1,0:T(8,128)(2,1)S(1)}, u32[]{:S(2)}, u32[]{:S(2)}) collective-permute-start(bf16[784,128]{1,0:T(8,128)(2,1)S(1)} %collective-permute-done.9.refs_13_), channel_id=1, source_target_pairs={{0,1},{1,0},{2,6},{3,7},{4,5},{5,4},{6,2},{7,3},{8,9},{9,8},{10,14... | collective-permute-start | bytes 602120 | tf_op jit(solution)/shard_map/ppermute | solution.py:563
  35.9 3.8 %collective-permute-start.21 = (bf16[784,128]{1,0:T(8,128)(2,1)S(1)}, bf16[784,128]{1,0:T(8,128)(2,1)S(1)}, u32[]{:S(2)}, u32[]{:S(2)}) collective-permute-start(bf16[784,128]{1,0:T(8,128)(2,1)S(1)} %collective-permute-done.5.refs_9_), channel_id=1, source_target_pairs={{0,2},{1,3},{2,0},{3,1},{4,6},{5,7},{6,4},{7,5},{8,10},{9,11},{10,... | collective-permute-start | bytes 602120 | tf_op jit(solution)/shard_map/ppermute | solution.py:563
  35.9 4.3 %collective-permute-start.24 = (bf16[784,128]{1,0:T(8,128)(2,1)S(1)}, bf16[784,128]{1,0:T(8,128)(2,1)S(1)}, u32[]{:S(2)}, u32[]{:S(2)}) collective-permute-start(bf16[784,128]{1,0:T(8,128)(2,1)S(1)} %collective-permute-done.8.refs_12_), channel_id=1, source_target_pairs={{0,2},{1,3},{2,0},{3,1},{4,6},{5,7},{6,4},{7,5},{8,10},{9,11},{10,... | collective-permute-start | bytes 602120 | tf_op jit(solution)/shard_map/ppermute | solution.py:563
  36.4 3.9 %collective-permute-start.28 = (bf16[784,128]{1,0:T(8,128)(2,1)S(1)}, bf16[784,128]{1,0:T(8,128)(2,1)S(1)}, u32[]{:S(2)}, u32[]{:S(2)}) collective-permute-start(bf16[784,128]{1,0:T(8,128)(2,1)S(1)} %collective-permute-done.12.refs_16_), channel_id=1, source_target_pairs={{0,2},{1,3},{2,0},{3,1},{4,6},{5,7},{6,4},{7,5},{8,10},{9,11},{10,... | collective-permute-start | bytes 602120 | tf_op jit(solution)/shard_map/ppermute | solution.py:563
  36.5 5.7 %collective-permute-start.14 = (bf16[784,128]{1,0:T(8,128)(2,1)S(1)}, bf16[784,128]{1,0:T(8,128)(2,1)S(1)}, u32[]{:S(2)}, u32[]{:S(2)}) collective-permute-start(bf16[784,128]{1,0:T(8,128)(2,1)S(1)} %collective-permute-done.10.refs_14_), channel_id=1, source_target_pairs={{0,1},{1,0},{2,6},{3,7},{4,5},{5,4},{6,2},{7,3},{8,9},{9,8},{10,14... | collective-permute-start | bytes 602120 | tf_op jit(solution)/shard_map/ppermute | solution.py:563
  39.7 2.5 %collective-permute-start.20 = (bf16[784,128]{1,0:T(8,128)(2,1)S(1)}, bf16[784,128]{1,0:T(8,128)(2,1)S(1)}, u32[]{:S(2)}, u32[]{:S(2)}) collective-permute-start(bf16[784,128]{1,0:T(8,128)(2,1)S(1)} %collective-permute-done.4.refs_8_), channel_id=1, source_target_pairs={{0,2},{1,3},{2,0},{3,1},{4,6},{5,7},{6,4},{7,5},{8,10},{9,11},{10,... | collective-permute-start | bytes 602120 | tf_op jit(solution)/shard_map/ppermute | solution.py:563
  39.7 2.5 %collective-permute-start.26 = (bf16[784,128]{1,0:T(8,128)(2,1)S(1)}, bf16[784,128]{1,0:T(8,128)(2,1)S(1)}, u32[]{:S(2)}, u32[]{:S(2)}) collective-permute-start(bf16[784,128]{1,0:T(8,128)(2,1)S(1)} %collective-permute-done.10.refs_14_), channel_id=1, source_target_pairs={{0,2},{1,3},{2,0},{3,1},{4,6},{5,7},{6,4},{7,5},{8,10},{9,11},{10,... | collective-permute-start | bytes 602120 | tf_op jit(solution)/shard_map/ppermute | solution.py:563
  40.2 2.0 %collective-permute-start.22 = (bf16[784,128]{1,0:T(8,128)(2,1)S(1)}, bf16[784,128]{1,0:T(8,128)(2,1)S(1)}, u32[]{:S(2)}, u32[]{:S(2)}) collective-permute-start(bf16[784,128]{1,0:T(8,128)(2,1)S(1)} %collective-permute-done.6.refs_10_), channel_id=1, source_target_pairs={{0,2},{1,3},{2,0},{3,1},{4,6},{5,7},{6,4},{7,5},{8,10},{9,11},{10,... | collective-permute-start | bytes 602120 | tf_op jit(solution)/shard_map/ppermute | solution.py:563
  40.3 2.0 %collective-permute-start.29 = (bf16[784,128]{1,0:T(8,128)(2,1)S(1)}, bf16[784,128]{1,0:T(8,128)(2,1)S(1)}, u32[]{:S(2)}, u32[]{:S(2)}) collective-permute-start(bf16[784,128]{1,0:T(8,128)(2,1)S(1)} %collective-permute-done.13.refs_17_), channel_id=1, source_target_pairs={{0,2},{1,3},{2,0},{3,1},{4,6},{5,7},{6,4},{7,5},{8,10},{9,11},{10,... | collective-permute-start | bytes 602120 | tf_op jit(solution)/shard_map/ppermute | solution.py:563
  42.2 1.4 collective-permute-start.30
  106.0 2.6 %collective-permute-start.34 = (bf16[4,784,128]{2,1,0:T(8,128)(2,1)}, bf16[4,784,128]{2,1,0:T(8,128)(2,1)S(1)}, u32[]{:S(2)}, u32[]{:S(2)}) collective-permute-start(bf16[4,784,128]{2,1,0:T(8,128)(2,1)} %get-tuple-element.50), channel_id=1, source_target_pairs={{0,2},{1,3},{2,0},{3,1},{4,6},{5,7},{6,4},{7,5},{8,10},{9,11},{10,... | collective-permute-start | bytes 2408456 | tf_op jit(solution)/shard_map/ppermute | solution.py:563
  106.2 6.5 %collective-permute-start.33 = (bf16[4,784,128]{2,1,0:T(8,128)(2,1)}, bf16[4,784,128]{2,1,0:T(8,128)(2,1)S(1)}, u32[]{:S(2)}, u32[]{:S(2)}) collective-permute-start(bf16[4,784,128]{2,1,0:T(8,128)(2,1)} %get-tuple-element.49), channel_id=1, source_target_pairs={{0,2},{1,3},{2,0},{3,1},{4,6},{5,7},{6,4},{7,5},{8,10},{9,11},{10,... | collective-permute-start | bytes 2408456 | tf_op jit(solution)/shard_map/ppermute | solution.py:563
  106.6 9.2 %collective-permute-start.31 = (bf16[4,784,128]{2,1,0:T(8,128)(2,1)}, bf16[4,784,128]{2,1,0:T(8,128)(2,1)S(1)}, u32[]{:S(2)}, u32[]{:S(2)}) collective-permute-start(bf16[4,784,128]{2,1,0:T(8,128)(2,1)} %get-tuple-element.47), channel_id=1, source_target_pairs={{0,2},{1,3},{2,0},{3,1},{4,6},{5,7},{6,4},{7,5},{8,10},{9,11},{10,... | collective-permute-start | bytes 2408456 | tf_op jit(solution)/shard_map/ppermute | solution.py:563
  106.7 10.2 %collective-permute-start.32 = (bf16[4,784,128]{2,1,0:T(8,128)(2,1)}, bf16[4,784,128]{2,1,0:T(8,128)(2,1)S(1)}, u32[]{:S(2)}, u32[]{:S(2)}) collective-permute-start(bf16[4,784,128]{2,1,0:T(8,128)(2,1)} %get-tuple-element.48), channel_id=1, source_target_pairs={{0,2},{1,3},{2,0},{3,1},{4,6},{5,7},{6,4},{7,5},{8,10},{9,11},{10,... | collective-permute-start | bytes 2408456 | tf_op jit(solution)/shard_map/ppermute | solution.py:563
  109.6 7.4 %collective-permute-start.36 = (bf16[784,128]{1,0:T(8,128)(2,1)S(1)}, bf16[784,128]{1,0:T(8,128)(2,1)S(1)}, u32[]{:S(2)}, u32[]{:S(2)}) collective-permute-start(bf16[784,128]{1,0:T(8,128)(2,1)S(1)} %fusion.16), channel_id=1, source_target_pairs={{0,4},{1,5},{2,3},{3,2},{4,0},{5,1},{6,7},{7,6},{8,12},{9,13},{10,... | collective-permute-start | bytes 602120 | tf_op jit(solution)/shard_map/ppermute | solution.py:563
  111.6 12.9 %collective-permute-start.39 = (bf16[784,128]{1,0:T(8,128)(2,1)S(1)}, bf16[784,128]{1,0:T(8,128)(2,1)S(1)}, u32[]{:S(2)}, u32[]{:S(2)}) collective-permute-start(bf16[784,128]{1,0:T(8,128)(2,1)S(1)} %fusion.2), channel_id=1, source_target_pairs={{0,4},{1,5},{2,3},{3,2},{4,0},{5,1},{6,7},{7,6},{8,12},{9,13},{10,... | collective-permute-start | bytes 602120 | tf_op jit(solution)/shard_map/ppermute | solution.py:563
  113.8 6.7 %collective-permute-start.35 = (bf16[784,128]{1,0:T(8,128)(2,1)S(1)}, bf16[784,128]{1,0:T(8,128)(2,1)S(1)}, u32[]{:S(2)}, u32[]{:S(2)}) collective-permute-start(bf16[784,128]{1,0:T(8,128)(2,1)S(1)} %fusion.3), channel_id=1, source_target_pairs={{0,4},{1,5},{2,3},{3,2},{4,0},{5,1},{6,7},{7,6},{8,12},{9,13},{10,... | collective-permute-start | bytes 602120 | tf_op jit(solution)/shard_map/ppermute | solution.py:563
  115.8 16.3 %collective-permute-start.43 = (bf16[784,128]{1,0:T(8,128)(2,1)S(1)}, bf16[784,128]{1,0:T(8,128)(2,1)S(1)}, u32[]{:S(2)}, u32[]{:S(2)}) collective-permute-start(bf16[784,128]{1,0:T(8,128)(2,1)S(1)} %fusion.1), channel_id=1, source_target_pairs={{0,4},{1,5},{2,3},{3,2},{4,0},{5,1},{6,7},{7,6},{8,12},{9,13},{10,... | collective-permute-start | bytes 602120 | tf_op jit(solution)/shard_map/ppermute | solution.py:563
  117.1 6.9 %collective-permute-start.40 = (bf16[784,128]{1,0:T(8,128)(2,1)S(1)}, bf16[784,128]{1,0:T(8,128)(2,1)S(1)}, u32[]{:S(2)}, u32[]{:S(2)}) collective-permute-start(bf16[784,128]{1,0:T(8,128)(2,1)S(1)} %fusion.14), channel_id=1, source_target_pairs={{0,1},{1,0},{2,6},{3,7},{4,5},{5,4},{6,2},{7,3},{8,9},{9,8},{10,14... | collective-permute-start | bytes 602120 | tf_op jit(solution)/shard_map/ppermute | solution.py:563
  120.5 11.6 %collective-permute-start.44 = (bf16[784,128]{1,0:T(8,128)(2,1)S(1)}, bf16[784,128]{1,0:T(8,128)(2,1)S(1)}, u32[]{:S(2)}, u32[]{:S(2)}) collective-permute-start(bf16[784,128]{1,0:T(8,128)(2,1)S(1)} %fusion.15), channel_id=1, source_target_pairs={{0,1},{1,0},{2,6},{3,7},{4,5},{5,4},{6,2},{7,3},{8,9},{9,8},{10,14... | collective-permute-start | bytes 602120 | tf_op jit(solution)/shard_map/ppermute | solution.py:563
  122.2 8.2 %collective-permute-start.38 = (bf16[2,784,128]{2,1,0:T(8,128)(2,1)S(1)}, bf16[2,784,128]{2,1,0:T(8,128)(2,1)S(1)}, u32[]{:S(2)}, u32[]{:S(2)}) collective-permute-start(bf16[2,784,128]{2,1,0:T(8,128)(2,1)S(1)} %add_convert_fusion.1), channel_id=1, source_target_pairs={{0,4},{1,5},{2,3},{3,2},{4,0},{5,1},{6,7},{7,6},{8,12},{9,13},{10,... | collective-permute-start | bytes 1204232 | tf_op jit(solution)/shard_map/ppermute | solution.py:563
  124.0 12.7 %collective-permute-start.37 = (bf16[2,784,128]{2,1,0:T(8,128)(2,1)S(1)}, bf16[2,784,128]{2,1,0:T(8,128)(2,1)S(1)}, u32[]{:S(2)}, u32[]{:S(2)}) collective-permute-start(bf16[2,784,128]{2,1,0:T(8,128)(2,1)S(1)} %add_convert_fusion), channel_id=1, source_target_pairs={{0,4},{1,5},{2,3},{3,2},{4,0},{5,1},{6,7},{7,6},{8,12},{9,13},{10,... | collective-permute-start | bytes 1204232 | tf_op jit(solution)/shard_map/ppermute | solution.py:563
  124.6 10.5 %collective-permute-start.42 = (bf16[784,128]{1,0:T(8,128)(2,1)S(1)}, bf16[784,128]{1,0:T(8,128)(2,1)S(1)}, u32[]{:S(2)}, u32[]{:S(2)}) collective-permute-start(bf16[784,128]{1,0:T(8,128)(2,1)S(1)} %fusion.7), channel_id=1, source_target_pairs={{0,16},{1,17},{2,10},{3,11},{4,20},{5,21},{6,14},{7,15},{8,24},{9,... | collective-permute-start | bytes 602120 | tf_op jit(solution)/shard_map/ppermute | solution.py:563
  130.5 6.2 %collective-permute-start.41 = (bf16[784,128]{1,0:T(8,128)(2,1)S(1)}, bf16[784,128]{1,0:T(8,128)(2,1)S(1)}, u32[]{:S(2)}, u32[]{:S(2)}) collective-permute-start(bf16[784,128]{1,0:T(8,128)(2,1)S(1)} %fusion.8), channel_id=1, source_target_pairs={{0,1},{1,0},{2,6},{3,7},{4,5},{5,4},{6,2},{7,3},{8,9},{9,8},{10,14... | collective-permute-start | bytes 602120 | tf_op jit(solution)/shard_map/ppermute | solution.py:563
  132.9 9.4 %collective-permute-start.47 = (bf16[784,128]{1,0:T(8,128)(2,1)}, bf16[784,128]{1,0:T(8,128)(2,1)S(1)}, u32[]{:S(2)}, u32[]{:S(2)}) collective-permute-start(bf16[784,128]{1,0:T(8,128)(2,1)} %fusion.5), channel_id=1, source_target_pairs={{0,16},{1,17},{2,10},{3,11},{4,20},{5,21},{6,14},{7,15},{8,24},{9,... | collective-permute-start | bytes 602120 | tf_op jit(solution)/shard_map/ppermute | solution.py:563
  138.3 6.0 %collective-permute-start.45 = (bf16[784,128]{1,0:T(8,128)(2,1)}, bf16[784,128]{1,0:T(8,128)(2,1)}, u32[]{:S(2)}, u32[]{:S(2)}) collective-permute-start(bf16[784,128]{1,0:T(8,128)(2,1)} %fusion.11), channel_id=1, source_target_pairs={{0,1},{1,0},{2,6},{3,7},{4,5},{5,4},{6,2},{7,3},{8,9},{9,8},{10,14... | collective-permute-start | bytes 602120 | tf_op jit(solution)/shard_map/ppermute | solution.py:563
  140.0 7.5 %collective-permute-start.46 = (bf16[784,128]{1,0:T(8,128)(2,1)}, bf16[784,128]{1,0:T(8,128)(2,1)}, u32[]{:S(2)}, u32[]{:S(2)}) collective-permute-start(bf16[784,128]{1,0:T(8,128)(2,1)} %fusion.10), channel_id=1, source_target_pairs={{0,8},{1,9},{2,18},{3,19},{4,12},{5,13},{6,22},{7,23},{8,0},{9,1},... | collective-permute-start | bytes 602120 | tf_op jit(solution)/shard_map/ppermute | solution.py:563
  (35 other events, 452.3 us)

commit v7 on v6

--- a/solution.py
+++ b/solution.py
@@ -68,7 +68,7 @@
                 ref[pl.ds(row, 2 * n), cols] = jnp.concatenate([piece[:, :LANES], piece[:, LANES:]], axis=0)
             return carry
 
-        lax.fori_loop(0, ref.shape[0] * per // 512, body, 0, unroll=8)
+        lax.fori_loop(0, ref.shape[0] * per // 512, body, 0, unroll=16)
     per_out = width // LANES
     tail = flat[flat.shape[0] - FF // LANES - 8 * per_out : flat.shape[0], :].astype(F32)
     for c in range(FF // LANES):
@@ -96,7 +96,7 @@
             flat[pl.ds(first + 256, 256), :] = out[:, LANES:]
             return carry
 
-        lax.fori_loop(0, ref.shape[0] * per // 512, body, 0, unroll=8)
+        lax.fori_loop(0, ref.shape[0] * per // 512, body, 0, unroll=16)
 
 
 def norm_stats(resid):
@@ -469,13 +469,23 @@
         dx_ref[...] = dr1[...] + dot_t(d3, wa[:, : 3 * D])
 
     def forward(r, carry):
-        for part in (project, attend, feed):
-            phase(functools.partial(part, r))
+        def first():
+            project(r)
+            attend(r)
+
+        phase(first)
+        phase(functools.partial(feed, r))
         return carry
 
     def backward(i, carry):
-        for part in (feed_back, attend_back, project_back):
-            phase(functools.partial(part, REC - 1 - i))
+        r = REC - 1 - i
+
+        def second():
+            attend_back(r)
+            project_back(r)
+
+        phase(functools.partial(feed_back, r))
+        phase(second)
         return carry
 
     lax.fori_loop(0, REC, forward, 0)
@@ -504,9 +514,12 @@
             cols = slice(c * CHUNK, (c + 1) * CHUNK)
             wo[cols, :] = t_dot(get(0, c, 0, REC * T), df[...]).astype(BF)
 
-    phase(grad_qkvo)
-    phase(grad_in)
-    phase(grad_out)
+    def grads():
+        grad_qkvo()
+        grad_in()
+        grad_out()
+
+    phase(grads)
     pack_weights(flat, wa, wi, wo, D)
     per_out = D // LANES
     rows = [gb1[0:1, c * LANES : (c + 1) * LANES] for c in range(FF // LANES)]

time: 152 us -> 149 us (0.980)
  Pallas kernels: 61.6 us -> 58.2 us
    pallas_call x1, Pallas kernels: 61.6 us -> 58.2 us  [core(): pl.pallas_call(functools.partial(core_kernel, width=D, length=T, shards=s...]
where the time goes in v7:
time: 149 us
  Pallas kernels  58.2 us (39%)
  starting transfers between devices  49.7 us (33%)
  waiting for transfers between devices  26.3 us (18%)
  other arithmetic  10.9 us (7%)
  local copies, waits for them, and re-layouts  2.36 us (2%)
    pallas_call x1, Pallas kernels, core(): pl.pallas_call(functools.partial(core_kernel, width=D, length=T, shards=s...  58.2 us
    ppermute x48, starting transfers between devices, exchange(): lax.ppermute(v, AXES, [(j, j ^ (one if j // RC & 1 else zero)) for j in r...  49.7 us
    ppermute x48, waiting for transfers between devices, exchange(): lax.ppermute(v, AXES, [(j, j ^ (one if j // RC & 1 else zero)) for j in r...  26.3 us
    convert_element_type x13, other arithmetic, total(): return v.astype(BF)  6.89 us
  transfers between devices with their start and end apart: 48, of which 15 were waited for; matrix products, arithmetic and copies ran while one was open for 5% of the time, Pallas kernels for 0%

profile of v7, /device:TPU:0, one launch (start us, length us, event | category | flops | bytes accessed | tf_op | source)
XLA Modules:
  0.0 148.6 jit_solution(4250978613381134023)
XLA Ops:
  0.7 1.2 fusion.17.refs_3_
  1.9 3.1 %collective-permute-start = (bf16[784,128]{1,0:T(8,128)(2,1)S(1)}, bf16[784,128]{1,0:T(8,128)(2,1)S(1)}, u32[]{:S(2)}, u32[]{:S(2)}) collective-permute-start(bf16[784,128]{1,0:T(8,128)(2,1)S(1)} %fusion.17.refs_3_), channel_id=1, source_target_pairs={{0,8},{1,9},{2,18},{3,19},{4,12},{5,13},{6,22},{7,23},{8,0},{9,1},... | collective-permute-start | bytes 602120 | tf_op jit(solution)/shard_map/ppermute | solution.py:576
  5.0 1.5 %collective-permute-start.7 = (bf16[784,128]{1,0:T(8,128)(2,1)S(1)}, bf16[784,128]{1,0:T(8,128)(2,1)S(1)}, u32[]{:S(2)}, u32[]{:S(2)}) collective-permute-start(bf16[784,128]{1,0:T(8,128)(2,1)S(1)} %fusion.17.refs_3_), channel_id=1, source_target_pairs={{0,4},{1,5},{2,3},{3,2},{4,0},{5,1},{6,7},{7,6},{8,12},{9,13},{10,... | collective-permute-start | bytes 602120 | tf_op jit(solution)/shard_map/ppermute | solution.py:576
  6.4 1.5 %collective-permute-start.3 = (bf16[784,128]{1,0:T(8,128)(2,1)S(1)}, bf16[784,128]{1,0:T(8,128)(2,1)S(1)}, u32[]{:S(2)}, u32[]{:S(2)}) collective-permute-start(bf16[784,128]{1,0:T(8,128)(2,1)S(1)} %fusion.17.refs_3_), channel_id=1, source_target_pairs={{0,1},{1,0},{2,6},{3,7},{4,5},{5,4},{6,2},{7,3},{8,9},{9,8},{10,14... | collective-permute-start | bytes 602120 | tf_op jit(solution)/shard_map/ppermute | solution.py:576
  8.0 2.5 %collective-permute-done.refs_4_ = bf16[784,128]{1,0:T(8,128)(2,1)S(1)} collective-permute-done((bf16[784,128]{1,0:T(8,128)(2,1)S(1)}, bf16[784,128]{1,0:T(8,128)(2,1)S(1)}, u32[]{:S(2)}, u32[]{:S(2)}) %collective-permute-start) | collective-permute-done | bytes 200736 | tf_op jit(solution)/shard_map/ppermute | solution.py:576
  10.4 2.3 %collective-permute-start.1 = (bf16[784,128]{1,0:T(8,128)(2,1)S(1)}, bf16[784,128]{1,0:T(8,128)(2,1)S(1)}, u32[]{:S(2)}, u32[]{:S(2)}) collective-permute-start(bf16[784,128]{1,0:T(8,128)(2,1)S(1)} %fusion.17.refs_3_), channel_id=1, source_target_pairs={{0,16},{1,17},{2,10},{3,11},{4,20},{5,21},{6,14},{7,15},{8,24},{9,... | collective-permute-start | bytes 602120 | tf_op jit(solution)/shard_map/ppermute | solution.py:576
  12.7 1.5 %collective-permute-start.11 = (bf16[784,128]{1,0:T(8,128)(2,1)S(1)}, bf16[784,128]{1,0:T(8,128)(2,1)S(1)}, u32[]{:S(2)}, u32[]{:S(2)}) collective-permute-start(bf16[784,128]{1,0:T(8,128)(2,1)S(1)} %collective-permute-done.7.refs_11_), channel_id=1, source_target_pairs={{0,1},{1,0},{2,6},{3,7},{4,5},{5,4},{6,2},{7,3},{8,9},{9,8},{10,14... | collective-permute-start | bytes 602120 | tf_op jit(solution)/shard_map/ppermute | solution.py:576
  14.3 1.5 %collective-permute-start.8 = (bf16[784,128]{1,0:T(8,128)(2,1)S(1)}, bf16[784,128]{1,0:T(8,128)(2,1)S(1)}, u32[]{:S(2)}, u32[]{:S(2)}) collective-permute-start(bf16[784,128]{1,0:T(8,128)(2,1)S(1)} %collective-permute-done.refs_4_), channel_id=1, source_target_pairs={{0,4},{1,5},{2,3},{3,2},{4,0},{5,1},{6,7},{7,6},{8,12},{9,13},{10,... | collective-permute-start | bytes 602120 | tf_op jit(solution)/shard_map/ppermute | solution.py:576
  16.3 1.3 collective-permute-start.2
  17.5 2.3 %collective-permute-start.9 = (bf16[784,128]{1,0:T(8,128)(2,1)S(1)}, bf16[784,128]{1,0:T(8,128)(2,1)S(1)}, u32[]{:S(2)}, u32[]{:S(2)}) collective-permute-start(bf16[784,128]{1,0:T(8,128)(2,1)S(1)} %collective-permute-done.1.refs_5_), channel_id=1, source_target_pairs={{0,4},{1,5},{2,3},{3,2},{4,0},{5,1},{6,7},{7,6},{8,12},{9,13},{10,... | collective-permute-start | bytes 602120 | tf_op jit(solution)/shard_map/ppermute | solution.py:576
  19.8 1.1 collective-permute-done.8.refs_12_
  21.0 1.1 collective-permute-start.5
  22.1 1.2 collective-permute-done.4.refs_8_
  23.2 2.1 %collective-permute-start.12 = (bf16[784,128]{1,0:T(8,128)(2,1)S(1)}, bf16[784,128]{1,0:T(8,128)(2,1)S(1)}, u32[]{:S(2)}, u32[]{:S(2)}) collective-permute-start(bf16[784,128]{1,0:T(8,128)(2,1)S(1)} %collective-permute-done.8.refs_12_), channel_id=1, source_target_pairs={{0,1},{1,0},{2,6},{3,7},{4,5},{5,4},{6,2},{7,3},{8,9},{9,8},{10,14... | collective-permute-start | bytes 602120 | tf_op jit(solution)/shard_map/ppermute | solution.py:576
  25.4 2.3 %collective-permute-start.10 = (bf16[784,128]{1,0:T(8,128)(2,1)S(1)}, bf16[784,128]{1,0:T(8,128)(2,1)S(1)}, u32[]{:S(2)}, u32[]{:S(2)}) collective-permute-start(bf16[784,128]{1,0:T(8,128)(2,1)S(1)} %collective-permute-done.2.refs_6_), channel_id=1, source_target_pairs={{0,4},{1,5},{2,3},{3,2},{4,0},{5,1},{6,7},{7,6},{8,12},{9,13},{10,... | collective-permute-start | bytes 602120 | tf_op jit(solution)/shard_map/ppermute | solution.py:576
  27.7 1.4 collective-permute-start.6
  29.1 0.9 collective-permute-done.12.refs_16_
  30.6 2.8 %collective-permute-done.10.refs_14_ = bf16[784,128]{1,0:T(8,128)(2,1)S(1)} collective-permute-done((bf16[784,128]{1,0:T(8,128)(2,1)S(1)}, bf16[784,128]{1,0:T(8,128)(2,1)S(1)}, u32[]{:S(2)}, u32[]{:S(2)}) %collective-permute-start.10) | collective-permute-done | bytes 200736 | tf_op jit(solution)/shard_map/ppermute | solution.py:576
  34.0 1.9 %collective-permute-start.13 = (bf16[784,128]{1,0:T(8,128)(2,1)S(1)}, bf16[784,128]{1,0:T(8,128)(2,1)S(1)}, u32[]{:S(2)}, u32[]{:S(2)}) collective-permute-start(bf16[784,128]{1,0:T(8,128)(2,1)S(1)} %collective-permute-done.9.refs_13_), channel_id=1, source_target_pairs={{0,1},{1,0},{2,6},{3,7},{4,5},{5,4},{6,2},{7,3},{8,9},{9,8},{10,14... | collective-permute-start | bytes 602120 | tf_op jit(solution)/shard_map/ppermute | solution.py:576
  37.1 2.6 %collective-permute-done.13.refs_17_ = bf16[784,128]{1,0:T(8,128)(2,1)S(1)} collective-permute-done((bf16[784,128]{1,0:T(8,128)(2,1)S(1)}, bf16[784,128]{1,0:T(8,128)(2,1)S(1)}, u32[]{:S(2)}, u32[]{:S(2)}) %collective-permute-start.13) | collective-permute-done | bytes 200736 | tf_op jit(solution)/shard_map/ppermute | solution.py:576
  40.8 1.5 collective-permute-done.14.refs_18_
  42.3 1.4 collective-permute-done.30.refs_34_
  44.4 58.2 %layer_core.1 = (f32[512,512]{1,0:T(8,128)}, f32[512,512]{1,0:T(8,128)}, bf16[16,784,128]{2,1,0:T(8,128)(2,1)}, bf16[4,784,128]{2,1,0:T(8,128)(2,1)}, bf16[4,784...) custom-call(bf16[512,512]{1,0:T(8,128)(2,1)} %bitcast.71, ...), custom_call_target="tpu_custom_call" | custom-call | tf_op jit(solution)/shard_map/layer_core/pallas_call | solution.py:559
  103.6 1.5 %collective-permute-done.34 = bf16[4,784,128]{2,1,0:T(8,128)(2,1)S(1)} collective-permute-done((bf16[4,784,128]{2,1,0:T(8,128)(2,1)}, bf16[4,784,128]{2,1,0:T(8,128)(2,1)S(1)}, u32[]{:S(2)}, u32[]{:S(2)}) %collective-permute-start.34) | collective-permute-done | bytes 802848 | tf_op jit(solution)/shard_map/ppermute | solution.py:576
  105.1 1.0 fusion.16
  106.1 1.0 collective-permute-start.36
  107.1 1.0 fusion.2
  108.1 1.1 collective-permute-start.39
  109.3 1.0 fusion.3
  110.3 1.0 collective-permute-start.35
  111.3 1.0 fusion.1
  112.3 1.1 collective-permute-start.43
  113.7 1.6 %collective-permute-start.40 = (bf16[784,128]{1,0:T(8,128)(2,1)S(1)}, bf16[784,128]{1,0:T(8,128)(2,1)S(1)}, u32[]{:S(2)}, u32[]{:S(2)}) collective-permute-start(bf16[784,128]{1,0:T(8,128)(2,1)S(1)} %fusion.14), channel_id=1, source_target_pairs={{0,1},{1,0},{2,6},{3,7},{4,5},{5,4},{6,2},{7,3},{8,9},{9,8},{10,14... | collective-permute-start | bytes 602120 | tf_op jit(solution)/shard_map/ppermute | solution.py:576
  115.2 1.7 %collective-permute-done.35 = bf16[784,128]{1,0:T(8,128)(2,1)S(1)} collective-permute-done((bf16[784,128]{1,0:T(8,128)(2,1)S(1)}, bf16[784,128]{1,0:T(8,128)(2,1)S(1)}, u32[]{:S(2)}, u32[]{:S(2)}) %collective-permute-start.35) | collective-permute-done | bytes 200736 | tf_op jit(solution)/shard_map/ppermute | solution.py:576
  117.1 1.6 %collective-permute-start.44 = (bf16[784,128]{1,0:T(8,128)(2,1)S(1)}, bf16[784,128]{1,0:T(8,128)(2,1)S(1)}, u32[]{:S(2)}, u32[]{:S(2)}) collective-permute-start(bf16[784,128]{1,0:T(8,128)(2,1)S(1)} %fusion.15), channel_id=1, source_target_pairs={{0,1},{1,0},{2,6},{3,7},{4,5},{5,4},{6,2},{7,3},{8,9},{9,8},{10,14... | collective-permute-start | bytes 602120 | tf_op jit(solution)/shard_map/ppermute | solution.py:576
  118.8 1.5 %collective-permute-start.38 = (bf16[2,784,128]{2,1,0:T(8,128)(2,1)S(1)}, bf16[2,784,128]{2,1,0:T(8,128)(2,1)S(1)}, u32[]{:S(2)}, u32[]{:S(2)}) collective-permute-start(bf16[2,784,128]{2,1,0:T(8,128)(2,1)S(1)} %add_convert_fusion.1), channel_id=1, source_target_pairs={{0,4},{1,5},{2,3},{3,2},{4,0},{5,1},{6,7},{7,6},{8,12},{9,13},{10,... | collective-permute-start | bytes 1204232 | tf_op jit(solution)/shard_map/ppermute | solution.py:576
  121.1 3.8 %collective-permute-start.42 = (bf16[784,128]{1,0:T(8,128)(2,1)S(1)}, bf16[784,128]{1,0:T(8,128)(2,1)S(1)}, u32[]{:S(2)}, u32[]{:S(2)}) collective-permute-start(bf16[784,128]{1,0:T(8,128)(2,1)S(1)} %fusion.7), channel_id=1, source_target_pairs={{0,16},{1,17},{2,10},{3,11},{4,20},{5,21},{6,14},{7,15},{8,24},{9,... | collective-permute-start | bytes 602120 | tf_op jit(solution)/shard_map/ppermute | solution.py:576
  124.9 2.0 %collective-permute-done.38 = bf16[2,784,128]{2,1,0:T(8,128)(2,1)S(1)} collective-permute-done((bf16[2,784,128]{2,1,0:T(8,128)(2,1)S(1)}, bf16[2,784,128]{2,1,0:T(8,128)(2,1)S(1)}, u32[]{:S(2)}, u32[]{:S(2)}) %collective-permute-start.38) | collective-permute-done | bytes 401440 | tf_op jit(solution)/shard_map/ppermute | solution.py:576
  127.1 1.6 %collective-permute-start.41 = (bf16[784,128]{1,0:T(8,128)(2,1)S(1)}, bf16[784,128]{1,0:T(8,128)(2,1)S(1)}, u32[]{:S(2)}, u32[]{:S(2)}) collective-permute-start(bf16[784,128]{1,0:T(8,128)(2,1)S(1)} %fusion.8), channel_id=1, source_target_pairs={{0,1},{1,0},{2,6},{3,7},{4,5},{5,4},{6,2},{7,3},{8,9},{9,8},{10,14... | collective-permute-start | bytes 602120 | tf_op jit(solution)/shard_map/ppermute | solution.py:576
  129.4 2.3 %collective-permute-start.47 = (bf16[784,128]{1,0:T(8,128)(2,1)}, bf16[784,128]{1,0:T(8,128)(2,1)S(1)}, u32[]{:S(2)}, u32[]{:S(2)}) collective-permute-start(bf16[784,128]{1,0:T(8,128)(2,1)} %fusion.5), channel_id=1, source_target_pairs={{0,16},{1,17},{2,10},{3,11},{4,20},{5,21},{6,14},{7,15},{8,24},{9,... | collective-permute-start | bytes 602120 | tf_op jit(solution)/shard_map/ppermute | solution.py:576
  131.7 1.5 %collective-permute-done.37 = bf16[2,784,128]{2,1,0:T(8,128)(2,1)S(1)} collective-permute-done((bf16[2,784,128]{2,1,0:T(8,128)(2,1)S(1)}, bf16[2,784,128]{2,1,0:T(8,128)(2,1)S(1)}, u32[]{:S(2)}, u32[]{:S(2)}) %collective-permute-start.37) | collective-permute-done | bytes 401440 | tf_op jit(solution)/shard_map/ppermute | solution.py:576
  133.3 0.8 fusion.10
  134.9 1.7 %collective-permute-start.45 = (bf16[784,128]{1,0:T(8,128)(2,1)}, bf16[784,128]{1,0:T(8,128)(2,1)}, u32[]{:S(2)}, u32[]{:S(2)}) collective-permute-start(bf16[784,128]{1,0:T(8,128)(2,1)} %fusion.11), channel_id=1, source_target_pairs={{0,1},{1,0},{2,6},{3,7},{4,5},{5,4},{6,2},{7,3},{8,9},{9,8},{10,14... | collective-permute-start | bytes 602120 | tf_op jit(solution)/shard_map/ppermute | solution.py:576
  136.5 2.3 %collective-permute-start.46 = (bf16[784,128]{1,0:T(8,128)(2,1)}, bf16[784,128]{1,0:T(8,128)(2,1)}, u32[]{:S(2)}, u32[]{:S(2)}) collective-permute-start(bf16[784,128]{1,0:T(8,128)(2,1)} %fusion.10), channel_id=1, source_target_pairs={{0,8},{1,9},{2,18},{3,19},{4,12},{5,13},{6,22},{7,23},{8,0},{9,1},... | collective-permute-start | bytes 602120 | tf_op jit(solution)/shard_map/ppermute | solution.py:576
  138.8 2.1 %collective-permute-done.45 = bf16[784,128]{1,0:T(8,128)(2,1)} collective-permute-done((bf16[784,128]{1,0:T(8,128)(2,1)}, bf16[784,128]{1,0:T(8,128)(2,1)}, u32[]{:S(2)}, u32[]{:S(2)}) %collective-permute-start.45) | collective-permute-done | bytes 200736 | tf_op jit(solution)/shard_map/ppermute | solution.py:576
  140.9 3.2 %collective-permute-done.46 = bf16[784,128]{1,0:T(8,128)(2,1)} collective-permute-done((bf16[784,128]{1,0:T(8,128)(2,1)}, bf16[784,128]{1,0:T(8,128)(2,1)}, u32[]{:S(2)}, u32[]{:S(2)}) %collective-permute-start.46) | collective-permute-done | bytes 200736 | tf_op jit(solution)/shard_map/ppermute | solution.py:576
  144.1 1.4 fusion.13
  146.0 2.6 %multiply_add_fusion = (f32[98496]{0:T(1024)}, f32[98496]{0:T(1024)}, f32[98496]{0:T(1024)}, f32[98496]{0:T(1024)}) fusion(f32[98496]{0:T(1024)} %param.11, f32[98496]{0:T(1024)} %param.9, f32[98496]{0:T(1024)} %param.10, f32[100352]{0:T(1024)S(1)} %bitcast.70, s32[]{:T(128)S(6)} %select_n.15), kind=kLoop, calls=%fused_computation.31 | loop fusion | flops 886464 | bytes 3151876 | tf_op jit(solution)/shard_map/add | solution.py:668
  (142 shorter events, 8.9 us)
Async XLA Ops:
  1.9 8.6 %collective-permute-start = (bf16[784,128]{1,0:T(8,128)(2,1)S(1)}, bf16[784,128]{1,0:T(8,128)(2,1)S(1)}, u32[]{:S(2)}, u32[]{:S(2)}) collective-permute-start(bf16[784,128]{1,0:T(8,128)(2,1)S(1)} %fusion.17.refs_3_), channel_id=1, source_target_pairs={{0,8},{1,9},{2,18},{3,19},{4,12},{5,13},{6,22},{7,23},{8,0},{9,1},... | collective-permute-start | bytes 602120 | tf_op jit(solution)/shard_map/ppermute | solution.py:576
  5.0 7.8 %collective-permute-start.7 = (bf16[784,128]{1,0:T(8,128)(2,1)S(1)}, bf16[784,128]{1,0:T(8,128)(2,1)S(1)}, u32[]{:S(2)}, u32[]{:S(2)}) collective-permute-start(bf16[784,128]{1,0:T(8,128)(2,1)S(1)} %fusion.17.refs_3_), channel_id=1, source_target_pairs={{0,4},{1,5},{2,3},{3,2},{4,0},{5,1},{6,7},{7,6},{8,12},{9,13},{10,... | collective-permute-start | bytes 602120 | tf_op jit(solution)/shard_map/ppermute | solution.py:576
  6.4 9.8 %collective-permute-start.3 = (bf16[784,128]{1,0:T(8,128)(2,1)S(1)}, bf16[784,128]{1,0:T(8,128)(2,1)S(1)}, u32[]{:S(2)}, u32[]{:S(2)}) collective-permute-start(bf16[784,128]{1,0:T(8,128)(2,1)S(1)} %fusion.17.refs_3_), channel_id=1, source_target_pairs={{0,1},{1,0},{2,6},{3,7},{4,5},{5,4},{6,2},{7,3},{8,9},{9,8},{10,14... | collective-permute-start | bytes 602120 | tf_op jit(solution)/shard_map/ppermute | solution.py:576
  10.4 7.1 %collective-permute-start.1 = (bf16[784,128]{1,0:T(8,128)(2,1)S(1)}, bf16[784,128]{1,0:T(8,128)(2,1)S(1)}, u32[]{:S(2)}, u32[]{:S(2)}) collective-permute-start(bf16[784,128]{1,0:T(8,128)(2,1)S(1)} %fusion.17.refs_3_), channel_id=1, source_target_pairs={{0,16},{1,17},{2,10},{3,11},{4,20},{5,21},{6,14},{7,15},{8,24},{9,... | collective-permute-start | bytes 602120 | tf_op jit(solution)/shard_map/ppermute | solution.py:576
  12.7 7.1 %collective-permute-start.11 = (bf16[784,128]{1,0:T(8,128)(2,1)S(1)}, bf16[784,128]{1,0:T(8,128)(2,1)S(1)}, u32[]{:S(2)}, u32[]{:S(2)}) collective-permute-start(bf16[784,128]{1,0:T(8,128)(2,1)S(1)} %collective-permute-done.7.refs_11_), channel_id=1, source_target_pairs={{0,1},{1,0},{2,6},{3,7},{4,5},{5,4},{6,2},{7,3},{8,9},{9,8},{10,14... | collective-permute-start | bytes 602120 | tf_op jit(solution)/shard_map/ppermute | solution.py:576
  14.3 6.7 %collective-permute-start.8 = (bf16[784,128]{1,0:T(8,128)(2,1)S(1)}, bf16[784,128]{1,0:T(8,128)(2,1)S(1)}, u32[]{:S(2)}, u32[]{:S(2)}) collective-permute-start(bf16[784,128]{1,0:T(8,128)(2,1)S(1)} %collective-permute-done.refs_4_), channel_id=1, source_target_pairs={{0,4},{1,5},{2,3},{3,2},{4,0},{5,1},{6,7},{7,6},{8,12},{9,13},{10,... | collective-permute-start | bytes 602120 | tf_op jit(solution)/shard_map/ppermute | solution.py:576
  15.8 7.5 %collective-permute-start.4 = (bf16[784,128]{1,0:T(8,128)(2,1)S(1)}, bf16[784,128]{1,0:T(8,128)(2,1)S(1)}, u32[]{:S(2)}, u32[]{:S(2)}) collective-permute-start(bf16[784,128]{1,0:T(8,128)(2,1)S(1)} %collective-permute-done.refs_4_), channel_id=1, source_target_pairs={{0,1},{1,0},{2,6},{3,7},{4,5},{5,4},{6,2},{7,3},{8,9},{9,8},{10,14... | collective-permute-start | bytes 602120 | tf_op jit(solution)/shard_map/ppermute | solution.py:576
  16.3 9.1 %collective-permute-start.2 = (bf16[784,128]{1,0:T(8,128)(2,1)S(1)}, bf16[784,128]{1,0:T(8,128)(2,1)S(1)}, u32[]{:S(2)}, u32[]{:S(2)}) collective-permute-start(bf16[784,128]{1,0:T(8,128)(2,1)S(1)} %collective-permute-done.refs_4_), channel_id=1, source_target_pairs={{0,16},{1,17},{2,10},{3,11},{4,20},{5,21},{6,14},{7,15},{8,24},{9,... | collective-permute-start | bytes 602120 | tf_op jit(solution)/shard_map/ppermute | solution.py:576
  17.5 7.8 %collective-permute-start.9 = (bf16[784,128]{1,0:T(8,128)(2,1)S(1)}, bf16[784,128]{1,0:T(8,128)(2,1)S(1)}, u32[]{:S(2)}, u32[]{:S(2)}) collective-permute-start(bf16[784,128]{1,0:T(8,128)(2,1)S(1)} %collective-permute-done.1.refs_5_), channel_id=1, source_target_pairs={{0,4},{1,5},{2,3},{3,2},{4,0},{5,1},{6,7},{7,6},{8,12},{9,13},{10,... | collective-permute-start | bytes 602120 | tf_op jit(solution)/shard_map/ppermute | solution.py:576
  19.8 7.9 %collective-permute-start.17 = (bf16[784,128]{1,0:T(8,128)(2,1)S(1)}, bf16[784,128]{1,0:T(8,128)(2,1)S(1)}, u32[]{:S(2)}, u32[]{:S(2)}) collective-permute-start(bf16[784,128]{1,0:T(8,128)(2,1)S(1)} %collective-permute-done.1.refs_5_), channel_id=1, source_target_pairs={{0,2},{1,3},{2,0},{3,1},{4,6},{5,7},{6,4},{7,5},{8,10},{9,11},{10,... | collective-permute-start | bytes 602120 | tf_op jit(solution)/shard_map/ppermute | solution.py:576
  21.0 8.2 %collective-permute-start.5 = (bf16[784,128]{1,0:T(8,128)(2,1)S(1)}, bf16[784,128]{1,0:T(8,128)(2,1)S(1)}, u32[]{:S(2)}, u32[]{:S(2)}) collective-permute-start(bf16[784,128]{1,0:T(8,128)(2,1)S(1)} %collective-permute-done.1.refs_5_), channel_id=1, source_target_pairs={{0,1},{1,0},{2,6},{3,7},{4,5},{5,4},{6,2},{7,3},{8,9},{9,8},{10,14... | collective-permute-start | bytes 602120 | tf_op jit(solution)/shard_map/ppermute | solution.py:576
  23.2 6.8 %collective-permute-start.12 = (bf16[784,128]{1,0:T(8,128)(2,1)S(1)}, bf16[784,128]{1,0:T(8,128)(2,1)S(1)}, u32[]{:S(2)}, u32[]{:S(2)}) collective-permute-start(bf16[784,128]{1,0:T(8,128)(2,1)S(1)} %collective-permute-done.8.refs_12_), channel_id=1, source_target_pairs={{0,1},{1,0},{2,6},{3,7},{4,5},{5,4},{6,2},{7,3},{8,9},{9,8},{10,14... | collective-permute-start | bytes 602120 | tf_op jit(solution)/shard_map/ppermute | solution.py:576
  25.4 4.7 %collective-permute-start.18 = (bf16[784,128]{1,0:T(8,128)(2,1)S(1)}, bf16[784,128]{1,0:T(8,128)(2,1)S(1)}, u32[]{:S(2)}, u32[]{:S(2)}) collective-permute-start(bf16[784,128]{1,0:T(8,128)(2,1)S(1)} %collective-permute-done.2.refs_6_), channel_id=1, source_target_pairs={{0,2},{1,3},{2,0},{3,1},{4,6},{5,7},{6,4},{7,5},{8,10},{9,11},{10,... | collective-permute-start | bytes 602120 | tf_op jit(solution)/shard_map/ppermute | solution.py:576
  25.4 8.0 %collective-permute-start.10 = (bf16[784,128]{1,0:T(8,128)(2,1)S(1)}, bf16[784,128]{1,0:T(8,128)(2,1)S(1)}, u32[]{:S(2)}, u32[]{:S(2)}) collective-permute-start(bf16[784,128]{1,0:T(8,128)(2,1)S(1)} %collective-permute-done.2.refs_6_), channel_id=1, source_target_pairs={{0,4},{1,5},{2,3},{3,2},{4,0},{5,1},{6,7},{7,6},{8,12},{9,13},{10,... | collective-permute-start | bytes 602120 | tf_op jit(solution)/shard_map/ppermute | solution.py:576
  27.7 5.7 %collective-permute-start.6 = (bf16[784,128]{1,0:T(8,128)(2,1)S(1)}, bf16[784,128]{1,0:T(8,128)(2,1)S(1)}, u32[]{:S(2)}, u32[]{:S(2)}) collective-permute-start(bf16[784,128]{1,0:T(8,128)(2,1)S(1)} %collective-permute-done.2.refs_6_), channel_id=1, source_target_pairs={{0,1},{1,0},{2,6},{3,7},{4,5},{5,4},{6,2},{7,3},{8,9},{9,8},{10,14... | collective-permute-start | bytes 602120 | tf_op jit(solution)/shard_map/ppermute | solution.py:576
  29.1 4.8 %collective-permute-start.15 = (bf16[784,128]{1,0:T(8,128)(2,1)S(1)}, bf16[784,128]{1,0:T(8,128)(2,1)S(1)}, u32[]{:S(2)}, u32[]{:S(2)}) collective-permute-start(bf16[784,128]{1,0:T(8,128)(2,1)S(1)} %fusion.17.refs_3_), channel_id=1, source_target_pairs={{0,2},{1,3},{2,0},{3,1},{4,6},{5,7},{6,4},{7,5},{8,10},{9,11},{10,... | collective-permute-start | bytes 602120 | tf_op jit(solution)/shard_map/ppermute | solution.py:576
  30.0 3.9 %collective-permute-start.16 = (bf16[784,128]{1,0:T(8,128)(2,1)S(1)}, bf16[784,128]{1,0:T(8,128)(2,1)S(1)}, u32[]{:S(2)}, u32[]{:S(2)}) collective-permute-start(bf16[784,128]{1,0:T(8,128)(2,1)S(1)} %collective-permute-done.refs_4_), channel_id=1, source_target_pairs={{0,2},{1,3},{2,0},{3,1},{4,6},{5,7},{6,4},{7,5},{8,10},{9,11},{10,... | collective-permute-start | bytes 602120 | tf_op jit(solution)/shard_map/ppermute | solution.py:576
  30.1 5.8 %collective-permute-start.19 = (bf16[784,128]{1,0:T(8,128)(2,1)S(1)}, bf16[784,128]{1,0:T(8,128)(2,1)S(1)}, u32[]{:S(2)}, u32[]{:S(2)}) collective-permute-start(bf16[784,128]{1,0:T(8,128)(2,1)S(1)} %collective-permute-done.3.refs_7_), channel_id=1, source_target_pairs={{0,2},{1,3},{2,0},{3,1},{4,6},{5,7},{6,4},{7,5},{8,10},{9,11},{10,... | collective-permute-start | bytes 602120 | tf_op jit(solution)/shard_map/ppermute | solution.py:576
  33.4 2.5 %collective-permute-start.23 = (bf16[784,128]{1,0:T(8,128)(2,1)S(1)}, bf16[784,128]{1,0:T(8,128)(2,1)S(1)}, u32[]{:S(2)}, u32[]{:S(2)}) collective-permute-start(bf16[784,128]{1,0:T(8,128)(2,1)S(1)} %collective-permute-done.7.refs_11_), channel_id=1, source_target_pairs={{0,2},{1,3},{2,0},{3,1},{4,6},{5,7},{6,4},{7,5},{8,10},{9,11},{10,... | collective-permute-start | bytes 602120 | tf_op jit(solution)/shard_map/ppermute | solution.py:576
  33.4 3.0 %collective-permute-start.27 = (bf16[784,128]{1,0:T(8,128)(2,1)S(1)}, bf16[784,128]{1,0:T(8,128)(2,1)S(1)}, u32[]{:S(2)}, u32[]{:S(2)}) collective-permute-start(bf16[784,128]{1,0:T(8,128)(2,1)S(1)} %collective-permute-done.11.refs_15_), channel_id=1, source_target_pairs={{0,2},{1,3},{2,0},{3,1},{4,6},{5,7},{6,4},{7,5},{8,10},{9,11},{10,... | collective-permute-start | bytes 602120 | tf_op jit(solution)/shard_map/ppermute | solution.py:576
  33.9 2.6 %collective-permute-start.25 = (bf16[784,128]{1,0:T(8,128)(2,1)S(1)}, bf16[784,128]{1,0:T(8,128)(2,1)S(1)}, u32[]{:S(2)}, u32[]{:S(2)}) collective-permute-start(bf16[784,128]{1,0:T(8,128)(2,1)S(1)} %collective-permute-done.9.refs_13_), channel_id=1, source_target_pairs={{0,2},{1,3},{2,0},{3,1},{4,6},{5,7},{6,4},{7,5},{8,10},{9,11},{10,... | collective-permute-start | bytes 602120 | tf_op jit(solution)/shard_map/ppermute | solution.py:576
  34.0 5.7 %collective-permute-start.13 = (bf16[784,128]{1,0:T(8,128)(2,1)S(1)}, bf16[784,128]{1,0:T(8,128)(2,1)S(1)}, u32[]{:S(2)}, u32[]{:S(2)}) collective-permute-start(bf16[784,128]{1,0:T(8,128)(2,1)S(1)} %collective-permute-done.9.refs_13_), channel_id=1, source_target_pairs={{0,1},{1,0},{2,6},{3,7},{4,5},{5,4},{6,2},{7,3},{8,9},{9,8},{10,14... | collective-permute-start | bytes 602120 | tf_op jit(solution)/shard_map/ppermute | solution.py:576
  35.9 3.8 %collective-permute-start.21 = (bf16[784,128]{1,0:T(8,128)(2,1)S(1)}, bf16[784,128]{1,0:T(8,128)(2,1)S(1)}, u32[]{:S(2)}, u32[]{:S(2)}) collective-permute-start(bf16[784,128]{1,0:T(8,128)(2,1)S(1)} %collective-permute-done.5.refs_9_), channel_id=1, source_target_pairs={{0,2},{1,3},{2,0},{3,1},{4,6},{5,7},{6,4},{7,5},{8,10},{9,11},{10,... | collective-permute-start | bytes 602120 | tf_op jit(solution)/shard_map/ppermute | solution.py:576
  35.9 4.3 %collective-permute-start.24 = (bf16[784,128]{1,0:T(8,128)(2,1)S(1)}, bf16[784,128]{1,0:T(8,128)(2,1)S(1)}, u32[]{:S(2)}, u32[]{:S(2)}) collective-permute-start(bf16[784,128]{1,0:T(8,128)(2,1)S(1)} %collective-permute-done.8.refs_12_), channel_id=1, source_target_pairs={{0,2},{1,3},{2,0},{3,1},{4,6},{5,7},{6,4},{7,5},{8,10},{9,11},{10,... | collective-permute-start | bytes 602120 | tf_op jit(solution)/shard_map/ppermute | solution.py:576
  36.4 3.9 %collective-permute-start.28 = (bf16[784,128]{1,0:T(8,128)(2,1)S(1)}, bf16[784,128]{1,0:T(8,128)(2,1)S(1)}, u32[]{:S(2)}, u32[]{:S(2)}) collective-permute-start(bf16[784,128]{1,0:T(8,128)(2,1)S(1)} %collective-permute-done.12.refs_16_), channel_id=1, source_target_pairs={{0,2},{1,3},{2,0},{3,1},{4,6},{5,7},{6,4},{7,5},{8,10},{9,11},{10,... | collective-permute-start | bytes 602120 | tf_op jit(solution)/shard_map/ppermute | solution.py:576
  36.5 5.7 %collective-permute-start.14 = (bf16[784,128]{1,0:T(8,128)(2,1)S(1)}, bf16[784,128]{1,0:T(8,128)(2,1)S(1)}, u32[]{:S(2)}, u32[]{:S(2)}) collective-permute-start(bf16[784,128]{1,0:T(8,128)(2,1)S(1)} %collective-permute-done.10.refs_14_), channel_id=1, source_target_pairs={{0,1},{1,0},{2,6},{3,7},{4,5},{5,4},{6,2},{7,3},{8,9},{9,8},{10,14... | collective-permute-start | bytes 602120 | tf_op jit(solution)/shard_map/ppermute | solution.py:576
  39.7 2.5 %collective-permute-start.20 = (bf16[784,128]{1,0:T(8,128)(2,1)S(1)}, bf16[784,128]{1,0:T(8,128)(2,1)S(1)}, u32[]{:S(2)}, u32[]{:S(2)}) collective-permute-start(bf16[784,128]{1,0:T(8,128)(2,1)S(1)} %collective-permute-done.4.refs_8_), channel_id=1, source_target_pairs={{0,2},{1,3},{2,0},{3,1},{4,6},{5,7},{6,4},{7,5},{8,10},{9,11},{10,... | collective-permute-start | bytes 602120 | tf_op jit(solution)/shard_map/ppermute | solution.py:576
  39.7 2.5 %collective-permute-start.26 = (bf16[784,128]{1,0:T(8,128)(2,1)S(1)}, bf16[784,128]{1,0:T(8,128)(2,1)S(1)}, u32[]{:S(2)}, u32[]{:S(2)}) collective-permute-start(bf16[784,128]{1,0:T(8,128)(2,1)S(1)} %collective-permute-done.10.refs_14_), channel_id=1, source_target_pairs={{0,2},{1,3},{2,0},{3,1},{4,6},{5,7},{6,4},{7,5},{8,10},{9,11},{10,... | collective-permute-start | bytes 602120 | tf_op jit(solution)/shard_map/ppermute | solution.py:576
  40.2 2.0 %collective-permute-start.22 = (bf16[784,128]{1,0:T(8,128)(2,1)S(1)}, bf16[784,128]{1,0:T(8,128)(2,1)S(1)}, u32[]{:S(2)}, u32[]{:S(2)}) collective-permute-start(bf16[784,128]{1,0:T(8,128)(2,1)S(1)} %collective-permute-done.6.refs_10_), channel_id=1, source_target_pairs={{0,2},{1,3},{2,0},{3,1},{4,6},{5,7},{6,4},{7,5},{8,10},{9,11},{10,... | collective-permute-start | bytes 602120 | tf_op jit(solution)/shard_map/ppermute | solution.py:576
  40.3 2.0 %collective-permute-start.29 = (bf16[784,128]{1,0:T(8,128)(2,1)S(1)}, bf16[784,128]{1,0:T(8,128)(2,1)S(1)}, u32[]{:S(2)}, u32[]{:S(2)}) collective-permute-start(bf16[784,128]{1,0:T(8,128)(2,1)S(1)} %collective-permute-done.13.refs_17_), channel_id=1, source_target_pairs={{0,2},{1,3},{2,0},{3,1},{4,6},{5,7},{6,4},{7,5},{8,10},{9,11},{10,... | collective-permute-start | bytes 602120 | tf_op jit(solution)/shard_map/ppermute | solution.py:576
  42.2 1.4 collective-permute-start.30
  102.5 2.6 %collective-permute-start.34 = (bf16[4,784,128]{2,1,0:T(8,128)(2,1)}, bf16[4,784,128]{2,1,0:T(8,128)(2,1)S(1)}, u32[]{:S(2)}, u32[]{:S(2)}) collective-permute-start(bf16[4,784,128]{2,1,0:T(8,128)(2,1)} %get-tuple-element.50), channel_id=1, source_target_pairs={{0,2},{1,3},{2,0},{3,1},{4,6},{5,7},{6,4},{7,5},{8,10},{9,11},{10,... | collective-permute-start | bytes 2408456 | tf_op jit(solution)/shard_map/ppermute | solution.py:576
  102.7 6.5 %collective-permute-start.33 = (bf16[4,784,128]{2,1,0:T(8,128)(2,1)}, bf16[4,784,128]{2,1,0:T(8,128)(2,1)S(1)}, u32[]{:S(2)}, u32[]{:S(2)}) collective-permute-start(bf16[4,784,128]{2,1,0:T(8,128)(2,1)} %get-tuple-element.49), channel_id=1, source_target_pairs={{0,2},{1,3},{2,0},{3,1},{4,6},{5,7},{6,4},{7,5},{8,10},{9,11},{10,... | collective-permute-start | bytes 2408456 | tf_op jit(solution)/shard_map/ppermute | solution.py:576
  103.1 9.2 %collective-permute-start.31 = (bf16[4,784,128]{2,1,0:T(8,128)(2,1)}, bf16[4,784,128]{2,1,0:T(8,128)(2,1)S(1)}, u32[]{:S(2)}, u32[]{:S(2)}) collective-permute-start(bf16[4,784,128]{2,1,0:T(8,128)(2,1)} %get-tuple-element.47), channel_id=1, source_target_pairs={{0,2},{1,3},{2,0},{3,1},{4,6},{5,7},{6,4},{7,5},{8,10},{9,11},{10,... | collective-permute-start | bytes 2408456 | tf_op jit(solution)/shard_map/ppermute | solution.py:576
  103.2 10.3 %collective-permute-start.32 = (bf16[4,784,128]{2,1,0:T(8,128)(2,1)}, bf16[4,784,128]{2,1,0:T(8,128)(2,1)S(1)}, u32[]{:S(2)}, u32[]{:S(2)}) collective-permute-start(bf16[4,784,128]{2,1,0:T(8,128)(2,1)} %get-tuple-element.48), channel_id=1, source_target_pairs={{0,2},{1,3},{2,0},{3,1},{4,6},{5,7},{6,4},{7,5},{8,10},{9,11},{10,... | collective-permute-start | bytes 2408456 | tf_op jit(solution)/shard_map/ppermute | solution.py:576
  106.1 7.4 %collective-permute-start.36 = (bf16[784,128]{1,0:T(8,128)(2,1)S(1)}, bf16[784,128]{1,0:T(8,128)(2,1)S(1)}, u32[]{:S(2)}, u32[]{:S(2)}) collective-permute-start(bf16[784,128]{1,0:T(8,128)(2,1)S(1)} %fusion.16), channel_id=1, source_target_pairs={{0,4},{1,5},{2,3},{3,2},{4,0},{5,1},{6,7},{7,6},{8,12},{9,13},{10,... | collective-permute-start | bytes 602120 | tf_op jit(solution)/shard_map/ppermute | solution.py:576
  108.1 12.9 %collective-permute-start.39 = (bf16[784,128]{1,0:T(8,128)(2,1)S(1)}, bf16[784,128]{1,0:T(8,128)(2,1)S(1)}, u32[]{:S(2)}, u32[]{:S(2)}) collective-permute-start(bf16[784,128]{1,0:T(8,128)(2,1)S(1)} %fusion.2), channel_id=1, source_target_pairs={{0,4},{1,5},{2,3},{3,2},{4,0},{5,1},{6,7},{7,6},{8,12},{9,13},{10,... | collective-permute-start | bytes 602120 | tf_op jit(solution)/shard_map/ppermute | solution.py:576
  110.3 6.7 %collective-permute-start.35 = (bf16[784,128]{1,0:T(8,128)(2,1)S(1)}, bf16[784,128]{1,0:T(8,128)(2,1)S(1)}, u32[]{:S(2)}, u32[]{:S(2)}) collective-permute-start(bf16[784,128]{1,0:T(8,128)(2,1)S(1)} %fusion.3), channel_id=1, source_target_pairs={{0,4},{1,5},{2,3},{3,2},{4,0},{5,1},{6,7},{7,6},{8,12},{9,13},{10,... | collective-permute-start | bytes 602120 | tf_op jit(solution)/shard_map/ppermute | solution.py:576
  112.3 16.3 %collective-permute-start.43 = (bf16[784,128]{1,0:T(8,128)(2,1)S(1)}, bf16[784,128]{1,0:T(8,128)(2,1)S(1)}, u32[]{:S(2)}, u32[]{:S(2)}) collective-permute-start(bf16[784,128]{1,0:T(8,128)(2,1)S(1)} %fusion.1), channel_id=1, source_target_pairs={{0,4},{1,5},{2,3},{3,2},{4,0},{5,1},{6,7},{7,6},{8,12},{9,13},{10,... | collective-permute-start | bytes 602120 | tf_op jit(solution)/shard_map/ppermute | solution.py:576
  113.7 6.9 %collective-permute-start.40 = (bf16[784,128]{1,0:T(8,128)(2,1)S(1)}, bf16[784,128]{1,0:T(8,128)(2,1)S(1)}, u32[]{:S(2)}, u32[]{:S(2)}) collective-permute-start(bf16[784,128]{1,0:T(8,128)(2,1)S(1)} %fusion.14), channel_id=1, source_target_pairs={{0,1},{1,0},{2,6},{3,7},{4,5},{5,4},{6,2},{7,3},{8,9},{9,8},{10,14... | collective-permute-start | bytes 602120 | tf_op jit(solution)/shard_map/ppermute | solution.py:576
  117.1 11.6 %collective-permute-start.44 = (bf16[784,128]{1,0:T(8,128)(2,1)S(1)}, bf16[784,128]{1,0:T(8,128)(2,1)S(1)}, u32[]{:S(2)}, u32[]{:S(2)}) collective-permute-start(bf16[784,128]{1,0:T(8,128)(2,1)S(1)} %fusion.15), channel_id=1, source_target_pairs={{0,1},{1,0},{2,6},{3,7},{4,5},{5,4},{6,2},{7,3},{8,9},{9,8},{10,14... | collective-permute-start | bytes 602120 | tf_op jit(solution)/shard_map/ppermute | solution.py:576
  118.8 8.2 %collective-permute-start.38 = (bf16[2,784,128]{2,1,0:T(8,128)(2,1)S(1)}, bf16[2,784,128]{2,1,0:T(8,128)(2,1)S(1)}, u32[]{:S(2)}, u32[]{:S(2)}) collective-permute-start(bf16[2,784,128]{2,1,0:T(8,128)(2,1)S(1)} %add_convert_fusion.1), channel_id=1, source_target_pairs={{0,4},{1,5},{2,3},{3,2},{4,0},{5,1},{6,7},{7,6},{8,12},{9,13},{10,... | collective-permute-start | bytes 1204232 | tf_op jit(solution)/shard_map/ppermute | solution.py:576
  120.5 12.7 %collective-permute-start.37 = (bf16[2,784,128]{2,1,0:T(8,128)(2,1)S(1)}, bf16[2,784,128]{2,1,0:T(8,128)(2,1)S(1)}, u32[]{:S(2)}, u32[]{:S(2)}) collective-permute-start(bf16[2,784,128]{2,1,0:T(8,128)(2,1)S(1)} %add_convert_fusion), channel_id=1, source_target_pairs={{0,4},{1,5},{2,3},{3,2},{4,0},{5,1},{6,7},{7,6},{8,12},{9,13},{10,... | collective-permute-start | bytes 1204232 | tf_op jit(solution)/shard_map/ppermute | solution.py:576
  121.1 10.6 %collective-permute-start.42 = (bf16[784,128]{1,0:T(8,128)(2,1)S(1)}, bf16[784,128]{1,0:T(8,128)(2,1)S(1)}, u32[]{:S(2)}, u32[]{:S(2)}) collective-permute-start(bf16[784,128]{1,0:T(8,128)(2,1)S(1)} %fusion.7), channel_id=1, source_target_pairs={{0,16},{1,17},{2,10},{3,11},{4,20},{5,21},{6,14},{7,15},{8,24},{9,... | collective-permute-start | bytes 602120 | tf_op jit(solution)/shard_map/ppermute | solution.py:576
  127.1 6.2 %collective-permute-start.41 = (bf16[784,128]{1,0:T(8,128)(2,1)S(1)}, bf16[784,128]{1,0:T(8,128)(2,1)S(1)}, u32[]{:S(2)}, u32[]{:S(2)}) collective-permute-start(bf16[784,128]{1,0:T(8,128)(2,1)S(1)} %fusion.8), channel_id=1, source_target_pairs={{0,1},{1,0},{2,6},{3,7},{4,5},{5,4},{6,2},{7,3},{8,9},{9,8},{10,14... | collective-permute-start | bytes 602120 | tf_op jit(solution)/shard_map/ppermute | solution.py:576
  129.4 9.4 %collective-permute-start.47 = (bf16[784,128]{1,0:T(8,128)(2,1)}, bf16[784,128]{1,0:T(8,128)(2,1)S(1)}, u32[]{:S(2)}, u32[]{:S(2)}) collective-permute-start(bf16[784,128]{1,0:T(8,128)(2,1)} %fusion.5), channel_id=1, source_target_pairs={{0,16},{1,17},{2,10},{3,11},{4,20},{5,21},{6,14},{7,15},{8,24},{9,... | collective-permute-start | bytes 602120 | tf_op jit(solution)/shard_map/ppermute | solution.py:576
  134.9 6.0 %collective-permute-start.45 = (bf16[784,128]{1,0:T(8,128)(2,1)}, bf16[784,128]{1,0:T(8,128)(2,1)}, u32[]{:S(2)}, u32[]{:S(2)}) collective-permute-start(bf16[784,128]{1,0:T(8,128)(2,1)} %fusion.11), channel_id=1, source_target_pairs={{0,1},{1,0},{2,6},{3,7},{4,5},{5,4},{6,2},{7,3},{8,9},{9,8},{10,14... | collective-permute-start | bytes 602120 | tf_op jit(solution)/shard_map/ppermute | solution.py:576
  136.5 7.5 %collective-permute-start.46 = (bf16[784,128]{1,0:T(8,128)(2,1)}, bf16[784,128]{1,0:T(8,128)(2,1)}, u32[]{:S(2)}, u32[]{:S(2)}) collective-permute-start(bf16[784,128]{1,0:T(8,128)(2,1)} %fusion.10), channel_id=1, source_target_pairs={{0,8},{1,9},{2,18},{3,19},{4,12},{5,13},{6,22},{7,23},{8,0},{9,1},... | collective-permute-start | bytes 602120 | tf_op jit(solution)/shard_map/ppermute | solution.py:576
  (35 other events, 452.3 us)

commit v8 on v7

--- a/solution.py
+++ b/solution.py
@@ -591,11 +591,11 @@
     return near + [exchange(after(v, late) if n % 4 < 2 else v, 4) for n, v in enumerate(near)]
 
 
-def total(*parts):
+def total(*parts, kind=BF):
     v = parts[0].astype(F32)
     for part in parts[1:]:
         v = v + part.astype(F32)
-    return v.astype(BF)
+    return v.astype(kind)
 
 
 def sum_windows(keep, *sent):
@@ -632,7 +632,8 @@
     two = exchange(add(*plane(2)), 2)
     one = exchange(add(*plane(1), turn), 3)
     second(0)
-    return (*plane(0), one, two)
+    early = total(*plane(0)[:3], kind=F32)
+    return (lax.optimization_barrier(early), back[0], one, two)
 
 
 def shards_fn(block_input, segment_ids, cotangent, master_weights, momentum, weight_average):

time: 149 us -> 147 us (0.987)
  waiting for transfers between devices: 26.3 us -> 23.6 us
  local copies, waits for them, and re-layouts: 2.36 us -> 4.32 us
  starting transfers between devices: 49.7 us -> 48.2 us
    ppermute x48, waiting for transfers between devices: 26.3 us -> 23.6 us  [exchange(): lax.ppermute(v, AXES, [(j, j ^ (one if j // RC & 1 else zero)) for j in r...]
    squeeze x2, local copies, waits for them, and re-layouts: 0.04 us -> 1.99 us  [single(): side[m] = (exchange(add(keep[4 * m + 2], got[m][2]), 0), far)]
    convert_element_type x13, other arithmetic: 6.89 us -> 8.69 us  [total(): return v.astype(kind)]
    ppermute x48, starting transfers between devices: 49.7 us -> 48.2 us  [exchange(): lax.ppermute(v, AXES, [(j, j ^ (one if j // RC & 1 else zero)) for j in r...]
  transfers between devices with their start and end apart: 48 -> 48, of which waited for: 15 -> 14; matrix products, arithmetic and copies ran while one was open for 5% -> 7% of each run, Pallas kernels for 0% -> 0%
where the time goes in v8:
time: 147 us; the launch traced here: 146 us
  Pallas kernels  58.2 us (40%)
  starting transfers between devices  48.2 us (33%)
  waiting for transfers between devices  23.6 us (16%)
  other arithmetic  10.2 us (7%)
  local copies, waits for them, and re-layouts  4.32 us (3%)
    pallas_call x1, Pallas kernels, core(): pl.pallas_call(functools.partial(core_kernel, width=D, length=T, shards=s...  58.2 us
    ppermute x48, starting transfers between devices, exchange(): lax.ppermute(v, AXES, [(j, j ^ (one if j // RC & 1 else zero)) for j in r...  48.2 us
    ppermute x48, waiting for transfers between devices, exchange(): lax.ppermute(v, AXES, [(j, j ^ (one if j // RC & 1 else zero)) for j in r...  23.6 us
    convert_element_type x13, other arithmetic, total(): return v.astype(kind)  8.69 us
  transfers between devices with their start and end apart: 48, of which 14 were waited for; matrix products, arithmetic and copies ran while one was open for 7% of the time, Pallas kernels for 0%

profile of v8, /device:TPU:0, one launch (start us, length us, event | category | flops | bytes accessed | tf_op | source)
XLA Modules:
  0.0 145.6 jit_solution(10391272889601573374)
XLA Ops:
  0.7 1.2 fusion.15.refs_3_
  1.9 3.1 %collective-permute-start = (bf16[784,128]{1,0:T(8,128)(2,1)S(1)}, bf16[784,128]{1,0:T(8,128)(2,1)S(1)}, u32[]{:S(2)}, u32[]{:S(2)}) collective-permute-start(bf16[784,128]{1,0:T(8,128)(2,1)S(1)} %fusion.15.refs_3_), channel_id=1, source_target_pairs={{0,8},{1,9},{2,18},{3,19},{4,12},{5,13},{6,22},{7,23},{8,0},{9,1},... | collective-permute-start | bytes 602120 | tf_op jit(solution)/shard_map/ppermute | solution.py:576
  5.0 1.5 %collective-permute-start.7 = (bf16[784,128]{1,0:T(8,128)(2,1)S(1)}, bf16[784,128]{1,0:T(8,128)(2,1)S(1)}, u32[]{:S(2)}, u32[]{:S(2)}) collective-permute-start(bf16[784,128]{1,0:T(8,128)(2,1)S(1)} %fusion.15.refs_3_), channel_id=1, source_target_pairs={{0,4},{1,5},{2,3},{3,2},{4,0},{5,1},{6,7},{7,6},{8,12},{9,13},{10,... | collective-permute-start | bytes 602120 | tf_op jit(solution)/shard_map/ppermute | solution.py:576
  6.4 1.5 %collective-permute-start.3 = (bf16[784,128]{1,0:T(8,128)(2,1)S(1)}, bf16[784,128]{1,0:T(8,128)(2,1)S(1)}, u32[]{:S(2)}, u32[]{:S(2)}) collective-permute-start(bf16[784,128]{1,0:T(8,128)(2,1)S(1)} %fusion.15.refs_3_), channel_id=1, source_target_pairs={{0,1},{1,0},{2,6},{3,7},{4,5},{5,4},{6,2},{7,3},{8,9},{9,8},{10,14... | collective-permute-start | bytes 602120 | tf_op jit(solution)/shard_map/ppermute | solution.py:576
  8.0 2.5 %collective-permute-done.refs_4_ = bf16[784,128]{1,0:T(8,128)(2,1)S(1)} collective-permute-done((bf16[784,128]{1,0:T(8,128)(2,1)S(1)}, bf16[784,128]{1,0:T(8,128)(2,1)S(1)}, u32[]{:S(2)}, u32[]{:S(2)}) %collective-permute-start) | collective-permute-done | bytes 200736 | tf_op jit(solution)/shard_map/ppermute | solution.py:576
  10.4 2.3 %collective-permute-start.1 = (bf16[784,128]{1,0:T(8,128)(2,1)S(1)}, bf16[784,128]{1,0:T(8,128)(2,1)S(1)}, u32[]{:S(2)}, u32[]{:S(2)}) collective-permute-start(bf16[784,128]{1,0:T(8,128)(2,1)S(1)} %fusion.15.refs_3_), channel_id=1, source_target_pairs={{0,16},{1,17},{2,10},{3,11},{4,20},{5,21},{6,14},{7,15},{8,24},{9,... | collective-permute-start | bytes 602120 | tf_op jit(solution)/shard_map/ppermute | solution.py:576
  12.7 1.5 %collective-permute-start.11 = (bf16[784,128]{1,0:T(8,128)(2,1)S(1)}, bf16[784,128]{1,0:T(8,128)(2,1)S(1)}, u32[]{:S(2)}, u32[]{:S(2)}) collective-permute-start(bf16[784,128]{1,0:T(8,128)(2,1)S(1)} %collective-permute-done.7.refs_11_), channel_id=1, source_target_pairs={{0,1},{1,0},{2,6},{3,7},{4,5},{5,4},{6,2},{7,3},{8,9},{9,8},{10,14... | collective-permute-start | bytes 602120 | tf_op jit(solution)/shard_map/ppermute | solution.py:576
  14.3 1.5 %collective-permute-start.8 = (bf16[784,128]{1,0:T(8,128)(2,1)S(1)}, bf16[784,128]{1,0:T(8,128)(2,1)S(1)}, u32[]{:S(2)}, u32[]{:S(2)}) collective-permute-start(bf16[784,128]{1,0:T(8,128)(2,1)S(1)} %collective-permute-done.refs_4_), channel_id=1, source_target_pairs={{0,4},{1,5},{2,3},{3,2},{4,0},{5,1},{6,7},{7,6},{8,12},{9,13},{10,... | collective-permute-start | bytes 602120 | tf_op jit(solution)/shard_map/ppermute | solution.py:576
  16.3 1.3 collective-permute-start.2
  17.5 2.3 %collective-permute-start.9 = (bf16[784,128]{1,0:T(8,128)(2,1)S(1)}, bf16[784,128]{1,0:T(8,128)(2,1)S(1)}, u32[]{:S(2)}, u32[]{:S(2)}) collective-permute-start(bf16[784,128]{1,0:T(8,128)(2,1)S(1)} %collective-permute-done.1.refs_5_), channel_id=1, source_target_pairs={{0,4},{1,5},{2,3},{3,2},{4,0},{5,1},{6,7},{7,6},{8,12},{9,13},{10,... | collective-permute-start | bytes 602120 | tf_op jit(solution)/shard_map/ppermute | solution.py:576
  19.8 1.1 collective-permute-done.8.refs_12_
  21.0 1.1 collective-permute-start.5
  22.1 1.2 collective-permute-done.4.refs_8_
  23.2 2.1 %collective-permute-start.12 = (bf16[784,128]{1,0:T(8,128)(2,1)S(1)}, bf16[784,128]{1,0:T(8,128)(2,1)S(1)}, u32[]{:S(2)}, u32[]{:S(2)}) collective-permute-start(bf16[784,128]{1,0:T(8,128)(2,1)S(1)} %collective-permute-done.8.refs_12_), channel_id=1, source_target_pairs={{0,1},{1,0},{2,6},{3,7},{4,5},{5,4},{6,2},{7,3},{8,9},{9,8},{10,14... | collective-permute-start | bytes 602120 | tf_op jit(solution)/shard_map/ppermute | solution.py:576
  25.4 2.3 %collective-permute-start.10 = (bf16[784,128]{1,0:T(8,128)(2,1)S(1)}, bf16[784,128]{1,0:T(8,128)(2,1)S(1)}, u32[]{:S(2)}, u32[]{:S(2)}) collective-permute-start(bf16[784,128]{1,0:T(8,128)(2,1)S(1)} %collective-permute-done.2.refs_6_), channel_id=1, source_target_pairs={{0,4},{1,5},{2,3},{3,2},{4,0},{5,1},{6,7},{7,6},{8,12},{9,13},{10,... | collective-permute-start | bytes 602120 | tf_op jit(solution)/shard_map/ppermute | solution.py:576
  27.7 1.4 collective-permute-start.6
  30.6 2.8 %collective-permute-done.10.refs_14_ = bf16[784,128]{1,0:T(8,128)(2,1)S(1)} collective-permute-done((bf16[784,128]{1,0:T(8,128)(2,1)S(1)}, bf16[784,128]{1,0:T(8,128)(2,1)S(1)}, u32[]{:S(2)}, u32[]{:S(2)}) %collective-permute-start.10) | collective-permute-done | bytes 200736 | tf_op jit(solution)/shard_map/ppermute | solution.py:576
  34.0 1.9 %collective-permute-start.13 = (bf16[784,128]{1,0:T(8,128)(2,1)S(1)}, bf16[784,128]{1,0:T(8,128)(2,1)S(1)}, u32[]{:S(2)}, u32[]{:S(2)}) collective-permute-start(bf16[784,128]{1,0:T(8,128)(2,1)S(1)} %collective-permute-done.9.refs_13_), channel_id=1, source_target_pairs={{0,1},{1,0},{2,6},{3,7},{4,5},{5,4},{6,2},{7,3},{8,9},{9,8},{10,14... | collective-permute-start | bytes 602120 | tf_op jit(solution)/shard_map/ppermute | solution.py:576
  37.1 2.6 %collective-permute-done.13.refs_17_ = bf16[784,128]{1,0:T(8,128)(2,1)S(1)} collective-permute-done((bf16[784,128]{1,0:T(8,128)(2,1)S(1)}, bf16[784,128]{1,0:T(8,128)(2,1)S(1)}, u32[]{:S(2)}, u32[]{:S(2)}) %collective-permute-start.13) | collective-permute-done | bytes 200736 | tf_op jit(solution)/shard_map/ppermute | solution.py:576
  40.8 1.5 %collective-permute-done.14.refs_18_ = bf16[784,128]{1,0:T(8,128)(2,1)S(1)} collective-permute-done((bf16[784,128]{1,0:T(8,128)(2,1)S(1)}, bf16[784,128]{1,0:T(8,128)(2,1)S(1)}, u32[]{:S(2)}, u32[]{:S(2)}) %collective-permute-start.14) | collective-permute-done | bytes 200736 | tf_op jit(solution)/shard_map/ppermute | solution.py:576
  42.3 1.4 collective-permute-done.30.refs_34_
  44.4 58.2 %layer_core.1 = (f32[512,512]{1,0:T(8,128)}, f32[512,512]{1,0:T(8,128)}, bf16[16,784,128]{2,1,0:T(8,128)(2,1)}, bf16[4,784,128]{2,1,0:T(8,128)(2,1)}, bf16[4,784...) custom-call(bf16[512,512]{1,0:T(8,128)(2,1)} %bitcast.67, ...), custom_call_target="tpu_custom_call" | custom-call | tf_op jit(solution)/shard_map/layer_core/pallas_call | solution.py:559
  103.6 1.6 %collective-permute-done.34 = bf16[4,784,128]{2,1,0:T(8,128)(2,1)} collective-permute-done((bf16[4,784,128]{2,1,0:T(8,128)(2,1)}, bf16[4,784,128]{2,1,0:T(8,128)(2,1)}, u32[]{:S(2)}, u32[]{:S(2)}) %collective-permute-start.34) | collective-permute-done | bytes 802848 | tf_op jit(solution)/shard_map/ppermute | solution.py:576
  105.3 1.1 fusion.14
  106.3 1.0 collective-permute-start.36
  107.3 0.9 slice_bitcast_fusion.3
  108.3 1.0 fusion.2
  109.3 1.1 collective-permute-start.39
  110.4 1.1 slice_bitcast_fusion.2
  111.5 1.0 fusion.3
  112.5 1.0 collective-permute-start.35
  113.5 1.0 fusion.1
  114.5 1.1 collective-permute-start.43
  115.7 1.0 fusion.12
  116.7 1.6 %collective-permute-start.40 = (bf16[784,128]{1,0:T(8,128)(2,1)S(1)}, bf16[784,128]{1,0:T(8,128)(2,1)S(1)}, u32[]{:S(2)}, u32[]{:S(2)}) collective-permute-start(bf16[784,128]{1,0:T(8,128)(2,1)S(1)} %fusion.12), channel_id=1, source_target_pairs={{0,1},{1,0},{2,6},{3,7},{4,5},{5,4},{6,2},{7,3},{8,9},{9,8},{10,14... | collective-permute-start | bytes 602120 | tf_op jit(solution)/shard_map/ppermute | solution.py:576
  118.3 1.0 fusion.13
  119.4 1.5 %collective-permute-start.44 = (bf16[784,128]{1,0:T(8,128)(2,1)S(1)}, bf16[784,128]{1,0:T(8,128)(2,1)S(1)}, u32[]{:S(2)}, u32[]{:S(2)}) collective-permute-start(bf16[784,128]{1,0:T(8,128)(2,1)S(1)} %fusion.13), channel_id=1, source_target_pairs={{0,1},{1,0},{2,6},{3,7},{4,5},{5,4},{6,2},{7,3},{8,9},{9,8},{10,14... | collective-permute-start | bytes 602120 | tf_op jit(solution)/shard_map/ppermute | solution.py:576
  121.6 1.9 %collective-permute-done.40 = bf16[784,128]{1,0:T(8,128)(2,1)S(1)} collective-permute-done((bf16[784,128]{1,0:T(8,128)(2,1)S(1)}, bf16[784,128]{1,0:T(8,128)(2,1)S(1)}, u32[]{:S(2)}, u32[]{:S(2)}) %collective-permute-start.40) | collective-permute-done | bytes 200736 | tf_op jit(solution)/shard_map/ppermute | solution.py:576
  124.3 1.0 fusion.7
  125.3 3.5 %collective-permute-start.42 = (bf16[784,128]{1,0:T(8,128)(2,1)S(1)}, bf16[784,128]{1,0:T(8,128)(2,1)S(1)}, u32[]{:S(2)}, u32[]{:S(2)}) collective-permute-start(bf16[784,128]{1,0:T(8,128)(2,1)S(1)} %fusion.7), channel_id=1, source_target_pairs={{0,16},{1,17},{2,10},{3,11},{4,20},{5,21},{6,14},{7,15},{8,24},{9,... | collective-permute-start | bytes 602120 | tf_op jit(solution)/shard_map/ppermute | solution.py:576
  129.2 1.6 %collective-permute-start.41 = (bf16[784,128]{1,0:T(8,128)(2,1)S(1)}, bf16[784,128]{1,0:T(8,128)(2,1)S(1)}, u32[]{:S(2)}, u32[]{:S(2)}) collective-permute-start(bf16[784,128]{1,0:T(8,128)(2,1)S(1)} %fusion.8), channel_id=1, source_target_pairs={{0,1},{1,0},{2,6},{3,7},{4,5},{5,4},{6,2},{7,3},{8,9},{9,8},{10,14... | collective-permute-start | bytes 602120 | tf_op jit(solution)/shard_map/ppermute | solution.py:576
  130.8 1.0 fusion.5
  131.8 1.8 %collective-permute-start.47 = (bf16[784,128]{1,0:T(8,128)(2,1)S(1)}, bf16[784,128]{1,0:T(8,128)(2,1)S(1)}, u32[]{:S(2)}, u32[]{:S(2)}) collective-permute-start(bf16[784,128]{1,0:T(8,128)(2,1)S(1)} %fusion.5), channel_id=1, source_target_pairs={{0,16},{1,17},{2,10},{3,11},{4,20},{5,21},{6,14},{7,15},{8,24},{9,... | collective-permute-start | bytes 602120 | tf_op jit(solution)/shard_map/ppermute | solution.py:576
  133.6 1.0 collective-permute-done.37
  135.6 2.2 %collective-permute-start.46 = (bf16[784,128]{1,0:T(8,128)(2,1)S(1)}, bf16[784,128]{1,0:T(8,128)(2,1)S(1)}, u32[]{:S(2)}, u32[]{:S(2)}) collective-permute-start(bf16[784,128]{1,0:T(8,128)(2,1)S(1)} %fusion.10), channel_id=1, source_target_pairs={{0,8},{1,9},{2,18},{3,19},{4,12},{5,13},{6,22},{7,23},{8,0},{9,1},... | collective-permute-start | bytes 602120 | tf_op jit(solution)/shard_map/ppermute | solution.py:576
  137.9 1.6 %collective-permute-start.45 = (bf16[784,128]{1,0:T(8,128)(2,1)S(1)}, bf16[784,128]{1,0:T(8,128)(2,1)S(1)}, u32[]{:S(2)}, u32[]{:S(2)}) collective-permute-start(bf16[784,128]{1,0:T(8,128)(2,1)S(1)} %fusion.11), channel_id=1, source_target_pairs={{0,1},{1,0},{2,6},{3,7},{4,5},{5,4},{6,2},{7,3},{8,9},{9,8},{10,14... | collective-permute-start | bytes 602120 | tf_op jit(solution)/shard_map/ppermute | solution.py:576
  139.5 4.1 %collective-permute-done.45 = bf16[784,128]{1,0:T(8,128)(2,1)S(1)} collective-permute-done((bf16[784,128]{1,0:T(8,128)(2,1)S(1)}, bf16[784,128]{1,0:T(8,128)(2,1)S(1)}, u32[]{:S(2)}, u32[]{:S(2)}) %collective-permute-start.45) | collective-permute-done | bytes 200736 | tf_op jit(solution)/shard_map/ppermute | solution.py:576
  144.3 1.4 multiply_add_fusion
  (145 shorter events, 9.9 us)
Async XLA Ops:
  1.9 8.6 %collective-permute-start = (bf16[784,128]{1,0:T(8,128)(2,1)S(1)}, bf16[784,128]{1,0:T(8,128)(2,1)S(1)}, u32[]{:S(2)}, u32[]{:S(2)}) collective-permute-start(bf16[784,128]{1,0:T(8,128)(2,1)S(1)} %fusion.15.refs_3_), channel_id=1, source_target_pairs={{0,8},{1,9},{2,18},{3,19},{4,12},{5,13},{6,22},{7,23},{8,0},{9,1},... | collective-permute-start | bytes 602120 | tf_op jit(solution)/shard_map/ppermute | solution.py:576
  5.0 7.8 %collective-permute-start.7 = (bf16[784,128]{1,0:T(8,128)(2,1)S(1)}, bf16[784,128]{1,0:T(8,128)(2,1)S(1)}, u32[]{:S(2)}, u32[]{:S(2)}) collective-permute-start(bf16[784,128]{1,0:T(8,128)(2,1)S(1)} %fusion.15.refs_3_), channel_id=1, source_target_pairs={{0,4},{1,5},{2,3},{3,2},{4,0},{5,1},{6,7},{7,6},{8,12},{9,13},{10,... | collective-permute-start | bytes 602120 | tf_op jit(solution)/shard_map/ppermute | solution.py:576
  6.4 9.8 %collective-permute-start.3 = (bf16[784,128]{1,0:T(8,128)(2,1)S(1)}, bf16[784,128]{1,0:T(8,128)(2,1)S(1)}, u32[]{:S(2)}, u32[]{:S(2)}) collective-permute-start(bf16[784,128]{1,0:T(8,128)(2,1)S(1)} %fusion.15.refs_3_), channel_id=1, source_target_pairs={{0,1},{1,0},{2,6},{3,7},{4,5},{5,4},{6,2},{7,3},{8,9},{9,8},{10,14... | collective-permute-start | bytes 602120 | tf_op jit(solution)/shard_map/ppermute | solution.py:576
  10.4 7.1 %collective-permute-start.1 = (bf16[784,128]{1,0:T(8,128)(2,1)S(1)}, bf16[784,128]{1,0:T(8,128)(2,1)S(1)}, u32[]{:S(2)}, u32[]{:S(2)}) collective-permute-start(bf16[784,128]{1,0:T(8,128)(2,1)S(1)} %fusion.15.refs_3_), channel_id=1, source_target_pairs={{0,16},{1,17},{2,10},{3,11},{4,20},{5,21},{6,14},{7,15},{8,24},{9,... | collective-permute-start | bytes 602120 | tf_op jit(solution)/shard_map/ppermute | solution.py:576
  12.7 7.1 %collective-permute-start.11 = (bf16[784,128]{1,0:T(8,128)(2,1)S(1)}, bf16[784,128]{1,0:T(8,128)(2,1)S(1)}, u32[]{:S(2)}, u32[]{:S(2)}) collective-permute-start(bf16[784,128]{1,0:T(8,128)(2,1)S(1)} %collective-permute-done.7.refs_11_), channel_id=1, source_target_pairs={{0,1},{1,0},{2,6},{3,7},{4,5},{5,4},{6,2},{7,3},{8,9},{9,8},{10,14... | collective-permute-start | bytes 602120 | tf_op jit(solution)/shard_map/ppermute | solution.py:576
  14.3 6.7 %collective-permute-start.8 = (bf16[784,128]{1,0:T(8,128)(2,1)S(1)}, bf16[784,128]{1,0:T(8,128)(2,1)S(1)}, u32[]{:S(2)}, u32[]{:S(2)}) collective-permute-start(bf16[784,128]{1,0:T(8,128)(2,1)S(1)} %collective-permute-done.refs_4_), channel_id=1, source_target_pairs={{0,4},{1,5},{2,3},{3,2},{4,0},{5,1},{6,7},{7,6},{8,12},{9,13},{10,... | collective-permute-start | bytes 602120 | tf_op jit(solution)/shard_map/ppermute | solution.py:576
  15.8 7.5 %collective-permute-start.4 = (bf16[784,128]{1,0:T(8,128)(2,1)S(1)}, bf16[784,128]{1,0:T(8,128)(2,1)S(1)}, u32[]{:S(2)}, u32[]{:S(2)}) collective-permute-start(bf16[784,128]{1,0:T(8,128)(2,1)S(1)} %collective-permute-done.refs_4_), channel_id=1, source_target_pairs={{0,1},{1,0},{2,6},{3,7},{4,5},{5,4},{6,2},{7,3},{8,9},{9,8},{10,14... | collective-permute-start | bytes 602120 | tf_op jit(solution)/shard_map/ppermute | solution.py:576
  16.3 9.1 %collective-permute-start.2 = (bf16[784,128]{1,0:T(8,128)(2,1)S(1)}, bf16[784,128]{1,0:T(8,128)(2,1)S(1)}, u32[]{:S(2)}, u32[]{:S(2)}) collective-permute-start(bf16[784,128]{1,0:T(8,128)(2,1)S(1)} %collective-permute-done.refs_4_), channel_id=1, source_target_pairs={{0,16},{1,17},{2,10},{3,11},{4,20},{5,21},{6,14},{7,15},{8,24},{9,... | collective-permute-start | bytes 602120 | tf_op jit(solution)/shard_map/ppermute | solution.py:576
  17.5 7.8 %collective-permute-start.9 = (bf16[784,128]{1,0:T(8,128)(2,1)S(1)}, bf16[784,128]{1,0:T(8,128)(2,1)S(1)}, u32[]{:S(2)}, u32[]{:S(2)}) collective-permute-start(bf16[784,128]{1,0:T(8,128)(2,1)S(1)} %collective-permute-done.1.refs_5_), channel_id=1, source_target_pairs={{0,4},{1,5},{2,3},{3,2},{4,0},{5,1},{6,7},{7,6},{8,12},{9,13},{10,... | collective-permute-start | bytes 602120 | tf_op jit(solution)/shard_map/ppermute | solution.py:576
  19.8 7.9 %collective-permute-start.17 = (bf16[784,128]{1,0:T(8,128)(2,1)S(1)}, bf16[784,128]{1,0:T(8,128)(2,1)S(1)}, u32[]{:S(2)}, u32[]{:S(2)}) collective-permute-start(bf16[784,128]{1,0:T(8,128)(2,1)S(1)} %collective-permute-done.1.refs_5_), channel_id=1, source_target_pairs={{0,2},{1,3},{2,0},{3,1},{4,6},{5,7},{6,4},{7,5},{8,10},{9,11},{10,... | collective-permute-start | bytes 602120 | tf_op jit(solution)/shard_map/ppermute | solution.py:576
  21.0 8.2 %collective-permute-start.5 = (bf16[784,128]{1,0:T(8,128)(2,1)S(1)}, bf16[784,128]{1,0:T(8,128)(2,1)S(1)}, u32[]{:S(2)}, u32[]{:S(2)}) collective-permute-start(bf16[784,128]{1,0:T(8,128)(2,1)S(1)} %collective-permute-done.1.refs_5_), channel_id=1, source_target_pairs={{0,1},{1,0},{2,6},{3,7},{4,5},{5,4},{6,2},{7,3},{8,9},{9,8},{10,14... | collective-permute-start | bytes 602120 | tf_op jit(solution)/shard_map/ppermute | solution.py:576
  23.2 6.8 %collective-permute-start.12 = (bf16[784,128]{1,0:T(8,128)(2,1)S(1)}, bf16[784,128]{1,0:T(8,128)(2,1)S(1)}, u32[]{:S(2)}, u32[]{:S(2)}) collective-permute-start(bf16[784,128]{1,0:T(8,128)(2,1)S(1)} %collective-permute-done.8.refs_12_), channel_id=1, source_target_pairs={{0,1},{1,0},{2,6},{3,7},{4,5},{5,4},{6,2},{7,3},{8,9},{9,8},{10,14... | collective-permute-start | bytes 602120 | tf_op jit(solution)/shard_map/ppermute | solution.py:576
  25.4 4.7 %collective-permute-start.18 = (bf16[784,128]{1,0:T(8,128)(2,1)S(1)}, bf16[784,128]{1,0:T(8,128)(2,1)S(1)}, u32[]{:S(2)}, u32[]{:S(2)}) collective-permute-start(bf16[784,128]{1,0:T(8,128)(2,1)S(1)} %collective-permute-done.2.refs_6_), channel_id=1, source_target_pairs={{0,2},{1,3},{2,0},{3,1},{4,6},{5,7},{6,4},{7,5},{8,10},{9,11},{10,... | collective-permute-start | bytes 602120 | tf_op jit(solution)/shard_map/ppermute | solution.py:576
  25.4 8.0 %collective-permute-start.10 = (bf16[784,128]{1,0:T(8,128)(2,1)S(1)}, bf16[784,128]{1,0:T(8,128)(2,1)S(1)}, u32[]{:S(2)}, u32[]{:S(2)}) collective-permute-start(bf16[784,128]{1,0:T(8,128)(2,1)S(1)} %collective-permute-done.2.refs_6_), channel_id=1, source_target_pairs={{0,4},{1,5},{2,3},{3,2},{4,0},{5,1},{6,7},{7,6},{8,12},{9,13},{10,... | collective-permute-start | bytes 602120 | tf_op jit(solution)/shard_map/ppermute | solution.py:576
  27.7 5.7 %collective-permute-start.6 = (bf16[784,128]{1,0:T(8,128)(2,1)S(1)}, bf16[784,128]{1,0:T(8,128)(2,1)S(1)}, u32[]{:S(2)}, u32[]{:S(2)}) collective-permute-start(bf16[784,128]{1,0:T(8,128)(2,1)S(1)} %collective-permute-done.2.refs_6_), channel_id=1, source_target_pairs={{0,1},{1,0},{2,6},{3,7},{4,5},{5,4},{6,2},{7,3},{8,9},{9,8},{10,14... | collective-permute-start | bytes 602120 | tf_op jit(solution)/shard_map/ppermute | solution.py:576
  29.1 4.8 %collective-permute-start.15 = (bf16[784,128]{1,0:T(8,128)(2,1)S(1)}, bf16[784,128]{1,0:T(8,128)(2,1)S(1)}, u32[]{:S(2)}, u32[]{:S(2)}) collective-permute-start(bf16[784,128]{1,0:T(8,128)(2,1)S(1)} %fusion.15.refs_3_), channel_id=1, source_target_pairs={{0,2},{1,3},{2,0},{3,1},{4,6},{5,7},{6,4},{7,5},{8,10},{9,11},{10,... | collective-permute-start | bytes 602120 | tf_op jit(solution)/shard_map/ppermute | solution.py:576
  30.0 3.9 %collective-permute-start.16 = (bf16[784,128]{1,0:T(8,128)(2,1)S(1)}, bf16[784,128]{1,0:T(8,128)(2,1)S(1)}, u32[]{:S(2)}, u32[]{:S(2)}) collective-permute-start(bf16[784,128]{1,0:T(8,128)(2,1)S(1)} %collective-permute-done.refs_4_), channel_id=1, source_target_pairs={{0,2},{1,3},{2,0},{3,1},{4,6},{5,7},{6,4},{7,5},{8,10},{9,11},{10,... | collective-permute-start | bytes 602120 | tf_op jit(solution)/shard_map/ppermute | solution.py:576
  30.1 5.8 %collective-permute-start.19 = (bf16[784,128]{1,0:T(8,128)(2,1)S(1)}, bf16[784,128]{1,0:T(8,128)(2,1)S(1)}, u32[]{:S(2)}, u32[]{:S(2)}) collective-permute-start(bf16[784,128]{1,0:T(8,128)(2,1)S(1)} %collective-permute-done.3.refs_7_), channel_id=1, source_target_pairs={{0,2},{1,3},{2,0},{3,1},{4,6},{5,7},{6,4},{7,5},{8,10},{9,11},{10,... | collective-permute-start | bytes 602120 | tf_op jit(solution)/shard_map/ppermute | solution.py:576
  33.4 2.5 %collective-permute-start.23 = (bf16[784,128]{1,0:T(8,128)(2,1)S(1)}, bf16[784,128]{1,0:T(8,128)(2,1)S(1)}, u32[]{:S(2)}, u32[]{:S(2)}) collective-permute-start(bf16[784,128]{1,0:T(8,128)(2,1)S(1)} %collective-permute-done.7.refs_11_), channel_id=1, source_target_pairs={{0,2},{1,3},{2,0},{3,1},{4,6},{5,7},{6,4},{7,5},{8,10},{9,11},{10,... | collective-permute-start | bytes 602120 | tf_op jit(solution)/shard_map/ppermute | solution.py:576
  33.4 3.0 %collective-permute-start.27 = (bf16[784,128]{1,0:T(8,128)(2,1)S(1)}, bf16[784,128]{1,0:T(8,128)(2,1)S(1)}, u32[]{:S(2)}, u32[]{:S(2)}) collective-permute-start(bf16[784,128]{1,0:T(8,128)(2,1)S(1)} %collective-permute-done.11.refs_15_), channel_id=1, source_target_pairs={{0,2},{1,3},{2,0},{3,1},{4,6},{5,7},{6,4},{7,5},{8,10},{9,11},{10,... | collective-permute-start | bytes 602120 | tf_op jit(solution)/shard_map/ppermute | solution.py:576
  33.9 2.6 %collective-permute-start.25 = (bf16[784,128]{1,0:T(8,128)(2,1)S(1)}, bf16[784,128]{1,0:T(8,128)(2,1)S(1)}, u32[]{:S(2)}, u32[]{:S(2)}) collective-permute-start(bf16[784,128]{1,0:T(8,128)(2,1)S(1)} %collective-permute-done.9.refs_13_), channel_id=1, source_target_pairs={{0,2},{1,3},{2,0},{3,1},{4,6},{5,7},{6,4},{7,5},{8,10},{9,11},{10,... | collective-permute-start | bytes 602120 | tf_op jit(solution)/shard_map/ppermute | solution.py:576
  34.0 5.7 %collective-permute-start.13 = (bf16[784,128]{1,0:T(8,128)(2,1)S(1)}, bf16[784,128]{1,0:T(8,128)(2,1)S(1)}, u32[]{:S(2)}, u32[]{:S(2)}) collective-permute-start(bf16[784,128]{1,0:T(8,128)(2,1)S(1)} %collective-permute-done.9.refs_13_), channel_id=1, source_target_pairs={{0,1},{1,0},{2,6},{3,7},{4,5},{5,4},{6,2},{7,3},{8,9},{9,8},{10,14... | collective-permute-start | bytes 602120 | tf_op jit(solution)/shard_map/ppermute | solution.py:576
  35.9 3.8 %collective-permute-start.21 = (bf16[784,128]{1,0:T(8,128)(2,1)S(1)}, bf16[784,128]{1,0:T(8,128)(2,1)S(1)}, u32[]{:S(2)}, u32[]{:S(2)}) collective-permute-start(bf16[784,128]{1,0:T(8,128)(2,1)S(1)} %collective-permute-done.5.refs_9_), channel_id=1, source_target_pairs={{0,2},{1,3},{2,0},{3,1},{4,6},{5,7},{6,4},{7,5},{8,10},{9,11},{10,... | collective-permute-start | bytes 602120 | tf_op jit(solution)/shard_map/ppermute | solution.py:576
  35.9 4.3 %collective-permute-start.24 = (bf16[784,128]{1,0:T(8,128)(2,1)S(1)}, bf16[784,128]{1,0:T(8,128)(2,1)S(1)}, u32[]{:S(2)}, u32[]{:S(2)}) collective-permute-start(bf16[784,128]{1,0:T(8,128)(2,1)S(1)} %collective-permute-done.8.refs_12_), channel_id=1, source_target_pairs={{0,2},{1,3},{2,0},{3,1},{4,6},{5,7},{6,4},{7,5},{8,10},{9,11},{10,... | collective-permute-start | bytes 602120 | tf_op jit(solution)/shard_map/ppermute | solution.py:576
  36.4 3.9 %collective-permute-start.28 = (bf16[784,128]{1,0:T(8,128)(2,1)S(1)}, bf16[784,128]{1,0:T(8,128)(2,1)S(1)}, u32[]{:S(2)}, u32[]{:S(2)}) collective-permute-start(bf16[784,128]{1,0:T(8,128)(2,1)S(1)} %collective-permute-done.12.refs_16_), channel_id=1, source_target_pairs={{0,2},{1,3},{2,0},{3,1},{4,6},{5,7},{6,4},{7,5},{8,10},{9,11},{10,... | collective-permute-start | bytes 602120 | tf_op jit(solution)/shard_map/ppermute | solution.py:576
  36.5 5.7 %collective-permute-start.14 = (bf16[784,128]{1,0:T(8,128)(2,1)S(1)}, bf16[784,128]{1,0:T(8,128)(2,1)S(1)}, u32[]{:S(2)}, u32[]{:S(2)}) collective-permute-start(bf16[784,128]{1,0:T(8,128)(2,1)S(1)} %collective-permute-done.10.refs_14_), channel_id=1, source_target_pairs={{0,1},{1,0},{2,6},{3,7},{4,5},{5,4},{6,2},{7,3},{8,9},{9,8},{10,14... | collective-permute-start | bytes 602120 | tf_op jit(solution)/shard_map/ppermute | solution.py:576
  39.7 2.5 %collective-permute-start.20 = (bf16[784,128]{1,0:T(8,128)(2,1)S(1)}, bf16[784,128]{1,0:T(8,128)(2,1)S(1)}, u32[]{:S(2)}, u32[]{:S(2)}) collective-permute-start(bf16[784,128]{1,0:T(8,128)(2,1)S(1)} %collective-permute-done.4.refs_8_), channel_id=1, source_target_pairs={{0,2},{1,3},{2,0},{3,1},{4,6},{5,7},{6,4},{7,5},{8,10},{9,11},{10,... | collective-permute-start | bytes 602120 | tf_op jit(solution)/shard_map/ppermute | solution.py:576
  39.7 2.5 %collective-permute-start.26 = (bf16[784,128]{1,0:T(8,128)(2,1)S(1)}, bf16[784,128]{1,0:T(8,128)(2,1)S(1)}, u32[]{:S(2)}, u32[]{:S(2)}) collective-permute-start(bf16[784,128]{1,0:T(8,128)(2,1)S(1)} %collective-permute-done.10.refs_14_), channel_id=1, source_target_pairs={{0,2},{1,3},{2,0},{3,1},{4,6},{5,7},{6,4},{7,5},{8,10},{9,11},{10,... | collective-permute-start | bytes 602120 | tf_op jit(solution)/shard_map/ppermute | solution.py:576
  40.2 2.0 %collective-permute-start.22 = (bf16[784,128]{1,0:T(8,128)(2,1)S(1)}, bf16[784,128]{1,0:T(8,128)(2,1)S(1)}, u32[]{:S(2)}, u32[]{:S(2)}) collective-permute-start(bf16[784,128]{1,0:T(8,128)(2,1)S(1)} %collective-permute-done.6.refs_10_), channel_id=1, source_target_pairs={{0,2},{1,3},{2,0},{3,1},{4,6},{5,7},{6,4},{7,5},{8,10},{9,11},{10,... | collective-permute-start | bytes 602120 | tf_op jit(solution)/shard_map/ppermute | solution.py:576
  40.3 2.0 %collective-permute-start.29 = (bf16[784,128]{1,0:T(8,128)(2,1)S(1)}, bf16[784,128]{1,0:T(8,128)(2,1)S(1)}, u32[]{:S(2)}, u32[]{:S(2)}) collective-permute-start(bf16[784,128]{1,0:T(8,128)(2,1)S(1)} %collective-permute-done.13.refs_17_), channel_id=1, source_target_pairs={{0,2},{1,3},{2,0},{3,1},{4,6},{5,7},{6,4},{7,5},{8,10},{9,11},{10,... | collective-permute-start | bytes 602120 | tf_op jit(solution)/shard_map/ppermute | solution.py:576
  42.2 1.4 collective-permute-start.30
  102.5 2.7 %collective-permute-start.34 = (bf16[4,784,128]{2,1,0:T(8,128)(2,1)}, bf16[4,784,128]{2,1,0:T(8,128)(2,1)}, u32[]{:S(2)}, u32[]{:S(2)}) collective-permute-start(bf16[4,784,128]{2,1,0:T(8,128)(2,1)} %get-tuple-element.50), channel_id=1, source_target_pairs={{0,2},{1,3},{2,0},{3,1},{4,6},{5,7},{6,4},{7,5},{8,10},{9,11},{10,... | collective-permute-start | bytes 2408456 | tf_op jit(solution)/shard_map/ppermute | solution.py:576
  102.7 7.7 %collective-permute-start.33 = (bf16[4,784,128]{2,1,0:T(8,128)(2,1)}, bf16[4,784,128]{2,1,0:T(8,128)(2,1)}, u32[]{:S(2)}, u32[]{:S(2)}) collective-permute-start(bf16[4,784,128]{2,1,0:T(8,128)(2,1)} %get-tuple-element.49), channel_id=1, source_target_pairs={{0,2},{1,3},{2,0},{3,1},{4,6},{5,7},{6,4},{7,5},{8,10},{9,11},{10,... | collective-permute-start | bytes 2408456 | tf_op jit(solution)/shard_map/ppermute | solution.py:576
  103.1 11.4 %collective-permute-start.31 = (bf16[4,784,128]{2,1,0:T(8,128)(2,1)}, bf16[4,784,128]{2,1,0:T(8,128)(2,1)S(1)}, u32[]{:S(2)}, u32[]{:S(2)}) collective-permute-start(bf16[4,784,128]{2,1,0:T(8,128)(2,1)} %get-tuple-element.47), channel_id=1, source_target_pairs={{0,2},{1,3},{2,0},{3,1},{4,6},{5,7},{6,4},{7,5},{8,10},{9,11},{10,... | collective-permute-start | bytes 2408456 | tf_op jit(solution)/shard_map/ppermute | solution.py:576
  103.3 12.4 %collective-permute-start.32 = (bf16[4,784,128]{2,1,0:T(8,128)(2,1)}, bf16[4,784,128]{2,1,0:T(8,128)(2,1)S(1)}, u32[]{:S(2)}, u32[]{:S(2)}) collective-permute-start(bf16[4,784,128]{2,1,0:T(8,128)(2,1)} %get-tuple-element.48), channel_id=1, source_target_pairs={{0,2},{1,3},{2,0},{3,1},{4,6},{5,7},{6,4},{7,5},{8,10},{9,11},{10,... | collective-permute-start | bytes 2408456 | tf_op jit(solution)/shard_map/ppermute | solution.py:576
  106.3 9.4 %collective-permute-start.36 = (bf16[784,128]{1,0:T(8,128)(2,1)S(1)}, bf16[784,128]{1,0:T(8,128)(2,1)S(1)}, u32[]{:S(2)}, u32[]{:S(2)}) collective-permute-start(bf16[784,128]{1,0:T(8,128)(2,1)S(1)} %fusion.14), channel_id=1, source_target_pairs={{0,4},{1,5},{2,3},{3,2},{4,0},{5,1},{6,7},{7,6},{8,12},{9,13},{10,... | collective-permute-start | bytes 602120 | tf_op jit(solution)/shard_map/ppermute | solution.py:576
  109.3 15.0 %collective-permute-start.39 = (bf16[784,128]{1,0:T(8,128)(2,1)S(1)}, bf16[784,128]{1,0:T(8,128)(2,1)S(1)}, u32[]{:S(2)}, u32[]{:S(2)}) collective-permute-start(bf16[784,128]{1,0:T(8,128)(2,1)S(1)} %fusion.2), channel_id=1, source_target_pairs={{0,4},{1,5},{2,3},{3,2},{4,0},{5,1},{6,7},{7,6},{8,12},{9,13},{10,... | collective-permute-start | bytes 602120 | tf_op jit(solution)/shard_map/ppermute | solution.py:576
  112.5 5.9 %collective-permute-start.35 = (bf16[784,128]{1,0:T(8,128)(2,1)S(1)}, bf16[784,128]{1,0:T(8,128)(2,1)S(1)}, u32[]{:S(2)}, u32[]{:S(2)}) collective-permute-start(bf16[784,128]{1,0:T(8,128)(2,1)S(1)} %fusion.3), channel_id=1, source_target_pairs={{0,4},{1,5},{2,3},{3,2},{4,0},{5,1},{6,7},{7,6},{8,12},{9,13},{10,... | collective-permute-start | bytes 602120 | tf_op jit(solution)/shard_map/ppermute | solution.py:576
  114.5 16.3 %collective-permute-start.43 = (bf16[784,128]{1,0:T(8,128)(2,1)S(1)}, bf16[784,128]{1,0:T(8,128)(2,1)S(1)}, u32[]{:S(2)}, u32[]{:S(2)}) collective-permute-start(bf16[784,128]{1,0:T(8,128)(2,1)S(1)} %fusion.1), channel_id=1, source_target_pairs={{0,4},{1,5},{2,3},{3,2},{4,0},{5,1},{6,7},{7,6},{8,12},{9,13},{10,... | collective-permute-start | bytes 602120 | tf_op jit(solution)/shard_map/ppermute | solution.py:576
  116.7 6.8 %collective-permute-start.40 = (bf16[784,128]{1,0:T(8,128)(2,1)S(1)}, bf16[784,128]{1,0:T(8,128)(2,1)S(1)}, u32[]{:S(2)}, u32[]{:S(2)}) collective-permute-start(bf16[784,128]{1,0:T(8,128)(2,1)S(1)} %fusion.12), channel_id=1, source_target_pairs={{0,1},{1,0},{2,6},{3,7},{4,5},{5,4},{6,2},{7,3},{8,9},{9,8},{10,14... | collective-permute-start | bytes 602120 | tf_op jit(solution)/shard_map/ppermute | solution.py:576
  119.4 11.4 %collective-permute-start.44 = (bf16[784,128]{1,0:T(8,128)(2,1)S(1)}, bf16[784,128]{1,0:T(8,128)(2,1)S(1)}, u32[]{:S(2)}, u32[]{:S(2)}) collective-permute-start(bf16[784,128]{1,0:T(8,128)(2,1)S(1)} %fusion.13), channel_id=1, source_target_pairs={{0,1},{1,0},{2,6},{3,7},{4,5},{5,4},{6,2},{7,3},{8,9},{9,8},{10,14... | collective-permute-start | bytes 602120 | tf_op jit(solution)/shard_map/ppermute | solution.py:576
  121.0 8.0 %collective-permute-start.38 = (bf16[2,784,128]{2,1,0:T(8,128)(2,1)S(1)}, bf16[2,784,128]{2,1,0:T(8,128)(2,1)S(1)}, u32[]{:S(2)}, u32[]{:S(2)}) collective-permute-start(bf16[2,784,128]{2,1,0:T(8,128)(2,1)S(1)} %add_convert_fusion.1), channel_id=1, source_target_pairs={{0,4},{1,5},{2,3},{3,2},{4,0},{5,1},{6,7},{7,6},{8,12},{9,13},{10,... | collective-permute-start | bytes 1204232 | tf_op jit(solution)/shard_map/ppermute | solution.py:576
  123.5 11.1 %collective-permute-start.37 = (bf16[2,784,128]{2,1,0:T(8,128)(2,1)S(1)}, bf16[2,784,128]{2,1,0:T(8,128)(2,1)S(1)}, u32[]{:S(2)}, u32[]{:S(2)}) collective-permute-start(bf16[2,784,128]{2,1,0:T(8,128)(2,1)S(1)} %add_convert_fusion), channel_id=1, source_target_pairs={{0,4},{1,5},{2,3},{3,2},{4,0},{5,1},{6,7},{7,6},{8,12},{9,13},{10,... | collective-permute-start | bytes 1204232 | tf_op jit(solution)/shard_map/ppermute | solution.py:576
  125.3 8.3 %collective-permute-start.42 = (bf16[784,128]{1,0:T(8,128)(2,1)S(1)}, bf16[784,128]{1,0:T(8,128)(2,1)S(1)}, u32[]{:S(2)}, u32[]{:S(2)}) collective-permute-start(bf16[784,128]{1,0:T(8,128)(2,1)S(1)} %fusion.7), channel_id=1, source_target_pairs={{0,16},{1,17},{2,10},{3,11},{4,20},{5,21},{6,14},{7,15},{8,24},{9,... | collective-permute-start | bytes 602120 | tf_op jit(solution)/shard_map/ppermute | solution.py:576
  129.2 6.3 %collective-permute-start.41 = (bf16[784,128]{1,0:T(8,128)(2,1)S(1)}, bf16[784,128]{1,0:T(8,128)(2,1)S(1)}, u32[]{:S(2)}, u32[]{:S(2)}) collective-permute-start(bf16[784,128]{1,0:T(8,128)(2,1)S(1)} %fusion.8), channel_id=1, source_target_pairs={{0,1},{1,0},{2,6},{3,7},{4,5},{5,4},{6,2},{7,3},{8,9},{9,8},{10,14... | collective-permute-start | bytes 602120 | tf_op jit(solution)/shard_map/ppermute | solution.py:576
  131.8 7.7 %collective-permute-start.47 = (bf16[784,128]{1,0:T(8,128)(2,1)S(1)}, bf16[784,128]{1,0:T(8,128)(2,1)S(1)}, u32[]{:S(2)}, u32[]{:S(2)}) collective-permute-start(bf16[784,128]{1,0:T(8,128)(2,1)S(1)} %fusion.5), channel_id=1, source_target_pairs={{0,16},{1,17},{2,10},{3,11},{4,20},{5,21},{6,14},{7,15},{8,24},{9,... | collective-permute-start | bytes 602120 | tf_op jit(solution)/shard_map/ppermute | solution.py:576
  135.6 8.1 %collective-permute-start.46 = (bf16[784,128]{1,0:T(8,128)(2,1)S(1)}, bf16[784,128]{1,0:T(8,128)(2,1)S(1)}, u32[]{:S(2)}, u32[]{:S(2)}) collective-permute-start(bf16[784,128]{1,0:T(8,128)(2,1)S(1)} %fusion.10), channel_id=1, source_target_pairs={{0,8},{1,9},{2,18},{3,19},{4,12},{5,13},{6,22},{7,23},{8,0},{9,1},... | collective-permute-start | bytes 602120 | tf_op jit(solution)/shard_map/ppermute | solution.py:576
  137.9 5.8 %collective-permute-start.45 = (bf16[784,128]{1,0:T(8,128)(2,1)S(1)}, bf16[784,128]{1,0:T(8,128)(2,1)S(1)}, u32[]{:S(2)}, u32[]{:S(2)}) collective-permute-start(bf16[784,128]{1,0:T(8,128)(2,1)S(1)} %fusion.11), channel_id=1, source_target_pairs={{0,1},{1,0},{2,6},{3,7},{4,5},{5,4},{6,2},{7,3},{8,9},{9,8},{10,14... | collective-permute-start | bytes 602120 | tf_op jit(solution)/shard_map/ppermute | solution.py:576
  (36 other events, 476.7 us)
